TPU v7x, 32 devices: a whole 2x2x4 slice. The times are simulated.
32 devices in a mesh: dp: 2 (over y), seq: 4 (over x, core), ffn: 4 (over z).
Axes of the slice: x: 2, y: 2, z: 4, core: 2. Of those that a mesh axis runs over, the one named last changes fastest.
Arguments:
- tokens: bfloat16 [8, 4096, 768], P(('dp', 'ffn'), 'seq'), may hold values from -6 to 6
- w_query: bfloat16 [768, 768], P(('dp', 'seq', 'ffn')), may hold values from -0.21875 to 0.21875
- w_key: bfloat16 [768, 768], P(('dp', 'seq', 'ffn')), may hold values from -0.21875 to 0.21875
- w_value: bfloat16 [768, 768], P(('dp', 'seq', 'ffn')), may hold values from -0.21875 to 0.21875
- w_output: bfloat16 [768, 768], P(('dp', 'seq', 'ffn')), may hold values from -0.875 to 0.875
- b_query: bfloat16 [768], P(('dp', 'seq', 'ffn')), may hold values from -3 to 3
- b_value: bfloat16 [768], P(('dp', 'seq', 'ffn')), may hold values from -3 to 3
- b_output: bfloat16 [768], P(('dp', 'seq', 'ffn')), may hold values from -3 to 3
- w_up: bfloat16 [768, 3072], P(('dp', 'seq'), 'ffn'), may hold values from -0.21875 to 0.21875
- b_up: bfloat16 [3072], P('ffn'), may hold values from -3 to 3
- w_down: bfloat16 [768, 3072], P(('dp', 'seq'), 'ffn'), may hold values from -0.109375 to 0.109375
- b_down: bfloat16 [768], P(('dp', 'seq', 'ffn')), may hold values from -3 to 3
- gain_attn: bfloat16 [768], P(('dp', 'seq', 'ffn')), may hold values from 0.25 to 1.75
- shift_attn: bfloat16 [768], P(('dp', 'seq', 'ffn')), may hold values from -2 to 2
- gain_ffn: bfloat16 [768], P(('dp', 'seq', 'ffn')), may hold values from 0.25 to 1.75
- shift_ffn: bfloat16 [768], P(('dp', 'seq', 'ffn')), may hold values from -2 to 2
- segment_ids: int32 [8, 4096], P(('dp', 'ffn')), may hold values from 0 to 15, never falling along the last dimension, each value on 1 to 2048 neighbouring positions
- random_blocks: int32 [8, 12, 64, 3], P(('dp', 'ffn'), 'seq'), may hold values from 0 to 63, as said below
- global_blocks: int32 [8, 2], P(('dp', 'ffn')), may hold values from 0 to 63, as said below
- cotangent: bfloat16 [8, 4096, 768], P(('dp', 'ffn'), 'seq'), may hold values from -6 to 6
Outputs:
- output: bfloat16 [8, 4096, 768], P(('dp', 'ffn'), 'seq')
- grad_tokens: float32 [8, 4096, 768], P(('dp', 'ffn'), 'seq')
- grad_w_query: float32 [768, 768], P(('dp', 'seq', 'ffn'))
- grad_w_key: float32 [768, 768], P(('dp', 'seq', 'ffn'))
- grad_w_value: float32 [768, 768], P(('dp', 'seq', 'ffn'))
- grad_w_output: float32 [768, 768], P(('dp', 'seq', 'ffn'))
- grad_b_query: float32 [768], P(('dp', 'seq', 'ffn'))
- grad_b_value: float32 [768], P(('dp', 'seq', 'ffn'))
- grad_b_output: float32 [768], P(('dp', 'seq', 'ffn'))
- grad_w_up: float32 [768, 3072], P(('dp', 'seq'), 'ffn')
- grad_b_up: float32 [3072], P('ffn')
- grad_w_down: float32 [768, 3072], P(('dp', 'seq'), 'ffn')
- grad_b_down: float32 [768], P(('dp', 'seq', 'ffn'))
- grad_gain_attn: float32 [768], P(('dp', 'seq', 'ffn'))
- grad_shift_attn: float32 [768], P(('dp', 'seq', 'ffn'))
- grad_gain_ffn: float32 [768], P(('dp', 'seq', 'ffn'))
- grad_shift_ffn: float32 [768], P(('dp', 'seq', 'ffn'))
Inputs may be any that keep to these rules, and one draw needn't show every extreme that they name: `segment_ids`: numbers never fall along a sequence; a document is the run of positions sharing one number. `random_blocks`: the 3 entries of one query block differ, and none is within one block of the query block or one of the sequence's global blocks. `global_blocks`: two different block numbers of the sequence; sequence 0 has the first and the last block.
All inputs are finite; a program needn't handle non-finite values.
Results may differ from a plain program's by a relative error of at most 0.014.
Values may be sent and summed in bfloat16 or wider, within the bound.
No kernel may reach another device: no remote copies, remote signals or barrier semaphores. Data moves between devices by JAX's collectives and lax.ppermute only.
A program may use at most 256 MiB of HBM per device.

v0:
```python
import jax
import jax.numpy as jnp
from jax import lax
from jax.sharding import PartitionSpec as P

HEAD_DIM = 64
BLOCK = 64


neg_fill = -1e30
norm_eps = 1e-12


def layer_norm(residual, gain, shift):
    center = residual - jnp.mean(residual, axis=-1, keepdims=True)
    spread = jnp.mean(center * center, axis=-1, keepdims=True)
    return center * lax.rsqrt(spread + norm_eps) * gain + shift


def gelu_exact(values):
    return jax.nn.gelu(values, approximate=False)


def contract_rows(left_mat, right_mat):
    return lax.dot_general(
        left_mat, right_mat, (((0,), (0,)), ((), ())), preferred_element_type=jnp.float32
    )


def contract_cols(left_mat, right_mat):
    return lax.dot_general(
        left_mat, right_mat, (((1,), (1,)), ((), ())), preferred_element_type=jnp.float32
    )


def block_tables(global_ids, nblocks):
    blocks = jnp.arange(nblocks, dtype=jnp.int32)
    nearby = blocks[:, None] + jnp.arange(-1, 2, dtype=jnp.int32)[None, :]
    inside = (nearby >= 0) & (nearby < nblocks)
    nearby = jnp.clip(nearby, 0, nblocks - 1)
    hits_glob = jnp.any(nearby[:, :, None] == global_ids[None, None, :], axis=-1)
    return (nearby, inside & jnp.logical_not(hits_glob))


def key_table(nearby, near_ok, rand_head, global_ids):
    nblocks = nearby.shape[0]
    key_index = jnp.concatenate(
        [nearby, rand_head, jnp.broadcast_to(global_ids[None, :], (nblocks, global_ids.shape[0]))],
        axis=1,
    )
    usable = jnp.concatenate(
        [near_ok, jnp.ones((nblocks, rand_head.shape[1] + global_ids.shape[0]), dtype=jnp.bool_)],
        axis=1,
    )
    return (key_index, usable)


def sparse_part(query_blk, key_blk, key_index, usable, seg_blocks, score_scale):
    nblocks, block_rows = (query_blk.shape[0], query_blk.shape[1])
    key_sel = key_blk[key_index].reshape(nblocks, -1, key_blk.shape[-1])
    seg_sel = seg_blocks[key_index].reshape(nblocks, -1)
    usable_keys = jnp.repeat(usable, block_rows, axis=1)
    allowed = usable_keys[:, None, :] & (seg_blocks[:, :, None] == seg_sel[:, None, :])
    scores = (
        jnp.einsum("nqd,nkd->nqk", query_blk, key_sel, preferred_element_type=jnp.float32)
        * score_scale
    )
    return (scores, allowed, key_sel)


def global_part(query_blk, key_flat, global_ids, seg_blocks, seq_ids, score_scale):
    query_glob = query_blk[global_ids]
    allowed = seg_blocks[global_ids][:, :, None] == seq_ids[None, None, :]
    scores = (
        jnp.einsum("gqd,kd->gqk", query_glob, key_flat, preferred_element_type=jnp.float32)
        * score_scale
    )
    return (scores, allowed, query_glob)


def soft_forward(scores, allowed):
    masked = jnp.where(allowed, scores, neg_fill)
    row_peak = jnp.max(masked, axis=-1, keepdims=True)
    exp_terms = jnp.where(allowed, jnp.exp(masked - row_peak), 0.0)
    row_total = jnp.sum(exp_terms, axis=-1, keepdims=True)
    return (exp_terms / row_total, (row_peak + jnp.log(row_total))[..., 0])


def soft_again(scores, allowed, log_total):
    masked = jnp.where(allowed, scores, neg_fill)
    return jnp.where(allowed, jnp.exp(masked - log_total[..., None]), 0.0)


def shards(
    tokens,
    w_query,
    w_key,
    w_value,
    w_output,
    b_query,
    b_value,
    b_output,
    w_up,
    b_up,
    w_down,
    b_down,
    gain_attn,
    shift_attn,
    gain_ffn,
    shift_ffn,
    segment_ids,
    random_blocks,
    global_blocks,
    cotangent,
):
    gathered_params = (
        lax.all_gather(w_query, ("dp", "seq", "ffn"), axis=0, tiled=True),
        lax.all_gather(w_key, ("dp", "seq", "ffn"), axis=0, tiled=True),
        lax.all_gather(w_value, ("dp", "seq", "ffn"), axis=0, tiled=True),
        lax.all_gather(w_output, ("dp", "seq", "ffn"), axis=0, tiled=True),
        lax.all_gather(b_query, ("dp", "seq", "ffn"), axis=0, tiled=True),
        lax.all_gather(b_value, ("dp", "seq", "ffn"), axis=0, tiled=True),
        lax.all_gather(b_output, ("dp", "seq", "ffn"), axis=0, tiled=True),
        lax.all_gather(b_down, ("dp", "seq", "ffn"), axis=0, tiled=True),
        lax.all_gather(gain_attn, ("dp", "seq", "ffn"), axis=0, tiled=True),
        lax.all_gather(shift_attn, ("dp", "seq", "ffn"), axis=0, tiled=True),
        lax.all_gather(gain_ffn, ("dp", "seq", "ffn"), axis=0, tiled=True),
        lax.all_gather(shift_ffn, ("dp", "seq", "ffn"), axis=0, tiled=True),
    )
    (
        query_full,
        key_full,
        value_full,
        output_full,
        bias_query,
        bias_value,
        bias_output,
        bias_down,
        gain_one,
        shift_one,
        gain_two,
        shift_two,
    ) = gathered_params
    bias_query = bias_query.astype(jnp.float32)
    bias_value = bias_value.astype(jnp.float32)
    bias_output = bias_output.astype(jnp.float32)
    bias_down = bias_down.astype(jnp.float32)
    gain_one = gain_one.astype(jnp.float32)
    shift_one = shift_one.astype(jnp.float32)
    gain_two = gain_two.astype(jnp.float32)
    shift_two = shift_two.astype(jnp.float32)
    features = tokens[0]
    query_tok = (
        jnp.dot(features, query_full, preferred_element_type=jnp.float32) + bias_query
    ).astype(jnp.bfloat16)
    key_tok = jnp.dot(features, key_full, preferred_element_type=jnp.float32).astype(jnp.bfloat16)
    value_tok = (
        jnp.dot(features, value_full, preferred_element_type=jnp.float32) + bias_value
    ).astype(jnp.bfloat16)
    query_heads, key_heads, value_heads = (
        lax.all_to_all(query_tok, "seq", split_axis=1, concat_axis=0, tiled=True),
        lax.all_to_all(key_tok, "seq", split_axis=1, concat_axis=0, tiled=True),
        lax.all_to_all(value_tok, "seq", split_axis=1, concat_axis=0, tiled=True),
    )
    seq_ids = segment_ids[0]
    global_ids = global_blocks[0]
    rand_local = random_blocks[0]
    length = seq_ids.shape[0]
    nblocks = length // BLOCK
    seg_blocks = seq_ids.reshape(nblocks, BLOCK)
    nearby, near_ok = block_tables(global_ids, nblocks)
    is_glob = jnp.any(jnp.arange(nblocks, dtype=jnp.int32)[:, None] == global_ids[None, :], axis=1)
    score_scale = HEAD_DIM ** (-0.5)

    def to_blocks(array_in):
        return array_in.reshape(nblocks, BLOCK, -1, HEAD_DIM).transpose(2, 0, 1, 3)

    def from_blocks(array_in):
        return array_in.transpose(1, 2, 0, 3).reshape(length, -1)

    def forward_head(operands):
        query_blk, key_blk, value_blk, rand_head = operands
        key_index, usable = key_table(nearby, near_ok, rand_head, global_ids)
        scores, allowed, key_sel = sparse_part(
            query_blk, key_blk, key_index, usable, seg_blocks, score_scale
        )
        value_sel = value_blk[key_index].reshape(nblocks, -1, HEAD_DIM)
        weights_sparse, lse_sparse = soft_forward(scores, allowed)
        context = jnp.einsum(
            "nqk,nkd->nqd",
            weights_sparse.astype(jnp.bfloat16),
            value_sel,
            preferred_element_type=jnp.float32,
        )
        key_flat = key_blk.reshape(-1, HEAD_DIM)
        value_flat = value_blk.reshape(-1, HEAD_DIM)
        scores_glob, allowed_glob, query_glob = global_part(
            query_blk, key_flat, global_ids, seg_blocks, seq_ids, score_scale
        )
        weights_glob, lse_glob = soft_forward(scores_glob, allowed_glob)
        context_glob = jnp.einsum(
            "gqk,kd->gqd",
            weights_glob.astype(jnp.bfloat16),
            value_flat,
            preferred_element_type=jnp.float32,
        )
        return (context.at[global_ids].set(context_glob), lse_sparse, lse_glob)

    contexts, lse_sparse_all, lse_glob_all = lax.map(
        forward_head,
        (to_blocks(query_heads), to_blocks(key_heads), to_blocks(value_heads), rand_local),
    )
    context_heads = from_blocks(contexts.astype(jnp.bfloat16))
    context_tok = lax.all_to_all(context_heads, "seq", split_axis=0, concat_axis=1, tiled=True)
    branch = jnp.dot(context_tok, output_full, preferred_element_type=jnp.float32) + bias_output
    resid_one = features.astype(jnp.float32) + branch
    normed_one = layer_norm(resid_one, gain_one, shift_one)
    normed_low = normed_one.astype(jnp.bfloat16)
    up_rows, down_rows = (
        lax.all_gather(w_up, ("dp", "seq"), axis=0, tiled=True),
        lax.all_gather(w_down, ("dp", "seq"), axis=0, tiled=True),
    )
    ffn_in = lax.all_gather(normed_low, "ffn", axis=0, tiled=True)
    up_full, down_full, bias_up = (up_rows, down_rows, b_up.astype(jnp.float32))
    pre_act = jnp.dot(ffn_in, up_full, preferred_element_type=jnp.float32) + bias_up
    hidden = gelu_exact(pre_act).astype(jnp.bfloat16)
    ffn_sum = lax.psum_scatter(
        contract_cols(hidden, down_full), "ffn", scatter_dimension=0, tiled=True
    )
    resid_two = normed_one + ffn_sum + bias_down
    normed_two = layer_norm(resid_two, gain_two, shift_two)
    grad_out = cotangent[0].astype(jnp.float32)
    norm_two_back = jax.vjp(layer_norm, resid_two, gain_two, shift_two)[1]
    grad_resid_two, grad_gain_two, grad_shift_two = norm_two_back(grad_out)
    grad_ffn = grad_resid_two.astype(jnp.bfloat16)
    grad_bias_down = jnp.sum(grad_ffn.astype(jnp.float32), axis=0)
    grad_ffn_in = lax.all_gather(grad_ffn, "ffn", axis=0, tiled=True)
    grad_hidden = jnp.dot(grad_ffn_in, down_full, preferred_element_type=jnp.float32)
    grad_down = contract_rows(grad_ffn_in, hidden)
    gelu_back = jax.vjp(gelu_exact, pre_act)[1]
    grad_pre = gelu_back(grad_hidden)[0].astype(jnp.bfloat16)
    grad_up = contract_rows(ffn_in, grad_pre)
    grad_bias_up = jnp.sum(grad_pre.astype(jnp.float32), axis=0)
    grad_normed = lax.psum_scatter(
        contract_cols(grad_pre, up_full), "ffn", scatter_dimension=0, tiled=True
    )
    groups = lax.axis_size(("dp", "seq"))
    bias_tiles = jnp.broadcast_to(grad_bias_up[None, :], (groups, grad_bias_up.shape[0]))
    grad_up, grad_down, bias_tiles = (
        lax.psum_scatter(grad_up, ("dp", "seq"), scatter_dimension=0, tiled=True),
        lax.psum_scatter(grad_down, ("dp", "seq"), scatter_dimension=0, tiled=True),
        lax.psum_scatter(bias_tiles, ("dp", "seq"), scatter_dimension=0, tiled=True),
    )
    grad_bias_up = bias_tiles[0]
    norm_one_back = jax.vjp(layer_norm, resid_one, gain_one, shift_one)[1]
    grad_resid_one, grad_gain_one, grad_shift_one = norm_one_back(grad_resid_two + grad_normed)
    grad_branch = grad_resid_one.astype(jnp.bfloat16)
    grad_bias_output = jnp.sum(grad_branch.astype(jnp.float32), axis=0)
    grad_output_w = contract_rows(context_tok, grad_branch)
    grad_context = contract_cols(grad_branch, output_full).astype(jnp.bfloat16)
    grad_context_heads = lax.all_to_all(
        grad_context, "seq", split_axis=1, concat_axis=0, tiled=True
    )

    def backward_head(operands):
        query_blk, key_blk, value_blk, rand_head, grad_ctx, lse_sparse, lse_glob = operands
        block_rows, head_width = (query_blk.shape[1], query_blk.shape[2])
        key_index, usable = key_table(nearby, near_ok, rand_head, global_ids)
        scores, allowed, key_sel = sparse_part(
            query_blk, key_blk, key_index, usable, seg_blocks, score_scale
        )
        value_sel = value_blk[key_index].reshape(nblocks, -1, head_width)
        weights_sparse = soft_again(scores, allowed, lse_sparse)
        grad_sparse = jnp.where(is_glob[:, None, None], jnp.zeros_like(grad_ctx), grad_ctx)
        grad_weights = jnp.einsum(
            "nqd,nkd->nqk", grad_sparse, value_sel, preferred_element_type=jnp.float32
        )
        shared = jnp.sum(weights_sparse * grad_weights, axis=-1, keepdims=True)
        grad_scores = (weights_sparse * (grad_weights - shared)).astype(jnp.bfloat16)
        grad_query = (
            jnp.einsum("nqk,nkd->nqd", grad_scores, key_sel, preferred_element_type=jnp.float32)
            * score_scale
        )
        grad_key_sel = (
            jnp.einsum("nqk,nqd->nkd", grad_scores, query_blk, preferred_element_type=jnp.float32)
            * score_scale
        )
        grad_value_sel = jnp.einsum(
            "nqk,nqd->nkd",
            weights_sparse.astype(jnp.bfloat16),
            grad_sparse,
            preferred_element_type=jnp.float32,
        )
        grad_key = (
            jnp.zeros((nblocks, block_rows, head_width), jnp.float32)
            .at[key_index]
            .add(grad_key_sel.reshape(nblocks, -1, block_rows, head_width))
        )
        grad_value = (
            jnp.zeros((nblocks, block_rows, head_width), jnp.float32)
            .at[key_index]
            .add(grad_value_sel.reshape(nblocks, -1, block_rows, head_width))
        )
        key_flat = key_blk.reshape(-1, head_width)
        value_flat = value_blk.reshape(-1, head_width)
        scores_glob, allowed_glob, query_glob = global_part(
            query_blk, key_flat, global_ids, seg_blocks, seq_ids, score_scale
        )
        weights_glob = soft_again(scores_glob, allowed_glob, lse_glob)
        grad_glob = grad_ctx[global_ids]
        grad_weights_glob = jnp.einsum(
            "gqd,kd->gqk", grad_glob, value_flat, preferred_element_type=jnp.float32
        )
        shared_glob = jnp.sum(weights_glob * grad_weights_glob, axis=-1, keepdims=True)
        grad_scores_glob = (weights_glob * (grad_weights_glob - shared_glob)).astype(jnp.bfloat16)
        grad_query = grad_query.at[global_ids].add(
            jnp.einsum(
                "gqk,kd->gqd", grad_scores_glob, key_flat, preferred_element_type=jnp.float32
            )
            * score_scale
        )
        grad_key = grad_key + (
            jnp.einsum(
                "gqk,gqd->kd", grad_scores_glob, query_glob, preferred_element_type=jnp.float32
            )
            * score_scale
        ).reshape(nblocks, block_rows, head_width)
        grad_value = grad_value + jnp.einsum(
            "gqk,gqd->kd",
            weights_glob.astype(jnp.bfloat16),
            grad_glob,
            preferred_element_type=jnp.float32,
        ).reshape(nblocks, block_rows, head_width)
        return (grad_query, grad_key, grad_value)

    grad_q_blk, grad_k_blk, grad_v_blk = lax.map(
        backward_head,
        (
            to_blocks(query_heads),
            to_blocks(key_heads),
            to_blocks(value_heads),
            rand_local,
            to_blocks(grad_context_heads),
            lse_sparse_all,
            lse_glob_all,
        ),
    )
    grad_q_tok, grad_k_tok, grad_v_tok = (
        lax.all_to_all(
            from_blocks(grad_q_blk.astype(jnp.bfloat16)),
            "seq",
            split_axis=0,
            concat_axis=1,
            tiled=True,
        ),
        lax.all_to_all(
            from_blocks(grad_k_blk.astype(jnp.bfloat16)),
            "seq",
            split_axis=0,
            concat_axis=1,
            tiled=True,
        ),
        lax.all_to_all(
            from_blocks(grad_v_blk.astype(jnp.bfloat16)),
            "seq",
            split_axis=0,
            concat_axis=1,
            tiled=True,
        ),
    )
    grad_query_w = contract_rows(features, grad_q_tok)
    grad_key_w = contract_rows(features, grad_k_tok)
    grad_value_w = contract_rows(features, grad_v_tok)
    grad_bias_query = jnp.sum(grad_q_tok.astype(jnp.float32), axis=0)
    grad_bias_value = jnp.sum(grad_v_tok.astype(jnp.float32), axis=0)
    grad_features = (
        grad_resid_one
        + contract_cols(grad_q_tok, query_full)
        + contract_cols(grad_k_tok, key_full)
        + contract_cols(grad_v_tok, value_full)
    )
    summed = (
        lax.psum_scatter(grad_query_w, ("dp", "seq", "ffn"), scatter_dimension=0, tiled=True),
        lax.psum_scatter(grad_key_w, ("dp", "seq", "ffn"), scatter_dimension=0, tiled=True),
        lax.psum_scatter(grad_value_w, ("dp", "seq", "ffn"), scatter_dimension=0, tiled=True),
        lax.psum_scatter(grad_output_w, ("dp", "seq", "ffn"), scatter_dimension=0, tiled=True),
        lax.psum_scatter(grad_bias_query, ("dp", "seq", "ffn"), scatter_dimension=0, tiled=True),
        lax.psum_scatter(grad_bias_value, ("dp", "seq", "ffn"), scatter_dimension=0, tiled=True),
        lax.psum_scatter(grad_bias_output, ("dp", "seq", "ffn"), scatter_dimension=0, tiled=True),
        lax.psum_scatter(grad_bias_down, ("dp", "seq", "ffn"), scatter_dimension=0, tiled=True),
        lax.psum_scatter(grad_gain_one, ("dp", "seq", "ffn"), scatter_dimension=0, tiled=True),
        lax.psum_scatter(grad_shift_one, ("dp", "seq", "ffn"), scatter_dimension=0, tiled=True),
        lax.psum_scatter(grad_gain_two, ("dp", "seq", "ffn"), scatter_dimension=0, tiled=True),
        lax.psum_scatter(grad_shift_two, ("dp", "seq", "ffn"), scatter_dimension=0, tiled=True),
    )
    return (
        normed_two.astype(jnp.bfloat16)[None],
        grad_features[None],
        summed[0],
        summed[1],
        summed[2],
        summed[3],
        summed[4],
        summed[5],
        summed[6],
        grad_up,
        grad_bias_up,
        grad_down,
        summed[7],
        summed[8],
        summed[9],
        summed[10],
        summed[11],
    )


def solution(mesh):
    return jax.shard_map(
        shards,
        mesh=mesh,
        in_specs=(
            P(("dp", "ffn"), "seq", None),
            P(("dp", "seq", "ffn"), None),
            P(("dp", "seq", "ffn"), None),
            P(("dp", "seq", "ffn"), None),
            P(("dp", "seq", "ffn"), None),
            P(("dp", "seq", "ffn")),
            P(("dp", "seq", "ffn")),
            P(("dp", "seq", "ffn")),
            P(("dp", "seq"), "ffn"),
            P("ffn"),
            P(("dp", "seq"), "ffn"),
            P(("dp", "seq", "ffn")),
            P(("dp", "seq", "ffn")),
            P(("dp", "seq", "ffn")),
            P(("dp", "seq", "ffn")),
            P(("dp", "seq", "ffn")),
            P(("dp", "ffn"), None),
            P(("dp", "ffn"), "seq", None, None),
            P(("dp", "ffn"), None),
            P(("dp", "ffn"), "seq", None),
        ),
        out_specs=(
            P(("dp", "ffn"), "seq", None),
            P(("dp", "ffn"), "seq", None),
            P(("dp", "seq", "ffn"), None),
            P(("dp", "seq", "ffn"), None),
            P(("dp", "seq", "ffn"), None),
            P(("dp", "seq", "ffn"), None),
            P(("dp", "seq", "ffn")),
            P(("dp", "seq", "ffn")),
            P(("dp", "seq", "ffn")),
            P(("dp", "seq"), "ffn"),
            P("ffn"),
            P(("dp", "seq"), "ffn"),
            P(("dp", "seq", "ffn")),
            P(("dp", "seq", "ffn")),
            P(("dp", "seq", "ffn")),
            P(("dp", "seq", "ffn")),
            P(("dp", "seq", "ffn")),
        ),
        check_vma=False,
    )
```

profile of v0, /device:TPU:0, one launch (start us, length us, event | category | flops | bytes accessed | tf_op | source)
XLA Modules:
  0.0 2412.0 jit_solution(8660120348839061264)
XLA Ops:
  16.1 42.2 %all-reduce.20 = (bf16[768]{0:T(1024)(128)(2,1)S(1)}, bf16[768]{0:T(1024)(128)(2,1)S(1)}, bf16[768]{0:T(1024)(128)(2,1)}, bf16[768]{0:T(1024)(128)(2,1)}, bf16[7...) all-reduce(bf16[768]{0:T(1024)(128)(2,1)S(1)} %dynamic-update-slice, ...), channel_id=1, replica_groups=mesh['dp'=2,'seq'=4,'ffn'=4] {'dp','seq','ffn'}, use_global_device_ids=true, to_apply=%add.2 | all-reduce | flops 6144 | bytes 24576
  75.7 48.1 %all-gather.9.cloned.1.call-done = bf16[768,768]{1,0:T(8,128)(2,1)} async-done(((bf16[24,768]{1,0:T(8,128)(2,1)}), bf16[768,768]{1,0:T(8,128)(2,1)}) %all-gather.9.cloned.1.call-update) | async-done | bytes 1179664 | tf_op jit(solution)/shard_map/all_gather | solution.py:117
  131.2 48.6 %all-gather.11.cloned.1.call-done = bf16[768,768]{1,0:T(8,128)(2,1)} async-done(((bf16[24,768]{1,0:T(8,128)(2,1)}), bf16[768,768]{1,0:T(8,128)(2,1)}) %all-gather.11.cloned.1.call-update) | async-done | bytes 1179664 | tf_op jit(solution)/shard_map/all_gather | solution.py:118
  217.6 194.2 %while.30 = (s32[]{:T(128)}, bf16[3,64,64,64]{3,2,1,0:T(8,128)(2,1)}, f32[3,64,64]{2,1,0:T(8,128)}, f32[3,2,64]{2,1,0:T(2,128)}, pred[64,3]{1,0:T(8,128)(4,1)S(1...) while((s32[]{:T(128)}, ...), condition=%wide.region_7.8_spmd.clone, body=%wide.region_1.7_spmd.clone.sunk | while | flops 719848192 | bytes 111221120 | solution.py:209
  455.5 116.3 %all-gather.17.cloned.1.call-done = bf16[4096,768]{0,1:T(8,128)(2,1)} async-done(((bf16[1024,768]{0,1:T(8,128)(2,1)}), bf16[4096,768]{0,1:T(8,128)(2,1)}) %all-gather.17.cloned.1.call-update) | async-done | bytes 6291472 | tf_op jit(solution)/shard_map/all_gather | solution.py:223
  571.8 35.6 %multiply_convert_fusion.2 = (bf16[4096,768]{1,0:T(8,128)(2,1)}, f32[4096,768]{1,0:T(8,128)}, f32[4096,768]{1,0:T(8,128)}) fusion(f32[768]{0:T(1024)S(1)} %convert_element_type.124, bf16[4096,768]{0,1:T(8,128)(2,1)} %all-gather.17.cloned.1.call-done, bf16[768,768]{1,0:T(8,128)(2,1)} %all-gather.19.cloned.1.call-done), kind=kOutput, calls=%fused_computation.93 | convolution fusion | flops 5039456256 | bytes 38931456 | tf_op jit(solution)/shard_map/dot_general | solution.py:225
  621.0 206.8 %reduce-scatter.15.cloned.1.call-done = f32[1024,768]{0,1:T(8,128)} async-done(((f32[4096,768]{0,1:T(8,128)}), f32[1024,768]{0,1:T(8,128)}) %reduce-scatter.15.cloned.1.call-update) | async-done | bytes 3145744 | tf_op jit(solution)/shard_map/reduce_scatter | solution.py:227
  836.7 116.5 %all-gather.23.cloned.1.call-done = bf16[4096,768]{0,1:T(8,128)(2,1)} async-done(((bf16[1024,768]{0,1:T(8,128)(2,1)}), bf16[4096,768]{0,1:T(8,128)(2,1)}) %all-gather.23.cloned.1.call-update) | async-done | bytes 6291472 | tf_op jit(solution)/shard_map/all_gather | solution.py:237
  1004.1 189.8 %reduce-scatter.17.cloned.1.call-done = f32[1024,768]{0,1:T(8,128)} async-done(((f32[4096,768]{0,1:T(8,128)}), f32[1024,768]{0,1:T(8,128)}) %reduce-scatter.17.cloned.1.call-update) | async-done | bytes 3145744 | tf_op jit(solution)/shard_map/reduce_scatter | solution.py:244
  1214.3 21.7 all-to-all-done.4
  1248.0 810.1 %while.31 = (s32[]{:T(128)}, bf16[3,64,64,64]{3,2,1,0:T(8,128)(2,1)}, bf16[3,64,64,64]{3,2,1,0:T(8,128)(2,1)}, bf16[3,64,64,64]{3,2,1,0:T(8,128)(2,1)}, pred[64,...) while((s32[]{:T(128)}, ...), condition=%wide.region_25.26_spmd.clone, body=%wide.region_19.25_spmd.clone.sunk | while | flops 1716011776 | bytes 317415104 | solution.py:336
  1383.5 78.1 %scatter_fusion.2 = f32[64,64,64]{2,1,0:T(8,128)} fusion(f32[64,64,64]{2,1,0:T(8,128)} %bitcast.384, s32[512]{0:T(512)S(1)} %reshape.926, f32[512,64,64]{2,1,0:T(8,128)} %bitcast.389), kind=kCustom, calls=%fused_computation.14.clone.clone.1 | custom fusion | flops 2097152 | bytes 25167872 | tf_op jit(solution)/shard_map/while/body/eval_jaxpr/scatter-add | solution.py:302
  1473.7 51.9 %scatter_fusion.3 = f32[64,64,64]{2,1,0:T(8,128)S(1)} fusion(f32[64,64,64]{2,1,0:T(8,128)S(1)} %bitcast.383, s32[512]{0:T(512)S(1)} %reshape.926, f32[512,64,64]{2,1,0:T(8,128)} %bitcast.390), kind=kCustom, calls=%fused_computation.13.clone.clone.1 | custom fusion | flops 2097152 | bytes 25167872 | tf_op jit(solution)/shard_map/while/body/eval_jaxpr/scatter-add | solution.py:297
  1644.1 78.1 %scatter_fusion.2 = f32[64,64,64]{2,1,0:T(8,128)} fusion(f32[64,64,64]{2,1,0:T(8,128)} %bitcast.384, s32[512]{0:T(512)S(1)} %reshape.926, f32[512,64,64]{2,1,0:T(8,128)} %bitcast.389), kind=kCustom, calls=%fused_computation.14.clone.clone.1 | custom fusion | flops 2097152 | bytes 25167872 | tf_op jit(solution)/shard_map/while/body/eval_jaxpr/scatter-add | solution.py:302
  1734.3 51.9 %scatter_fusion.3 = f32[64,64,64]{2,1,0:T(8,128)S(1)} fusion(f32[64,64,64]{2,1,0:T(8,128)S(1)} %bitcast.383, s32[512]{0:T(512)S(1)} %reshape.926, f32[512,64,64]{2,1,0:T(8,128)} %bitcast.390), kind=kCustom, calls=%fused_computation.13.clone.clone.1 | custom fusion | flops 2097152 | bytes 25167872 | tf_op jit(solution)/shard_map/while/body/eval_jaxpr/scatter-add | solution.py:297
  1904.7 78.2 %scatter_fusion.2 = f32[64,64,64]{2,1,0:T(8,128)} fusion(f32[64,64,64]{2,1,0:T(8,128)} %bitcast.384, s32[512]{0:T(512)S(1)} %reshape.926, f32[512,64,64]{2,1,0:T(8,128)} %bitcast.389), kind=kCustom, calls=%fused_computation.14.clone.clone.1 | custom fusion | flops 2097152 | bytes 25167872 | tf_op jit(solution)/shard_map/while/body/eval_jaxpr/scatter-add | solution.py:302
  1995.1 51.9 %scatter_fusion.3 = f32[64,64,64]{2,1,0:T(8,128)S(1)} fusion(f32[64,64,64]{2,1,0:T(8,128)S(1)} %bitcast.383, s32[512]{0:T(512)S(1)} %reshape.926, f32[512,64,64]{2,1,0:T(8,128)} %bitcast.390), kind=kCustom, calls=%fused_computation.13.clone.clone.1 | custom fusion | flops 2097152 | bytes 25167872 | tf_op jit(solution)/shard_map/while/body/eval_jaxpr/scatter-add | solution.py:297
  2067.4 22.5 all_to_all.140
  2106.2 22.7 all_to_all.141
  2145.4 23.1 all_to_all.142
  2176.6 23.7 all-reduce.13
  2204.8 40.0 %all-reduce.19 = (f32[768]{0:T(1024)S(1)}, f32[768]{0:T(1024)S(1)}, f32[768]{0:T(1024)S(1)}, f32[768]{0:T(1024)S(1)}, f32[768]{0:T(1024)S(1)}, /*index=5*/f32[768]{0:T(1024)S(1)}, f32[768]{0:T(1024)S(1)}, f32[768]{0:T(1024)S(1)}) all-reduce(f32[768]{0:T(1024)S(1)} %reduce_sum.207, ...), channel_id=8, replica_groups=mesh['dp'=2,'seq'=4,'ffn'=4] {'dp','seq','ffn'}, use_global_device_ids=true, to_apply=%region_31.32.clone | all-reduce | flops 6144 | bytes 49152
  2261.3 39.3 %reduce-scatter.29.cloned.1.call-done = f32[24,768]{1,0:T(8,128)} async-done(((f32[768,768]{1,0:T(8,128)}), f32[24,768]{1,0:T(8,128)}) %reduce-scatter.29.cloned.1.call-update) | async-done | bytes 73744
  2300.6 104.7 %reduce-scatter.27.cloned.1.call-done = f32[24,768]{1,0:T(8,128)} async-done(((f32[768,768]{1,0:T(8,128)}), f32[24,768]{1,0:T(8,128)}) %reduce-scatter.27.cloned.1.call-update) | async-done | bytes 73744
  (610 shorter events, 876.4 us)
Async XLA Ops:
  7.2 60.5 %all-gather.13.cloned.1.call-start = ((), (), s32[]{:S(2)}) async-start(), calls=%async_computation.18 | async-start | bytes 1216512 | tf_op jit(solution)/shard_map/all_gather | solution.py:119
  7.9 115.8 %all-gather.9.cloned.1.call-start = ((), (), s32[]{:S(2)}) async-start(), calls=%async_computation.16 | async-start | bytes 1216512 | tf_op jit(solution)/shard_map/all_gather | solution.py:117
  8.7 171.1 %all-gather.11.cloned.1.call-start = ((), (), s32[]{:S(2)}) async-start(), calls=%async_computation.17 | async-start | bytes 1216512 | tf_op jit(solution)/shard_map/all_gather | solution.py:118
  72.0 51.8 %copy-start.25 = (bf16[1,1024,768]{2,1,0:T(8,128)(2,1)S(1)}, bf16[1,1024,768]{2,1,0:T(8,128)(2,1)}, u32[]{:S(2)}) copy-start(bf16[1,1024,768]{2,1,0:T(8,128)(2,1)} %param.24) | copy-start | bytes 4718596
  72.0 55.6 %all-to-all-start.2 = ((bf16[1024,4,192]{0,2,1:T(8,128)(2,1)}), bf16[1024,4,192]{0,2,1:T(8,128)(2,1)S(1)}, u32[]{:S(2)}, u32[]{:S(2)}) async-start(bf16[1024,4,192]{0,2,1:T(8,128)(2,1)} %bitcast.423), calls=%async_computation.2 | async-start | bytes 3145728 | tf_op jit(solution)/shard_map/all_to_all | solution.py:163
  127.6 56.5 %all-to-all-start = ((bf16[1024,4,192]{0,2,1:T(8,128)(2,1)}), bf16[1024,4,192]{0,2,1:T(8,128)(2,1)S(1)}, u32[]{:S(2)}, u32[]{:S(2)}) async-start(bf16[1024,4,192]{0,2,1:T(8,128)(2,1)} %bitcast.422), calls=%async_computation | async-start | bytes 3145728 | tf_op jit(solution)/shard_map/all_to_all | solution.py:161
  184.1 25.1 %all-to-all-start.1 = ((bf16[1024,4,192]{0,2,1:T(8,128)(2,1)}), bf16[1024,4,192]{0,2,1:T(8,128)(2,1)}, u32[]{:S(2)}, u32[]{:S(2)}) async-start(bf16[1024,4,192]{0,2,1:T(8,128)(2,1)} %bitcast.420), calls=%async_computation.1 | async-start | bytes 3145728 | tf_op jit(solution)/shard_map/all_to_all | solution.py:162
  188.6 239.8 %all-gather.15.cloned.1.call-start = ((), (), s32[]{:S(2)}) async-start(), calls=%async_computation.19 | async-start | bytes 1216512 | tf_op jit(solution)/shard_map/all_gather | solution.py:120
  422.3 25.3 %all-to-all-start.3 = ((bf16[4,1024,192]{1,2,0:T(8,128)(2,1)}), bf16[4,1024,192]{1,2,0:T(8,128)(2,1)S(1)}, u32[]{:S(2)}, u32[]{:S(2)}) async-start(bf16[4,1024,192]{1,2,0:T(8,128)(2,1)} %copy.297), calls=%async_computation.3 | async-start | bytes 3145728 | tf_op jit(solution)/shard_map/all_to_all | solution.py:214
  426.0 29.5 %all-gather.19.cloned.1.call-start = ((), (), s32[]{:S(2)}) async-start(), calls=%async_computation.21 | async-start | bytes 1327104 | tf_op jit(solution)/shard_map/all_gather | solution.py:220
  426.6 145.3 %all-gather.17.cloned.1.call-start = ((), (), s32[]{:S(2)}) async-start(), calls=%async_computation.20 | async-start | bytes 7864320 | tf_op jit(solution)/shard_map/all_gather | solution.py:223
  454.7 152.7 %all-gather.21.cloned.1.call-start = ((), (), s32[]{:S(2)}) async-start(), calls=%async_computation.22 | async-start | bytes 1327104 | tf_op jit(solution)/shard_map/all_gather | solution.py:221
  455.4 372.4 %reduce-scatter.15.cloned.1.call-start = ((), (), s32[]{:S(2)}) async-start(), calls=%async_computation.23 | async-start | bytes 15728640 | tf_op jit(solution)/shard_map/reduce_scatter | solution.py:227
  617.6 335.6 %all-gather.23.cloned.1.call-start = ((), (), s32[]{:S(2)}) async-start(), calls=%async_computation.24 | async-start | bytes 7864320 | tf_op jit(solution)/shard_map/all_gather | solution.py:237
  836.6 357.3 %reduce-scatter.17.cloned.1.call-start = ((), (), s32[]{:S(2)}) async-start(), calls=%async_computation.25 | async-start | bytes 15728640 | tf_op jit(solution)/shard_map/reduce_scatter | solution.py:244
  983.7 1277.6 %reduce-scatter.21.cloned.1.call-start = ((), (), s32[]{:S(2)}) async-start(), calls=%async_computation.27 | async-start | bytes 2654208 | tf_op jit(solution)/shard_map/reduce_scatter | solution.py:250
  994.0 1267.2 %reduce-scatter.23.cloned.1.call-start = ((), (), s32[]{:S(2)}) async-start(), calls=%async_computation.28 | async-start | bytes 2654208 | tf_op jit(solution)/shard_map/reduce_scatter | solution.py:251
  1004.1 196.2 %copy-start.44 = (f32[1024]{0:T(1024)S(1)}, f32[1024]{0:T(1024)}, u32[]{:S(2)}) copy-start(f32[1024]{0:T(1024)} %copy-done.43) | copy-start | bytes 12292
  1206.0 30.1 %all-to-all-start.4 = ((bf16[1024,4,192]{0,2,1:T(8,128)(2,1)}), bf16[1024,4,192]{0,2,1:T(8,128)(2,1)S(1)}, u32[]{:S(2)}, u32[]{:S(2)}) async-start(bf16[1024,4,192]{0,2,1:T(8,128)(2,1)} %bitcast.421), calls=%async_computation.6 | async-start | bytes 3145728 | tf_op jit(solution)/shard_map/all_to_all | solution.py:261
  1209.7 1051.6 %reduce-scatter.19.cloned.1.call-start = ((), (), s32[]{:S(2)}) async-start(), calls=%async_computation.26 | async-start | bytes 2433024 | tf_op jit(solution)/shard_map/reduce_scatter | solution.py:386
  1214.3 1047.0 %reduce-scatter.25.cloned.1.call-start = ((), (), s32[]{:S(2)}) async-start(), calls=%async_computation.29 | async-start | bytes 2433024
  2097.3 203.3 %reduce-scatter.29.cloned.1.call-start = ((), (), s32[]{:S(2)}) async-start(), calls=%async_computation.31 | async-start | bytes 2433024
  2134.8 270.5 %reduce-scatter.27.cloned.1.call-start = ((), (), s32[]{:S(2)}) async-start(), calls=%async_computation.30 | async-start | bytes 2433024
  2176.5 27.5 %copy-start.22 = (bf16[4,1024,192]{1,2,0:T(8,128)(2,1)S(1)}, bf16[4,1024,192]{1,2,0:T(8,128)(2,1)}, u32[]{:S(2)}) copy-start(bf16[4,1024,192]{1,2,0:T(8,128)(2,1)} %copy-done.21) | copy-start | bytes 4718596
  (88 other events, 495.4 us)
Sparse Core Ops, SparseCore 0:
  10.8 56.7 all-gather.12
  70.5 53.2 all-gather.8
  126.6 53.1 all-gather.10
  191.9 54.5 all-gather.14
  428.4 26.0 all-gather.18
  456.5 115.3 all-gather.16
  573.7 22.2 all-gather.20
  617.7 210.0 reduce-scatter.14
  836.7 116.3 all-gather.22
  983.8 210.0 reduce-scatter.16
  1197.8 50.2 reduce-scatter.20
  1252.3 42.4 reduce-scatter.22
  1300.7 99.0 reduce-scatter.18
  2097.4 99.5 reduce-scatter.24
  2202.7 97.9 reduce-scatter.28
  2307.2 98.0 reduce-scatter.26
where the time goes:
time: 2430 us; the launch traced here: 2410 us
  waiting for transfers between devices  924 us (38%)
  local copies, waits for them, and re-layouts  472 us (19%)
  other arithmetic  461 us (19%)
  matrix products  316 us (13%)
  blocking collectives  174 us (7%)
  loops' own time  29.2 us (1%)
    scatter-add x3, other arithmetic, backward_head(): grad_value = jnp.zeros((nblocks, block_rows, head_width), jnp.float32).at...  234 us
    reduce_scatter x1, waiting for transfers between devices, shards(): lax.psum_scatter(contract_cols(hidden, down_full), 'ffn', scatter_dimensi...  207 us
    reduce_scatter x1, waiting for transfers between devices, shards(): lax.psum_scatter(contract_cols(grad_pre, up_full), 'ffn', scatter_dimensi...  190 us
    scatter-add x3, other arithmetic, backward_head(): grad_key = jnp.zeros((nblocks, block_rows, head_width), jnp.float32).at[k...  156 us
    unnamed x19, waiting for transfers between devices  147 us
    all_gather x1, waiting for transfers between devices, shards(): grad_ffn_in = lax.all_gather(grad_ffn, 'ffn', axis=0, tiled=True)  116 us
    all_gather x1, waiting for transfers between devices, shards(): ffn_in = lax.all_gather(normed_low, 'ffn', axis=0, tiled=True)  116 us
    unnamed x3, blocking collectives  106 us
  transfers between devices with their start and end apart: 21, of which 11 were waited for; matrix products, arithmetic and copies ran while one was open for 49% of the time, Pallas kernels for 0%

commit v1 on v0

v1 whole, which is shorter than its diff:
```python
import functools
import jax
import jax.numpy as jnp
from jax import lax
from jax.experimental import pallas as pl
from jax.sharding import PartitionSpec as P
from jax.experimental.pallas import tpu as pltpu

HEAD_DIM = 64
BLOCK = 64
PAIR = 2 * BLOCK
MASKED = -1e30
bf16 = jnp.bfloat16
f32 = jnp.float32


def dot_nn(a, b):
    return lax.dot_general(a, b, (((1,), (0,)), ((), ())), preferred_element_type=f32)


def dot_nt(a, b):
    return lax.dot_general(a, b, (((1,), (1,)), ((), ())), preferred_element_type=f32)


def dot_tn(a, b):
    return lax.dot_general(a, b, (((0,), (0,)), ((), ())), preferred_element_type=f32)


def pair_table(rand_local, global_ids, flip, nblocks):
    heads = rand_local.shape[0]
    null = nblocks
    first = (2 * jnp.arange(nblocks // 2, dtype=jnp.int32)) ^ flip

    def near(block):
        bad = (block < 0) | (block >= nblocks) | (block == global_ids[0]) | (block == global_ids[1])
        return jnp.where(bad, null, block ^ flip)

    rand_first = rand_local[:, first, :] ^ flip
    rand_second = rand_local[:, first + 1, :] ^ flip
    nears = jnp.stack([near(first), near(first + 1), near(first - 1), near(first + 2)], axis=1)
    nears = jnp.broadcast_to(nears[None], (heads,) + nears.shape)
    return jnp.concatenate(
        [nears[:, :, 0:3], rand_first, nears[:, :, 3:4], rand_second], axis=2
    ).astype(jnp.int32).reshape(-1)


def slots(tab_ref, gl_ref, head, pair, npairs):
    at = (head * npairs + pair) * 10
    got = [pl.multiple_of(tab_ref[at + j] * BLOCK, BLOCK) for j in range(10)]
    glob = [pl.multiple_of(gl_ref[j] * BLOCK, BLOCK) for j in range(2)]
    return got[0:2] + glob, got[2:6], got[6:10]


def stack_rows(ref, offsets, lanes):
    return jnp.concatenate([ref[pl.ds(o, BLOCK), lanes] for o in offsets], axis=0)


def lane_halves(width, dtype):
    lane = lax.broadcasted_iota(jnp.int32, (1, width), 1) % PAIR
    first = (lane < BLOCK).astype(dtype)
    second = (lane >= BLOCK).astype(dtype)
    return first, second


def fill_kv(kv_refs, k_sc, v_sc, heads):
    rows = kv_refs[0].shape[0]
    kw = heads * PAIR
    for c, ref in enumerate(kv_refs):
        k_sc[pl.ds(c * rows, rows), :] = ref[:, 0:kw]
        v_sc[pl.ds(c * rows, rows), :] = ref[:, kw:]
    last = len(kv_refs) * rows
    lane = lax.broadcasted_iota(jnp.int32, (BLOCK, kw), 1) % PAIR
    k_sc[pl.ds(last, BLOCK), :] = (lane == BLOCK + 16).astype(f32).astype(bf16)
    v_sc[pl.ds(last, BLOCK), :] = jnp.zeros((BLOCK, v_sc.shape[1]), bf16)


def global_columns(src_ref, rows, gl_ref):
    lane = lax.broadcasted_iota(jnp.int32, (1, PAIR), 1)
    parts = []
    for g in range(2):
        block = gl_ref[g]
        at = pl.multiple_of((block // 2) * PAIR, PAIR)
        both = src_ref[rows, pl.ds(at, PAIR)].astype(f32)
        moved = pltpu.roll(both, BLOCK, 1)
        parts.append(jnp.where(block % 2 == g, both, moved))
    return jnp.where(lane < BLOCK, parts[0], parts[1])


def put_global_columns(dst_ref, rows, gl_ref, value, per_chunk):
    lane = lax.broadcasted_iota(jnp.int32, (1, PAIR), 1)
    moved = pltpu.roll(value, BLOCK, 1)
    for g in range(2):
        block = gl_ref[g]
        pair = block // 2
        half = block % 2
        chunk = pair // per_chunk
        at = pl.multiple_of((pair % per_chunk) * PAIR, PAIR)
        src = jnp.where(half == g, value, moved)
        old = dst_ref[chunk, rows, pl.ds(at, PAIR)].astype(f32)
        new = jnp.where((lane >= BLOCK) == (half == 1), src, old)
        dst_ref[chunk, rows, pl.ds(at, PAIR)] = new.astype(dst_ref.dtype)


def forward_kernel(heads, chunks, tab_ref, gl_ref, *refs):
    kv_refs, q_refs = refs[0:chunks], refs[chunks : 2 * chunks]
    out_ref, lse_ref, lseg_ref, k_sc, v_sc, q_sc, s_sc = refs[2 * chunks :]
    rows = kv_refs[0].shape[0]
    length = rows * chunks
    npairs = length // PAIR
    per_chunk = npairs // chunks
    fill_kv(kv_refs, k_sc, v_sc, heads)
    for c in range(chunks):
        q_sc[:, c * rows : (c + 1) * rows] = q_refs[c][...]
    first, second = lane_halves(PAIR, bf16)
    lane = lax.broadcasted_iota(jnp.int32, (1, PAIR), 1)

    @pl.loop(0, npairs)
    def _(pair):
        chunk = pair // per_chunk
        local = pl.multiple_of((pair % per_chunk) * PAIR, PAIR)
        at = pl.multiple_of(pair * PAIR, PAIR)
        for h in range(heads):
            shared, mine, other = slots(tab_ref, gl_ref, h, pair, npairs)
            kl = slice(h * PAIR, (h + 1) * PAIR)
            vl = slice((h // 2) * PAIR, (h // 2 + 1) * PAIR)
            off = BLOCK * (h % 2)
            q = q_sc[kl, pl.ds(at, PAIR)]
            s_sh = dot_nn(stack_rows(k_sc, shared, kl), q)
            k_pr = jnp.concatenate([stack_rows(k_sc, mine, kl), stack_rows(k_sc, other, kl)], axis=1)
            s_pr = dot_nn(k_pr, jnp.concatenate([q * first, q * second], axis=0))
            peak = jnp.maximum(jnp.max(s_sh, axis=0, keepdims=True), jnp.max(s_pr, axis=0, keepdims=True))
            e_sh = jnp.exp(s_sh - peak)
            e_pr = jnp.exp(s_pr - peak)
            total = jnp.sum(e_sh, axis=0, keepdims=True) + jnp.sum(e_pr, axis=0, keepdims=True)
            inv = 1.0 / total
            p_sh = (e_sh * inv).astype(bf16)
            p_pr = (e_pr * inv).astype(bf16)
            v_pr = jnp.concatenate([stack_rows(v_sc, mine, vl), stack_rows(v_sc, other, vl)], axis=1)
            o_sh = dot_tn(stack_rows(v_sc, shared, vl), p_sh)
            o_pr = dot_tn(v_pr, p_pr)
            ctx = o_sh[off : off + BLOCK] + jnp.where(
                lane < BLOCK, o_pr[off : off + BLOCK], o_pr[PAIR + off : PAIR + off + BLOCK]
            )
            out_ref[chunk, h * BLOCK : (h + 1) * BLOCK, pl.ds(local, PAIR)] = ctx.astype(bf16)
            lse_ref[h, pl.ds(pair, 1), :] = peak + jnp.log(total)

    step = 512
    for h in range(heads):
        kl = slice(h * PAIR, (h + 1) * PAIR)
        vl = slice((h // 2) * PAIR, (h // 2 + 1) * PAIR)
        off = BLOCK * (h % 2)
        q = global_columns(q_sc, kl, gl_ref).astype(bf16)

        def score(c, peak):
            at = pl.multiple_of(c * step, step)
            s = dot_nn(k_sc[pl.ds(at, step), kl], q)
            s_sc[pl.ds(at, step), :] = s
            return jnp.maximum(peak, jnp.max(s, axis=0, keepdims=True))

        peak = lax.fori_loop(0, length // step, score, jnp.full((1, PAIR), MASKED, f32))

        def gather(c, carry):
            total, ctx = carry
            at = pl.multiple_of(c * step, step)
            e = jnp.exp(s_sc[pl.ds(at, step), :] - peak)
            ctx = ctx + dot_tn(v_sc[pl.ds(at, step), vl], e.astype(bf16))
            return total + jnp.sum(e, axis=0, keepdims=True), ctx

        total, ctx = lax.fori_loop(
            0, length // step, gather, (jnp.zeros((1, PAIR), f32), jnp.zeros((PAIR, PAIR), f32))
        )
        ctx = ctx[off : off + BLOCK] * (1.0 / total)
        put_global_columns(out_ref, slice(h * BLOCK, (h + 1) * BLOCK), gl_ref, ctx, per_chunk)
        lseg_ref[h : h + 1, :] = peak + jnp.log(total)


def attention_forward(tab, gl, kv, q):
    chunks = len(kv)
    rows = kv[0].shape[0]
    heads = q[0].shape[0] // PAIR
    vw = kv[0].shape[1] - heads * PAIR
    length = rows * chunks
    whole = lambda: pl.BlockSpec(memory_space=pltpu.VMEM)
    return pl.pallas_call(
        functools.partial(forward_kernel, heads, chunks),
        out_shape=(
            jax.ShapeDtypeStruct((chunks, heads * HEAD_DIM, rows), bf16),
            jax.ShapeDtypeStruct((heads, length // PAIR, PAIR), f32),
            jax.ShapeDtypeStruct((heads, PAIR), f32),
        ),
        in_specs=[pl.BlockSpec(memory_space=pltpu.SMEM)] * 2 + [whole()] * (2 * chunks),
        out_specs=(whole(), whole(), whole()),
        scratch_shapes=[
            pltpu.VMEM((length + BLOCK, heads * PAIR), bf16),
            pltpu.VMEM((length + BLOCK, vw), bf16),
            pltpu.VMEM((heads * PAIR, length), bf16),
            pltpu.VMEM((length, PAIR), f32),
        ],
        compiler_params=pltpu.CompilerParams(vmem_limit_bytes=56 << 20),
        cost_estimate=pl.CostEstimate(flops=8_000_000_000, bytes_accessed=12_000_000, transcendentals=8_000_000),
        name="attention_forward",
    )(tab, gl, *kv, *q)


def backward_kernel(heads, chunks, tab_ref, gl_ref, *refs):
    kv_refs, q_refs, do_refs = refs[0:chunks], refs[chunks : 2 * chunks], refs[2 * chunks : 3 * chunks]
    lse_ref, lseg_ref, dq_ref, dkv_ref, k_sc, v_sc, q_sc, do_sc, acc, p_sc, d_sc, dqg_sc = refs[3 * chunks :]
    rows = kv_refs[0].shape[0]
    length = rows * chunks
    npairs = length // PAIR
    per_chunk = npairs // chunks
    fill_kv(kv_refs, k_sc, v_sc, heads)
    for c in range(chunks):
        q_sc[:, c * rows : (c + 1) * rows] = q_refs[c][...]
        do_sc[:, c * rows : (c + 1) * rows] = do_refs[c][...]
    first, second = lane_halves(PAIR, bf16)
    first2, second2 = lane_halves(2 * PAIR, bf16)
    ffirst, fsecond = lane_halves(PAIR, f32)
    lane = lax.broadcasted_iota(jnp.int32, (1, PAIR), 1)
    zeros = jnp.zeros((BLOCK, PAIR), bf16)

    def value_rows(do, h):
        return jnp.concatenate([do, zeros] if h % 2 == 0 else [zeros, do], axis=0)

    def sources(q, do):
        top = jnp.concatenate([q[0:BLOCK], zeros], axis=1)
        return jnp.concatenate([top, jnp.concatenate([zeros, do], axis=1)], axis=0)

    step = 512
    for h in range(heads):
        kl = slice(h * PAIR, (h + 1) * PAIR)
        vl = slice((h // 2) * PAIR, (h // 2 + 1) * PAIR)
        q = global_columns(q_sc, kl, gl_ref).astype(bf16)
        do = global_columns(do_sc, slice(h * BLOCK, (h + 1) * BLOCK), gl_ref).astype(bf16)
        do_v = value_rows(do, h)
        lse = lseg_ref[h : h + 1, :]
        src = sources(q, do)

        def weigh(c, delta):
            at = pl.multiple_of(c * step, step)
            p = jnp.exp(dot_nn(k_sc[pl.ds(at, step), kl], q) - lse)
            dp = dot_nn(v_sc[pl.ds(at, step), vl], do_v)
            p_sc[pl.ds(at, step), :] = p
            d_sc[pl.ds(at, step), :] = dp
            return delta + jnp.sum(p * dp, axis=0, keepdims=True)

        delta = lax.fori_loop(0, length // step, weigh, jnp.zeros((1, PAIR), f32))

        def spread(c, dq):
            at = pl.multiple_of(c * step, step)
            p = p_sc[pl.ds(at, step), :]
            ds = (p * (d_sc[pl.ds(at, step), :] - delta)).astype(bf16)
            both = jnp.concatenate([ds, p.astype(bf16)], axis=1)
            acc[h, pl.ds(at, step), :] = dot_nt(both, src)
            return dq + dot_tn(k_sc[pl.ds(at, step), kl], ds)

        dq = lax.fori_loop(0, length // step, spread, jnp.zeros((PAIR, PAIR), f32))
        dqg_sc[h] = dq[0:BLOCK] * (HEAD_DIM ** -0.5)
        acc[h, pl.ds(length, BLOCK), :] = jnp.zeros((BLOCK, PAIR), f32)

    @pl.loop(0, npairs)
    def _(pair):
        chunk = pair // per_chunk
        local = pl.multiple_of((pair % per_chunk) * PAIR, PAIR)
        at = pl.multiple_of(pair * PAIR, PAIR)
        hit_first = (gl_ref[0] == 2 * pair) | (gl_ref[1] == 2 * pair)
        hit_second = (gl_ref[0] == 2 * pair + 1) | (gl_ref[1] == 2 * pair + 1)
        shut = ffirst * jnp.where(hit_first, -MASKED, 0.0) + fsecond * jnp.where(hit_second, -MASKED, 0.0)
        for h in range(heads):
            shared, mine, other = slots(tab_ref, gl_ref, h, pair, npairs)
            kl = slice(h * PAIR, (h + 1) * PAIR)
            vl = slice((h // 2) * PAIR, (h // 2 + 1) * PAIR)
            q = q_sc[kl, pl.ds(at, PAIR)]
            do = do_sc[h * BLOCK : (h + 1) * BLOCK, pl.ds(at, PAIR)]
            do_v = value_rows(do, h)
            lse = lse_ref[h, pl.ds(pair, 1), :] + shut
            k_sh = stack_rows(k_sc, shared, kl)
            k_pr = jnp.concatenate([stack_rows(k_sc, mine, kl), stack_rows(k_sc, other, kl)], axis=1)
            p_sh = jnp.exp(dot_nn(k_sh, q) - lse)
            p_pr = jnp.exp(dot_nn(k_pr, jnp.concatenate([q * first, q * second], axis=0)) - lse)
            d_sh = dot_nn(stack_rows(v_sc, shared, vl), do_v)
            v_pr = jnp.concatenate([stack_rows(v_sc, mine, vl), stack_rows(v_sc, other, vl)], axis=1)
            d_pr = dot_nn(v_pr, jnp.concatenate([do_v * first, do_v * second], axis=0))
            delta = jnp.sum(p_sh * d_sh, axis=0, keepdims=True) + jnp.sum(p_pr * d_pr, axis=0, keepdims=True)
            ds_sh = (p_sh * (d_sh - delta)).astype(bf16)
            ds_pr = (p_pr * (d_pr - delta)).astype(bf16)
            src = sources(q, do)
            g_sh = dot_nt(jnp.concatenate([ds_sh, p_sh.astype(bf16)], axis=1), src)
            src2 = jnp.concatenate([src * first2, src * second2], axis=0)
            g_pr = dot_nt(jnp.concatenate([ds_pr, p_pr.astype(bf16)], axis=1), src2)
            for j, o in enumerate(shared):
                acc[h, pl.ds(o, BLOCK), :] += g_sh[j * BLOCK : (j + 1) * BLOCK]
            for j, o in enumerate(mine):
                acc[h, pl.ds(o, BLOCK), :] += g_pr[j * BLOCK : (j + 1) * BLOCK, 0:PAIR]
            for j, o in enumerate(other):
                acc[h, pl.ds(o, BLOCK), :] += g_pr[j * BLOCK : (j + 1) * BLOCK, PAIR:]
            t_sh = dot_tn(k_sh, ds_sh)
            t_pr = dot_tn(k_pr, ds_pr)
            dq = t_sh[0:BLOCK] + jnp.where(lane < BLOCK, t_pr[0:BLOCK], t_pr[PAIR : PAIR + BLOCK])
            dq_ref[chunk, h * BLOCK : (h + 1) * BLOCK, pl.ds(local, PAIR)] = (dq * (HEAD_DIM ** -0.5)).astype(bf16)

    for h in range(heads):
        put_global_columns(dq_ref, slice(h * BLOCK, (h + 1) * BLOCK), gl_ref, dqg_sc[h], per_chunk)
        for c in range(chunks):
            dkv_ref[c, :, h * PAIR : (h + 1) * PAIR] = acc[h, pl.ds(c * rows, rows), :].astype(bf16)


def attention_backward(tab, gl, kv, q, do, lse, lseg):
    chunks = len(kv)
    rows = kv[0].shape[0]
    heads = q[0].shape[0] // PAIR
    vw = kv[0].shape[1] - heads * PAIR
    length = rows * chunks
    whole = lambda: pl.BlockSpec(memory_space=pltpu.VMEM)
    return pl.pallas_call(
        functools.partial(backward_kernel, heads, chunks),
        out_shape=(
            jax.ShapeDtypeStruct((chunks, heads * HEAD_DIM, rows), bf16),
            jax.ShapeDtypeStruct((chunks, rows, heads * PAIR), bf16),
        ),
        in_specs=[pl.BlockSpec(memory_space=pltpu.SMEM)] * 2 + [whole()] * (3 * chunks + 2),
        out_specs=(whole(), whole()),
        scratch_shapes=[
            pltpu.VMEM((length + BLOCK, heads * PAIR), bf16),
            pltpu.VMEM((length + BLOCK, vw), bf16),
            pltpu.VMEM((heads * PAIR, length), bf16),
            pltpu.VMEM((heads * HEAD_DIM, length), bf16),
            pltpu.VMEM((heads, length + BLOCK, PAIR), f32),
            pltpu.VMEM((length, PAIR), f32),
            pltpu.VMEM((length, PAIR), f32),
            pltpu.VMEM((heads, BLOCK, PAIR), f32),
        ],
        compiler_params=pltpu.CompilerParams(vmem_limit_bytes=60 << 20),
        cost_estimate=pl.CostEstimate(flops=25_000_000_000, bytes_accessed=20_000_000, transcendentals=8_000_000),
        name="attention_backward",
    )(tab, gl, *kv, *q, *do, lse, lseg)


def project(chunks_x, segs, w_q, w_kv, b_q, b_v, heads):
    kv_all, q_all = [], []
    kw = heads * PAIR
    for x, seg in zip(chunks_x, segs):
        y = jnp.dot(x, w_kv, preferred_element_type=f32) + b_v
        col = jnp.arange(y.shape[1], dtype=jnp.int32)[None, :]
        spot = col % PAIR - BLOCK
        mark = ((col < kw) & (spot == seg[:, None])).astype(f32)
        kv_all.append((y + mark).astype(bf16))
        z = lax.dot_general(w_q, x, (((0,), (1,)), ((), ())), preferred_element_type=f32) + b_q[:, None]
        row = jnp.arange(z.shape[0], dtype=jnp.int32)[:, None] % PAIR - BLOCK
        barred = (row >= 0) & (row <= 16) & (row != seg[None, :])
        q_all.append(jnp.where(barred, MASKED, z.astype(bf16).astype(f32) * HEAD_DIM ** -0.5).astype(bf16))
    return kv_all, q_all


norm_eps = 1e-12
ALL = ("dp", "seq", "ffn")


def layer_norm(residual, gain, shift):
    center = residual - jnp.mean(residual, axis=-1, keepdims=True)
    spread = jnp.mean(center * center, axis=-1, keepdims=True)
    return center * lax.rsqrt(spread + norm_eps) * gain + shift


def gelu_exact(values):
    return jax.nn.gelu(values, approximate=False)


def flip_send(array, axis, bits):
    count = lax.axis_size(axis)
    return lax.ppermute(array, axis, [(i, i ^ bits) for i in range(count)])


def shards(
    tokens, w_query, w_key, w_value, w_output, b_query, b_value, b_output, w_up, b_up, w_down, b_down,
    gain_attn, shift_attn, gain_ffn, shift_ffn, segment_ids, random_blocks, global_blocks, cotangent,
):
    seq_n, dp_n, ffn_n = lax.axis_size("seq"), lax.axis_size("dp"), lax.axis_size("ffn")
    me = lax.axis_index("seq")
    own, width = w_query.shape
    group = width // seq_n
    heads = group // HEAD_DIM
    features = tokens[0]
    rows = features.shape[0]

    near = [features] + [None] * (seq_n - 1)
    for k in range(1, seq_n):
        bit = k & -k
        near[k] = flip_send(features if bit == k else near[k ^ bit], "seq", bit)

    def by_group(w):
        return w.reshape(own, seq_n, group).transpose(1, 0, 2)

    note = jnp.pad(jnp.stack([b_query, b_value]), ((0, 0), (0, 3 * group - own)))
    pack = jnp.concatenate([by_group(w_query), by_group(w_key), by_group(w_value)], axis=2)
    pack = jnp.concatenate([pack, jnp.broadcast_to(note[None], (seq_n,) + note.shape)], axis=1)
    pack = lax.all_to_all(pack, "seq", split_axis=0, concat_axis=0, tiled=True)
    pack = lax.all_gather(pack, ("dp", "ffn"), axis=0, tiled=False).reshape(
        dp_n, ffn_n, seq_n, own + 2, 3 * group
    ).transpose(0, 2, 1, 3, 4)
    w_own = pack[:, :, :, :own].reshape(width, 3 * group)
    biases = lax.dynamic_slice(
        pack[:, :, :, own:, :own].transpose(3, 0, 1, 2, 4).reshape(2, width), (0, me * group), (2, group)
    ).astype(f32)
    w_q, w_k, w_v = w_own[:, :group], w_own[:, group : 2 * group], w_own[:, 2 * group :]

    def padded(w):
        lead = w.shape[:-1]
        return jnp.pad(w.reshape(lead + (heads, HEAD_DIM)), ((0, 0),) * len(lead) + ((0, 0), (0, HEAD_DIM))).reshape(
            lead + (heads * PAIR,)
        )

    spare = -group % PAIR
    w_kv = jnp.concatenate([padded(w_k), w_v, jnp.zeros((width, spare), bf16)], axis=1)
    b_kv = jnp.concatenate([jnp.zeros((heads * PAIR,), f32), biases[1], jnp.zeros((spare,), f32)])
    seg = segment_ids[0].reshape(seq_n, rows)
    segs = [lax.dynamic_index_in_dim(seg, me ^ k, keepdims=False) for k in range(seq_n)]
    kv, q = project(near, segs, padded(w_q), w_kv, padded(biases[0]), b_kv, heads)

    vectors = jnp.stack([b_output, b_down, gain_attn, shift_attn, gain_ffn, shift_ffn])
    vectors = jnp.pad(vectors, ((0, 0), (0, width - own)))
    rest = jnp.concatenate([w_up, w_down, w_output, b_up[None], vectors], axis=0)
    up_rows = w_up.shape[0]
    rest = lax.all_gather(rest, ALL, axis=0, tiled=False).reshape(dp_n * seq_n, ffn_n, rest.shape[0], width)
    up_blocks = rest[:, :, :up_rows].transpose(1, 0, 2, 3).reshape(ffn_n, width, -1)
    down_blocks = rest[:, :, up_rows : 2 * up_rows].transpose(1, 0, 2, 3).reshape(ffn_n, width, -1)
    at = 2 * up_rows
    output_full = rest[:, :, at : at + own].reshape(width, width)
    bias_up = rest[0, :, at + own].astype(f32)
    vecs = rest[:, :, at + own + 1 :, :own].transpose(2, 0, 1, 3).reshape(6, width).astype(f32)
    bias_output, bias_down, gain_one, shift_one, gain_two, shift_two = [vecs[i] for i in range(6)]

    nblocks = seq_n * rows // BLOCK
    flip = me.astype(jnp.int32) * (nblocks // seq_n)
    tab = pair_table(random_blocks[0], global_blocks[0], flip, nblocks)
    gl = global_blocks[0] ^ flip
    ctx, lse, lseg = attention_forward(tab, gl, kv, q)
    ctx_parts = [ctx[0]] + [flip_send(ctx[k], "seq", k) for k in range(1, seq_n)]
    ctx_tok = jnp.concatenate(ctx_parts, axis=0)
    relative = jnp.arange(seq_n) ^ me
    w_o = output_full.reshape(seq_n, group, width)[relative].reshape(width, width)

    branch = dot_tn(ctx_tok, w_o) + bias_output
    resid_one = features.astype(f32) + branch
    normed_one = layer_norm(resid_one, gain_one, shift_one)
    normed_low = normed_one.astype(bf16)
    pre_act = [dot_nn(normed_low, up_blocks[f]) + bias_up[f] for f in range(ffn_n)]
    hidden = [gelu_exact(p).astype(bf16) for p in pre_act]
    ffn_sum = sum(dot_nt(hidden[f], down_blocks[f]) for f in range(ffn_n))
    resid_two = normed_one + ffn_sum + bias_down
    normed_two = layer_norm(resid_two, gain_two, shift_two)
    grad_resid_two, grad_gain_two, grad_shift_two = jax.vjp(layer_norm, resid_two, gain_two, shift_two)[1](
        cotangent[0].astype(f32)
    )
    grad_ffn = grad_resid_two.astype(bf16)
    grad_bias_down = jnp.sum(grad_ffn.astype(f32), axis=0)
    grad_pre = [
        jax.vjp(gelu_exact, pre_act[f])[1](dot_nn(grad_ffn, down_blocks[f]))[0].astype(bf16) for f in range(ffn_n)
    ]
    grad_normed = sum(dot_nt(grad_pre[f], up_blocks[f]) for f in range(ffn_n))
    grad_resid_one, grad_gain_one, grad_shift_one = jax.vjp(layer_norm, resid_one, gain_one, shift_one)[1](
        grad_resid_two + grad_normed
    )
    grad_branch = grad_resid_one.astype(bf16)
    grad_bias_output = jnp.sum(grad_branch.astype(f32), axis=0)
    grad_ctx = dot_nt(w_o, grad_branch).astype(bf16).reshape(seq_n, group, rows)
    do = [grad_ctx[0]] + [flip_send(grad_ctx[k], "seq", k) for k in range(1, seq_n)]

    grad_down = jnp.stack([dot_tn(grad_ffn, hidden[f]).astype(bf16) for f in range(ffn_n)])
    grad_up = jnp.stack([dot_tn(normed_low, grad_pre[f]).astype(bf16) for f in range(ffn_n)])
    grad_bias_up = jnp.stack([jnp.sum(g.astype(f32), axis=0) for g in grad_pre])
    grad_out = dot_nn(ctx_tok, grad_branch).astype(bf16).reshape(seq_n, group, width)[relative].reshape(width, width)
    outer = dp_n * seq_n

    def placed(g):
        return g.reshape(ffn_n, outer, up_rows, width).transpose(1, 0, 2, 3)

    vec_grads = jnp.stack(
        [grad_bias_output, grad_bias_down, grad_gain_one, grad_shift_one, grad_gain_two, grad_shift_two]
    ).astype(bf16)
    vec_grads = vec_grads.reshape(6, outer, ffn_n, own).transpose(1, 2, 0, 3)
    vec_grads = jnp.pad(vec_grads, ((0, 0), (0, 0), (0, 0), (0, width - own)))
    sums = jnp.concatenate(
        [
            placed(grad_up),
            placed(grad_down),
            grad_out.reshape(outer, ffn_n, own, width),
            jnp.broadcast_to(grad_bias_up.astype(bf16)[None, :, None], (outer, ffn_n, 1, width)),
            vec_grads,
        ],
        axis=2,
    )
    sums = jnp.pad(sums, ((0, 0), (0, 0), (0, -sums.shape[2] % 32), (0, 0)))
    per = sums.shape[2]
    sums = lax.psum_scatter(
        sums.reshape(outer * ffn_n * per, width), ALL, scatter_dimension=0, tiled=True
    ).astype(f32)
    out_up, out_down, out_output = sums[:up_rows], sums[up_rows:at], sums[at : at + own]
    out_bias_up = sums[at + own]
    out_vecs = sums[at + own + 1 : at + own + 7, :own]

    dq, dkv = attention_backward(tab, gl, kv, q, do, lse, lseg)
    w_kv_pairs = jnp.concatenate(
        [w_k.reshape(width, heads, HEAD_DIM), w_v.reshape(width, heads, HEAD_DIM)], axis=2
    ).reshape(width, heads * PAIR)
    part = [
        lax.dot_general(dq[k], w_q, (((0,), (1,)), ((), ())), preferred_element_type=f32) + dot_nt(dkv[k], w_kv_pairs)
        for k in range(seq_n)
    ]
    bit = 1
    while bit < seq_n:
        for k in range(seq_n):
            if k & -k == bit and k != bit:
                part[k ^ bit] = part[k ^ bit] + flip_send(part[k].astype(bf16), "seq", bit).astype(f32)
        bit *= 2
    grad_features = grad_resid_one + part[0]
    bit = 1
    while bit < seq_n:
        grad_features = grad_features + flip_send(part[bit].astype(bf16), "seq", bit).astype(f32)
        bit *= 2

    grad_q = sum(
        lax.dot_general(near[k], dq[k], (((0,), (1,)), ((), ())), preferred_element_type=f32) for k in range(seq_n)
    )
    grad_kv = sum(dot_tn(near[k], dkv[k]) for k in range(seq_n)).reshape(width, heads, 2, HEAD_DIM)
    grad_w = jnp.concatenate(
        [grad_q, grad_kv[:, :, 0].reshape(width, group), grad_kv[:, :, 1].reshape(width, group)], axis=1
    )
    sum_q = jnp.sum(dq.astype(f32), axis=(0, 2))
    sum_v = jnp.sum(dkv.astype(f32), axis=(0, 1)).reshape(heads, 2, HEAD_DIM)[:, 1].reshape(group)
    sum_b = lax.dynamic_update_slice(jnp.zeros((2, width), f32), jnp.stack([sum_q, sum_v]), (0, me * group))
    sum_b = sum_b.reshape(2, dp_n, seq_n, ffn_n, own).transpose(1, 3, 2, 0, 4)
    sum_b = jnp.pad(sum_b, ((0, 0),) * 4 + ((0, 3 * group - own),))
    grad_w = grad_w.reshape(dp_n, seq_n, ffn_n, own, 3 * group).transpose(0, 2, 1, 3, 4)
    grad_w = jnp.concatenate([grad_w, sum_b], axis=3).astype(bf16)
    grad_w = jnp.pad(grad_w, ((0, 0),) * 3 + ((0, -(own + 2) % 32), (0, 0)))
    per = grad_w.shape[3]
    grad_w = lax.psum_scatter(
        grad_w.reshape(dp_n * ffn_n * seq_n * per, 3 * group), ("dp", "ffn"), scatter_dimension=0, tiled=True
    ).reshape(seq_n, per, 3 * group)
    grad_w = lax.all_to_all(grad_w, "seq", split_axis=0, concat_axis=0, tiled=True).astype(f32)
    out_qkv = [
        grad_w[:, :own, i * group : (i + 1) * group].transpose(1, 0, 2).reshape(own, width) for i in range(3)
    ]
    out_b = jnp.sum(grad_w[:, own : own + 2, :own], axis=0)
    return (
        normed_two.astype(bf16)[None],
        grad_features[None],
        out_qkv[0],
        out_qkv[1],
        out_qkv[2],
        out_output,
        out_b[0],
        out_b[1],
        out_vecs[0],
        out_up,
        out_bias_up,
        out_down,
        out_vecs[1],
        out_vecs[2],
        out_vecs[3],
        out_vecs[4],
        out_vecs[5],
    )


def solution(mesh):
    return jax.shard_map(
        shards,
        mesh=mesh,
        in_specs=(
            P(("dp", "ffn"), "seq", None),
            P(("dp", "seq", "ffn"), None),
            P(("dp", "seq", "ffn"), None),
            P(("dp", "seq", "ffn"), None),
            P(("dp", "seq", "ffn"), None),
            P(("dp", "seq", "ffn")),
            P(("dp", "seq", "ffn")),
            P(("dp", "seq", "ffn")),
            P(("dp", "seq"), "ffn"),
            P("ffn"),
            P(("dp", "seq"), "ffn"),
            P(("dp", "seq", "ffn")),
            P(("dp", "seq", "ffn")),
            P(("dp", "seq", "ffn")),
            P(("dp", "seq", "ffn")),
            P(("dp", "seq", "ffn")),
            P(("dp", "ffn"), None),
            P(("dp", "ffn"), "seq", None, None),
            P(("dp", "ffn"), None),
            P(("dp", "ffn"), "seq", None),
        ),
        out_specs=(
            P(("dp", "ffn"), "seq", None),
            P(("dp", "ffn"), "seq", None),
            P(("dp", "seq", "ffn"), None),
            P(("dp", "seq", "ffn"), None),
            P(("dp", "seq", "ffn"), None),
            P(("dp", "seq", "ffn"), None),
            P(("dp", "seq", "ffn")),
            P(("dp", "seq", "ffn")),
            P(("dp", "seq", "ffn")),
            P(("dp", "seq"), "ffn"),
            P("ffn"),
            P(("dp", "seq"), "ffn"),
            P(("dp", "seq", "ffn")),
            P(("dp", "seq", "ffn")),
            P(("dp", "seq", "ffn")),
            P(("dp", "seq", "ffn")),
            P(("dp", "seq", "ffn")),
        ),
        check_vma=False,
    )
```

time: 2430 us -> 675 us (0.28)
  waiting for transfers between devices: 924 us -> 133 us
  other arithmetic: 461 us -> 43.3 us
  local copies, waits for them, and re-layouts: 472 us -> 160 us
  matrix products: 316 us -> 142 us
  blocking collectives: 174 us -> 51.5 us
  Pallas kernels: 0 us -> 106 us
  loops' own time: 29.2 us -> 0 us
    scatter-add x9 -> x0, other arithmetic: 396 us -> none  [the longest x3 234 us: backward_head(): grad_value = jnp.zeros((nblocks, block_rows, head_width), jnp.float32).at...]
    all_gather x8 -> x1, waiting for transfers between devices: 339 us -> 0.01 us  [shards(): lax.all_gather(rest, ALL, axis=0, tiled=False)]
    reduce_scatter x5 -> x2, waiting for transfers between devices: 397 us -> 74.7 us  [the longest x1 74.7 us: shards(): lax.psum_scatter(sums.reshape(outer * ffn_n * per, width), ALL, scatter_d...]
    gather x33 -> x4, local copies, waits for them, and re-layouts: 200 us -> 4.89 us  [the longest x1 2.01 us: shards(): dot_nn(ctx_tok, grad_branch).astype(bf16).reshape(seq_n, group, width)]
    dot_general x57 -> x51, matrix products: 293 us -> 142 us  [the longest x9 54.1 us: dot_nn(): lax.dot_general(a, b, (((1,), (0,)), ((), ())), preferred_element_type=f32)]
    unnamed x19 -> x3, waiting for transfers between devices: 147 us -> 0.05 us
    pallas_call x0 -> x2, Pallas kernels: none -> 106 us  [the longest x1 66.3 us: attention_backward(): pl.pallas_call(functools.partial(backward_kernel, heads, chunks), out_sha...]
    unnamed x3 -> x0, blocking collectives: 106 us -> none
  transfers between devices with their start and end apart: 21 -> 17, of which waited for: 11 -> 5; matrix products, arithmetic and copies ran while one was open for 49% -> 29% of each run, Pallas kernels for 0% -> 6%
where the time goes in v1:
time: 675 us; the launch traced here: 669 us
  local copies, waits for them, and re-layouts  160 us (24%)
  matrix products  142 us (21%)
  waiting for transfers between devices  133 us (20%)
  Pallas kernels  106 us (16%)
  blocking collectives  51.5 us (8%)
  other arithmetic  43.3 us (6%)
  starting transfers between devices  16.3 us (2%)
  between operations  15.8 us (2%)
    reduce_scatter x1, waiting for transfers between devices, shards(): lax.psum_scatter(sums.reshape(outer * ffn_n * per, width), ALL, scatter_d...  74.7 us
    pallas_call x1, Pallas kernels, attention_backward(): pl.pallas_call(functools.partial(backward_kernel, heads, chunks), out_sha...  66.3 us
    dot_general x9, matrix products, dot_nn(): lax.dot_general(a, b, (((1,), (0,)), ((), ())), preferred_element_type=f32)  54.1 us
    all_gather x1, blocking collectives, shards(): lax.all_gather(pack, ('dp', 'ffn'), axis=0, tiled=False)  51.5 us
    concatenate x1, local copies, waits for them, and re-layouts, shards(): jnp.concatenate([placed(grad_up), placed(grad_down), grad_out.reshape(out...  48.8 us
    pallas_call x1, Pallas kernels, attention_forward(): pl.pallas_call(functools.partial(forward_kernel, heads, chunks), out_shap...  40.1 us
    unnamed x250, local copies, waits for them, and re-layouts  33.9 us
    all_to_all x1, waiting for transfers between devices, shards(): pack = lax.all_to_all(pack, 'seq', split_axis=0, concat_axis=0, tiled=True)  29.5 us
  transfers between devices with their start and end apart: 17, of which 5 were waited for; matrix products, arithmetic and copies ran while one was open for 29% of the time, Pallas kernels for 6%

profile of v1, /device:TPU:0, one launch (start us, length us, event | category | flops | bytes accessed | tf_op | source)
XLA Modules:
  0.0 669.3 jit_solution(14510733317206904674)
XLA Ops:
  8.9 5.1 concatenate.58
  39.4 29.5 %all-to-all-done = bf16[4,26,576]{2,1,0:T(8,128)(2,1)S(1)} async-done(((bf16[4,26,576]{2,1,0:T(8,128)(2,1)}), bf16[4,26,576]{2,1,0:T(8,128)(2,1)S(1)}, u32[]{:S(2)}, u32[]{:S(2)}) %all-to-all-start) | async-done | bytes 119840 | tf_op jit(solution)/shard_map/all_to_all | solution.py:397
  68.9 51.5 %all-gather = bf16[32,26,576]{2,1,0:T(8,128)(2,1)S(1)} all-gather(bf16[4,26,576]{2,1,0:T(8,128)(2,1)S(1)} %all-to-all-done), channel_id=2, replica_groups=mesh['dp'=2,'seq'=4,'ffn'=4] {'dp','ffn'}, dimensions={0}, use_global_device_ids=true | all-gather | bytes 1078272 | tf_op jit(solution)/shard_map/all_gather | solution.py:398
  145.9 4.2 fusion.29.refs_2_
  154.8 40.1 %attention_forward.1 = (bf16[4,192,1024]{2,1,0:T(8,128)(2,1)}, f32[3,32,128]{2,1,0:T(8,128)}, f32[3,128]{1,0:T(4,128)}) custom-call(s32[960]{0:T(1024)} %reshape.513.tab_ref, s32[2]{0:T(128)} %xor_bitcast_fusion.2.gl_ref, bf16[1024,640]{1,0:T(8,128)(2,1)} %fusion.31.refs_0_, bf16[1024,640]{1,0:T(8,128)(2,1)} %fusion.30.refs_1_, ...), custom_call_target="tpu_custom_call" | custom-call | flops 8000000000 | bytes 12000000 | tf_op jit(solution)/shard_map/attention_forward/pallas_call | solution.py:184
  206.2 8.3 %slice_bitcast_fusion = (bf16[4,8,96,768]{3,2,0,1:T(8,128)(2,1)}, bf16[4,8,96,768]{3,2,0,1:T(8,128)(2,1)}) fusion(bf16[8,4,223,768]{3,2,1,0:T(8,128)(2,1)} %bitcast.311), kind=kLoop, calls=%fused_computation.11 | loop fusion | bytes 18874368 | tf_op jit(solution)/shard_map/transpose | solution.py:426
  220.9 5.2 fusion.144
  226.8 9.8 %multiply_convert_fusion = (bf16[1024,768]{1,0:T(8,128)(2,1)S(1)}, f32[1024,768]{1,0:T(8,128)}, f32[1024,768]{1,0:T(8,128)}) fusion(f32[768]{0:T(1024)S(1)} %get-tuple-element.142, bf16[1024,768]{0,1:T(8,128)(2,1)S(1)} %fusion.33, bf16[768,768]{1,0:T(8,128)(2,1)S(1)} %bitcast.318), kind=kOutput, calls=%fused_computation.40 | convolution fusion | flops 1259864064 | bytes 10619904 | tf_op jit(solution)/shard_map/dot_general | solution.py:18
  236.6 10.0 %multiply_convert_fusion.1 = (bf16[1024,768]{1,0:T(8,128)(2,1)S(1)}, f32[1024,768]{1,0:T(8,128)}, f32[1024,768]{1,0:T(8,128)}) fusion(f32[768]{0:T(1024)S(1)} %copy-done.88, bf16[1024,768]{0,1:T(8,128)(2,1)S(1)} %fusion.33, bf16[768,768]{1,0:T(8,128)(2,1)S(1)} %bitcast.338), kind=kOutput, calls=%fused_computation.53 | convolution fusion | flops 1259864064 | bytes 10619904 | tf_op jit(solution)/shard_map/dot_general | solution.py:18
  248.1 10.1 %multiply_convert_fusion.3 = (bf16[1024,768]{1,0:T(8,128)(2,1)S(1)}, f32[1024,768]{1,0:T(8,128)}, f32[1024,768]{1,0:T(8,128)}) fusion(f32[768]{0:T(1024)S(1)} %copy-done.86, bf16[1024,768]{0,1:T(8,128)(2,1)S(1)} %fusion.33, bf16[768,768]{1,0:T(8,128)(2,1)S(1)} %bitcast.330), kind=kOutput, calls=%fused_computation.79 | convolution fusion | flops 1259864064 | bytes 10619904 | tf_op jit(solution)/shard_map/dot_general | solution.py:18
  259.6 9.9 %multiply_convert_fusion.2 = (bf16[1024,768]{1,0:T(8,128)(2,1)S(1)}, f32[1024,768]{1,0:T(8,128)}, f32[1024,768]{1,0:T(8,128)}) fusion(f32[768]{0:T(1024)S(1)} %copy-done.87, bf16[1024,768]{0,1:T(8,128)(2,1)S(1)} %fusion.33, bf16[768,768]{1,0:T(8,128)(2,1)S(1)} %bitcast.334), kind=kOutput, calls=%fused_computation.66 | convolution fusion | flops 1259864064 | bytes 10619904 | tf_op jit(solution)/shard_map/dot_general | solution.py:18
  279.7 3.9 fusion.3
  312.8 4.0 multiply_reduce_fusion
  325.5 3.7 convolution_convert_fusion.1
  334.7 3.8 convolution_convert_fusion.9
  342.1 66.3 %attention_backward.1 = (bf16[4,192,1024]{2,1,0:T(8,128)(2,1)}, bf16[4,1024,384]{2,1,0:T(8,128)(2,1)}) custom-call(s32[960]{0:T(1024)} %reshape.513.tab_ref, s32[2]{0:T(128)} %xor_bitcast_fusion.2.gl_ref, bf16[1024,640]{1,0:T(8,128)(2,1)} %fusion.31.refs_0_, bf16[1024,640]{1,0:T(8,128)(2,1)} %fusion.30.refs_1_, bf16[1024,640]{1,0:T(8,128)(2,1)} %fusion.29.refs_2_, ...), custom_call_target="tpu_custom_call" | custom-call | flops 24999999488 | bytes 20000000 | tf_op jit(solution)/shard_map/attention_backward/pallas_call | solution.py:315
  453.3 48.8 %concatenate.65 = bf16[8,4,223,768]{3,2,0,1:T(8,128)(2,1)} concatenate(bf16[8,4,96,768]{3,2,0,1:T(8,128)(2,1)} %maximum_bitcast_fusion, bf16[8,4,96,768]{3,2,0,1:T(8,128)(2,1)} %maximum_bitcast_fusion.1, bf16[8,4,24,768]{3,2,0,1:T(8,128)(2,1)} %copy.256, bf16[8,4,1,768]{3,2,0,1:T(2,128)(2,1)} %broadcast_in_dim.57, bf16[8,4,6,768]{3,2,0,1:T(8,128)(2,1)S(1)} %copy-done.32), dimensions={2} | concatenate | bytes 21921792 | tf_op jit(solution)/shard_map/concatenate | solution.py:483
  502.1 6.0 copy.282
  508.1 5.2 pad.44.clone
  526.1 3.8 fusion.74
  529.9 4.0 all-to-all-start.1
  537.5 23.6 %all-to-all-done.1 = bf16[4,32,576]{2,1,0:T(8,128)(2,1)} async-done(((bf16[4,32,576]{2,1,0:T(8,128)(2,1)}), bf16[4,32,576]{2,1,0:T(8,128)(2,1)}, u32[]{:S(2)}, u32[]{:S(2)}) %all-to-all-start.1) | async-done | bytes 147488 | tf_op jit(solution)/shard_map/all_to_all | solution.py:541
  572.1 6.9 %add_bitcast_fusion = f32[1,1024,768]{1,2,0:T(8,128)} fusion(bf16[1024,768]{0,1:T(8,128)(2,1)} %collective-permute-done.11, bf16[1024,768]{0,1:T(8,128)(2,1)} %collective-permute-done.9, f32[1024,768]{0,1:T(8,128)} %fusion.93, f32[1024,768]{0,1:T(8,128)} %fusion.74, f32[1024,768]{0,1:T(8,128)S(1)} %copy-done.5, f32[1024]{0:T(1024)S(1)} %copy-done.68), kind=kLoop, calls=%fused_computation.27 | loop fusion | flops 5505024 | bytes 15732736 | tf_op jit(solution)/shard_map/broadcast_in_dim | solution.py:548
  582.5 74.7 %reduce-scatter.5.cloned.1.call-done = bf16[224,768]{1,0:T(8,128)(2,1)} async-done(((bf16[7168,768]{1,0:T(8,128)(2,1)}), bf16[224,768]{1,0:T(8,128)(2,1)}) %reduce-scatter.5.cloned.1.call-update) | async-done | bytes 344080 | tf_op jit(solution)/shard_map/reduce_scatter | solution.py:495
  (461 shorter events, 215.0 us)
Async XLA Ops:
  7.3 191.2 %all-gather.5.cloned.1.call-start = ((), (), s32[]{:S(2)}) async-start(), calls=%async_computation.6 | async-start | bytes 11354112 | tf_op jit(solution)/shard_map/all_gather | solution.py:424
  16.6 124.7 %collective-permute-start = (bf16[1024,768]{0,1:T(8,128)(2,1)}, bf16[1024,768]{0,1:T(8,128)(2,1)S(1)}, u32[]{:S(2)}, u32[]{:S(2)}) collective-permute-start(bf16[1024,768]{0,1:T(8,128)(2,1)} %bitcast.322), channel_id=1, source_target_pairs={{0,4},{4,0},{8,12},{12,8},{1,5},{5,1},{9,13},{13,9},{2,6},{6,2},{1... | collective-permute-start | bytes 4718600 | tf_op jit(solution)/shard_map/ppermute | solution.py:371
  17.0 119.1 %collective-permute-start.1 = (bf16[1024,768]{0,1:T(8,128)(2,1)}, bf16[1024,768]{0,1:T(8,128)(2,1)}, u32[]{:S(2)}, u32[]{:S(2)}) collective-permute-start(bf16[1024,768]{0,1:T(8,128)(2,1)} %bitcast.323), channel_id=1, source_target_pairs={{0,8},{4,12},{8,0},{12,4},{1,9},{5,13},{9,1},{13,5},{2,10},{6,14},... | collective-permute-start | bytes 4718600 | tf_op jit(solution)/shard_map/ppermute | solution.py:371
  20.8 48.0 %all-to-all-start = ((bf16[4,26,576]{2,1,0:T(8,128)(2,1)}), bf16[4,26,576]{2,1,0:T(8,128)(2,1)S(1)}, u32[]{:S(2)}, u32[]{:S(2)}) async-start(bf16[4,26,576]{2,1,0:T(8,128)(2,1)} %copy.223), calls=%async_computation | async-start | bytes 327680 | tf_op jit(solution)/shard_map/all_to_all | solution.py:397
  24.3 505.6 %reduce-scatter.3.cloned.1.call-start = ((), (), s32[]{:S(2)}) async-start(), calls=%async_computation.4 | async-start | bytes 1474560 | tf_op jit(solution)/shard_map/reduce_scatter | solution.py:538
  37.7 166.8 %copy-start.82 = (s32[1024]{0:T(1024)}, s32[1024]{0:T(1024)S(1)}, u32[]{:S(2)}) copy-start(s32[1024]{0:T(1024)S(1)} %pad_clamp_fusion) | copy-start | bytes 12292
  136.2 14.0 %collective-permute-start.2 = (bf16[1024,768]{0,1:T(8,128)(2,1)}, bf16[1024,768]{0,1:T(8,128)(2,1)S(1)}, u32[]{:S(2)}, u32[]{:S(2)}) collective-permute-start(bf16[1024,768]{0,1:T(8,128)(2,1)} %collective-permute-done.1), channel_id=1, source_target_pairs={{0,4},{4,0},{8,12},{12,8},{1,5},{5,1},{9,13},{13,9},{2,6},{6,2},{1... | collective-permute-start | bytes 4718600 | tf_op jit(solution)/shard_map/ppermute | solution.py:371
  196.3 18.2 %collective-permute-start.5 = (bf16[192,1024]{1,0:T(8,128)(2,1)S(1)}, bf16[192,1024]{1,0:T(8,128)(2,1)S(1)}, u32[]{:S(2)}, u32[]{:S(2)}) collective-permute-start(bf16[192,1024]{1,0:T(8,128)(2,1)S(1)} %get-tuple-element.184), channel_id=1, source_target_pairs={{0,12},{4,8},{8,4},{12,0},{1,13},{5,9},{9,5},{13,1},{2,14},{6,10},... | collective-permute-start | bytes 1179656 | tf_op jit(solution)/shard_map/ppermute | solution.py:371
  197.4 19.0 %collective-permute-start.4 = (bf16[192,1024]{1,0:T(8,128)(2,1)S(1)}, bf16[192,1024]{1,0:T(8,128)(2,1)}, u32[]{:S(2)}, u32[]{:S(2)}) collective-permute-start(bf16[192,1024]{1,0:T(8,128)(2,1)S(1)} %get-tuple-element.185), channel_id=1, source_target_pairs={{0,8},{4,12},{8,0},{12,4},{1,9},{5,13},{9,1},{13,5},{2,10},{6,14},... | collective-permute-start | bytes 1179656 | tf_op jit(solution)/shard_map/ppermute | solution.py:371
  198.5 17.8 %collective-permute-start.3 = (bf16[192,1024]{1,0:T(8,128)(2,1)S(1)}, bf16[192,1024]{1,0:T(8,128)(2,1)}, u32[]{:S(2)}, u32[]{:S(2)}) collective-permute-start(bf16[192,1024]{1,0:T(8,128)(2,1)S(1)} %get-tuple-element.186), channel_id=1, source_target_pairs={{0,4},{4,0},{8,12},{12,8},{1,5},{5,1},{9,13},{13,9},{2,6},{6,2},{1... | collective-permute-start | bytes 1179656 | tf_op jit(solution)/shard_map/ppermute | solution.py:371
  226.2 31.9 %copy-start.39 = (bf16[1,8,96,768]{3,2,0,1:T(8,128)(2,1)}, bf16[1,8,96,768]{3,2,0,1:T(8,128)(2,1)S(1)}, u32[]{:S(2)}) copy-start(bf16[1,8,96,768]{3,2,0,1:T(8,128)(2,1)S(1)} %get-tuple-element.173) | copy-start | bytes 3538948
  226.2 33.4 %copy-start.41 = (bf16[1,8,96,768]{3,2,0,1:T(8,128)(2,1)}, bf16[1,8,96,768]{3,2,0,1:T(8,128)(2,1)S(1)}, u32[]{:S(2)}) copy-start(bf16[1,8,96,768]{3,2,0,1:T(8,128)(2,1)S(1)} %get-tuple-element.231) | copy-start | bytes 3538948
  226.7 32.9 %copy-start.29 = (bf16[1024,768]{0,1:T(8,128)(2,1)}, bf16[1024,768]{0,1:T(8,128)(2,1)S(1)}, u32[]{:S(2)}) copy-start(bf16[1024,768]{0,1:T(8,128)(2,1)S(1)} %fusion.33) | copy-start | bytes 4718596
  236.6 34.5 %copy-start.20 = (bf16[1024,768]{1,0:T(8,128)(2,1)}, bf16[1024,768]{1,0:T(8,128)(2,1)S(1)}, u32[]{:S(2)}) copy-start(bf16[1024,768]{1,0:T(8,128)(2,1)S(1)} %get-tuple-element.160) | copy-start | bytes 4718596
  322.4 16.1 %collective-permute-start.6 = (bf16[192,1024]{1,0:T(8,128)(2,1)}, bf16[192,1024]{1,0:T(8,128)(2,1)}, u32[]{:S(2)}, u32[]{:S(2)}) collective-permute-start(bf16[192,1024]{1,0:T(8,128)(2,1)} %get-tuple-element.181), channel_id=1, source_target_pairs={{0,4},{4,0},{8,12},{12,8},{1,5},{5,1},{9,13},{13,9},{2,6},{6,2},{1... | collective-permute-start | bytes 1179656 | tf_op jit(solution)/shard_map/ppermute | solution.py:371
  322.4 16.1 %collective-permute-start.7 = (bf16[192,1024]{1,0:T(8,128)(2,1)S(1)}, bf16[192,1024]{1,0:T(8,128)(2,1)}, u32[]{:S(2)}, u32[]{:S(2)}) collective-permute-start(bf16[192,1024]{1,0:T(8,128)(2,1)S(1)} %get-tuple-element.180), channel_id=1, source_target_pairs={{0,8},{4,12},{8,0},{12,4},{1,9},{5,13},{9,1},{13,5},{2,10},{6,14},... | collective-permute-start | bytes 1179656 | tf_op jit(solution)/shard_map/ppermute | solution.py:371
  323.3 18.8 %collective-permute-start.8 = (bf16[192,1024]{1,0:T(8,128)(2,1)S(1)}, bf16[192,1024]{1,0:T(8,128)(2,1)}, u32[]{:S(2)}, u32[]{:S(2)}) collective-permute-start(bf16[192,1024]{1,0:T(8,128)(2,1)S(1)} %get-tuple-element.179), channel_id=1, source_target_pairs={{0,12},{4,8},{8,4},{12,0},{1,13},{5,9},{9,5},{13,1},{2,14},{6,10},... | collective-permute-start | bytes 1179656 | tf_op jit(solution)/shard_map/ppermute | solution.py:371
  438.8 218.3 %reduce-scatter.5.cloned.1.call-start = ((), (), s32[]{:S(2)}) async-start(), calls=%async_computation.5 | async-start | bytes 11354112 | tf_op jit(solution)/shard_map/reduce_scatter | solution.py:495
  516.2 4.6 collective-permute-start.10
  519.4 52.6 %collective-permute-start.9 = (bf16[1024,768]{0,1:T(8,128)(2,1)}, bf16[1024,768]{0,1:T(8,128)(2,1)}, u32[]{:S(2)}, u32[]{:S(2)}) collective-permute-start(bf16[1024,768]{0,1:T(8,128)(2,1)} %add_convert_fusion.2), channel_id=1, source_target_pairs={{0,4},{4,0},{8,12},{12,8},{1,5},{5,1},{9,13},{13,9},{2,6},{6,2},{1... | collective-permute-start | bytes 4718600 | tf_op jit(solution)/shard_map/ppermute | solution.py:371
  522.5 49.5 %collective-permute-start.11 = (bf16[1024,768]{0,1:T(8,128)(2,1)}, bf16[1024,768]{0,1:T(8,128)(2,1)}, u32[]{:S(2)}, u32[]{:S(2)}) collective-permute-start(bf16[1024,768]{0,1:T(8,128)(2,1)} %add_convert_fusion), channel_id=1, source_target_pairs={{0,8},{4,12},{8,0},{12,4},{1,9},{5,13},{9,1},{13,5},{2,10},{6,14},... | collective-permute-start | bytes 4718600 | tf_op jit(solution)/shard_map/ppermute | solution.py:371
  529.9 31.2 %all-to-all-start.1 = ((bf16[4,32,576]{2,1,0:T(8,128)(2,1)}), bf16[4,32,576]{2,1,0:T(8,128)(2,1)}, u32[]{:S(2)}, u32[]{:S(2)}) async-start(bf16[4,32,576]{2,1,0:T(8,128)(2,1)} %bitcast.366), calls=%async_computation.2 | async-start | bytes 327680 | tf_op jit(solution)/shard_map/all_to_all | solution.py:541
  533.9 38.2 %copy-start.5 = (f32[1024,768]{0,1:T(8,128)S(1)}, f32[1024,768]{0,1:T(8,128)}, u32[]{:S(2)}) copy-start(f32[1024,768]{0,1:T(8,128)} %copy-done.4) | copy-start | bytes 9437188
  533.9 38.2 %copy-start.68 = (f32[1024]{0:T(1024)S(1)}, f32[1024]{0:T(1024)}, u32[]{:S(2)}) copy-start(f32[1024]{0:T(1024)} %copy-done.67) | copy-start | bytes 12292
  (110 other events, 593.7 us)
Sparse Core Ops, SparseCore 0:
  14.1 119.4 all-gather.4
  439.0 63.6 reduce-scatter.2
  513.4 143.6 reduce-scatter.4

commit v2 on v1

v2 whole, which is shorter than its diff:
```python
import functools
import jax
import jax.numpy as jnp
from jax import lax
from jax.experimental import pallas as pl
from jax.sharding import PartitionSpec as P
from jax.experimental.pallas import tpu as pltpu

HEAD_DIM = 64
BLOCK = 64
PAIR = 2 * BLOCK
MASKED = -1e30
bf16 = jnp.bfloat16
f32 = jnp.float32


def dot_nn(a, b):
    return lax.dot_general(a, b, (((1,), (0,)), ((), ())), preferred_element_type=f32)


def dot_nt(a, b):
    return lax.dot_general(a, b, (((1,), (1,)), ((), ())), preferred_element_type=f32)


def dot_tn(a, b):
    return lax.dot_general(a, b, (((0,), (0,)), ((), ())), preferred_element_type=f32)


def pair_table(rand_local, global_ids, flip, nblocks):
    heads = rand_local.shape[0]
    null = nblocks
    first = (2 * jnp.arange(nblocks // 2, dtype=jnp.int32)) ^ flip

    def near(block):
        bad = (block < 0) | (block >= nblocks) | (block == global_ids[0]) | (block == global_ids[1])
        return jnp.where(bad, null, block ^ flip)

    rand_first = rand_local[:, first, :] ^ flip
    rand_second = rand_local[:, first + 1, :] ^ flip
    nears = jnp.stack([near(first), near(first + 1), near(first - 1), near(first + 2)], axis=1)
    nears = jnp.broadcast_to(nears[None], (heads,) + nears.shape)
    return jnp.concatenate(
        [nears[:, :, 0:3], rand_first, nears[:, :, 3:4], rand_second], axis=2
    ).astype(jnp.int32).reshape(-1)


def slots(tab_ref, gl_ref, head, pair, npairs):
    at = (head * npairs + pair) * 10
    got = [pl.multiple_of(tab_ref[at + j] * BLOCK, BLOCK) for j in range(10)]
    glob = [pl.multiple_of(gl_ref[j] * BLOCK, BLOCK) for j in range(2)]
    return got[0:2] + glob, got[2:6], got[6:10]


def stack_rows(ref, offsets, lanes):
    return jnp.concatenate([ref[pl.ds(o, BLOCK), lanes] for o in offsets], axis=0)


def lane_halves(width, dtype):
    lane = lax.broadcasted_iota(jnp.int32, (1, width), 1) % PAIR
    first = (lane < BLOCK).astype(dtype)
    second = (lane >= BLOCK).astype(dtype)
    return first, second


VALUE_GROUP = (0, 0, 1)
VALUE_ROW = (0, BLOCK, BLOCK)


def key_lanes(h):
    return slice(h * PAIR, (h + 1) * PAIR)


def value_lanes(h):
    return slice(VALUE_GROUP[h] * PAIR, (VALUE_GROUP[h] + 1) * PAIR)


def query_columns(q_ref, mask_ref, h, at):
    return jnp.concatenate([q_ref[h * BLOCK : (h + 1) * BLOCK, pl.ds(at, PAIR)], mask_ref[:, pl.ds(at, PAIR)]], axis=0)


def global_queries(q_ref, mask_ref, h, gl_ref):
    return jnp.concatenate(
        [
            global_columns(q_ref, slice(h * BLOCK, (h + 1) * BLOCK), gl_ref),
            global_columns(mask_ref, slice(0, BLOCK), gl_ref),
        ],
        axis=0,
    ).astype(bf16)


def global_columns(src_ref, rows, gl_ref):
    lane = lax.broadcasted_iota(jnp.int32, (1, PAIR), 1)
    parts = []
    for g in range(2):
        block = gl_ref[g]
        at = pl.multiple_of((block // 2) * PAIR, PAIR)
        both = src_ref[rows, pl.ds(at, PAIR)].astype(f32)
        moved = pltpu.roll(both, BLOCK, 1)
        parts.append(jnp.where(block % 2 == g, both, moved))
    return jnp.where(lane < BLOCK, parts[0], parts[1])


def put_global_columns(dst_ref, rows, gl_ref, value, per_chunk):
    lane = lax.broadcasted_iota(jnp.int32, (1, PAIR), 1)
    moved = pltpu.roll(value, BLOCK, 1)
    for g in range(2):
        block = gl_ref[g]
        pair = block // 2
        half = block % 2
        chunk = pair // per_chunk
        at = pl.multiple_of((pair % per_chunk) * PAIR, PAIR)
        src = jnp.where(half == g, value, moved)
        old = dst_ref[chunk, rows, pl.ds(at, PAIR)].astype(f32)
        new = jnp.where((lane >= BLOCK) == (half == 1), src, old)
        dst_ref[chunk, rows, pl.ds(at, PAIR)] = new.astype(dst_ref.dtype)


def project_rows(x, seg, wkv_ref, bkv_ref, wq_ref, bq_ref, k_ref, v_ref, q_ref, mask_ref, at):
    n = x.shape[0]
    y = dot_nn(x, wkv_ref[...]) + bkv_ref[...]
    spot = lax.broadcasted_iota(jnp.int32, (PAIR, n), 0) - BLOCK
    mark = jnp.transpose((spot == seg).astype(f32), (1, 0))
    lane = lax.broadcasted_iota(jnp.int32, (1, PAIR), 1)
    rows = pl.ds(at, n)
    k_ref[rows, 0:PAIR] = (y[:, 0:PAIR] + mark).astype(bf16)
    k_ref[rows, PAIR : 2 * PAIR] = (y[:, PAIR : 2 * PAIR] + mark).astype(bf16)
    both = y[:, 2 * PAIR : 3 * PAIR]
    k_ref[rows, 2 * PAIR : 3 * PAIR] = jnp.where(lane < BLOCK, both, mark).astype(bf16)
    v_ref[rows, 0:PAIR] = y[:, 3 * PAIR : 4 * PAIR].astype(bf16)
    v_ref[rows, PAIR : 2 * PAIR] = both.astype(bf16)
    z = (dot_nt(wq_ref[...], x) + bq_ref[...]).astype(bf16)
    q_ref[:, rows] = (z.astype(f32) * HEAD_DIM ** -0.5).astype(bf16)
    row = lax.broadcasted_iota(jnp.int32, (BLOCK, n), 0)
    mask_ref[:, rows] = jnp.where((row <= 16) & (row != seg), MASKED, 0.0).astype(bf16)


def forward_kernel(heads, chunks, tab_ref, gl_ref, *refs):
    x_refs = refs[0:chunks]
    (seg_ref, wkv_ref, bkv_ref, wq_ref, bq_ref, out_ref, lse_ref, lseg_ref, k_sc, v_sc, q_sc, mask_sc, s_sc) = refs[chunks:]
    rows = x_refs[0].shape[0]
    length = rows * chunks
    npairs = length // PAIR
    per_chunk = npairs // chunks
    tile = 256
    for c in range(chunks):

        @pl.loop(0, rows // tile)
        def _(t):
            at = pl.multiple_of(t * tile, tile)
            project_rows(
                x_refs[c][pl.ds(at, tile), :], seg_ref[c : c + 1, pl.ds(at, tile)], wkv_ref, bkv_ref, wq_ref, bq_ref,
                k_sc, v_sc, q_sc, mask_sc, pl.multiple_of(c * rows + t * tile, tile),
            )

    null_lane = lax.broadcasted_iota(jnp.int32, (BLOCK, heads * PAIR), 1) % PAIR
    k_sc[pl.ds(length, BLOCK), :] = (null_lane == BLOCK + 16).astype(f32).astype(bf16)
    v_sc[pl.ds(length, BLOCK), :] = jnp.zeros((BLOCK, 2 * PAIR), bf16)
    first, second = lane_halves(PAIR, bf16)
    lane = lax.broadcasted_iota(jnp.int32, (1, PAIR), 1)

    @pl.loop(0, npairs)
    def _(pair):
        chunk = pair // per_chunk
        local = pl.multiple_of((pair % per_chunk) * PAIR, PAIR)
        at = pl.multiple_of(pair * PAIR, PAIR)
        for h in range(heads):
            shared, mine, other = slots(tab_ref, gl_ref, h, pair, npairs)
            kl, vl, off = key_lanes(h), value_lanes(h), VALUE_ROW[h]
            q = query_columns(q_sc, mask_sc, h, at)
            s_sh = dot_nn(stack_rows(k_sc, shared, kl), q)
            k_pr = jnp.concatenate([stack_rows(k_sc, mine, kl), stack_rows(k_sc, other, kl)], axis=1)
            s_pr = dot_nn(k_pr, jnp.concatenate([q * first, q * second], axis=0))
            peak = jnp.maximum(jnp.max(s_sh, axis=0, keepdims=True), jnp.max(s_pr, axis=0, keepdims=True))
            e_sh = jnp.exp(s_sh - peak)
            e_pr = jnp.exp(s_pr - peak)
            total = jnp.sum(e_sh, axis=0, keepdims=True) + jnp.sum(e_pr, axis=0, keepdims=True)
            inv = 1.0 / total
            p_sh = (e_sh * inv).astype(bf16)
            p_pr = (e_pr * inv).astype(bf16)
            v_pr = jnp.concatenate([stack_rows(v_sc, mine, vl), stack_rows(v_sc, other, vl)], axis=1)
            o_sh = dot_tn(stack_rows(v_sc, shared, vl), p_sh)
            o_pr = dot_tn(v_pr, p_pr)
            ctx = o_sh[off : off + BLOCK] + jnp.where(
                lane < BLOCK, o_pr[off : off + BLOCK], o_pr[PAIR + off : PAIR + off + BLOCK]
            )
            out_ref[chunk, h * BLOCK : (h + 1) * BLOCK, pl.ds(local, PAIR)] = ctx.astype(bf16)
            lse_ref[h, pl.ds(pair, 1), :] = peak + jnp.log(total)

    step = 512
    for h in range(heads):
        kl, vl, off = key_lanes(h), value_lanes(h), VALUE_ROW[h]
        q = global_queries(q_sc, mask_sc, h, gl_ref)

        def score(c, peak):
            at = pl.multiple_of(c * step, step)
            s = dot_nn(k_sc[pl.ds(at, step), kl], q)
            s_sc[pl.ds(at, step), :] = s
            return jnp.maximum(peak, jnp.max(s, axis=0, keepdims=True))

        peak = lax.fori_loop(0, length // step, score, jnp.full((1, PAIR), MASKED, f32))

        def gather(c, carry):
            total, ctx = carry
            at = pl.multiple_of(c * step, step)
            e = jnp.exp(s_sc[pl.ds(at, step), :] - peak)
            ctx = ctx + dot_tn(v_sc[pl.ds(at, step), vl], e.astype(bf16))
            return total + jnp.sum(e, axis=0, keepdims=True), ctx

        total, ctx = lax.fori_loop(
            0, length // step, gather, (jnp.zeros((1, PAIR), f32), jnp.zeros((PAIR, PAIR), f32))
        )
        ctx = ctx[off : off + BLOCK] * (1.0 / total)
        put_global_columns(out_ref, slice(h * BLOCK, (h + 1) * BLOCK), gl_ref, ctx, per_chunk)
        lseg_ref[h : h + 1, :] = peak + jnp.log(total)


def attention_forward(tab, gl, x, seg, w_kv, b_kv, w_q, b_q):
    chunks = len(x)
    rows = x[0].shape[0]
    length = rows * chunks
    heads = w_q.shape[0] // HEAD_DIM
    whole = lambda: pl.BlockSpec(memory_space=pltpu.VMEM)
    return pl.pallas_call(
        functools.partial(forward_kernel, heads, chunks),
        out_shape=(
            jax.ShapeDtypeStruct((chunks, heads * HEAD_DIM, rows), bf16),
            jax.ShapeDtypeStruct((heads, length // PAIR, PAIR), f32),
            jax.ShapeDtypeStruct((heads, PAIR), f32),
            jax.ShapeDtypeStruct((length + BLOCK, heads * PAIR), bf16),
            jax.ShapeDtypeStruct((length + BLOCK, 2 * PAIR), bf16),
            jax.ShapeDtypeStruct((heads * HEAD_DIM, length), bf16),
            jax.ShapeDtypeStruct((BLOCK, length), bf16),
        ),
        in_specs=[pl.BlockSpec(memory_space=pltpu.SMEM)] * 2 + [whole() for _ in range(chunks + 5)],
        out_specs=tuple(whole() for _ in range(7)),
        scratch_shapes=[pltpu.VMEM((length, PAIR), f32)],
        compiler_params=pltpu.CompilerParams(vmem_limit_bytes=56 << 20),
        cost_estimate=pl.CostEstimate(flops=12_000_000_000, bytes_accessed=16_000_000, transcendentals=8_000_000),
        name="attention_forward",
    )(tab, gl, *x, seg, w_kv, b_kv, w_q, b_q)


def backward_kernel(heads, chunks, tab_ref, gl_ref, *refs):
    do_refs = refs[:chunks]
    (k_sc, v_sc, q_sc, mask_sc, lse_ref, lseg_ref, wq_ref, wkv_ref, dq_ref, dkv_ref, first_ref, part_ref,
     do_sc, acc, p_sc, d_sc, dqg_sc) = refs[chunks:]
    rows = do_refs[0].shape[1]
    length = rows * chunks
    npairs = length // PAIR
    per_chunk = npairs // chunks
    for c in range(chunks):
        do_sc[:, c * rows : (c + 1) * rows] = do_refs[c][...]
    first, second = lane_halves(PAIR, bf16)
    first2, second2 = lane_halves(2 * PAIR, bf16)
    ffirst, fsecond = lane_halves(PAIR, f32)
    lane = lax.broadcasted_iota(jnp.int32, (1, PAIR), 1)
    zeros = jnp.zeros((BLOCK, PAIR), bf16)

    def value_rows(do, h):
        return jnp.concatenate([zeros, do] if VALUE_ROW[h] else [do, zeros], axis=0)

    def sources(q, do):
        top = jnp.concatenate([q[0:BLOCK], zeros], axis=1)
        return jnp.concatenate([top, jnp.concatenate([zeros, do], axis=1)], axis=0)

    step = 512
    for h in range(heads):
        kl, vl = key_lanes(h), value_lanes(h)
        q = global_queries(q_sc, mask_sc, h, gl_ref)
        do = global_columns(do_sc, slice(h * BLOCK, (h + 1) * BLOCK), gl_ref).astype(bf16)
        do_v = value_rows(do, h)
        lse = lseg_ref[h : h + 1, :]
        src = sources(q, do)

        def weigh(c, delta):
            at = pl.multiple_of(c * step, step)
            p = jnp.exp(dot_nn(k_sc[pl.ds(at, step), kl], q) - lse)
            dp = dot_nn(v_sc[pl.ds(at, step), vl], do_v)
            p_sc[pl.ds(at, step), :] = p
            d_sc[pl.ds(at, step), :] = dp
            return delta + jnp.sum(p * dp, axis=0, keepdims=True)

        delta = lax.fori_loop(0, length // step, weigh, jnp.zeros((1, PAIR), f32))

        def spread(c, dq):
            at = pl.multiple_of(c * step, step)
            p = p_sc[pl.ds(at, step), :]
            ds = (p * (d_sc[pl.ds(at, step), :] - delta)).astype(bf16)
            both = jnp.concatenate([ds, p.astype(bf16)], axis=1)
            acc[h, pl.ds(at, step), :] = dot_nt(both, src)
            return dq + dot_tn(k_sc[pl.ds(at, step), kl], ds)

        dq = lax.fori_loop(0, length // step, spread, jnp.zeros((PAIR, PAIR), f32))
        dqg_sc[h] = dq[0:BLOCK] * (HEAD_DIM ** -0.5)
        acc[h, pl.ds(length, BLOCK), :] = jnp.zeros((BLOCK, PAIR), f32)

    @pl.loop(0, npairs)
    def _(pair):
        chunk = pair // per_chunk
        local = pl.multiple_of((pair % per_chunk) * PAIR, PAIR)
        at = pl.multiple_of(pair * PAIR, PAIR)
        hit_first = (gl_ref[0] == 2 * pair) | (gl_ref[1] == 2 * pair)
        hit_second = (gl_ref[0] == 2 * pair + 1) | (gl_ref[1] == 2 * pair + 1)
        shut = ffirst * jnp.where(hit_first, -MASKED, 0.0) + fsecond * jnp.where(hit_second, -MASKED, 0.0)
        for h in range(heads):
            shared, mine, other = slots(tab_ref, gl_ref, h, pair, npairs)
            kl, vl = key_lanes(h), value_lanes(h)
            q = query_columns(q_sc, mask_sc, h, at)
            do = do_sc[h * BLOCK : (h + 1) * BLOCK, pl.ds(at, PAIR)]
            do_v = value_rows(do, h)
            lse = lse_ref[h, pl.ds(pair, 1), :] + shut
            k_sh = stack_rows(k_sc, shared, kl)
            k_pr = jnp.concatenate([stack_rows(k_sc, mine, kl), stack_rows(k_sc, other, kl)], axis=1)
            p_sh = jnp.exp(dot_nn(k_sh, q) - lse)
            p_pr = jnp.exp(dot_nn(k_pr, jnp.concatenate([q * first, q * second], axis=0)) - lse)
            d_sh = dot_nn(stack_rows(v_sc, shared, vl), do_v)
            v_pr = jnp.concatenate([stack_rows(v_sc, mine, vl), stack_rows(v_sc, other, vl)], axis=1)
            d_pr = dot_nn(v_pr, jnp.concatenate([do_v * first, do_v * second], axis=0))
            delta = jnp.sum(p_sh * d_sh, axis=0, keepdims=True) + jnp.sum(p_pr * d_pr, axis=0, keepdims=True)
            ds_sh = (p_sh * (d_sh - delta)).astype(bf16)
            ds_pr = (p_pr * (d_pr - delta)).astype(bf16)
            src = sources(q, do)
            g_sh = dot_nt(jnp.concatenate([ds_sh, p_sh.astype(bf16)], axis=1), src)
            src2 = jnp.concatenate([src * first2, src * second2], axis=0)
            g_pr = dot_nt(jnp.concatenate([ds_pr, p_pr.astype(bf16)], axis=1), src2)
            for j, o in enumerate(shared):
                acc[h, pl.ds(o, BLOCK), :] += g_sh[j * BLOCK : (j + 1) * BLOCK]
            for j, o in enumerate(mine):
                acc[h, pl.ds(o, BLOCK), :] += g_pr[j * BLOCK : (j + 1) * BLOCK, 0:PAIR]
            for j, o in enumerate(other):
                acc[h, pl.ds(o, BLOCK), :] += g_pr[j * BLOCK : (j + 1) * BLOCK, PAIR:]
            t_sh = dot_tn(k_sh, ds_sh)
            t_pr = dot_tn(k_pr, ds_pr)
            dq = t_sh[0:BLOCK] + jnp.where(lane < BLOCK, t_pr[0:BLOCK], t_pr[PAIR : PAIR + BLOCK])
            dq_ref[chunk, h * BLOCK : (h + 1) * BLOCK, pl.ds(local, PAIR)] = (dq * (HEAD_DIM ** -0.5)).astype(bf16)

    for h in range(heads):
        put_global_columns(dq_ref, slice(h * BLOCK, (h + 1) * BLOCK), gl_ref, dqg_sc[h], per_chunk)
        for c in range(chunks):
            dkv_ref[c, :, h * PAIR : (h + 1) * PAIR] = acc[h, pl.ds(c * rows, rows), :].astype(bf16)
    tile = 256
    for c in range(chunks):

        @pl.loop(0, rows // tile)
        def _(t):
            at = pl.multiple_of(t * tile, tile)
            got = dot_tn(dq_ref[c, :, pl.ds(at, tile)], wq_ref[...]) + dot_nn(dkv_ref[c, pl.ds(at, tile), :], wkv_ref[...])
            if c == 0:
                first_ref[pl.ds(at, tile), :] = got
            else:
                part_ref[c - 1, pl.ds(at, tile), :] = got.astype(bf16)


def attention_backward(tab, gl, do, k, v, q, mask, lse, lseg, w_q, w_kv):
    chunks = len(do)
    group, rows = do[0].shape
    heads = group // HEAD_DIM
    width = w_q.shape[1]
    length = rows * chunks
    whole = lambda: pl.BlockSpec(memory_space=pltpu.VMEM)
    return pl.pallas_call(
        functools.partial(backward_kernel, heads, chunks),
        out_shape=(
            jax.ShapeDtypeStruct((chunks, group, rows), bf16),
            jax.ShapeDtypeStruct((chunks, rows, heads * PAIR), bf16),
            jax.ShapeDtypeStruct((rows, width), f32),
            jax.ShapeDtypeStruct((chunks - 1, rows, width), bf16),
        ),
        in_specs=[pl.BlockSpec(memory_space=pltpu.SMEM)] * 2 + [whole() for _ in range(chunks + 8)],
        out_specs=tuple(whole() for _ in range(4)),
        scratch_shapes=[
            pltpu.VMEM((group, length), bf16),
            pltpu.VMEM((heads, length + BLOCK, PAIR), f32),
            pltpu.VMEM((length, PAIR), f32),
            pltpu.VMEM((length, PAIR), f32),
            pltpu.VMEM((heads, BLOCK, PAIR), f32),
        ],
        compiler_params=pltpu.CompilerParams(vmem_limit_bytes=60 << 20),
        cost_estimate=pl.CostEstimate(flops=30_000_000_000, bytes_accessed=24_000_000, transcendentals=8_000_000),
        name="attention_backward",
    )(tab, gl, *do, k, v, q, mask, lse, lseg, w_q, w_kv)


def weights_kernel(chunks, *refs):
    x_refs = refs[:chunks]
    dq_ref, dkv_ref, gw_ref, sq_ref, skv_ref, acc = refs[chunks:]
    group = dq_ref.shape[1]
    total_q = jnp.zeros((group, 1), f32)
    total_kv = jnp.zeros((1, dkv_ref.shape[2]), f32)
    for c in range(chunks):
        x = x_refs[c][...]
        got_q = dot_nn(dq_ref[c], x)
        got_kv = dot_tn(dkv_ref[c], x)
        if c == 0:
            acc[0:group, :] = got_q
            acc[group:, :] = got_kv
        else:
            acc[0:group, :] += got_q
            acc[group:, :] += got_kv
        total_q = total_q + jnp.sum(dq_ref[c].astype(f32), axis=1, keepdims=True)
        total_kv = total_kv + jnp.sum(dkv_ref[c].astype(f32), axis=0, keepdims=True)
    gw_ref[...] = jnp.transpose(acc[...], (1, 0)).astype(bf16)
    sq_ref[...] = total_q
    skv_ref[...] = total_kv


def projection_gradients(x, dq, dkv):
    chunks, group, rows = dq.shape
    width = x[0].shape[1]
    lanes = dkv.shape[2]
    whole = lambda: pl.BlockSpec(memory_space=pltpu.VMEM)
    return pl.pallas_call(
        functools.partial(weights_kernel, chunks),
        out_shape=(
            jax.ShapeDtypeStruct((width, group + lanes), bf16),
            jax.ShapeDtypeStruct((group, 1), f32),
            jax.ShapeDtypeStruct((1, lanes), f32),
        ),
        in_specs=[whole() for _ in range(chunks + 2)],
        out_specs=tuple(whole() for _ in range(3)),
        scratch_shapes=[pltpu.VMEM((group + lanes, width), f32)],
        compiler_params=pltpu.CompilerParams(vmem_limit_bytes=40 << 20),
        cost_estimate=pl.CostEstimate(flops=4_000_000_000, bytes_accessed=12_000_000, transcendentals=0),
        name="projection_gradients",
    )(*x, dq, dkv)


NORM_EPS = 1e-12


def transposed(value):
    return jnp.transpose(value.astype(f32), (1, 0)).astype(bf16)


def unit_rows(value):
    center = value - jnp.mean(value, axis=-1, keepdims=True)
    scale = lax.rsqrt(jnp.mean(center * center, axis=-1, keepdims=True) + NORM_EPS)
    return center * scale, scale


def unit_rows_back(grad, unit, scale):
    return scale * (
        grad - jnp.mean(grad, axis=-1, keepdims=True) - unit * jnp.mean(grad * unit, axis=-1, keepdims=True)
    )


def rows_kernel(parts, blocks, up_rows, me_ref, *refs):
    ctx_refs = refs[:parts]
    (x_ref, cot_ref, rest_ref, wo_ref, vec_ref, bup_ref, out_ref, resid_ref, hid_ref, pre_ref, nlt_ref, gft_ref,
     gb_ref, do_ref, sums_ref, gbup_ref, slope_sc) = refs[parts:]
    group = ctx_refs[0].shape[0]
    width = x_ref.shape[1]

    def up(f):
        return rest_ref[:, f, 0:up_rows, :].reshape(width, rest_ref.shape[3])

    def down(f):
        return rest_ref[:, f, up_rows : 2 * up_rows, :].reshape(width, rest_ref.shape[3])

    def own_rows(k):
        return pl.ds(pl.multiple_of((me_ref[0] ^ k) * group, group), group)

    @pl.when(pl.program_id(0) == 0)
    def _():
        sums_ref[...] = jnp.zeros_like(sums_ref)
        gbup_ref[...] = jnp.zeros_like(gbup_ref)

    ctx = jnp.concatenate([r[...] for r in ctx_refs], axis=0)
    w_o = jnp.concatenate([wo_ref[own_rows(k), :] for k in range(parts)], axis=0)
    resid_one = x_ref[...].astype(f32) + (dot_tn(ctx, w_o) + vec_ref[0:1, :])
    unit_one, scale_one = unit_rows(resid_one)
    normed_one = unit_one * vec_ref[2:3, :] + vec_ref[3:4, :]
    low = normed_one.astype(bf16)
    nlt_ref[...] = transposed(normed_one)
    total = normed_one + vec_ref[1:2, :]
    pre = dot_nn(low, up(0)) + bup_ref[0:1, :]
    for f in range(blocks):
        later = dot_nn(low, up(f + 1)) + bup_ref[f + 1 : f + 2, :] if f + 1 < blocks else None
        phi = 0.5 + 0.5 * lax.erf(pre * (0.5 ** 0.5))
        slope_sc[f] = phi + pre * (jnp.exp(-0.5 * pre * pre) * 0.3989422804014327)
        hid = (pre * phi).astype(bf16)
        hid_ref[f] = hid
        total = total + dot_nt(hid, down(f))
        pre = later
    unit_two, scale_two = unit_rows(total)
    out_ref[...] = (unit_two * vec_ref[4:5, :] + vec_ref[5:6, :]).astype(bf16)
    cot = cot_ref[...].astype(f32)
    grad_two = unit_rows_back(cot * vec_ref[4:5, :], unit_two, scale_two)
    grad_ffn = grad_two.astype(bf16)
    gft_ref[...] = transposed(grad_two)
    grad_normed = grad_two
    back = dot_nn(grad_ffn, down(0))
    for f in range(blocks):
        later = dot_nn(grad_ffn, down(f + 1)) if f + 1 < blocks else None
        grad_pre = (back * slope_sc[f]).astype(bf16)
        pre_ref[f] = grad_pre
        gbup_ref[f : f + 1, :] += jnp.sum(grad_pre.astype(f32), axis=0, keepdims=True)
        grad_normed = grad_normed + dot_nt(grad_pre, up(f))
        back = later
    resid = unit_rows_back(grad_normed * vec_ref[2:3, :], unit_one, scale_one)
    resid_ref[...] = resid
    branch = resid.astype(bf16)
    gb_ref[...] = branch
    do = dot_nt(w_o, branch).astype(bf16)
    for k in range(parts):
        do_ref[k] = do[k * group : (k + 1) * group]
    for row, value in enumerate(
        (branch.astype(f32), grad_ffn.astype(f32), grad_normed * unit_one, grad_normed, cot * unit_two, cot)
    ):
        sums_ref[row : row + 1, :] += jnp.sum(value, axis=0, keepdims=True)


def rows_chain(me, ctx_parts, x, cot, rest, up_rows, w_o, vecs, bias_up):
    parts = len(ctx_parts)
    group, rows = ctx_parts[0].shape
    width = x.shape[1]
    outer, blocks, per, hidden = rest.shape
    tile = 256
    once = lambda shape: pl.BlockSpec(shape, lambda i: (0,) * len(shape), pipeline_mode=pl.Buffered(1))
    tall = pl.BlockSpec((tile, width), lambda i: (i, 0))
    wide = pl.BlockSpec((width, tile), lambda i: (0, i))
    cube = pl.BlockSpec((blocks, tile, hidden), lambda i: (0, i, 0))
    return pl.pallas_call(
        functools.partial(rows_kernel, parts, blocks, up_rows),
        grid=(rows // tile,),
        out_shape=(
            jax.ShapeDtypeStruct((rows, width), bf16),
            jax.ShapeDtypeStruct((rows, width), f32),
            jax.ShapeDtypeStruct((blocks, rows, hidden), bf16),
            jax.ShapeDtypeStruct((blocks, rows, hidden), bf16),
            jax.ShapeDtypeStruct((width, rows), bf16),
            jax.ShapeDtypeStruct((width, rows), bf16),
            jax.ShapeDtypeStruct((rows, width), bf16),
            jax.ShapeDtypeStruct((parts, group, rows), bf16),
            jax.ShapeDtypeStruct((8, width), f32),
            jax.ShapeDtypeStruct((8, hidden), f32),
        ),
        in_specs=[pl.BlockSpec(memory_space=pltpu.SMEM)]
        + [pl.BlockSpec((group, tile), lambda i: (0, i))] * parts
        + [tall, tall, once(rest.shape), once(w_o.shape), once(vecs.shape), once(bias_up.shape)],
        out_specs=(
            tall, tall, cube, cube, wide, wide, tall, pl.BlockSpec((parts, group, tile), lambda i: (0, 0, i)),
            pl.BlockSpec((8, width), lambda i: (0, 0)), pl.BlockSpec((8, hidden), lambda i: (0, 0)),
        ),
        scratch_shapes=[pltpu.VMEM((blocks, tile, hidden), f32)],
        compiler_params=pltpu.CompilerParams(vmem_limit_bytes=60 << 20),
        cost_estimate=pl.CostEstimate(flops=22_000_000_000, bytes_accessed=40_000_000, transcendentals=6_000_000),
        name="rows_chain",
    )(me, *ctx_parts, x, cot, rest, w_o, vecs, bias_up)


def outer_kernel(up_rows, small_rows, nlt_ref, gft_ref, pre_ref, hid_ref, small_ref, out_ref):
    slabs, hidden = out_ref.shape[0], out_ref.shape[3]
    up = dot_nn(nlt_ref[...], pre_ref[0]).astype(bf16)
    out_ref[:, 0, 0:up_rows, :] = up.reshape(slabs, up_rows, hidden)
    down = dot_nn(gft_ref[...], hid_ref[0]).astype(bf16)
    out_ref[:, 0, up_rows : 2 * up_rows, :] = down.reshape(slabs, up_rows, hidden)
    if small_rows:
        out_ref[:, 0, 2 * up_rows :, :] = small_ref[:, 0]


def outer_products(nlt, gft, pre, hid, small, slabs, up_rows):
    blocks, rows, hidden = pre.shape
    width = nlt.shape[0]
    small_rows = small.shape[2] if slabs == small.shape[0] else 0
    per = 2 * up_rows + small_rows
    once = lambda shape: pl.BlockSpec(shape, lambda i: (0,) * len(shape), pipeline_mode=pl.Buffered(1))
    return pl.pallas_call(
        functools.partial(outer_kernel, up_rows, small_rows),
        grid=(blocks,),
        out_shape=jax.ShapeDtypeStruct((slabs, blocks, per, hidden), bf16),
        in_specs=[
            once(nlt.shape),
            once(gft.shape),
            pl.BlockSpec((1, rows, hidden), lambda i: (i, 0, 0)),
            pl.BlockSpec((1, rows, hidden), lambda i: (i, 0, 0)),
            pl.BlockSpec((small.shape[0], 1) + small.shape[2:], lambda i: (0, i, 0, 0)),
        ],
        out_specs=pl.BlockSpec((slabs, 1, per, hidden), lambda i: (0, i, 0, 0)),
        compiler_params=pltpu.CompilerParams(vmem_limit_bytes=48 << 20),
        cost_estimate=pl.CostEstimate(flops=10_000_000_000, bytes_accessed=28_000_000, transcendentals=0),
        name="outer_products",
    )(nlt, gft, pre, hid, small)


ALL = ("dp", "seq", "ffn")


def flip_send(array, axis, bits):
    count = lax.axis_size(axis)
    return lax.ppermute(array, axis, [(i, i ^ bits) for i in range(count)])


def bits_of(axis):
    return lax.axis_size(axis).bit_length() - 1


def gather_doubling(array, axis):
    index = lax.axis_index(axis)
    size = lax.axis_size(axis)
    shape = array.shape
    bits = bits_of(axis)
    for place, bit in enumerate(reversed(range(bits))):
        other = flip_send(array, axis, 1 << bit)
        mine_second = ((index >> bit) & 1) == 1
        array = jnp.where(mine_second, jnp.stack([other, array], axis=place), jnp.stack([array, other], axis=place))
    return array.reshape((size,) + shape)


def scatter_halving(array, axis, dim):
    index = lax.axis_index(axis)
    for bit in range(bits_of(axis)):
        shape = array.shape
        array = array.reshape(shape[:dim] + (shape[dim] // 2, 2) + shape[dim + 1 :])
        mine = (index >> bit) & 1
        keep = lax.dynamic_index_in_dim(array, mine, dim + 1, keepdims=False)
        send = lax.dynamic_index_in_dim(array, 1 - mine, dim + 1, keepdims=False)
        array = keep + flip_send(send, axis, 1 << bit)
    return array.reshape(array.shape[:dim] + array.shape[dim + 1 :])


def shards(
    tokens, w_query, w_key, w_value, w_output, b_query, b_value, b_output, w_up, b_up, w_down, b_down,
    gain_attn, shift_attn, gain_ffn, shift_ffn, segment_ids, random_blocks, global_blocks, cotangent,
):
    seq_n, dp_n, ffn_n = lax.axis_size("seq"), lax.axis_size("dp"), lax.axis_size("ffn")
    outer = dp_n * seq_n
    me = lax.axis_index("seq")
    own, width = w_query.shape
    group = width // seq_n
    heads = group // HEAD_DIM
    features = tokens[0]
    rows = features.shape[0]
    relative = [me ^ k for k in range(seq_n)]

    def by_group(w):
        return w.reshape(own, seq_n, group).transpose(1, 0, 2)

    note = jnp.pad(jnp.stack([b_query, b_value]), ((0, 0), (0, 3 * group - own)))
    pack = jnp.concatenate([by_group(w_query), by_group(w_key), by_group(w_value)], axis=2)
    pack = jnp.concatenate([pack, jnp.broadcast_to(note[None], (seq_n,) + note.shape)], axis=1)
    got = [lax.dynamic_index_in_dim(pack, relative[k], keepdims=False) for k in range(seq_n)]
    got = [got[0]] + [flip_send(got[k], "seq", k) for k in range(1, seq_n)]
    got, features = lax.optimization_barrier((got, features))

    near = [features] + [None] * (seq_n - 1)
    for k in sorted(range(1, seq_n), key=lambda k: (k & (k - 1), -k)):
        bit = k & -k
        near[k] = flip_send(features if bit == k else near[k ^ bit], "seq", bit)

    pack = gather_doubling(gather_doubling(jnp.stack(got), "ffn"), "dp")
    order = jnp.stack(relative)
    pack = pack[:, :, order].transpose(0, 2, 1, 3, 4)
    w_own = pack[:, :, :, :own].reshape(width, 3 * group)
    biases = lax.dynamic_slice(
        pack[:, :, :, own:, :own].transpose(3, 0, 1, 2, 4).reshape(2, width), (0, me * group), (2, group)
    ).astype(f32)
    blank = jnp.zeros((width, HEAD_DIM), bf16)
    part_of = lambda i, h: w_own[:, i * group + h * HEAD_DIM : i * group + (h + 1) * HEAD_DIM]
    w_kv = jnp.concatenate(
        [part_of(1, 0), blank, part_of(1, 1), blank, part_of(1, 2), part_of(2, 2), part_of(2, 0), part_of(2, 1)], axis=1
    )
    b_value_own = biases[1].reshape(heads, HEAD_DIM)
    b_kv = jnp.concatenate([jnp.zeros((5 * HEAD_DIM,), f32), b_value_own[2], b_value_own[0], b_value_own[1]])[None]
    w_q_t = w_own[:, :group].T
    w_kv_t = jnp.concatenate([part_of(i, h) for h in range(heads) for i in (1, 2)], axis=1).T
    seg = segment_ids[0].reshape(seq_n, rows)[order]

    vectors = jnp.stack([b_output, b_down, gain_attn, shift_attn, gain_ffn, shift_ffn])
    vectors = jnp.pad(vectors, ((0, 0), (0, width - own)))
    rest = jnp.concatenate([w_up, w_down, w_output, b_up[None], vectors], axis=0)
    up_rows = w_up.shape[0]
    rest = lax.all_gather(rest, ALL, axis=0, tiled=False).reshape(outer, ffn_n, rest.shape[0], width)
    at = 2 * up_rows
    w_o = rest[:, :, at : at + own].reshape(width, width)
    bias_up = rest[0, :, at + own].astype(f32)
    vecs = rest[:, :, at + own + 1 :, :own].transpose(2, 0, 1, 3).reshape(6, width).astype(f32)
    direct = up_rows % 16 == 0
    if not direct:
        rest = rest[:, :, :at].reshape(outer, ffn_n, 2, up_rows, width).transpose(1, 2, 0, 3, 4)
        rest = rest.reshape(1, ffn_n, 2 * outer * up_rows, width)
    slabs, slab_rows = (outer, up_rows) if direct else (1, outer * up_rows)

    nblocks = seq_n * rows // BLOCK
    flip = me.astype(jnp.int32) * (nblocks // seq_n)
    tab = pair_table(random_blocks[0], global_blocks[0], flip, nblocks)
    gl = global_blocks[0] ^ flip
    ctx, lse, lseg, k_all, v_all, q_all, mask_all = attention_forward(
        tab, gl, near, seg, w_kv, b_kv, w_q_t, biases[0][:, None]
    )
    ctx_parts = [ctx[0]] + [flip_send(ctx[k], "seq", k) for k in range(1, seq_n)]

    (out, grad_resid_one, hidden, grad_pre, normed_t, grad_ffn_t, grad_branch, grad_ctx, sums, grad_bias_up) = rows_chain(
        me.astype(jnp.int32)[None], ctx_parts, features, cotangent[0], rest, slab_rows, w_o,
        jnp.pad(vecs, ((0, 2), (0, 0))), bias_up,
    )
    do = [grad_ctx[0]] + [flip_send(grad_ctx[k], "seq", k) for k in range(1, seq_n)]

    grad_out = dot_nn(jnp.concatenate(ctx_parts, axis=0), grad_branch).astype(bf16)
    grad_out = grad_out.reshape(seq_n, group, width)[order].reshape(outer, ffn_n, own, width)
    vec_grads = sums[:6].astype(bf16).reshape(6, outer, ffn_n, own).transpose(1, 2, 0, 3)
    vec_grads = jnp.pad(vec_grads, ((0, 0), (0, 0), (0, 25 - own), (0, width - own)))
    small = jnp.concatenate(
        [
            grad_out,
            jnp.broadcast_to(grad_bias_up[None, :ffn_n, None].astype(bf16), (outer, ffn_n, 1, width)),
            vec_grads,
        ],
        axis=2,
    )
    payload = outer_products(normed_t, grad_ffn_t, grad_pre, hidden, small, slabs, slab_rows)
    if not direct:
        payload = payload.reshape(ffn_n, 2, outer, up_rows, width).transpose(2, 0, 1, 3, 4)
        payload = jnp.concatenate([payload.reshape(outer, ffn_n, at, width), small], axis=2)
        payload = jnp.pad(payload, ((0, 0), (0, 0), (0, -payload.shape[2] % 32), (0, 0)))
    payload, do = lax.optimization_barrier((payload, do))
    per = payload.shape[2]
    total = lax.psum_scatter(payload.reshape(-1, width), ALL, scatter_dimension=0, tiled=True).astype(f32)
    out_up, out_down, out_output = total[:up_rows], total[up_rows:at], total[at : at + own]
    out_bias_up = total[at + own]
    out_vecs = total[at + own + 1 : at + own + 7, :own]

    dq, dkv, part_first, parts = attention_backward(
        tab, gl, do, k_all, v_all, q_all, mask_all, lse, lseg, w_q_t, w_kv_t
    )
    part = [None] + [parts[k - 1] for k in range(1, seq_n)]
    grad_features = grad_resid_one + part_first
    bit = 1
    while bit < seq_n:
        for k in range(seq_n):
            if k & -k == bit and k != bit:
                came = flip_send(part[k], "seq", bit).astype(f32)
                part[k ^ bit] = (part[k ^ bit].astype(f32) + came).astype(bf16)
        bit *= 2
    bit = seq_n // 2
    while bit:
        grad_features = grad_features + flip_send(part[bit], "seq", bit).astype(f32)
        bit //= 2

    grad_w, sum_q, sum_kv = projection_gradients(near, dq, dkv)
    sum_v = sum_kv.reshape(heads, 2, HEAD_DIM)[:, 1].reshape(group)
    sum_b = lax.dynamic_update_slice(jnp.zeros((2, width), f32), jnp.stack([sum_q[:, 0], sum_v]), (0, me * group))
    sum_b = sum_b.astype(bf16).reshape(2, dp_n, seq_n, ffn_n, own).transpose(1, 2, 3, 0, 4)
    sum_b = jnp.pad(sum_b, ((0, 0),) * 3 + ((0, 30 - own), (0, 3 * group - own)))
    grad_w = jnp.concatenate([grad_w.reshape(dp_n, seq_n, ffn_n, own, 3 * group), sum_b], axis=3)
    grad_w = scatter_halving(scatter_halving(grad_w, "dp", 0), "ffn", 1)
    sent = [lax.dynamic_index_in_dim(grad_w, relative[k], keepdims=False) for k in range(seq_n)]
    sent = [sent[0]] + [flip_send(sent[k], "seq", k) for k in range(1, seq_n)]
    grad_w = jnp.stack(sent)[order].astype(f32)
    out_query = grad_w[:, :own, :group].transpose(1, 0, 2).reshape(own, width)
    pairs = grad_w[:, :own, group:].reshape(seq_n, own, heads, 2, HEAD_DIM).transpose(3, 1, 0, 2, 4)
    out_key, out_value = pairs[0].reshape(own, width), pairs[1].reshape(own, width)
    out_b = jnp.sum(grad_w[:, own : own + 2, :own], axis=0)
    return (
        out[None],
        grad_features[None],
        out_query,
        out_key,
        out_value,
        out_output,
        out_b[0],
        out_b[1],
        out_vecs[0],
        out_up,
        out_bias_up,
        out_down,
        out_vecs[1],
        out_vecs[2],
        out_vecs[3],
        out_vecs[4],
        out_vecs[5],
    )


def solution(mesh):
    return jax.shard_map(
        shards,
        mesh=mesh,
        in_specs=(
            P(("dp", "ffn"), "seq", None),
            P(("dp", "seq", "ffn"), None),
            P(("dp", "seq", "ffn"), None),
            P(("dp", "seq", "ffn"), None),
            P(("dp", "seq", "ffn"), None),
            P(("dp", "seq", "ffn")),
            P(("dp", "seq", "ffn")),
            P(("dp", "seq", "ffn")),
            P(("dp", "seq"), "ffn"),
            P("ffn"),
            P(("dp", "seq"), "ffn"),
            P(("dp", "seq", "ffn")),
            P(("dp", "seq", "ffn")),
            P(("dp", "seq", "ffn")),
            P(("dp", "seq", "ffn")),
            P(("dp", "seq", "ffn")),
            P(("dp", "ffn"), None),
            P(("dp", "ffn"), "seq", None, None),
            P(("dp", "ffn"), None),
            P(("dp", "ffn"), "seq", None),
        ),
        out_specs=(
            P(("dp", "ffn"), "seq", None),
            P(("dp", "ffn"), "seq", None),
            P(("dp", "seq", "ffn"), None),
            P(("dp", "seq", "ffn"), None),
            P(("dp", "seq", "ffn"), None),
            P(("dp", "seq", "ffn"), None),
            P(("dp", "seq", "ffn")),
            P(("dp", "seq", "ffn")),
            P(("dp", "seq", "ffn")),
            P(("dp", "seq"), "ffn"),
            P("ffn"),
            P(("dp", "seq"), "ffn"),
            P(("dp", "seq", "ffn")),
            P(("dp", "seq", "ffn")),
            P(("dp", "seq", "ffn")),
            P(("dp", "seq", "ffn")),
            P(("dp", "seq", "ffn")),
        ),
        check_vma=False,
    )
```

time: 675 us -> 409 us (0.61)
  matrix products: 142 us -> 3.16 us
  local copies, waits for them, and re-layouts: 160 us -> 57.8 us
  Pallas kernels: 106 us -> 184 us
  blocking collectives: 51.5 us -> 0 us
  waiting for transfers between devices: 133 us -> 105 us
  other arithmetic: 43.3 us -> 21.2 us
    ppermute x12 -> x24, waiting for transfers between devices: 5.43 us -> 105 us  [flip_send(): return lax.ppermute(array, axis, [(i, i ^ bits) for i in range(count)])]
    dot_general x42 -> x0, matrix products: 88.1 us -> none  [the longest x13 26.5 us: dot_tn(): lax.dot_general(a, b, (((0,), (0,)), ((), ())), preferred_element_type=f32)]
    reduce_scatter x2 -> x1, waiting for transfers between devices: 74.7 us -> 0.01 us  [shards(): lax.psum_scatter(payload.reshape(-1, width), ALL, scatter_dimension=0, ti...]
    pallas_call x0 -> x3, Pallas kernels: none -> 59.2 us  [the longest x1 38.4 us: rows_chain(): pl.pallas_call(functools.partial(rows_kernel, parts, blocks, up_rows), gr...]
    all_to_all x2 -> x0, waiting for transfers between devices: 53.1 us -> none  [the longest x1 29.5 us: shards(): pack = lax.all_to_all(pack, 'seq', split_axis=0, concat_axis=0, tiled=True)]
    concatenate x5 -> x2, local copies, waits for them, and re-layouts: 54.6 us -> 2 us  [the longest x1 1.99 us: shards(): jnp.concatenate([part_of(1, 0), blank, part_of(1, 1), blank, part_of(1, 2...]
    all_gather x1 -> x0, blocking collectives: 51.5 us -> none  [shards(): lax.all_gather(pack, ('dp', 'ffn'), axis=0, tiled=False)]
    dot_general x9 -> x1, matrix products: 54.1 us -> 3.16 us  [dot_nn(): lax.dot_general(a, b, (((1,), (0,)), ((), ())), preferred_element_type=f32)]
  transfers between devices with their start and end apart: 17 -> 26, of which waited for: 5 -> 12; matrix products, arithmetic and copies ran while one was open for 29% -> 15% of each run, Pallas kernels for 6% -> 36%
where the time goes in v2:
time: 409 us; the launch traced here: 406 us
  Pallas kernels  184 us (45%)
  waiting for transfers between devices  105 us (26%)
  local copies, waits for them, and re-layouts  57.8 us (14%)
  other arithmetic  21.2 us (5%)
  starting transfers between devices  19.9 us (5%)
  between operations  14.8 us (4%)
    ppermute x24, waiting for transfers between devices, flip_send(): return lax.ppermute(array, axis, [(i, i ^ bits) for i in range(count)])  105 us
    pallas_call x1, Pallas kernels, attention_backward(): pl.pallas_call(functools.partial(backward_kernel, heads, chunks), out_sha...  75.8 us
    pallas_call x1, Pallas kernels, attention_forward(): pl.pallas_call(functools.partial(forward_kernel, heads, chunks), out_shap...  49.4 us
    pallas_call x1, Pallas kernels, rows_chain(): pl.pallas_call(functools.partial(rows_kernel, parts, blocks, up_rows), gr...  38.4 us
    ppermute x24, starting transfers between devices, flip_send(): return lax.ppermute(array, axis, [(i, i ^ bits) for i in range(count)])  19.8 us
    pallas_call x1, Pallas kernels, outer_products(): pl.pallas_call(functools.partial(outer_kernel, up_rows, small_rows), grid...  14.3 us
  transfers between devices with their start and end apart: 26, of which 12 were waited for; matrix products, arithmetic and copies ran while one was open for 15% of the time, Pallas kernels for 36%

profile of v2, /device:TPU:0, one launch (start us, length us, event | category | flops | bytes accessed | tf_op | source)
XLA Modules:
  0.0 406.5 jit_solution(11340720263718466753)
XLA Ops:
  8.8 5.1 %concatenate.69 = bf16[223,768]{1,0:T(8,128)(2,1)} concatenate(bf16[96,768]{1,0:T(8,128)(2,1)} %param.28, bf16[96,768]{1,0:T(8,128)(2,1)} %param.30, bf16[24,768]{1,0:T(8,128)(2,1)} %param.24, bf16[1,768]{1,0:T(2,128)(2,1)S(1)} %broadcast_in_dim.62, bf16[6,768]{1,0:T(8,128)(2,1)S(1)} %pad.23), dimensions={0} | concatenate | bytes 685056 | tf_op jit(solution)/shard_map/concatenate | solution.py:671
  18.3 2.6 collective-permute-start.1
  26.1 2.6 collective-permute-start.6
  31.3 12.3 %collective-permute-done.6 = bf16[4,26,576]{2,1,0:T(8,128)(2,1)S(1)} collective-permute-done((bf16[4,26,576]{2,1,0:T(8,128)(2,1)S(1)}, bf16[4,26,576]{2,1,0:T(8,128)(2,1)S(1)}, u32[]{:S(2)}, u32[]{:S(2)}) %collective-permute-start.6) | collective-permute-done | bytes 119840 | tf_op jit(solution)/shard_map/ppermute | solution.py:591
  45.3 15.4 %collective-permute-done.7 = bf16[2,4,26,576]{3,2,1,0:T(8,128)(2,1)S(1)} collective-permute-done((bf16[2,4,26,576]{3,2,1,0:T(8,128)(2,1)S(1)}, bf16[2,4,26,576]{3,2,1,0:T(8,128)(2,1)S(1)}, u32[]{:S(2)}, u32[]{:S(2)}) %collective-permute-start.7) | collective-permute-done | bytes 239648 | tf_op jit(solution)/shard_map/ppermute | solution.py:591
  67.2 6.1 %collective-permute-done.4.refs_2_ = bf16[1024,768]{1,0:T(8,128)(2,1)} collective-permute-done((bf16[1024,768]{1,0:T(8,128)(2,1)S(1)}, bf16[1024,768]{1,0:T(8,128)(2,1)}, u32[]{:S(2)}, u32[]{:S(2)}) %collective-permute-start.4) | collective-permute-done | bytes 1572896 | tf_op jit(solution)/shard_map/ppermute | solution.py:591
  75.2 2.4 gather_fusion.3
  85.7 49.4 %attention_forward.1 = (bf16[4,192,1024]{2,1,0:T(8,128)(2,1)}, f32[3,32,128]{2,1,0:T(8,128)}, f32[3,128]{1,0:T(4,128)}, bf16[4160,384]{1,0:T(8,128)(2,1)}, bf16[...) custom-call(s32[960]{0:T(1024)} %reshape.498.tab_ref, s32[2]{0:T(128)} %xor_bitcast_fusion.2.gl_ref, ...), custom_call_target="tpu_custom_call" | custom-call | flops 12000000000 | bytes 16000000 | tf_op jit(solution)/shard_map/attention_forward/pallas_call | solution.py:223
  140.3 2.4 slice.259
  144.9 4.3 %collective-permute-done.10.refs_2_ = bf16[192,1024]{1,0:T(8,128)(2,1)S(1)} collective-permute-done((bf16[192,1024]{1,0:T(8,128)(2,1)S(1)}, bf16[192,1024]{1,0:T(8,128)(2,1)S(1)}, u32[]{:S(2)}, u32[]{:S(2)}) %collective-permute-start.10) | collective-permute-done | bytes 393248 | tf_op jit(solution)/shard_map/ppermute | solution.py:591
  149.2 7.8 %collective-permute-done.11.refs_3_ = bf16[192,1024]{1,0:T(8,128)(2,1)S(1)} collective-permute-done((bf16[192,1024]{1,0:T(8,128)(2,1)S(1)}, bf16[192,1024]{1,0:T(8,128)(2,1)S(1)}, u32[]{:S(2)}, u32[]{:S(2)}) %collective-permute-start.11) | collective-permute-done | bytes 393248 | tf_op jit(solution)/shard_map/ppermute | solution.py:591
  157.9 38.4 %rows_chain.1 = (bf16[1024,768]{1,0:T(8,128)(2,1)}, f32[1024,768]{1,0:T(8,128)}, bf16[4,1024,768]{2,1,0:T(8,128)(2,1)}, bf16[4,1024,768]{2,1,0:T(8,128)(2,1)}, b...) custom-call(s32[1]{0:T(128)} %bitcast.me_ref, ...), custom_call_target="tpu_custom_call" | custom-call | flops 22000001024 | bytes 40000000 | tf_op jit(solution)/shard_map/rows_chain/pallas_call | solution.py:523
  196.3 3.2 fusion.12
  205.6 14.3 %outer_products.1 = bf16[8,4,224,768]{3,2,1,0:T(8,128)(2,1)} custom-call(bf16[768,1024]{1,0:T(8,128)(2,1)S(1)} %copy-done.4, bf16[768,1024]{1,0:T(8,128)(2,1)S(1)} %copy-done.5, bf16[4,1024,768]{2,1,0:T(8,128)(2,1)} %get-tuple-element.61.pre_ref, bf16[4,1024,768]{2,1,0:T(8,128)(2,1)} %get-tuple-element.62.hid_ref, bf16[8,4,32,768]{3,2,1,0:T(8,128)(2,1)S(1)} %fusion.3.small_ref), custom_call_target="tpu_custom_call" | custom-call | flops 10000000000 | bytes 28000000 | tf_op jit(solution)/shard_map/outer_products/pallas_call | solution.py:568
  219.9 2.9 collective-permute-done.14.refs_3_
  225.6 75.8 %attention_backward.1 = (bf16[4,192,1024]{2,1,0:T(8,128)(2,1)}, bf16[4,1024,384]{2,1,0:T(8,128)(2,1)}, f32[1024,768]{1,0:T(8,128)}, bf16[3,1024,768]{2,1,0:T(8,128)(2,1)}) custom-call(s32[960]{0:T(1024)} %reshape.498.tab_ref, s32[2]{0:T(128)} %xor_bitcast_fusion.2.gl_ref, bf16[192,1024]{1,0:T(8,128)(2,1)} %get-tuple-element.67.refs_0_, ...), custom_call_target="tpu_custom_call" | custom-call | flops 30000001024 | bytes 24000000 | tf_op jit(solution)/shard_map/attention_backward/pallas_call | solution.py:361
  301.5 4.0 slice_bitcast_fusion.1
  306.7 6.5 %projection_gradients.1 = (bf16[768,576]{1,0:T(8,128)(2,1)S(1)}, f32[192,1]{1,0:T(8,128)S(1)}, f32[1,384]{1,0:T(1,128)S(1)}) custom-call(bf16[1024,768]{1,0:T(8,128)(2,1)S(1)} %bitcast.160, bf16[1024,768]{1,0:T(8,128)(2,1)} %collective-permute-done.3.refs_1_, bf16[1024,768]{1,0:T(8,128)(2,1)} %collective-permute-done.4.refs_2_, ...), custom_call_target="tpu_custom_call" | custom-call | flops 4000000000 | bytes 12000000 | tf_op jit(solution)/shard_map/projection_gradients/pallas_call | solution.py:412
  315.6 19.2 %collective-permute-done.18 = bf16[1,4,4,32,576]{4,3,2,1,0:T(8,128)(2,1)S(1)} collective-permute-done((bf16[1,4,4,32,576]{4,3,2,1,0:T(8,128)(2,1)S(1)}, bf16[1,4,4,32,576]{4,3,2,1,0:T(8,128)(2,1)S(1)}, u32[]{:S(2)}, u32[]{:S(2)}) %collective-permute-start.18) | collective-permute-done | bytes 589856 | tf_op jit(solution)/shard_map/ppermute | solution.py:591
  336.3 3.5 fusion
  340.1 12.9 %collective-permute-done.19 = bf16[4,2,32,576]{3,2,1,0:T(8,128)(2,1)S(1)} collective-permute-done((bf16[4,2,32,576]{3,2,1,0:T(8,128)(2,1)S(1)}, bf16[4,2,32,576]{3,2,1,0:T(8,128)(2,1)S(1)}, u32[]{:S(2)}, u32[]{:S(2)}) %collective-permute-start.19) | collective-permute-done | bytes 294944 | tf_op jit(solution)/shard_map/ppermute | solution.py:591
  354.9 7.9 %collective-permute-done.20 = bf16[4,1,32,576]{3,2,1,0:T(8,128)(2,1)S(1)} collective-permute-done((bf16[4,1,32,576]{3,2,1,0:T(8,128)(2,1)S(1)}, bf16[4,1,32,576]{3,2,1,0:T(8,128)(2,1)S(1)}, u32[]{:S(2)}, u32[]{:S(2)}) %collective-permute-start.20) | collective-permute-done | bytes 147488 | tf_op jit(solution)/shard_map/ppermute | solution.py:591
  364.8 14.3 %collective-permute-done.22 = bf16[32,576]{1,0:T(8,128)(2,1)S(1)} collective-permute-done((bf16[32,576]{1,0:T(8,128)(2,1)S(1)}, bf16[32,576]{1,0:T(8,128)(2,1)S(1)}, u32[]{:S(2)}, u32[]{:S(2)}) %collective-permute-start.22) | collective-permute-done | bytes 36896 | tf_op jit(solution)/shard_map/ppermute | solution.py:591
  389.1 5.1 %add_bitcast_fusion = f32[1,1024,768]{2,1,0:T(8,128)} fusion(bf16[1024,768]{1,0:T(8,128)(2,1)} %collective-permute-done.17, bf16[1024,768]{1,0:T(8,128)(2,1)} %collective-permute-done.16, f32[1024,768]{1,0:T(8,128)S(1)} %copy-done.6, f32[1024,768]{1,0:T(8,128)} %get-tuple-element.77), kind=kLoop, calls=%fused_computation.9 | loop fusion | flops 3932160 | bytes 12582912 | tf_op jit(solution)/shard_map/broadcast_in_dim | solution.py:756
  (213 shorter events, 73.2 us)
Async XLA Ops:
  7.2 132.3 %all-gather.4.cloned.1.call-start = ((), (), s32[]{:S(2)}) async-start(), calls=%async_computation.2 | async-start | bytes 11354112 | tf_op jit(solution)/shard_map/all_gather | solution.py:673
  14.0 380.2 %reduce-scatter.2.cloned.1.call-start = ((), (), s32[]{:S(2)}) async-start(), calls=%async_computation.1 | async-start | bytes 11354112 | tf_op jit(solution)/shard_map/reduce_scatter | solution.py:718
  17.8 4.7 %collective-permute-start = (bf16[26,576]{1,0:T(8,128)(2,1)S(1)}, bf16[26,576]{1,0:T(8,128)(2,1)S(1)}, u32[]{:S(2)}, u32[]{:S(2)}) collective-permute-start(bf16[26,576]{1,0:T(8,128)(2,1)S(1)} %bitcast.199), channel_id=1, source_target_pairs={{0,4},{4,0},{8,12},{12,8},{1,5},{5,1},{9,13},{13,9},{2,6},{6,2},{1... | collective-permute-start | bytes 89864 | tf_op jit(solution)/shard_map/ppermute | solution.py:591
  18.3 4.8 %collective-permute-start.1 = (bf16[26,576]{1,0:T(8,128)(2,1)S(1)}, bf16[26,576]{1,0:T(8,128)(2,1)S(1)}, u32[]{:S(2)}, u32[]{:S(2)}) collective-permute-start(bf16[26,576]{1,0:T(8,128)(2,1)S(1)} %bitcast.200), channel_id=1, source_target_pairs={{0,8},{4,12},{8,0},{12,4},{1,9},{5,13},{9,1},{13,5},{2,10},{6,14},... | collective-permute-start | bytes 89864 | tf_op jit(solution)/shard_map/ppermute | solution.py:591
  24.5 48.9 %collective-permute-start.4 = (bf16[1024,768]{1,0:T(8,128)(2,1)S(1)}, bf16[1024,768]{1,0:T(8,128)(2,1)}, u32[]{:S(2)}, u32[]{:S(2)}) collective-permute-start(bf16[1024,768]{1,0:T(8,128)(2,1)S(1)} %bitcast.158), channel_id=1, source_target_pairs={{0,8},{4,12},{8,0},{12,4},{1,9},{5,13},{9,1},{13,5},{2,10},{6,14},... | collective-permute-start | bytes 4718600 | tf_op jit(solution)/shard_map/ppermute | solution.py:591
  26.1 17.5 %collective-permute-start.6 = (bf16[4,26,576]{2,1,0:T(8,128)(2,1)S(1)}, bf16[4,26,576]{2,1,0:T(8,128)(2,1)S(1)}, u32[]{:S(2)}, u32[]{:S(2)}) collective-permute-start(bf16[4,26,576]{2,1,0:T(8,128)(2,1)S(1)} %get-tuple-element.117), channel_id=1, source_target_pairs={{0,2},{1,3},{2,0},{3,1},{4,6},{5,7},{6,4},{7,5},{8,10},{9,11},{10,... | collective-permute-start | bytes 359432 | tf_op jit(solution)/shard_map/ppermute | solution.py:591
  43.7 17.0 %collective-permute-start.7 = (bf16[2,4,26,576]{3,2,1,0:T(8,128)(2,1)S(1)}, bf16[2,4,26,576]{3,2,1,0:T(8,128)(2,1)S(1)}, u32[]{:S(2)}, u32[]{:S(2)}) collective-permute-start(bf16[2,4,26,576]{3,2,1,0:T(8,128)(2,1)S(1)} %maximum_select_fusion.2), channel_id=1, source_target_pairs={{0,1},{1,0},{2,3},{3,2},{4,5},{5,4},{6,7},{7,6},{8,9},{9,8},{10,11... | collective-permute-start | bytes 718856 | tf_op jit(solution)/shard_map/ppermute | solution.py:591
  62.1 12.2 %collective-permute-start.8 = (bf16[4,4,26,576]{3,0,2,1:T(4,128)(2,1)}, bf16[4,4,26,576]{3,0,2,1:T(4,128)(2,1)S(1)}, u32[]{:S(2)}, u32[]{:S(2)}) collective-permute-start(bf16[4,4,26,576]{3,0,2,1:T(4,128)(2,1)} %copy.143), channel_id=1, source_target_pairs={{0,16},{16,0},{1,17},{17,1},{2,18},{18,2},{3,19},{19,3},{4,20},{20... | collective-permute-start | bytes 1437704 | tf_op jit(solution)/shard_map/ppermute | solution.py:591
  67.2 18.4 %collective-permute-start.3 = (bf16[1024,768]{1,0:T(8,128)(2,1)S(1)}, bf16[1024,768]{1,0:T(8,128)(2,1)}, u32[]{:S(2)}, u32[]{:S(2)}) collective-permute-start(bf16[1024,768]{1,0:T(8,128)(2,1)S(1)} %bitcast.159), channel_id=1, source_target_pairs={{0,4},{4,0},{8,12},{12,8},{1,5},{5,1},{9,13},{13,9},{2,6},{6,2},{1... | collective-permute-start | bytes 4718600 | tf_op jit(solution)/shard_map/ppermute | solution.py:591
  73.4 12.3 %collective-permute-start.5 = (bf16[1024,768]{1,0:T(8,128)(2,1)}, bf16[1024,768]{1,0:T(8,128)(2,1)}, u32[]{:S(2)}, u32[]{:S(2)}) collective-permute-start(bf16[1024,768]{1,0:T(8,128)(2,1)} %collective-permute-done.4.refs_2_), channel_id=1, source_target_pairs={{0,4},{4,0},{8,12},{12,8},{1,5},{5,1},{9,13},{13,9},{2,6},{6,2},{1... | collective-permute-start | bytes 4718600 | tf_op jit(solution)/shard_map/ppermute | solution.py:591
  137.3 11.9 %collective-permute-start.10 = (bf16[192,1024]{1,0:T(8,128)(2,1)S(1)}, bf16[192,1024]{1,0:T(8,128)(2,1)S(1)}, u32[]{:S(2)}, u32[]{:S(2)}) collective-permute-start(bf16[192,1024]{1,0:T(8,128)(2,1)S(1)} %get-tuple-element.92), channel_id=1, source_target_pairs={{0,8},{4,12},{8,0},{12,4},{1,9},{5,13},{9,1},{13,5},{2,10},{6,14},... | collective-permute-start | bytes 1179656 | tf_op jit(solution)/shard_map/ppermute | solution.py:591
  138.2 18.8 %collective-permute-start.11 = (bf16[192,1024]{1,0:T(8,128)(2,1)S(1)}, bf16[192,1024]{1,0:T(8,128)(2,1)S(1)}, u32[]{:S(2)}, u32[]{:S(2)}) collective-permute-start(bf16[192,1024]{1,0:T(8,128)(2,1)S(1)} %get-tuple-element.91), channel_id=1, source_target_pairs={{0,12},{4,8},{8,4},{12,0},{1,13},{5,9},{9,5},{13,1},{2,14},{6,10},... | collective-permute-start | bytes 1179656 | tf_op jit(solution)/shard_map/ppermute | solution.py:591
  139.2 17.8 %collective-permute-start.9 = (bf16[192,1024]{1,0:T(8,128)(2,1)S(1)}, bf16[192,1024]{1,0:T(8,128)(2,1)S(1)}, u32[]{:S(2)}, u32[]{:S(2)}) collective-permute-start(bf16[192,1024]{1,0:T(8,128)(2,1)S(1)} %get-tuple-element.93), channel_id=1, source_target_pairs={{0,4},{4,0},{8,12},{12,8},{1,5},{5,1},{9,13},{13,9},{2,6},{6,2},{1... | collective-permute-start | bytes 1179656 | tf_op jit(solution)/shard_map/ppermute | solution.py:591
  203.5 16.5 %collective-permute-start.12 = (bf16[192,1024]{1,0:T(8,128)(2,1)S(1)}, bf16[192,1024]{1,0:T(8,128)(2,1)S(1)}, u32[]{:S(2)}, u32[]{:S(2)}) collective-permute-start(bf16[192,1024]{1,0:T(8,128)(2,1)S(1)} %get-tuple-element.89), channel_id=1, source_target_pairs={{0,4},{4,0},{8,12},{12,8},{1,5},{5,1},{9,13},{13,9},{2,6},{6,2},{1... | collective-permute-start | bytes 1179656 | tf_op jit(solution)/shard_map/ppermute | solution.py:591
  203.6 16.3 %collective-permute-start.13 = (bf16[192,1024]{1,0:T(8,128)(2,1)S(1)}, bf16[192,1024]{1,0:T(8,128)(2,1)S(1)}, u32[]{:S(2)}, u32[]{:S(2)}) collective-permute-start(bf16[192,1024]{1,0:T(8,128)(2,1)S(1)} %get-tuple-element.88), channel_id=1, source_target_pairs={{0,8},{4,12},{8,0},{12,4},{1,9},{5,13},{9,1},{13,5},{2,10},{6,14},... | collective-permute-start | bytes 1179656 | tf_op jit(solution)/shard_map/ppermute | solution.py:591
  204.5 18.3 %collective-permute-start.14 = (bf16[192,1024]{1,0:T(8,128)(2,1)S(1)}, bf16[192,1024]{1,0:T(8,128)(2,1)S(1)}, u32[]{:S(2)}, u32[]{:S(2)}) collective-permute-start(bf16[192,1024]{1,0:T(8,128)(2,1)S(1)} %get-tuple-element.87), channel_id=1, source_target_pairs={{0,12},{4,8},{8,4},{12,0},{1,13},{5,9},{9,5},{13,1},{2,14},{6,10},... | collective-permute-start | bytes 1179656 | tf_op jit(solution)/shard_map/ppermute | solution.py:591
  305.5 30.8 %collective-permute-start.15 = (bf16[1024,768]{1,0:T(8,128)(2,1)}, bf16[1024,768]{1,0:T(8,128)(2,1)}, u32[]{:S(2)}, u32[]{:S(2)}) collective-permute-start(bf16[1024,768]{1,0:T(8,128)(2,1)} %get-tuple-element.85), channel_id=1, source_target_pairs={{0,4},{4,0},{8,12},{12,8},{1,5},{5,1},{9,13},{13,9},{2,6},{6,2},{1... | collective-permute-start | bytes 4718600 | tf_op jit(solution)/shard_map/ppermute | solution.py:591
  314.1 20.6 %collective-permute-start.18 = (bf16[1,4,4,32,576]{4,3,2,1,0:T(8,128)(2,1)S(1)}, bf16[1,4,4,32,576]{4,3,2,1,0:T(8,128)(2,1)S(1)}, u32[]{:S(2)}, u32[]{:S(2)}) collective-permute-start(bf16[1,4,4,32,576]{4,3,2,1,0:T(8,128)(2,1)S(1)} %constant_dynamic-slice_fusion.1), channel_id=1, source_target_pairs={{0,16},{16,0},{1,17},{17,1},{2,18},{18,2},{3,19},{19,3},{4,20},{20... | collective-permute-start | bytes 1769480 | tf_op jit(solution)/shard_map/ppermute | solution.py:591
  315.5 73.6 %collective-permute-start.17 = (bf16[1024,768]{1,0:T(8,128)(2,1)}, bf16[1024,768]{1,0:T(8,128)(2,1)}, u32[]{:S(2)}, u32[]{:S(2)}) collective-permute-start(bf16[1024,768]{1,0:T(8,128)(2,1)} %get-tuple-element.86), channel_id=1, source_target_pairs={{0,4},{4,0},{8,12},{12,8},{1,5},{5,1},{9,13},{13,9},{2,6},{6,2},{1... | collective-permute-start | bytes 4718600 | tf_op jit(solution)/shard_map/ppermute | solution.py:591
  334.9 18.1 %collective-permute-start.19 = (bf16[4,2,32,576]{3,2,1,0:T(8,128)(2,1)S(1)}, bf16[4,2,32,576]{3,2,1,0:T(8,128)(2,1)S(1)}, u32[]{:S(2)}, u32[]{:S(2)}) collective-permute-start(bf16[4,2,32,576]{3,2,1,0:T(8,128)(2,1)S(1)} %dynamic-slice_bitcast_fusion), channel_id=1, source_target_pairs={{0,1},{1,0},{2,3},{3,2},{4,5},{5,4},{6,7},{7,6},{8,9},{9,8},{10,11... | collective-permute-start | bytes 884744 | tf_op jit(solution)/shard_map/ppermute | solution.py:591
  339.8 49.3 %collective-permute-start.16 = (bf16[1024,768]{1,0:T(8,128)(2,1)}, bf16[1024,768]{1,0:T(8,128)(2,1)}, u32[]{:S(2)}, u32[]{:S(2)}) collective-permute-start(bf16[1024,768]{1,0:T(8,128)(2,1)} %fusion), channel_id=1, source_target_pairs={{0,8},{4,12},{8,0},{12,4},{1,9},{5,13},{9,1},{13,5},{2,10},{6,14},... | collective-permute-start | bytes 4718600 | tf_op jit(solution)/shard_map/ppermute | solution.py:591
  353.1 9.7 %collective-permute-start.20 = (bf16[4,1,32,576]{3,2,1,0:T(8,128)(2,1)S(1)}, bf16[4,1,32,576]{3,2,1,0:T(8,128)(2,1)S(1)}, u32[]{:S(2)}, u32[]{:S(2)}) collective-permute-start(bf16[4,1,32,576]{3,2,1,0:T(8,128)(2,1)S(1)} %constant_dynamic-slice_fusion), channel_id=1, source_target_pairs={{0,2},{1,3},{2,0},{3,1},{4,6},{5,7},{6,4},{7,5},{8,10},{9,11},{10,... | collective-permute-start | bytes 442376 | tf_op jit(solution)/shard_map/ppermute | solution.py:591
  362.9 16.2 %collective-permute-start.22 = (bf16[32,576]{1,0:T(8,128)(2,1)S(1)}, bf16[32,576]{1,0:T(8,128)(2,1)S(1)}, u32[]{:S(2)}, u32[]{:S(2)}) collective-permute-start(bf16[32,576]{1,0:T(8,128)(2,1)S(1)} %get-tuple-element.113), channel_id=1, source_target_pairs={{0,8},{4,12},{8,0},{12,4},{1,9},{5,13},{9,1},{13,5},{2,10},{6,14},... | collective-permute-start | bytes 110600 | tf_op jit(solution)/shard_map/ppermute | solution.py:591
  363.0 16.1 %collective-permute-start.23 = (bf16[32,576]{1,0:T(8,128)(2,1)S(1)}, bf16[32,576]{1,0:T(8,128)(2,1)S(1)}, u32[]{:S(2)}, u32[]{:S(2)}) collective-permute-start(bf16[32,576]{1,0:T(8,128)(2,1)S(1)} %get-tuple-element.112), channel_id=1, source_target_pairs={{0,12},{4,8},{8,4},{12,0},{1,13},{5,9},{9,5},{13,1},{2,14},{6,10},... | collective-permute-start | bytes 110600 | tf_op jit(solution)/shard_map/ppermute | solution.py:591
  (23 other events, 145.7 us)
Sparse Core Ops, SparseCore 0:
  14.1 105.9 all-gather.3
  223.0 153.4 reduce-scatter.1

commit v3 on v2

v3 whole, which is shorter than its diff:
```python
import functools
import jax
import jax.numpy as jnp
from jax import lax
from jax.experimental import pallas as pl
from jax.sharding import PartitionSpec as P
from jax.experimental.pallas import tpu as pltpu

HEAD_DIM = 64
BLOCK = 64
PAIR = 2 * BLOCK
MASKED = -1e30
bf16 = jnp.bfloat16
f32 = jnp.float32


def dot_nn(a, b):
    return lax.dot_general(a, b, (((1,), (0,)), ((), ())), preferred_element_type=f32)


def dot_nt(a, b):
    return lax.dot_general(a, b, (((1,), (1,)), ((), ())), preferred_element_type=f32)


def dot_tn(a, b):
    return lax.dot_general(a, b, (((0,), (0,)), ((), ())), preferred_element_type=f32)


def pair_table(rand_local, global_ids, flip, nblocks):
    heads = rand_local.shape[0]
    null = nblocks
    first = (2 * jnp.arange(nblocks // 2, dtype=jnp.int32)) ^ flip

    def near(block):
        bad = (block < 0) | (block >= nblocks) | (block == global_ids[0]) | (block == global_ids[1])
        return jnp.where(bad, null, block ^ flip)

    rand_first = rand_local[:, first, :] ^ flip
    rand_second = rand_local[:, first + 1, :] ^ flip
    nears = jnp.stack([near(first), near(first + 1), near(first - 1), near(first + 2)], axis=1)
    nears = jnp.broadcast_to(nears[None], (heads,) + nears.shape)
    return jnp.concatenate(
        [nears[:, :, 0:3], rand_first, nears[:, :, 3:4], rand_second], axis=2
    ).astype(jnp.int32).reshape(-1)


def slots(tab_ref, gl_ref, head, pair, npairs):
    at = (head * npairs + pair) * 10
    got = [pl.multiple_of(tab_ref[at + j] * BLOCK, BLOCK) for j in range(10)]
    glob = [pl.multiple_of(gl_ref[j] * BLOCK, BLOCK) for j in range(2)]
    return got[0:2] + glob, got[2:6], got[6:10]


def stack_rows(ref, offsets, lanes):
    return jnp.concatenate([ref[pl.ds(o, BLOCK), lanes] for o in offsets], axis=0)


def lane_halves(width, dtype):
    lane = lax.broadcasted_iota(jnp.int32, (1, width), 1) % PAIR
    first = (lane < BLOCK).astype(dtype)
    second = (lane >= BLOCK).astype(dtype)
    return first, second


UNROLL = 4


def head_lanes(h):
    return slice(h * PAIR, (h + 1) * PAIR)


def query_columns(q_ref, mask_ref, h, at):
    return jnp.concatenate([q_ref[h * BLOCK : (h + 1) * BLOCK, pl.ds(at, PAIR)], mask_ref[:, pl.ds(at, PAIR)]], axis=0)


def global_queries(q_ref, mask_ref, h, gl_ref):
    return jnp.concatenate(
        [
            global_columns(q_ref, slice(h * BLOCK, (h + 1) * BLOCK), gl_ref),
            global_columns(mask_ref, slice(0, BLOCK), gl_ref),
        ],
        axis=0,
    ).astype(bf16)


def global_columns(src_ref, rows, gl_ref):
    lane = lax.broadcasted_iota(jnp.int32, (1, PAIR), 1)
    parts = []
    for g in range(2):
        block = gl_ref[g]
        at = pl.multiple_of((block // 2) * PAIR, PAIR)
        both = src_ref[rows, pl.ds(at, PAIR)].astype(f32)
        moved = pltpu.roll(both, BLOCK, 1)
        parts.append(jnp.where(block % 2 == g, both, moved))
    return jnp.where(lane < BLOCK, parts[0], parts[1])


def put_global_columns(dst_ref, rows, gl_ref, value, per_chunk):
    lane = lax.broadcasted_iota(jnp.int32, (1, PAIR), 1)
    moved = pltpu.roll(value, BLOCK, 1)
    for g in range(2):
        block = gl_ref[g]
        pair = block // 2
        half = block % 2
        chunk = pair // per_chunk
        at = pl.multiple_of((pair % per_chunk) * PAIR, PAIR)
        src = jnp.where(half == g, value, moved)
        old = dst_ref[chunk, rows, pl.ds(at, PAIR)].astype(f32)
        new = jnp.where((lane >= BLOCK) == (half == 1), src, old)
        dst_ref[chunk, rows, pl.ds(at, PAIR)] = new.astype(dst_ref.dtype)


def project_rows(x, seg, w_ref, wq, bkv_ref, bq_ref, k_ref, v_ref, q_ref, mask_ref, at):
    n = x.shape[0]
    lanes = v_ref.shape[1]
    y = dot_nn(x, w_ref[:, 0:lanes]) + bkv_ref[...]
    spot = lax.broadcasted_iota(jnp.int32, (PAIR, n), 0) - BLOCK
    mark = jnp.transpose((spot == seg).astype(f32), (1, 0))
    lane = lax.broadcasted_iota(jnp.int32, (1, PAIR), 1)
    rows = pl.ds(at, n)
    v_ref[rows, :] = y.astype(bf16)
    for h in range(lanes // PAIR):
        k_ref[rows, head_lanes(h)] = jnp.where(lane < BLOCK, y[:, head_lanes(h)], mark).astype(bf16)
    z = (dot_nt(wq, x) + bq_ref[...]).astype(bf16)
    q_ref[:, rows] = (z.astype(f32) * HEAD_DIM ** -0.5).astype(bf16)
    row = lax.broadcasted_iota(jnp.int32, (BLOCK, n), 0)
    mask_ref[:, rows] = jnp.where((row <= 16) & (row != seg), MASKED, 0.0).astype(bf16)


def query_weights(w_ref, heads):
    at = heads * PAIR
    cols = w_ref[:, at : at + 2 * PAIR].astype(f32)
    return jnp.transpose(cols, (1, 0))[0 : heads * HEAD_DIM].astype(bf16)


def forward_kernel(heads, chunks, tab_ref, gl_ref, *refs):
    x_refs = refs[0:chunks]
    seg_ref, w_ref, bkv_ref, bq_ref = refs[chunks : chunks + 4]
    out_refs = refs[chunks + 4 : 2 * chunks + 4]
    lse_ref, lseg_ref, k_sc, v_sc, q_sc, mask_sc, s_sc, out_ref = refs[2 * chunks + 4 :]
    rows = x_refs[0].shape[0]
    length = rows * chunks
    npairs = length // PAIR
    per_chunk = npairs // chunks
    tile = 256
    wq = query_weights(w_ref, heads)
    for c in range(chunks):

        @pl.loop(0, rows // tile)
        def _(t):
            at = pl.multiple_of(t * tile, tile)
            project_rows(
                x_refs[c][pl.ds(at, tile), :], seg_ref[c : c + 1, pl.ds(at, tile)], w_ref, wq, bkv_ref, bq_ref,
                k_sc, v_sc, q_sc, mask_sc, pl.multiple_of(c * rows + t * tile, tile),
            )

    null_lane = lax.broadcasted_iota(jnp.int32, (BLOCK, heads * PAIR), 1) % PAIR
    k_sc[pl.ds(length, BLOCK), :] = (null_lane == BLOCK + 16).astype(f32).astype(bf16)
    v_sc[pl.ds(length, BLOCK), :] = jnp.zeros((BLOCK, heads * PAIR), bf16)
    first, second = lane_halves(PAIR, bf16)
    lane = lax.broadcasted_iota(jnp.int32, (1, PAIR), 1)

    def one_pair(pair):
        chunk = pair // per_chunk
        local = pl.multiple_of((pair % per_chunk) * PAIR, PAIR)
        at = pl.multiple_of(pair * PAIR, PAIR)
        for h in range(heads):
            shared, mine, other = slots(tab_ref, gl_ref, h, pair, npairs)
            kl = head_lanes(h)
            q = query_columns(q_sc, mask_sc, h, at)
            s_sh = dot_nn(stack_rows(k_sc, shared, kl), q)
            k_pr = jnp.concatenate([stack_rows(k_sc, mine, kl), stack_rows(k_sc, other, kl)], axis=1)
            s_pr = dot_nn(k_pr, jnp.concatenate([q * first, q * second], axis=0))
            peak = jnp.maximum(jnp.max(s_sh, axis=0, keepdims=True), jnp.max(s_pr, axis=0, keepdims=True))
            e_sh = jnp.exp(s_sh - peak)
            e_pr = jnp.exp(s_pr - peak)
            total = jnp.sum(e_sh, axis=0, keepdims=True) + jnp.sum(e_pr, axis=0, keepdims=True)
            inv = 1.0 / total
            p_sh = (e_sh * inv).astype(bf16)
            p_pr = (e_pr * inv).astype(bf16)
            v_pr = jnp.concatenate([stack_rows(v_sc, mine, kl), stack_rows(v_sc, other, kl)], axis=1)
            o_sh = dot_tn(stack_rows(v_sc, shared, kl), p_sh)
            o_pr = dot_tn(v_pr, p_pr)
            ctx = o_sh[BLOCK:PAIR] + jnp.where(lane < BLOCK, o_pr[BLOCK:PAIR], o_pr[PAIR + BLOCK : 2 * PAIR])
            out_ref[chunk, h * BLOCK : (h + 1) * BLOCK, pl.ds(local, PAIR)] = ctx.astype(bf16)
            lse_ref[h, pl.ds(pair, 1), :] = peak + jnp.log(total)

    @pl.loop(0, npairs // UNROLL)
    def _(some):
        for i in range(UNROLL):
            one_pair(UNROLL * some + i)

    step = 512
    queries = [global_queries(q_sc, mask_sc, h, gl_ref) for h in range(heads)]

    def score(c, peaks):
        at = pl.multiple_of(c * step, step)
        new = []
        for h in range(heads):
            got = dot_nn(k_sc[pl.ds(at, step), head_lanes(h)], queries[h])
            s_sc[h, pl.ds(at, step), :] = got
            new.append(jnp.maximum(peaks[h], jnp.max(got, axis=0, keepdims=True)))
        return tuple(new)

    peaks = lax.fori_loop(0, length // step, score, (jnp.full((1, PAIR), MASKED, f32),) * heads)

    def gather(c, carry):
        at = pl.multiple_of(c * step, step)
        new = []
        for h in range(heads):
            total, ctx = carry[h]
            e = jnp.exp(s_sc[h, pl.ds(at, step), :] - peaks[h])
            ctx = ctx + dot_tn(v_sc[pl.ds(at, step), head_lanes(h)], e.astype(bf16))
            new.append((total + jnp.sum(e, axis=0, keepdims=True), ctx))
        return tuple(new)

    start = (jnp.zeros((1, PAIR), f32), jnp.zeros((PAIR, PAIR), f32))
    sums = lax.fori_loop(0, length // step, gather, (start,) * heads)
    for h in range(heads):
        total, ctx = sums[h]
        ctx = ctx[BLOCK:PAIR] * (1.0 / total)
        put_global_columns(out_ref, slice(h * BLOCK, (h + 1) * BLOCK), gl_ref, ctx, per_chunk)
        lseg_ref[h : h + 1, :] = peaks[h] + jnp.log(total)
    for c in range(chunks):
        out_refs[c][...] = out_ref[c]


def attention_forward(tab, gl, x, seg, w, b_kv, b_q):
    chunks = len(x)
    rows = x[0].shape[0]
    length = rows * chunks
    heads = b_q.shape[0] // HEAD_DIM
    whole = lambda: pl.BlockSpec(memory_space=pltpu.VMEM)
    got = pl.pallas_call(
        functools.partial(forward_kernel, heads, chunks),
        out_shape=(jax.ShapeDtypeStruct((heads * HEAD_DIM, rows), bf16),) * chunks
        + (
            jax.ShapeDtypeStruct((heads, length // PAIR, PAIR), f32),
            jax.ShapeDtypeStruct((heads, PAIR), f32),
            jax.ShapeDtypeStruct((length + BLOCK, heads * PAIR), bf16),
            jax.ShapeDtypeStruct((length + BLOCK, heads * PAIR), bf16),
            jax.ShapeDtypeStruct((heads * HEAD_DIM, length), bf16),
            jax.ShapeDtypeStruct((BLOCK, length), bf16),
        ),
        in_specs=[pl.BlockSpec(memory_space=pltpu.SMEM)] * 2 + [whole() for _ in range(chunks + 4)],
        out_specs=tuple(whole() for _ in range(chunks + 6)),
        scratch_shapes=[
            pltpu.VMEM((heads, length, PAIR), f32),
            pltpu.VMEM((chunks, heads * HEAD_DIM, rows), bf16),
        ],
        compiler_params=pltpu.CompilerParams(vmem_limit_bytes=56 << 20),
        cost_estimate=pl.CostEstimate(flops=12_000_000_000, bytes_accessed=16_000_000, transcendentals=8_000_000),
        name="attention_forward",
    )(tab, gl, *x, seg, w, b_kv, b_q)
    return got[:chunks], got[chunks:]


def backward_kernel(heads, chunks, tab_ref, gl_ref, *refs):
    do_refs = refs[:chunks]
    (k_sc, v_sc, q_sc, mask_sc, lse_ref, lseg_ref, w_ref, dq_ref, dkv_ref, first_ref) = refs[chunks : chunks + 10]
    part_refs = refs[chunks + 10 : 2 * chunks + 9]
    do_sc, acc, p_sc, d_sc, dqg_sc = refs[2 * chunks + 9 :]
    rows = do_refs[0].shape[1]
    length = rows * chunks
    npairs = length // PAIR
    per_chunk = npairs // chunks
    for c in range(chunks):
        do_sc[:, c * rows : (c + 1) * rows] = do_refs[c][...]
    first, second = lane_halves(PAIR, bf16)
    first2, second2 = lane_halves(2 * PAIR, bf16)
    ffirst, fsecond = lane_halves(PAIR, f32)
    lane = lax.broadcasted_iota(jnp.int32, (1, PAIR), 1)
    zeros = jnp.zeros((BLOCK, PAIR), bf16)

    def value_rows(do):
        return jnp.concatenate([zeros, do], axis=0)

    def sources(q, do):
        top = jnp.concatenate([q[0:BLOCK], zeros], axis=1)
        return jnp.concatenate([top, jnp.concatenate([zeros, do], axis=1)], axis=0)

    step = 512
    queries = [global_queries(q_sc, mask_sc, h, gl_ref) for h in range(heads)]
    grads = [global_columns(do_sc, slice(h * BLOCK, (h + 1) * BLOCK), gl_ref).astype(bf16) for h in range(heads)]

    def weigh(c, deltas):
        at = pl.multiple_of(c * step, step)
        new = []
        for h in range(heads):
            p = jnp.exp(dot_nn(k_sc[pl.ds(at, step), head_lanes(h)], queries[h]) - lseg_ref[h : h + 1, :])
            dp = dot_nn(v_sc[pl.ds(at, step), head_lanes(h)], value_rows(grads[h]))
            p_sc[h, pl.ds(at, step), :] = p
            d_sc[h, pl.ds(at, step), :] = dp
            new.append(deltas[h] + jnp.sum(p * dp, axis=0, keepdims=True))
        return tuple(new)

    deltas = lax.fori_loop(0, length // step, weigh, (jnp.zeros((1, PAIR), f32),) * heads)

    def spread(c, dqs):
        at = pl.multiple_of(c * step, step)
        new = []
        for h in range(heads):
            p = p_sc[h, pl.ds(at, step), :]
            ds = (p * (d_sc[h, pl.ds(at, step), :] - deltas[h])).astype(bf16)
            both = jnp.concatenate([ds, p.astype(bf16)], axis=1)
            acc[h, pl.ds(at, step), :] = dot_nt(both, sources(queries[h], grads[h]))
            new.append(dqs[h] + dot_tn(k_sc[pl.ds(at, step), head_lanes(h)], ds))
        return tuple(new)

    dqs = lax.fori_loop(0, length // step, spread, (jnp.zeros((PAIR, PAIR), f32),) * heads)
    for h in range(heads):
        dqg_sc[h] = dqs[h][0:BLOCK] * (HEAD_DIM ** -0.5)
        acc[h, pl.ds(length, BLOCK), :] = jnp.zeros((BLOCK, PAIR), f32)

    def one_pair(pair):
        chunk = pair // per_chunk
        local = pl.multiple_of((pair % per_chunk) * PAIR, PAIR)
        at = pl.multiple_of(pair * PAIR, PAIR)
        hit_first = (gl_ref[0] == 2 * pair) | (gl_ref[1] == 2 * pair)
        hit_second = (gl_ref[0] == 2 * pair + 1) | (gl_ref[1] == 2 * pair + 1)
        shut = ffirst * jnp.where(hit_first, -MASKED, 0.0) + fsecond * jnp.where(hit_second, -MASKED, 0.0)
        for h in range(heads):
            shared, mine, other = slots(tab_ref, gl_ref, h, pair, npairs)
            kl = head_lanes(h)
            q = query_columns(q_sc, mask_sc, h, at)
            do = do_sc[h * BLOCK : (h + 1) * BLOCK, pl.ds(at, PAIR)]
            do_v = value_rows(do)
            lse = lse_ref[h, pl.ds(pair, 1), :] + shut
            k_sh = stack_rows(k_sc, shared, kl)
            k_pr = jnp.concatenate([stack_rows(k_sc, mine, kl), stack_rows(k_sc, other, kl)], axis=1)
            p_sh = jnp.exp(dot_nn(k_sh, q) - lse)
            p_pr = jnp.exp(dot_nn(k_pr, jnp.concatenate([q * first, q * second], axis=0)) - lse)
            d_sh = dot_nn(stack_rows(v_sc, shared, kl), do_v)
            v_pr = jnp.concatenate([stack_rows(v_sc, mine, kl), stack_rows(v_sc, other, kl)], axis=1)
            d_pr = dot_nn(v_pr, jnp.concatenate([do_v * first, do_v * second], axis=0))
            delta = jnp.sum(p_sh * d_sh, axis=0, keepdims=True) + jnp.sum(p_pr * d_pr, axis=0, keepdims=True)
            ds_sh = (p_sh * (d_sh - delta)).astype(bf16)
            ds_pr = (p_pr * (d_pr - delta)).astype(bf16)
            src = sources(q, do)
            g_sh = dot_nt(jnp.concatenate([ds_sh, p_sh.astype(bf16)], axis=1), src)
            src2 = jnp.concatenate([src * first2, src * second2], axis=0)
            g_pr = dot_nt(jnp.concatenate([ds_pr, p_pr.astype(bf16)], axis=1), src2)
            for j, o in enumerate(shared):
                acc[h, pl.ds(o, BLOCK), :] += g_sh[j * BLOCK : (j + 1) * BLOCK]
            for j, o in enumerate(mine):
                acc[h, pl.ds(o, BLOCK), :] += g_pr[j * BLOCK : (j + 1) * BLOCK, 0:PAIR]
            for j, o in enumerate(other):
                acc[h, pl.ds(o, BLOCK), :] += g_pr[j * BLOCK : (j + 1) * BLOCK, PAIR:]
            t_sh = dot_tn(k_sh, ds_sh)
            t_pr = dot_tn(k_pr, ds_pr)
            dq = t_sh[0:BLOCK] + jnp.where(lane < BLOCK, t_pr[0:BLOCK], t_pr[PAIR : PAIR + BLOCK])
            dq_ref[chunk, h * BLOCK : (h + 1) * BLOCK, pl.ds(local, PAIR)] = (dq * (HEAD_DIM ** -0.5)).astype(bf16)

    @pl.loop(0, npairs // UNROLL)
    def _(some):
        for i in range(UNROLL):
            one_pair(UNROLL * some + i)

    for h in range(heads):
        put_global_columns(dq_ref, slice(h * BLOCK, (h + 1) * BLOCK), gl_ref, dqg_sc[h], per_chunk)
        for c in range(chunks):
            dkv_ref[c, :, h * PAIR : (h + 1) * PAIR] = acc[h, pl.ds(c * rows, rows), :].astype(bf16)
    tile = 256
    wq = query_weights(w_ref, heads)
    for c in range(chunks):

        @pl.loop(0, rows // tile)
        def _(t):
            at = pl.multiple_of(t * tile, tile)
            got = dot_tn(dq_ref[c, :, pl.ds(at, tile)], wq)
            got = got + dot_nt(dkv_ref[c, pl.ds(at, tile), :], w_ref[:, 0 : heads * PAIR])
            if c == 0:
                first_ref[pl.ds(at, tile), :] = got
            else:
                part_refs[c - 1][pl.ds(at, tile), :] = got.astype(bf16)


def attention_backward(tab, gl, do, k, v, q, mask, lse, lseg, w):
    chunks = len(do)
    group, rows = do[0].shape
    heads = group // HEAD_DIM
    width = w.shape[0]
    length = rows * chunks
    whole = lambda: pl.BlockSpec(memory_space=pltpu.VMEM)
    return pl.pallas_call(
        functools.partial(backward_kernel, heads, chunks),
        out_shape=(
            jax.ShapeDtypeStruct((chunks, group, rows), bf16),
            jax.ShapeDtypeStruct((chunks, rows, heads * PAIR), bf16),
            jax.ShapeDtypeStruct((rows, width), f32),
        )
        + (jax.ShapeDtypeStruct((rows, width), bf16),) * (chunks - 1),
        in_specs=[pl.BlockSpec(memory_space=pltpu.SMEM)] * 2 + [whole() for _ in range(chunks + 7)],
        out_specs=tuple(whole() for _ in range(chunks + 2)),
        scratch_shapes=[
            pltpu.VMEM((group, length), bf16),
            pltpu.VMEM((heads, length + BLOCK, PAIR), f32),
            pltpu.VMEM((heads, length, PAIR), f32),
            pltpu.VMEM((heads, length, PAIR), f32),
            pltpu.VMEM((heads, BLOCK, PAIR), f32),
        ],
        compiler_params=pltpu.CompilerParams(vmem_limit_bytes=60 << 20),
        cost_estimate=pl.CostEstimate(flops=30_000_000_000, bytes_accessed=24_000_000, transcendentals=8_000_000),
        name="attention_backward",
    )(tab, gl, *do, k, v, q, mask, lse, lseg, w)


def round_up(value, to):
    return -(-value // to) * to


def half_columns(ref, index, place):
    at = index // 2 * PAIR
    both = ref[:, at : at + PAIR].astype(f32)
    return both if index % 2 == place else pltpu.roll(both, BLOCK, 1)


def two_halves(first, second):
    lane = lax.broadcasted_iota(jnp.int32, (1, PAIR), 1)
    return jnp.where(lane < BLOCK, first, second)


def pack_kernel(seq_n, wq_ref, wk_ref, wv_ref, wo_ref, up_ref, down_ref, bup_ref, vec_ref, pack_ref, rest_ref):
    own, width = wq_ref.shape
    heads = width // HEAD_DIM // seq_n
    blocks, inner = pack_ref.shape[0], pack_ref.shape[2]
    for s in range(seq_n):
        pieces = [
            two_halves(half_columns(wk_ref, s * heads + h, 0), half_columns(wv_ref, s * heads + h, 1))
            for h in range(heads)
        ]
        for h in range(0, heads, 2):
            second = half_columns(wq_ref, s * heads + h + 1, 1) if h + 1 < heads else jnp.zeros((own, PAIR), f32)
            pieces.append(two_halves(half_columns(wq_ref, s * heads + h, 0), second))
        piece = jnp.concatenate(pieces, axis=1).astype(bf16)
        notes = jnp.concatenate([vec_ref[...], jnp.zeros((8, piece.shape[1] - width), bf16)], axis=1) if (
            piece.shape[1] > width
        ) else vec_ref[:, 0 : piece.shape[1]]
        for b in range(blocks):
            for i in range(inner):
                pack_ref[b, s, i, 0:own, :] = piece
                pack_ref[b, s, i, own : own + 8, :] = notes
    u = up_ref.shape[0]
    rest_ref[0:u, :] = up_ref[...]
    rest_ref[u : 2 * u, :] = down_ref[...]
    rest_ref[2 * u : 2 * u + own, :] = wo_ref[...]
    row = lax.broadcasted_iota(jnp.int32, (8, 1), 0)
    block = jnp.where(row == 7, bup_ref[...].astype(f32), vec_ref[...].astype(f32))
    rest_ref[2 * u + own : 2 * u + own + 8, :] = block.astype(bf16)


def packed_weights(w_q, w_k, w_v, w_o, w_up, w_down, b_up, vec, dp_n, seq_n, ffn_n):
    own, width = w_q.shape
    heads = width // HEAD_DIM // seq_n
    lanes = heads * PAIR + round_up(heads * HEAD_DIM, PAIR)
    u = w_up.shape[0]
    if own % 8 or u % 16:
        group = heads * HEAD_DIM
        cols = lambda w: w.reshape(own, seq_n, heads, HEAD_DIM).transpose(1, 0, 2, 3)
        kv = jnp.stack([cols(w_k), cols(w_v)], axis=3).reshape(seq_n, own, 2 * group)
        piece = jnp.concatenate([kv, cols(w_q).reshape(seq_n, own, group)], axis=2)
        piece = jnp.pad(piece, ((0, 0), (0, round_up(own, 8) - own), (0, lanes - 3 * group)))
        notes = jnp.broadcast_to(vec[None, :, :lanes], (seq_n, 8, lanes))
        piece = jnp.concatenate([piece, notes], axis=1)
        pack = jnp.broadcast_to(piece[None, :, None], (dp_n, seq_n, ffn_n) + piece.shape[1:])
        w_o = jnp.pad(w_o, ((0, round_up(own, 8) - own), (0, 0)))
        return pack, jnp.concatenate([w_up, w_down, w_o, vec[:7], b_up], axis=0)
    whole = lambda: pl.BlockSpec(memory_space=pltpu.VMEM)
    return pl.pallas_call(
        functools.partial(pack_kernel, seq_n),
        out_shape=(
            jax.ShapeDtypeStruct((dp_n, seq_n, ffn_n, own + 8, lanes), bf16),
            jax.ShapeDtypeStruct((2 * u + own + 8, width), bf16),
        ),
        in_specs=[whole() for _ in range(8)],
        out_specs=(whole(), whole()),
        name="packed_weights",
    )(w_q, w_k, w_v, w_o, w_up, w_down, b_up, vec)


def weights_kernel(chunks, direct, *refs):
    x_refs = refs[:chunks]
    dq_ref, dkv_ref, out_ref, sums_ref, acc = refs[chunks:]
    group, rows = dq_ref.shape[1], dq_ref.shape[2]
    lanes = dkv_ref.shape[2]
    ones = jnp.ones((8, rows), bf16)
    sum_q = jnp.zeros((8, group), f32)
    sum_kv = jnp.zeros((8, lanes), f32)
    acc[lanes + group :, :] = jnp.zeros((acc.shape[0] - lanes - group, acc.shape[1]), f32)
    for c in range(chunks):
        x = x_refs[c][...]
        got_kv = dot_tn(dkv_ref[c], x)
        got_q = dot_nn(dq_ref[c], x)
        if c == 0:
            acc[0:lanes, :] = got_kv
            acc[lanes : lanes + group, :] = got_q
        else:
            acc[0:lanes, :] += got_kv
            acc[lanes : lanes + group, :] += got_q
        sum_q = sum_q + dot_nt(ones, dq_ref[c])
        sum_kv = sum_kv + dot_nn(ones, dkv_ref[c])
    grad = jnp.transpose(acc[...], (1, 0))
    blank = jnp.zeros((8, acc.shape[0] - lanes - group), f32)
    sums = jnp.concatenate([sum_kv, sum_q, blank], axis=1)
    sums_ref[...] = sums
    if direct:
        blocks, per, _ = out_ref.shape
        own = per - 8
        grad = grad.astype(f32).reshape(blocks, own, acc.shape[0])
        for b in range(blocks):
            out_ref[b, 0:own, :] = grad[b].astype(bf16)
            out_ref[b, own:, :] = sums.astype(bf16)
    else:
        out_ref[...] = grad.astype(bf16)


def projection_gradients(x, dq, dkv, own, devices):
    chunks, group, rows = dq.shape
    width = x[0].shape[1]
    lanes = dkv.shape[2]
    full = lanes + round_up(group, PAIR)
    direct = own % 8 == 0
    whole = lambda: pl.BlockSpec(memory_space=pltpu.VMEM)
    out, sums = pl.pallas_call(
        functools.partial(weights_kernel, chunks, direct),
        out_shape=(
            jax.ShapeDtypeStruct((devices, own + 8, full) if direct else (width, full), bf16),
            jax.ShapeDtypeStruct((8, full), f32),
        ),
        in_specs=[whole() for _ in range(chunks + 2)],
        out_specs=(whole(), whole()),
        scratch_shapes=[pltpu.VMEM((full, width), f32)],
        compiler_params=pltpu.CompilerParams(vmem_limit_bytes=40 << 20),
        cost_estimate=pl.CostEstimate(flops=4_000_000_000, bytes_accessed=12_000_000, transcendentals=0),
        name="projection_gradients",
    )(*x, dq, dkv)
    if not direct:
        out = jnp.pad(out.reshape(devices, own, full), ((0, 0), (0, round_up(own, 8) - own), (0, 0)))
        out = jnp.concatenate([out, jnp.broadcast_to(sums[None].astype(bf16), (devices, 8, full))], axis=1)
    return out


def unpack_kernel(own, got_ref, q_ref, k_ref, v_ref, sums_ref, tot):
    dp_n, seq_n, ffn_n, per, full = got_ref.shape
    width = q_ref.shape[1]
    heads = width // HEAD_DIM // seq_n
    for s in range(seq_n):
        total = jnp.zeros((per, full), f32)
        for d in range(dp_n):
            for f in range(ffn_n):
                total = total + got_ref[d, s, f].astype(f32)
        tot[s] = total
        sums_ref[s : s + 1, :] = total[per - 8 : per - 7, :]
    for w in range(width // PAIR):
        spots = [((2 * w + i) // heads, (2 * w + i) % heads) for i in range(2)]
        cols = slice(w * PAIR, (w + 1) * PAIR)
        for ref, where in (
            (k_ref, lambda h: 2 * h),
            (v_ref, lambda h: 2 * h + 1),
            (q_ref, lambda h: 2 * heads + h),
        ):
            both = [half_columns(tot.at[g], where(h), i) for i, (g, h) in enumerate(spots)]
            ref[:, cols] = two_halves(*both)[0:own]


def unpacked_gradients(got, own, width):
    dp_n, seq_n, ffn_n, per, full = got.shape
    whole = lambda: pl.BlockSpec(memory_space=pltpu.VMEM)
    return pl.pallas_call(
        functools.partial(unpack_kernel, own),
        out_shape=(jax.ShapeDtypeStruct((own, width), f32),) * 3 + (jax.ShapeDtypeStruct((seq_n, full), f32),),
        in_specs=[whole()],
        out_specs=tuple(whole() for _ in range(4)),
        scratch_shapes=[pltpu.VMEM((seq_n, per, full), f32)],
        compiler_params=pltpu.CompilerParams(vmem_limit_bytes=32 << 20),
        name="unpacked_gradients",
    )(got)


NORM_EPS = 1e-12


def transposed(value):
    return jnp.transpose(value.astype(f32), (1, 0)).astype(bf16)


def unit_rows(value):
    center = value - jnp.mean(value, axis=-1, keepdims=True)
    scale = lax.rsqrt(jnp.mean(center * center, axis=-1, keepdims=True) + NORM_EPS)
    return center * scale, scale


def unit_rows_back(grad, unit, scale):
    return scale * (
        grad - jnp.mean(grad, axis=-1, keepdims=True) - unit * jnp.mean(grad * unit, axis=-1, keepdims=True)
    )


def rows_kernel(parts, blocks, up_rows, me_ref, *refs):
    ctx_refs = refs[:parts]
    (x_ref, cot_ref, rest_ref, wo_ref, vec_ref, bup_ref, out_ref, resid_ref, hid_ref, pre_ref, nlt_ref, gft_ref,
     gb_ref) = refs[parts : parts + 13]
    do_refs = refs[parts + 13 : 2 * parts + 13]
    sums_ref, gbup_ref, slope_sc = refs[2 * parts + 13 :]
    group = ctx_refs[0].shape[0]
    width = x_ref.shape[1]

    def up(f):
        return rest_ref[:, f, 0:up_rows, :].reshape(width, rest_ref.shape[3])

    def down(f):
        return rest_ref[:, f, up_rows : 2 * up_rows, :].reshape(width, rest_ref.shape[3])

    def own_rows(k):
        return pl.ds(pl.multiple_of((me_ref[0] ^ k) * group, group), group)

    @pl.when(pl.program_id(0) == 0)
    def _():
        sums_ref[...] = jnp.zeros_like(sums_ref)
        gbup_ref[...] = jnp.zeros_like(gbup_ref)

    ctx = jnp.concatenate([r[...] for r in ctx_refs], axis=0)
    w_o = jnp.concatenate([wo_ref[own_rows(k), :] for k in range(parts)], axis=0)
    resid_one = x_ref[...].astype(f32) + (dot_tn(ctx, w_o) + vec_ref[0:1, :])
    unit_one, scale_one = unit_rows(resid_one)
    normed_one = unit_one * vec_ref[2:3, :] + vec_ref[3:4, :]
    low = normed_one.astype(bf16)
    nlt_ref[...] = transposed(normed_one)
    total = normed_one + vec_ref[1:2, :]
    pre = dot_nn(low, up(0)) + bup_ref[0:1, :]
    for f in range(blocks):
        later = dot_nn(low, up(f + 1)) + bup_ref[f + 1 : f + 2, :] if f + 1 < blocks else None
        phi = 0.5 + 0.5 * lax.erf(pre * (0.5 ** 0.5))
        slope_sc[f] = phi + pre * (jnp.exp(-0.5 * pre * pre) * 0.3989422804014327)
        hid = (pre * phi).astype(bf16)
        hid_ref[f] = hid
        total = total + dot_nt(hid, down(f))
        pre = later
    unit_two, scale_two = unit_rows(total)
    out_ref[...] = (unit_two * vec_ref[4:5, :] + vec_ref[5:6, :]).astype(bf16)
    cot = cot_ref[...].astype(f32)
    grad_two = unit_rows_back(cot * vec_ref[4:5, :], unit_two, scale_two)
    grad_ffn = grad_two.astype(bf16)
    gft_ref[...] = transposed(grad_two)
    grad_normed = grad_two
    back = dot_nn(grad_ffn, down(0))
    for f in range(blocks):
        later = dot_nn(grad_ffn, down(f + 1)) if f + 1 < blocks else None
        grad_pre = (back * slope_sc[f]).astype(bf16)
        pre_ref[f] = grad_pre
        gbup_ref[f : f + 1, :] += jnp.sum(grad_pre.astype(f32), axis=0, keepdims=True)
        grad_normed = grad_normed + dot_nt(grad_pre, up(f))
        back = later
    resid = unit_rows_back(grad_normed * vec_ref[2:3, :], unit_one, scale_one)
    resid_ref[...] = resid
    branch = resid.astype(bf16)
    gb_ref[...] = branch
    do = dot_nt(w_o, branch).astype(bf16)
    for k in range(parts):
        do_refs[k][...] = do[k * group : (k + 1) * group]
    for row, value in enumerate(
        (branch.astype(f32), grad_ffn.astype(f32), grad_normed * unit_one, grad_normed, cot * unit_two, cot)
    ):
        sums_ref[row : row + 1, :] += jnp.sum(value, axis=0, keepdims=True)


def rows_chain(me, ctx_parts, x, cot, rest, up_rows, w_o, vecs, bias_up):
    parts = len(ctx_parts)
    group, rows = ctx_parts[0].shape
    width = x.shape[1]
    outer, blocks, per, hidden = rest.shape
    tile = 256
    once = lambda shape: pl.BlockSpec(shape, lambda i: (0,) * len(shape), pipeline_mode=pl.Buffered(1))
    tall = pl.BlockSpec((tile, width), lambda i: (i, 0))
    wide = pl.BlockSpec((width, tile), lambda i: (0, i))
    cube = pl.BlockSpec((blocks, tile, hidden), lambda i: (0, i, 0))
    return pl.pallas_call(
        functools.partial(rows_kernel, parts, blocks, up_rows),
        grid=(rows // tile,),
        out_shape=(
            jax.ShapeDtypeStruct((rows, width), bf16),
            jax.ShapeDtypeStruct((rows, width), f32),
            jax.ShapeDtypeStruct((blocks, rows, hidden), bf16),
            jax.ShapeDtypeStruct((blocks, rows, hidden), bf16),
            jax.ShapeDtypeStruct((width, rows), bf16),
            jax.ShapeDtypeStruct((width, rows), bf16),
            jax.ShapeDtypeStruct((rows, width), bf16),
        )
        + (jax.ShapeDtypeStruct((group, rows), bf16),) * parts
        + (jax.ShapeDtypeStruct((8, width), f32), jax.ShapeDtypeStruct((8, hidden), f32)),
        in_specs=[pl.BlockSpec(memory_space=pltpu.SMEM)]
        + [pl.BlockSpec((group, tile), lambda i: (0, i))] * parts
        + [tall, tall, once(rest.shape), once(w_o.shape), once(vecs.shape), once(bias_up.shape)],
        out_specs=(
            tall, tall, cube, cube, wide, wide, tall,
        )
        + (pl.BlockSpec((group, tile), lambda i: (0, i)),) * parts
        + (pl.BlockSpec((8, width), lambda i: (0, 0)), pl.BlockSpec((8, hidden), lambda i: (0, 0))),
        scratch_shapes=[pltpu.VMEM((blocks, tile, hidden), f32)],
        compiler_params=pltpu.CompilerParams(vmem_limit_bytes=60 << 20),
        cost_estimate=pl.CostEstimate(flops=22_000_000_000, bytes_accessed=40_000_000, transcendentals=6_000_000),
        name="rows_chain",
    )(me, *ctx_parts, x, cot, rest, w_o, vecs, bias_up)


def outer_kernel(parts, up_rows, own, me_ref, *refs):
    ctx_refs = refs[:parts]
    nlt_ref, gft_ref, gb_ref, pre_ref, hid_ref, small_ref, out_ref, wo_sc = refs[parts:]
    slabs, hidden = out_ref.shape[0], out_ref.shape[3]
    group = ctx_refs[0].shape[0]
    f = pl.program_id(0)
    up = dot_nn(nlt_ref[...], pre_ref[0]).astype(bf16)
    out_ref[:, 0, 0:up_rows, :] = up.reshape(slabs, up_rows, hidden)
    down = dot_nn(gft_ref[...], hid_ref[0]).astype(bf16)
    out_ref[:, 0, up_rows : 2 * up_rows, :] = down.reshape(slabs, up_rows, hidden)
    if not own:
        return

    @pl.when(f == 0)
    def _():
        for k in range(parts):
            wo_sc[k] = dot_nn(ctx_refs[k][...], gb_ref[...])

    share = slabs // parts
    stride = group // share
    for k in range(parts):
        for j in range(share):
            rows = pl.ds(pl.multiple_of(j * stride + f * own, 8), own)
            out_ref[(me_ref[0] ^ k) * share + j, 0, 2 * up_rows : 2 * up_rows + own, :] = wo_sc[k, rows, :].astype(bf16)
    out_ref[:, 0, 2 * up_rows + own :, :] = small_ref[:, 0]


def outer_products(me, ctx_parts, nlt, gft, gb, pre, hid, small, slabs, up_rows, own):
    blocks, rows, hidden = pre.shape
    parts = len(ctx_parts)
    group = ctx_parts[0].shape[0]
    per = 2 * up_rows + (own + 8 if own else 0)
    once = lambda shape: pl.BlockSpec(shape, lambda i: (0,) * len(shape), pipeline_mode=pl.Buffered(1))
    return pl.pallas_call(
        functools.partial(outer_kernel, parts, up_rows, own),
        grid=(blocks,),
        out_shape=jax.ShapeDtypeStruct((slabs, blocks, per, hidden), bf16),
        in_specs=[pl.BlockSpec(memory_space=pltpu.SMEM)]
        + [once(c.shape) for c in ctx_parts]
        + [
            once(nlt.shape),
            once(gft.shape),
            once(gb.shape),
            pl.BlockSpec((1, rows, hidden), lambda i: (i, 0, 0)),
            pl.BlockSpec((1, rows, hidden), lambda i: (i, 0, 0)),
            pl.BlockSpec((small.shape[0], 1) + small.shape[2:], lambda i: (0, i, 0, 0)),
        ],
        out_specs=pl.BlockSpec((slabs, 1, per, hidden), lambda i: (0, i, 0, 0)),
        scratch_shapes=[pltpu.VMEM((parts, group, gb.shape[1]), f32)],
        compiler_params=pltpu.CompilerParams(vmem_limit_bytes=48 << 20),
        cost_estimate=pl.CostEstimate(flops=11_000_000_000, bytes_accessed=28_000_000, transcendentals=0),
        name="outer_products",
    )(me, *ctx_parts, nlt, gft, gb, pre, hid, small)


ALL = ("dp", "seq", "ffn")


def flip_send(array, axis, bits):
    count = lax.axis_size(axis)
    return lax.ppermute(array, axis, [(i, i ^ bits) for i in range(count)])


def shards(
    tokens, w_query, w_key, w_value, w_output, b_query, b_value, b_output, w_up, b_up, w_down, b_down,
    gain_attn, shift_attn, gain_ffn, shift_ffn, segment_ids, random_blocks, global_blocks, cotangent,
):
    seq_n, dp_n, ffn_n = lax.axis_size("seq"), lax.axis_size("dp"), lax.axis_size("ffn")
    outer, devices = dp_n * seq_n, dp_n * seq_n * ffn_n
    me = lax.axis_index("seq")
    here = (lax.axis_index("dp") * seq_n + me) * ffn_n + lax.axis_index("ffn")
    own, width = w_query.shape
    own_pad = round_up(own, 8)
    group = width // seq_n
    heads = group // HEAD_DIM
    features = tokens[0]
    rows = features.shape[0]
    order = jnp.stack([me ^ k for k in range(seq_n)])
    me_ref = me.astype(jnp.int32)[None]

    near = [features] + [None] * (seq_n - 1)
    for k in sorted(range(1, seq_n), key=lambda k: (k & (k - 1), -k)):
        bit = k & -k
        near[k] = flip_send(features if bit == k else near[k ^ bit], "seq", bit)

    vec = jnp.stack([b_output, b_down, gain_attn, shift_attn, gain_ffn, shift_ffn, b_query, b_value])
    vec = jnp.pad(vec, ((0, 0), (0, width - own)))
    pack, rest = packed_weights(
        w_query, w_key, w_value, w_output, w_up, w_down, b_up[None], vec, dp_n, seq_n, ffn_n
    )
    lanes = pack.shape[4]
    pack = lax.all_to_all(
        pack.reshape(devices, own_pad + 8, lanes), ALL, split_axis=0, concat_axis=0, tiled=True
    )
    rest = lax.all_gather(rest, ALL, axis=0, tiled=False)
    w_own = pack[:, :own].reshape(width, lanes)
    share = devices // seq_n
    biases = lax.dynamic_slice(pack, (share * me, own_pad + 6, 0), (share, 2, own))
    biases = biases.transpose(1, 0, 2).reshape(2, group).astype(f32)
    by_head = biases[1].reshape(heads, 1, HEAD_DIM)
    b_kv = jnp.concatenate([jnp.zeros_like(by_head), by_head], axis=1).reshape(1, heads * PAIR)
    seg = segment_ids[0].reshape(seq_n, rows)[order]

    nblocks = seq_n * rows // BLOCK
    flip = me.astype(jnp.int32) * (nblocks // seq_n)
    tab = pair_table(random_blocks[0], global_blocks[0], flip, nblocks)
    gl = global_blocks[0] ^ flip
    ctx, (lse, lseg, k_all, v_all, q_all, mask_all) = attention_forward(
        tab, gl, near, seg, w_own, b_kv, biases[0][:, None]
    )
    ctx_parts = [ctx[0]] + [flip_send(ctx[k], "seq", k) for k in range(1, seq_n)]

    up_rows = w_up.shape[0]
    at = 2 * up_rows
    rest = rest.reshape(outer, ffn_n, rest.shape[1], width)
    w_o = rest[:, :, at : at + own].reshape(width, width)
    bias_up = rest[0, :, at + own_pad + 7].astype(f32)
    vecs = rest[:, :, at + own_pad :, :own].transpose(2, 0, 1, 3).reshape(8, width).astype(f32)
    direct = up_rows % 16 == 0 and own % 8 == 0 and outer % seq_n == 0 and (outer // seq_n) * ffn_n * own == group
    if not direct:
        rest = rest[:, :, :at].reshape(outer, ffn_n, 2, up_rows, width).transpose(1, 2, 0, 3, 4)
        rest = rest.reshape(1, ffn_n, 2 * outer * up_rows, width)
    slabs, slab_rows = (outer, up_rows) if direct else (1, outer * up_rows)

    got = rows_chain(me_ref, ctx_parts, features, cotangent[0], rest, slab_rows, w_o, vecs, bias_up)
    out, grad_resid_one, hidden, grad_pre, normed_t, grad_ffn_t, grad_branch = got[:7]
    grad_ctx, (sums, grad_bias_up) = got[7 : 7 + seq_n], got[7 + seq_n :]
    do = [grad_ctx[0]] + [flip_send(grad_ctx[k], "seq", k) for k in range(1, seq_n)]

    vec_grads = sums[:6].astype(bf16).reshape(6, outer, ffn_n, own).transpose(1, 2, 0, 3)
    vec_grads = jnp.pad(vec_grads, ((0, 0), (0, 0), (0, 1), (0, width - own)))
    top = jnp.broadcast_to(grad_bias_up[None, :ffn_n, None].astype(bf16), (outer, ffn_n, 1, width))
    small = jnp.concatenate([top, vec_grads], axis=2)
    payload = outer_products(
        me_ref, ctx_parts, normed_t, grad_ffn_t, grad_branch, grad_pre, hidden, small, slabs, slab_rows,
        own if direct else 0,
    )
    if not direct:
        grad_out = dot_nn(jnp.concatenate(ctx_parts, axis=0), grad_branch).astype(bf16)
        grad_out = grad_out.reshape(seq_n, group, width)[order].reshape(outer, ffn_n, own, width)
        payload = payload.reshape(ffn_n, 2, outer, up_rows, width).transpose(2, 0, 1, 3, 4)
        payload = jnp.concatenate([payload.reshape(outer, ffn_n, at, width), grad_out, small], axis=2)
        payload = jnp.pad(payload, ((0, 0), (0, 0), (0, -payload.shape[2] % 32), (0, 0)))
    payload, do = lax.optimization_barrier((payload, do))
    total = lax.psum_scatter(payload.reshape(-1, width), ALL, scatter_dimension=0, tiled=True)
    total = total.astype(f32)
    out_up, out_down, out_output = total[:up_rows], total[up_rows:at], total[at : at + own]
    out_bias_up = total[at + own]
    out_vecs = total[at + own + 1 : at + own + 7, :own]

    got = attention_backward(tab, gl, do, k_all, v_all, q_all, mask_all, lse, lseg, w_own)
    dq, dkv, part_first = got[:3]
    part = [None] + list(got[3:])
    grad_features = grad_resid_one + part_first
    bit = 1
    while bit < seq_n:
        for k in range(seq_n):
            if k & -k == bit and k != bit:
                came = flip_send(part[k], "seq", bit).astype(f32)
                part[k ^ bit] = (part[k ^ bit].astype(f32) + came).astype(bf16)
        bit *= 2
    grad_w = projection_gradients(near, dq, dkv, own, devices)
    grad_w, part = lax.optimization_barrier((grad_w, part[1:]))
    part = [None] + part
    bit = seq_n // 2
    while bit:
        grad_features = grad_features + flip_send(part[bit], "seq", bit).astype(f32)
        bit //= 2
    grad_w = lax.all_to_all(grad_w, ALL, split_axis=0, concat_axis=0, tiled=True)
    out_query, out_key, out_value, col_sums = unpacked_gradients(
        grad_w.reshape(dp_n, seq_n, ffn_n, own_pad + 8, lanes), own, width
    )
    row = lax.dynamic_index_in_dim(col_sums, here // share, keepdims=False)
    row = jnp.stack([row[heads * PAIR : heads * PAIR + group], row[: heads * PAIR].reshape(heads, 2, HEAD_DIM)[:, 1].reshape(group)])
    out_b = lax.dynamic_slice(row, (0, here % share * own), (2, own))
    return (
        out[None],
        grad_features[None],
        out_query,
        out_key,
        out_value,
        out_output,
        out_b[0],
        out_b[1],
        out_vecs[0],
        out_up,
        out_bias_up,
        out_down,
        out_vecs[1],
        out_vecs[2],
        out_vecs[3],
        out_vecs[4],
        out_vecs[5],
    )


def solution(mesh):
    return jax.shard_map(
        shards,
        mesh=mesh,
        in_specs=(
            P(("dp", "ffn"), "seq", None),
            P(("dp", "seq", "ffn"), None),
            P(("dp", "seq", "ffn"), None),
            P(("dp", "seq", "ffn"), None),
            P(("dp", "seq", "ffn"), None),
            P(("dp", "seq", "ffn")),
            P(("dp", "seq", "ffn")),
            P(("dp", "seq", "ffn")),
            P(("dp", "seq"), "ffn"),
            P("ffn"),
            P(("dp", "seq"), "ffn"),
            P(("dp", "seq", "ffn")),
            P(("dp", "seq", "ffn")),
            P(("dp", "seq", "ffn")),
            P(("dp", "seq", "ffn")),
            P(("dp", "seq", "ffn")),
            P(("dp", "ffn"), None),
            P(("dp", "ffn"), "seq", None, None),
            P(("dp", "ffn"), None),
            P(("dp", "ffn"), "seq", None),
        ),
        out_specs=(
            P(("dp", "ffn"), "seq", None),
            P(("dp", "ffn"), "seq", None),
            P(("dp", "seq", "ffn"), None),
            P(("dp", "seq", "ffn"), None),
            P(("dp", "seq", "ffn"), None),
            P(("dp", "seq", "ffn"), None),
            P(("dp", "seq", "ffn")),
            P(("dp", "seq", "ffn")),
            P(("dp", "seq", "ffn")),
            P(("dp", "seq"), "ffn"),
            P("ffn"),
            P(("dp", "seq"), "ffn"),
            P(("dp", "seq", "ffn")),
            P(("dp", "seq", "ffn")),
            P(("dp", "seq", "ffn")),
            P(("dp", "seq", "ffn")),
            P(("dp", "seq", "ffn")),
        ),
        check_vma=False,
    )
```

time: 409 us -> 374 us (0.914)
  local copies, waits for them, and re-layouts: 57.8 us -> 32.8 us
  Pallas kernels: 184 us -> 166 us
  waiting for transfers between devices: 105 us -> 121 us
  other arithmetic: 21.2 us -> 16 us
    pallas_call x1, Pallas kernels: 49.4 us -> 34.2 us  [attention_forward(): pl.pallas_call(functools.partial(forward_kernel, heads, chunks), out_shap...]
    ppermute x24 -> x12, waiting for transfers between devices: 105 us -> 117 us  [flip_send(): return lax.ppermute(array, axis, [(i, i ^ bits) for i in range(count)])]
    all_to_all x0 -> x2, starting transfers between devices: none -> 11.5 us  [the longest x1 6.47 us: shards(): lax.all_to_all(grad_w, ALL, split_axis=0, concat_axis=0, tiled=True)]
    pallas_call x1, Pallas kernels: 75.8 us -> 66 us  [attention_backward(): pl.pallas_call(functools.partial(backward_kernel, heads, chunks), out_sha...]
    ppermute x24 -> x12, starting transfers between devices: 19.8 us -> 10.9 us  [flip_send(): return lax.ppermute(array, axis, [(i, i ^ bits) for i in range(count)])]
    squeeze x7 -> x0, local copies, waits for them, and re-layouts: 8.77 us -> none  [the longest x1 4 us: shards(): part = [None] + [parts[k - 1] for k in range(1, seq_n)]]
    concatenate x3 -> x1, local copies, waits for them, and re-layouts: 7.11 us -> 0.01 us  [shards(): jnp.concatenate([jnp.zeros_like(by_head), by_head], axis=1)]
    pallas_call x2 -> x4, Pallas kernels: 20.8 us -> 27.2 us  [the longest x1 16.3 us: outer_products(): pl.pallas_call(functools.partial(outer_kernel, parts, up_rows, own), grid...]
  transfers between devices with their start and end apart: 26 -> 16, of which waited for: 12 -> 6; matrix products, arithmetic and copies ran while one was open for 15% -> 8% of each run, Pallas kernels for 36% -> 34%
where the time goes in v3:
time: 374 us; the launch traced here: 373 us
  Pallas kernels  166 us (44%)
  waiting for transfers between devices  121 us (32%)
  local copies, waits for them, and re-layouts  32.8 us (9%)
  starting transfers between devices  22.5 us (6%)
  other arithmetic  16 us (4%)
  between operations  14.4 us (4%)
    ppermute x12, waiting for transfers between devices, flip_send(): return lax.ppermute(array, axis, [(i, i ^ bits) for i in range(count)])  117 us
    pallas_call x1, Pallas kernels, attention_backward(): pl.pallas_call(functools.partial(backward_kernel, heads, chunks), out_sha...  66 us
    pallas_call x1, Pallas kernels, rows_chain(): pl.pallas_call(functools.partial(rows_kernel, parts, blocks, up_rows), gr...  38.2 us
    pallas_call x1, Pallas kernels, attention_forward(): pl.pallas_call(functools.partial(forward_kernel, heads, chunks), out_shap...  34.2 us
    pallas_call x1, Pallas kernels, outer_products(): pl.pallas_call(functools.partial(outer_kernel, parts, up_rows, own), grid...  16.3 us
    unnamed x46, local copies, waits for them, and re-layouts  11.6 us
    ppermute x12, starting transfers between devices, flip_send(): return lax.ppermute(array, axis, [(i, i ^ bits) for i in range(count)])  10.9 us
    pallas_call x1, Pallas kernels, projection_gradients(): pl.pallas_call(functools.partial(weights_kernel, chunks, direct), out_sha...  7.81 us
  transfers between devices with their start and end apart: 16, of which 6 were waited for; matrix products, arithmetic and copies ran while one was open for 8% of the time, Pallas kernels for 34%

profile of v3, /device:TPU:0, one launch (start us, length us, event | category | flops | bytes accessed | tf_op | source)
XLA Modules:
  0.0 372.8 jit_solution(10385506833384857926)
XLA Ops:
  9.9 2.3 packed_weights.1
  12.3 3.0 collective-permute-start.1
  15.3 5.0 %all-to-all-start = ((bf16[32,32,640]{2,1,0:T(8,128)(2,1)}), bf16[32,32,640]{2,1,0:T(8,128)(2,1)}, u32[]{:S(2)}, u32[]{:S(2)}) async-start(bf16[32,32,640]{2,1,0:T(8,128)(2,1)} %bitcast.74), calls=%async_computation | async-start | bytes 2621440 | tf_op jit(solution)/shard_map/all_to_all | solution.py:797
  24.1 49.1 %collective-permute-done.1.refs_2_ = bf16[1024,768]{1,0:T(8,128)(2,1)S(1)} collective-permute-done((bf16[1024,768]{1,0:T(8,128)(2,1)}, bf16[1024,768]{1,0:T(8,128)(2,1)S(1)}, u32[]{:S(2)}, u32[]{:S(2)}) %collective-permute-start.1) | collective-permute-done | bytes 1572896 | tf_op jit(solution)/shard_map/ppermute | solution.py:766
  82.1 2.3 slice.132
  84.3 34.2 %attention_forward.1 = (bf16[192,1024]{1,0:T(8,128)(2,1)}, bf16[192,1024]{1,0:T(8,128)(2,1)}, bf16[192,1024]{1,0:T(8,128)(2,1)}, bf16[192,1024]{1,0:T(8,128)(2,1...) custom-call(s32[960]{0:T(1024)} %reshape.377.tab_ref, ...), custom_call_target="tpu_custom_call" | custom-call | flops 12000000000 | bytes 16000000 | tf_op jit(solution)/shard_map/attention_forward/pallas_call | solution.py:234
  119.1 2.7 collective-permute-start.4
  121.8 3.3 all-gather.3.cloned.1.call-done
  125.1 2.4 slice.135
  131.9 7.3 %collective-permute-done.5.refs_3_ = bf16[192,1024]{1,0:T(8,128)(2,1)S(1)} collective-permute-done((bf16[192,1024]{1,0:T(8,128)(2,1)}, bf16[192,1024]{1,0:T(8,128)(2,1)S(1)}, u32[]{:S(2)}, u32[]{:S(2)}) %collective-permute-start.5) | collective-permute-done | bytes 393248 | tf_op jit(solution)/shard_map/ppermute | solution.py:766
  140.0 38.2 %rows_chain.1 = (bf16[1024,768]{1,0:T(8,128)(2,1)}, f32[1024,768]{1,0:T(8,128)}, bf16[4,1024,768]{2,1,0:T(8,128)(2,1)}, bf16[4,1024,768]{2,1,0:T(8,128)(2,1)}, b...) custom-call(s32[1]{0:T(128)} %bitcast.me_ref, ...), custom_call_target="tpu_custom_call" | custom-call | flops 22000001024 | bytes 40000000 | tf_op jit(solution)/shard_map/rows_chain/pallas_call | solution.py:677
  180.2 1.8 collective-permute-start.7
  185.2 1.4 copy-done.12
  188.0 16.3 %outer_products.1 = bf16[8,4,224,768]{3,2,1,0:T(8,128)(2,1)} custom-call(s32[1]{0:T(128)} %bitcast.me_ref, bf16[192,1024]{1,0:T(8,128)(2,1)S(1)} %copy-done.14, bf16[192,1024]{1,0:T(8,128)(2,1)S(1)} %copy-done.5, bf16[192,1024]{1,0:T(8,128)(2,1)S(1)} %copy-done.7, bf16[192,1024]{1,0:T(8,128)(2,1)S(1)} %copy-done.9, bf16[768,1024]{1,0:T(8,128)(2,1)S(1)} %copy-done.12, ...), custom_call_target="tpu_custom_call" | custom-call | flops 11000000512 | bytes 28000000 | tf_op jit(solution)/shard_map/outer_products/pallas_call | solution.py:739
  205.3 66.0 %attention_backward.1 = (bf16[4,192,1024]{2,1,0:T(8,128)(2,1)}, bf16[4,1024,384]{2,1,0:T(8,128)(2,1)}, f32[1024,768]{1,0:T(8,128)}, bf16[1024,768]{1,0:T(8,128)(...) custom-call(s32[960]{0:T(1024)} %reshape.377.tab_ref, s32[2]{0:T(128)} %xor_bitcast_fusion.2.gl_ref, ...), custom_call_target="tpu_custom_call" | custom-call | flops 30000001024 | bytes 24000000 | tf_op jit(solution)/shard_map/attention_backward/pallas_call | solution.py:385
  271.8 1.9 copy-done.10
  273.7 1.4 copy-done.11
  275.2 7.8 %projection_gradients.1 = (bf16[32,32,640]{2,1,0:T(8,128)(2,1)}, f32[8,640]{1,0:T(8,128)}) custom-call(bf16[1024,768]{1,0:T(8,128)(2,1)S(1)} %bitcast.72, bf16[1024,768]{1,0:T(8,128)(2,1)} %collective-permute-done.refs_1_, bf16[1024,768]{1,0:T(8,128)(2,1)S(1)} %copy-done.3, bf16[1024,768]{1,0:T(8,128)(2,1)} %collective-permute-done.2.refs_3_, ...), custom_call_target="tpu_custom_call" | custom-call | flops 4000000000 | bytes 12000000 | tf_op jit(solution)/shard_map/projection_gradients/pallas_call | solution.py:524
  283.0 1.5 add_convert_fusion
  284.5 6.5 %all-to-all-start.1 = ((bf16[32,32,640]{2,1,0:T(8,128)(2,1)}), bf16[32,32,640]{2,1,0:T(8,128)(2,1)S(1)}, u32[]{:S(2)}, u32[]{:S(2)}) async-start(bf16[32,32,640]{2,1,0:T(8,128)(2,1)} %get-tuple-element.99), calls=%async_computation.1 | async-start | bytes 2621440 | tf_op jit(solution)/shard_map/all_to_all | solution.py:874
  291.0 1.8 collective-permute-start.10
  292.8 59.2 %collective-permute-done.10 = bf16[1024,768]{1,0:T(8,128)(2,1)S(1)} collective-permute-done((bf16[1024,768]{1,0:T(8,128)(2,1)}, bf16[1024,768]{1,0:T(8,128)(2,1)S(1)}, u32[]{:S(2)}, u32[]{:S(2)}) %collective-permute-start.10) | collective-permute-done | bytes 1572896 | tf_op jit(solution)/shard_map/ppermute | solution.py:766
  352.0 5.6 %add_bitcast_fusion = f32[1,1024,768]{2,1,0:T(8,128)} fusion(bf16[1024,768]{1,0:T(8,128)(2,1)} %collective-permute-done.11, bf16[1024,768]{1,0:T(8,128)(2,1)S(1)} %collective-permute-done.10, f32[1024,768]{1,0:T(8,128)} %get-tuple-element.68, f32[1024,768]{1,0:T(8,128)} %get-tuple-element.90), kind=kLoop, calls=%fused_computation.3 | loop fusion | flops 3932160 | bytes 12582912 | tf_op jit(solution)/shard_map/broadcast_in_dim | solution.py:883
  362.7 1.8 fusion.13
  (123 shorter events, 35.5 us)
Async XLA Ops:
  7.2 117.9 %all-gather.3.cloned.1.call-start = ((), (), s32[]{:S(2)}) async-start(), calls=%async_computation.4 | async-start | bytes 11354112 | tf_op jit(solution)/shard_map/all_gather | solution.py:800
  12.2 8.4 %copy-start.18 = (s32[1,2]{1,0:T(1,128)S(1)}, s32[1,2]{1,0:T(1,128)}, u32[]{:S(2)}) copy-start(s32[1,2]{1,0:T(1,128)} %param.38) | copy-start | bytes 28
  12.2 11.7 %copy-start.17 = (s32[1,3,64,3]{2,0,3,1:T(1,128)S(1)}, s32[1,3,64,3]{2,0,3,1:T(1,128)}, u32[]{:S(2)}) copy-start(s32[1,3,64,3]{2,0,3,1:T(1,128)} %param.37) | copy-start | bytes 6916
  12.3 60.9 %collective-permute-start.1 = (bf16[1024,768]{1,0:T(8,128)(2,1)}, bf16[1024,768]{1,0:T(8,128)(2,1)S(1)}, u32[]{:S(2)}, u32[]{:S(2)}) collective-permute-start(bf16[1024,768]{1,0:T(8,128)(2,1)} %bitcast.68), channel_id=1, source_target_pairs={{0,8},{4,12},{8,0},{12,4},{1,9},{5,13},{9,1},{13,5},{2,10},{6,14},... | collective-permute-start | bytes 4718600 | tf_op jit(solution)/shard_map/ppermute | solution.py:766
  15.3 62.1 %copy-start.16 = (s32[1,4096]{1,0:T(1,128)S(1)}, s32[1,4096]{1,0:T(1,128)}, u32[]{:S(2)}) copy-start(s32[1,4096]{1,0:T(1,128)} %param.36) | copy-start | bytes 49156
  15.3 64.6 %all-to-all-start = ((bf16[32,32,640]{2,1,0:T(8,128)(2,1)}), bf16[32,32,640]{2,1,0:T(8,128)(2,1)}, u32[]{:S(2)}, u32[]{:S(2)}) async-start(bf16[32,32,640]{2,1,0:T(8,128)(2,1)} %bitcast.74), calls=%async_computation | async-start | bytes 2621440 | tf_op jit(solution)/shard_map/all_to_all | solution.py:797
  20.3 340.3 %reduce-scatter.2.cloned.1.call-start = ((), (), s32[]{:S(2)}) async-start(), calls=%async_computation.3 | async-start | bytes 11354112 | tf_op jit(solution)/shard_map/reduce_scatter | solution.py:850
  20.4 64.0 %collective-permute-start = (bf16[1024,768]{1,0:T(8,128)(2,1)S(1)}, bf16[1024,768]{1,0:T(8,128)(2,1)}, u32[]{:S(2)}, u32[]{:S(2)}) collective-permute-start(bf16[1024,768]{1,0:T(8,128)(2,1)S(1)} %bitcast.71), channel_id=1, source_target_pairs={{0,4},{4,0},{8,12},{12,8},{1,5},{5,1},{9,13},{13,9},{2,6},{6,2},{1... | collective-permute-start | bytes 4718600 | tf_op jit(solution)/shard_map/ppermute | solution.py:766
  73.2 11.1 %copy-start.2 = (bf16[1024,768]{1,0:T(8,128)(2,1)}, bf16[1024,768]{1,0:T(8,128)(2,1)S(1)}, u32[]{:S(2)}) copy-start(bf16[1024,768]{1,0:T(8,128)(2,1)S(1)} %collective-permute-done.1.refs_2_) | copy-start | bytes 4718596
  73.2 11.1 %collective-permute-start.2 = (bf16[1024,768]{1,0:T(8,128)(2,1)S(1)}, bf16[1024,768]{1,0:T(8,128)(2,1)}, u32[]{:S(2)}, u32[]{:S(2)}) collective-permute-start(bf16[1024,768]{1,0:T(8,128)(2,1)S(1)} %collective-permute-done.1.refs_2_), channel_id=1, source_target_pairs={{0,4},{4,0},{8,12},{12,8},{1,5},{5,1},{9,13},{13,9},{2,6},{6,2},{1... | collective-permute-start | bytes 4718600 | tf_op jit(solution)/shard_map/ppermute | solution.py:766
  118.5 12.0 %collective-permute-start.3 = (bf16[192,1024]{1,0:T(8,128)(2,1)}, bf16[192,1024]{1,0:T(8,128)(2,1)S(1)}, u32[]{:S(2)}, u32[]{:S(2)}) collective-permute-start(bf16[192,1024]{1,0:T(8,128)(2,1)} %get-tuple-element.63), channel_id=1, source_target_pairs={{0,4},{4,0},{8,12},{12,8},{1,5},{5,1},{9,13},{13,9},{2,6},{6,2},{1... | collective-permute-start | bytes 1179656 | tf_op jit(solution)/shard_map/ppermute | solution.py:766
  119.1 12.8 %collective-permute-start.4 = (bf16[192,1024]{1,0:T(8,128)(2,1)}, bf16[192,1024]{1,0:T(8,128)(2,1)S(1)}, u32[]{:S(2)}, u32[]{:S(2)}) collective-permute-start(bf16[192,1024]{1,0:T(8,128)(2,1)} %get-tuple-element.64), channel_id=1, source_target_pairs={{0,8},{4,12},{8,0},{12,4},{1,9},{5,13},{9,1},{13,5},{2,10},{6,14},... | collective-permute-start | bytes 1179656 | tf_op jit(solution)/shard_map/ppermute | solution.py:766
  121.8 17.4 %collective-permute-start.5 = (bf16[192,1024]{1,0:T(8,128)(2,1)}, bf16[192,1024]{1,0:T(8,128)(2,1)S(1)}, u32[]{:S(2)}, u32[]{:S(2)}) collective-permute-start(bf16[192,1024]{1,0:T(8,128)(2,1)} %get-tuple-element.65), channel_id=1, source_target_pairs={{0,12},{4,8},{8,4},{12,0},{1,13},{5,9},{9,5},{13,1},{2,14},{6,10},... | collective-permute-start | bytes 1179656 | tf_op jit(solution)/shard_map/ppermute | solution.py:766
  130.6 8.7 %copy-start.4 = (bf16[192,1024]{1,0:T(8,128)(2,1)}, bf16[192,1024]{1,0:T(8,128)(2,1)S(1)}, u32[]{:S(2)}) copy-start(bf16[192,1024]{1,0:T(8,128)(2,1)S(1)} %collective-permute-done.3.refs_1_) | copy-start | bytes 1179652
  140.0 42.2 %copy-start.14 = (bf16[192,1024]{1,0:T(8,128)(2,1)S(1)}, bf16[192,1024]{1,0:T(8,128)(2,1)}, u32[]{:S(2)}) copy-start(bf16[192,1024]{1,0:T(8,128)(2,1)} %get-tuple-element.62.refs_0_) | copy-start | bytes 1179652
  179.8 24.4 %collective-permute-start.6 = (bf16[192,1024]{1,0:T(8,128)(2,1)}, bf16[192,1024]{1,0:T(8,128)(2,1)S(1)}, u32[]{:S(2)}, u32[]{:S(2)}) collective-permute-start(bf16[192,1024]{1,0:T(8,128)(2,1)} %get-tuple-element.77), channel_id=1, source_target_pairs={{0,4},{4,0},{8,12},{12,8},{1,5},{5,1},{9,13},{13,9},{2,6},{6,2},{1... | collective-permute-start | bytes 1179656 | tf_op jit(solution)/shard_map/ppermute | solution.py:766
  180.2 24.0 %collective-permute-start.7 = (bf16[192,1024]{1,0:T(8,128)(2,1)}, bf16[192,1024]{1,0:T(8,128)(2,1)S(1)}, u32[]{:S(2)}, u32[]{:S(2)}) collective-permute-start(bf16[192,1024]{1,0:T(8,128)(2,1)} %get-tuple-element.78), channel_id=1, source_target_pairs={{0,8},{4,12},{8,0},{12,4},{1,9},{5,13},{9,1},{13,5},{2,10},{6,14},... | collective-permute-start | bytes 1179656 | tf_op jit(solution)/shard_map/ppermute | solution.py:766
  182.0 22.3 %collective-permute-start.8 = (bf16[192,1024]{1,0:T(8,128)(2,1)}, bf16[192,1024]{1,0:T(8,128)(2,1)S(1)}, u32[]{:S(2)}, u32[]{:S(2)}) collective-permute-start(bf16[192,1024]{1,0:T(8,128)(2,1)} %get-tuple-element.79), channel_id=1, source_target_pairs={{0,12},{4,8},{8,4},{12,0},{1,13},{5,9},{9,5},{13,1},{2,14},{6,10},... | collective-permute-start | bytes 1179656 | tf_op jit(solution)/shard_map/ppermute | solution.py:766
  205.3 66.5 %copy-start.1 = (bf16[1,1024,768]{2,1,0:T(8,128)(2,1)S(1)}, bf16[1,1024,768]{2,1,0:T(8,128)(2,1)}, u32[]{:S(2)}) copy-start(bf16[1,1024,768]{2,1,0:T(8,128)(2,1)} %param.20) | copy-start | bytes 4718596
  205.3 66.5 %copy-start.3 = (bf16[1024,768]{1,0:T(8,128)(2,1)S(1)}, bf16[1024,768]{1,0:T(8,128)(2,1)}, u32[]{:S(2)}) copy-start(bf16[1024,768]{1,0:T(8,128)(2,1)} %copy-done.2) | copy-start | bytes 4718596
  271.4 11.6 %collective-permute-start.9 = (bf16[1024,768]{1,0:T(8,128)(2,1)}, bf16[1024,768]{1,0:T(8,128)(2,1)S(1)}, u32[]{:S(2)}, u32[]{:S(2)}) collective-permute-start(bf16[1024,768]{1,0:T(8,128)(2,1)} %get-tuple-element.96), channel_id=1, source_target_pairs={{0,4},{4,0},{8,12},{12,8},{1,5},{5,1},{9,13},{13,9},{2,6},{6,2},{1... | collective-permute-start | bytes 4718600 | tf_op jit(solution)/shard_map/ppermute | solution.py:766
  284.5 73.2 %all-to-all-start.1 = ((bf16[32,32,640]{2,1,0:T(8,128)(2,1)}), bf16[32,32,640]{2,1,0:T(8,128)(2,1)S(1)}, u32[]{:S(2)}, u32[]{:S(2)}) async-start(bf16[32,32,640]{2,1,0:T(8,128)(2,1)} %get-tuple-element.99), calls=%async_computation.1 | async-start | bytes 2621440 | tf_op jit(solution)/shard_map/all_to_all | solution.py:874
  291.0 61.1 %collective-permute-start.10 = (bf16[1024,768]{1,0:T(8,128)(2,1)}, bf16[1024,768]{1,0:T(8,128)(2,1)S(1)}, u32[]{:S(2)}, u32[]{:S(2)}) collective-permute-start(bf16[1024,768]{1,0:T(8,128)(2,1)} %add_convert_fusion), channel_id=1, source_target_pairs={{0,8},{4,12},{8,0},{12,4},{1,9},{5,13},{9,1},{13,5},{2,10},{6,14},... | collective-permute-start | bytes 4718600 | tf_op jit(solution)/shard_map/ppermute | solution.py:766
  292.8 59.2 %collective-permute-start.11 = (bf16[1024,768]{1,0:T(8,128)(2,1)}, bf16[1024,768]{1,0:T(8,128)(2,1)}, u32[]{:S(2)}, u32[]{:S(2)}) collective-permute-start(bf16[1024,768]{1,0:T(8,128)(2,1)} %get-tuple-element.98), channel_id=1, source_target_pairs={{0,4},{4,0},{8,12},{12,8},{1,5},{5,1},{9,13},{13,9},{2,6},{6,2},{1... | collective-permute-start | bytes 4718600 | tf_op jit(solution)/shard_map/ppermute | solution.py:766
  (14 other events, 35.8 us)
Sparse Core Ops, SparseCore 0:
  12.4 112.6 all-gather.2
  204.4 156.0 reduce-scatter.1

commit v4 on v3

--- a/solution.py
+++ b/solution.py
@@ -63,6 +63,9 @@
 
 
 UNROLL = 4
+BACK_UNROLL = 4
+APART = 64
+VMEM_BYTES = 62 << 20
 
 
 def head_lanes(h):
@@ -248,7 +251,7 @@
             pltpu.VMEM((heads, length, PAIR), f32),
             pltpu.VMEM((chunks, heads * HEAD_DIM, rows), bf16),
         ],
-        compiler_params=pltpu.CompilerParams(vmem_limit_bytes=56 << 20),
+        compiler_params=pltpu.CompilerParams(vmem_limit_bytes=VMEM_BYTES),
         cost_estimate=pl.CostEstimate(flops=12_000_000_000, bytes_accessed=16_000_000, transcendentals=8_000_000),
         name="attention_forward",
     )(tab, gl, *x, seg, w, b_kv, b_q)
@@ -257,38 +260,56 @@
 
 def backward_kernel(heads, chunks, tab_ref, gl_ref, *refs):
     do_refs = refs[:chunks]
-    (k_sc, v_sc, q_sc, mask_sc, lse_ref, lseg_ref, w_ref, dq_ref, dkv_ref, first_ref) = refs[chunks : chunks + 10]
-    part_refs = refs[chunks + 10 : 2 * chunks + 9]
-    do_sc, acc, p_sc, d_sc, dqg_sc = refs[2 * chunks + 9 :]
+    (k_ref, kv_ref, q_ref, mask_ref, seg_ref, lse_ref, lseg_ref, w_ref, resid_ref, dq_ref, dkv_ref, first_ref) = refs[
+        chunks : chunks + 12
+    ]
+    part_refs = refs[chunks + 12 : 2 * chunks + 11]
+    do_sc, acc, p_sc, d_sc, seg_sc, line_sc = refs[2 * chunks + 11 :]
     rows = do_refs[0].shape[1]
     length = rows * chunks
     npairs = length // PAIR
     per_chunk = npairs // chunks
+    scale = HEAD_DIM ** -0.5
     for c in range(chunks):
         do_sc[:, c * rows : (c + 1) * rows] = do_refs[c][...]
-    first, second = lane_halves(PAIR, bf16)
+        for t in range(per_chunk):
+            line = seg_ref[c : c + 1, t * PAIR : (t + 1) * PAIR].astype(f32)
+            line_sc[c * per_chunk + t] = line
+            to = c * rows + t * PAIR
+            seg_sc[to : to + PAIR, :] = jnp.transpose(jnp.broadcast_to(line, (PAIR, PAIR)), (1, 0))
+    seg_sc[length : length + BLOCK, :] = jnp.full((BLOCK, PAIR), -1.0, f32)
     first2, second2 = lane_halves(2 * PAIR, bf16)
     ffirst, fsecond = lane_halves(PAIR, f32)
     lane = lax.broadcasted_iota(jnp.int32, (1, PAIR), 1)
+    line_row = lax.broadcasted_iota(jnp.int32, (PAIR, 1), 0)
     zeros = jnp.zeros((BLOCK, PAIR), bf16)
-
-    def value_rows(do):
-        return jnp.concatenate([zeros, do], axis=0)
+    blank = jnp.zeros((PAIR, PAIR), bf16)
+
+    def head_rows(h):
+        return slice(h * BLOCK, (h + 1) * BLOCK)
+
+    def joint(q, mask, do):
+        left = jnp.concatenate([q, mask, blank], axis=0)
+        right = jnp.concatenate([blank, zeros, do], axis=0)
+        return jnp.concatenate([left, right], axis=1)
 
     def sources(q, do):
-        top = jnp.concatenate([q[0:BLOCK], zeros], axis=1)
+        top = jnp.concatenate([q, zeros], axis=1)
         return jnp.concatenate([top, jnp.concatenate([zeros, do], axis=1)], axis=0)
 
     step = 512
-    queries = [global_queries(q_sc, mask_sc, h, gl_ref) for h in range(heads)]
-    grads = [global_columns(do_sc, slice(h * BLOCK, (h + 1) * BLOCK), gl_ref).astype(bf16) for h in range(heads)]
+    mask_glob = global_columns(mask_ref, slice(0, BLOCK), gl_ref).astype(bf16)
+    q_glob = [global_columns(q_ref, head_rows(h), gl_ref).astype(bf16) for h in range(heads)]
+    do_glob = [global_columns(do_sc, head_rows(h), gl_ref).astype(bf16) for h in range(heads)]
 
     def weigh(c, deltas):
         at = pl.multiple_of(c * step, step)
         new = []
         for h in range(heads):
-            p = jnp.exp(dot_nn(k_sc[pl.ds(at, step), head_lanes(h)], queries[h]) - lseg_ref[h : h + 1, :])
-            dp = dot_nn(v_sc[pl.ds(at, step), head_lanes(h)], value_rows(grads[h]))
+            left = jnp.concatenate([k_ref[pl.ds(at, step), head_lanes(h)], kv_ref[pl.ds(at, step), head_lanes(h)]], axis=1)
+            both = dot_nn(left, joint(q_glob[h], mask_glob, do_glob[h]))
+            p = jnp.exp(both[:, 0:PAIR] - lseg_ref[h : h + 1, :])
+            dp = both[:, PAIR:]
             p_sc[h, pl.ds(at, step), :] = p
             d_sc[h, pl.ds(at, step), :] = dp
             new.append(deltas[h] + jnp.sum(p * dp, axis=0, keepdims=True))
@@ -303,13 +324,12 @@
             p = p_sc[h, pl.ds(at, step), :]
             ds = (p * (d_sc[h, pl.ds(at, step), :] - deltas[h])).astype(bf16)
             both = jnp.concatenate([ds, p.astype(bf16)], axis=1)
-            acc[h, pl.ds(at, step), :] = dot_nt(both, sources(queries[h], grads[h]))
-            new.append(dqs[h] + dot_tn(k_sc[pl.ds(at, step), head_lanes(h)], ds))
+            acc[h, pl.ds(at, step), :] = dot_nt(both, sources(q_glob[h], do_glob[h]))
+            new.append(dqs[h] + dot_tn(k_ref[pl.ds(at, step), head_lanes(h)], ds))
         return tuple(new)
 
     dqs = lax.fori_loop(0, length // step, spread, (jnp.zeros((PAIR, PAIR), f32),) * heads)
     for h in range(heads):
-        dqg_sc[h] = dqs[h][0:BLOCK] * (HEAD_DIM ** -0.5)
         acc[h, pl.ds(length, BLOCK), :] = jnp.zeros((BLOCK, PAIR), f32)
 
     def one_pair(pair):
@@ -319,26 +339,31 @@
         hit_first = (gl_ref[0] == 2 * pair) | (gl_ref[1] == 2 * pair)
         hit_second = (gl_ref[0] == 2 * pair + 1) | (gl_ref[1] == 2 * pair + 1)
         shut = ffirst * jnp.where(hit_first, -MASKED, 0.0) + fsecond * jnp.where(hit_second, -MASKED, 0.0)
+        every = slice(0, PAIR)
         for h in range(heads):
+            kl = head_lanes(h)
             shared, mine, other = slots(tab_ref, gl_ref, h, pair, npairs)
-            kl = head_lanes(h)
-            q = query_columns(q_sc, mask_sc, h, at)
-            do = do_sc[h * BLOCK : (h + 1) * BLOCK, pl.ds(at, PAIR)]
-            do_v = value_rows(do)
+            q = q_ref[head_rows(h), pl.ds(at, PAIR)]
+            do = do_sc[head_rows(h), pl.ds(at, PAIR)]
             lse = lse_ref[h, pl.ds(pair, 1), :] + shut
-            k_sh = stack_rows(k_sc, shared, kl)
-            k_pr = jnp.concatenate([stack_rows(k_sc, mine, kl), stack_rows(k_sc, other, kl)], axis=1)
-            p_sh = jnp.exp(dot_nn(k_sh, q) - lse)
-            p_pr = jnp.exp(dot_nn(k_pr, jnp.concatenate([q * first, q * second], axis=0)) - lse)
-            d_sh = dot_nn(stack_rows(v_sc, shared, kl), do_v)
-            v_pr = jnp.concatenate([stack_rows(v_sc, mine, kl), stack_rows(v_sc, other, kl)], axis=1)
-            d_pr = dot_nn(v_pr, jnp.concatenate([do_v * first, do_v * second], axis=0))
+            src = sources(q, do)
+            src2 = jnp.concatenate([src * first2, src * second2], axis=0)
+            k_sh = stack_rows(k_ref, shared, kl)
+            two_sh = dot_nn(
+                jnp.concatenate([k_sh, stack_rows(kv_ref, shared, kl)], axis=1),
+                joint(q, mask_ref[:, pl.ds(at, PAIR)], do),
+            )
+            kv_pr = jnp.concatenate([stack_rows(kv_ref, mine, kl), stack_rows(kv_ref, other, kl)], axis=1)
+            two_pr = dot_nn(kv_pr, src2)
+            seg_pr = jnp.where(lane < BLOCK, stack_rows(seg_sc, mine, every), stack_rows(seg_sc, other, every))
+            agree = seg_pr == line_sc[pair]
+            p_sh = jnp.exp(two_sh[:, 0:PAIR] - lse)
+            p_pr = jnp.where(agree, jnp.exp(two_pr[:, 0:PAIR] - lse), 0.0)
+            d_sh, d_pr = two_sh[:, PAIR:], two_pr[:, PAIR:]
             delta = jnp.sum(p_sh * d_sh, axis=0, keepdims=True) + jnp.sum(p_pr * d_pr, axis=0, keepdims=True)
             ds_sh = (p_sh * (d_sh - delta)).astype(bf16)
             ds_pr = (p_pr * (d_pr - delta)).astype(bf16)
-            src = sources(q, do)
             g_sh = dot_nt(jnp.concatenate([ds_sh, p_sh.astype(bf16)], axis=1), src)
-            src2 = jnp.concatenate([src * first2, src * second2], axis=0)
             g_pr = dot_nt(jnp.concatenate([ds_pr, p_pr.astype(bf16)], axis=1), src2)
             for j, o in enumerate(shared):
                 acc[h, pl.ds(o, BLOCK), :] += g_sh[j * BLOCK : (j + 1) * BLOCK]
@@ -346,20 +371,20 @@
                 acc[h, pl.ds(o, BLOCK), :] += g_pr[j * BLOCK : (j + 1) * BLOCK, 0:PAIR]
             for j, o in enumerate(other):
                 acc[h, pl.ds(o, BLOCK), :] += g_pr[j * BLOCK : (j + 1) * BLOCK, PAIR:]
-            t_sh = dot_tn(k_sh, ds_sh)
-            t_pr = dot_tn(k_pr, ds_pr)
-            dq = t_sh[0:BLOCK] + jnp.where(lane < BLOCK, t_pr[0:BLOCK], t_pr[PAIR : PAIR + BLOCK])
-            dq_ref[chunk, h * BLOCK : (h + 1) * BLOCK, pl.ds(local, PAIR)] = (dq * (HEAD_DIM ** -0.5)).astype(bf16)
-
-    @pl.loop(0, npairs // UNROLL)
+            t_pr = dot_tn(ds_pr, kv_pr)
+            dq = dot_tn(ds_sh, k_sh) + jnp.where(line_row < BLOCK, t_pr[:, 0:PAIR], t_pr[:, PAIR:])
+            dq = jnp.transpose(dq, (1, 0))[0:BLOCK]
+            dq_ref[chunk, head_rows(h), pl.ds(local, PAIR)] = (dq * scale).astype(bf16)
+
+    @pl.loop(0, npairs // BACK_UNROLL)
     def _(some):
-        for i in range(UNROLL):
-            one_pair(UNROLL * some + i)
+        for i in range(BACK_UNROLL):
+            one_pair(BACK_UNROLL * some + i)
 
     for h in range(heads):
-        put_global_columns(dq_ref, slice(h * BLOCK, (h + 1) * BLOCK), gl_ref, dqg_sc[h], per_chunk)
+        put_global_columns(dq_ref, head_rows(h), gl_ref, dqs[h][0:BLOCK] * scale, per_chunk)
         for c in range(chunks):
-            dkv_ref[c, :, h * PAIR : (h + 1) * PAIR] = acc[h, pl.ds(c * rows, rows), :].astype(bf16)
+            dkv_ref[c, :, head_lanes(h)] = acc[h, pl.ds(c * rows, rows), :].astype(bf16)
     tile = 256
     wq = query_weights(w_ref, heads)
     for c in range(chunks):
@@ -370,12 +395,12 @@
             got = dot_tn(dq_ref[c, :, pl.ds(at, tile)], wq)
             got = got + dot_nt(dkv_ref[c, pl.ds(at, tile), :], w_ref[:, 0 : heads * PAIR])
             if c == 0:
-                first_ref[pl.ds(at, tile), :] = got
+                first_ref[pl.ds(at, tile), :] = resid_ref[pl.ds(at, tile), :] + got
             else:
                 part_refs[c - 1][pl.ds(at, tile), :] = got.astype(bf16)
 
 
-def attention_backward(tab, gl, do, k, v, q, mask, lse, lseg, w):
+def attention_backward(tab, gl, do, k, kv, q, mask, seg, lse, lseg, w, resid):
     chunks = len(do)
     group, rows = do[0].shape
     heads = group // HEAD_DIM
@@ -390,19 +415,20 @@
             jax.ShapeDtypeStruct((rows, width), f32),
         )
         + (jax.ShapeDtypeStruct((rows, width), bf16),) * (chunks - 1),
-        in_specs=[pl.BlockSpec(memory_space=pltpu.SMEM)] * 2 + [whole() for _ in range(chunks + 7)],
+        in_specs=[pl.BlockSpec(memory_space=pltpu.SMEM)] * 2 + [whole() for _ in range(chunks + 9)],
         out_specs=tuple(whole() for _ in range(chunks + 2)),
         scratch_shapes=[
             pltpu.VMEM((group, length), bf16),
             pltpu.VMEM((heads, length + BLOCK, PAIR), f32),
             pltpu.VMEM((heads, length, PAIR), f32),
             pltpu.VMEM((heads, length, PAIR), f32),
-            pltpu.VMEM((heads, BLOCK, PAIR), f32),
+            pltpu.VMEM((length + BLOCK, PAIR), f32),
+            pltpu.VMEM((length // PAIR, 1, PAIR), f32),
         ],
-        compiler_params=pltpu.CompilerParams(vmem_limit_bytes=60 << 20),
+        compiler_params=pltpu.CompilerParams(vmem_limit_bytes=VMEM_BYTES),
         cost_estimate=pl.CostEstimate(flops=30_000_000_000, bytes_accessed=24_000_000, transcendentals=8_000_000),
         name="attention_backward",
-    )(tab, gl, *do, k, v, q, mask, lse, lseg, w)
+    )(tab, gl, *do, k, kv, q, mask, seg, lse, lseg, w, resid)
 
 
 def round_up(value, to):
@@ -530,7 +556,7 @@
         in_specs=[whole() for _ in range(chunks + 2)],
         out_specs=(whole(), whole()),
         scratch_shapes=[pltpu.VMEM((full, width), f32)],
-        compiler_params=pltpu.CompilerParams(vmem_limit_bytes=40 << 20),
+        compiler_params=pltpu.CompilerParams(vmem_limit_bytes=VMEM_BYTES),
         cost_estimate=pl.CostEstimate(flops=4_000_000_000, bytes_accessed=12_000_000, transcendentals=0),
         name="projection_gradients",
     )(*x, dq, dkv)
@@ -572,7 +598,7 @@
         in_specs=[whole()],
         out_specs=tuple(whole() for _ in range(4)),
         scratch_shapes=[pltpu.VMEM((seq_n, per, full), f32)],
-        compiler_params=pltpu.CompilerParams(vmem_limit_bytes=32 << 20),
+        compiler_params=pltpu.CompilerParams(vmem_limit_bytes=VMEM_BYTES),
         name="unpacked_gradients",
     )(got)
 
@@ -697,22 +723,27 @@
         + (pl.BlockSpec((group, tile), lambda i: (0, i)),) * parts
         + (pl.BlockSpec((8, width), lambda i: (0, 0)), pl.BlockSpec((8, hidden), lambda i: (0, 0))),
         scratch_shapes=[pltpu.VMEM((blocks, tile, hidden), f32)],
-        compiler_params=pltpu.CompilerParams(vmem_limit_bytes=60 << 20),
+        compiler_params=pltpu.CompilerParams(vmem_limit_bytes=VMEM_BYTES),
         cost_estimate=pl.CostEstimate(flops=22_000_000_000, bytes_accessed=40_000_000, transcendentals=6_000_000),
         name="rows_chain",
     )(me, *ctx_parts, x, cot, rest, w_o, vecs, bias_up)
 
 
-def outer_kernel(parts, up_rows, own, me_ref, *refs):
+def outer_kernel(parts, up_rows, own, apart, me_ref, *refs):
     ctx_refs = refs[:parts]
-    nlt_ref, gft_ref, gb_ref, pre_ref, hid_ref, small_ref, out_ref, wo_sc = refs[parts:]
+    nlt_ref, gft_ref, gb_ref, pre_ref, hid_ref, small_ref, out_ref = refs[parts : parts + 7]
+    wo_sc = refs[-1]
     slabs, hidden = out_ref.shape[0], out_ref.shape[3]
     group = ctx_refs[0].shape[0]
     f = pl.program_id(0)
-    up = dot_nn(nlt_ref[...], pre_ref[0]).astype(bf16)
-    out_ref[:, 0, 0:up_rows, :] = up.reshape(slabs, up_rows, hidden)
+    up = dot_nn(nlt_ref[...], pre_ref[0]).astype(bf16).reshape(slabs, up_rows, hidden)
+    if apart:
+        refs[parts + 7][:, 0, :, :] = up[:, 0:apart]
+    out_ref[:, 0, 0 : up_rows - apart, :] = up[:, apart:]
+    at = up_rows - apart
     down = dot_nn(gft_ref[...], hid_ref[0]).astype(bf16)
-    out_ref[:, 0, up_rows : 2 * up_rows, :] = down.reshape(slabs, up_rows, hidden)
+    out_ref[:, 0, at : at + up_rows, :] = down.reshape(slabs, up_rows, hidden)
+    at += up_rows
     if not own:
         return
 
@@ -726,20 +757,21 @@
     for k in range(parts):
         for j in range(share):
             rows = pl.ds(pl.multiple_of(j * stride + f * own, 8), own)
-            out_ref[(me_ref[0] ^ k) * share + j, 0, 2 * up_rows : 2 * up_rows + own, :] = wo_sc[k, rows, :].astype(bf16)
-    out_ref[:, 0, 2 * up_rows + own :, :] = small_ref[:, 0]
-
-
-def outer_products(me, ctx_parts, nlt, gft, gb, pre, hid, small, slabs, up_rows, own):
+            out_ref[(me_ref[0] ^ k) * share + j, 0, at : at + own, :] = wo_sc[k, rows, :].astype(bf16)
+    out_ref[:, 0, at + own :, :] = small_ref[:, 0]
+
+
+def outer_products(me, ctx_parts, nlt, gft, gb, pre, hid, small, slabs, up_rows, own, apart):
     blocks, rows, hidden = pre.shape
     parts = len(ctx_parts)
     group = ctx_parts[0].shape[0]
-    per = 2 * up_rows + (own + 8 if own else 0)
+    per = 2 * up_rows - apart + (own + 8 if own else 0)
+    sizes = (per, apart) if apart else (per,)
     once = lambda shape: pl.BlockSpec(shape, lambda i: (0,) * len(shape), pipeline_mode=pl.Buffered(1))
     return pl.pallas_call(
-        functools.partial(outer_kernel, parts, up_rows, own),
+        functools.partial(outer_kernel, parts, up_rows, own, apart),
         grid=(blocks,),
-        out_shape=jax.ShapeDtypeStruct((slabs, blocks, per, hidden), bf16),
+        out_shape=tuple(jax.ShapeDtypeStruct((slabs, blocks, r, hidden), bf16) for r in sizes),
         in_specs=[pl.BlockSpec(memory_space=pltpu.SMEM)]
         + [once(c.shape) for c in ctx_parts]
         + [
@@ -750,12 +782,39 @@
             pl.BlockSpec((1, rows, hidden), lambda i: (i, 0, 0)),
             pl.BlockSpec((small.shape[0], 1) + small.shape[2:], lambda i: (0, i, 0, 0)),
         ],
-        out_specs=pl.BlockSpec((slabs, 1, per, hidden), lambda i: (0, i, 0, 0)),
+        out_specs=tuple(pl.BlockSpec((slabs, 1, r, hidden), lambda i: (0, i, 0, 0)) for r in sizes),
         scratch_shapes=[pltpu.VMEM((parts, group, gb.shape[1]), f32)],
-        compiler_params=pltpu.CompilerParams(vmem_limit_bytes=48 << 20),
+        compiler_params=pltpu.CompilerParams(vmem_limit_bytes=VMEM_BYTES),
         cost_estimate=pl.CostEstimate(flops=11_000_000_000, bytes_accessed=28_000_000, transcendentals=0),
         name="outer_products",
     )(me, *ctx_parts, nlt, gft, gb, pre, hid, small)
+
+
+def finish_kernel(up_rows, own, apart_ref, total_ref, up_ref, down_ref, wo_ref, small_ref):
+    apart = apart_ref.shape[1]
+    total = jnp.zeros(apart_ref.shape[1:], f32)
+    for d in range(apart_ref.shape[0]):
+        total = total + apart_ref[d].astype(f32)
+    up_ref[0:apart, :] = total
+    rest = total_ref[...].astype(f32)
+    at = up_rows - apart
+    up_ref[apart:, :] = rest[0:at]
+    down_ref[...] = rest[at : at + up_rows]
+    at += up_rows
+    wo_ref[...] = rest[at : at + own]
+    small_ref[...] = rest[at + own : at + own + 8]
+
+
+def finished(apart, total, up_rows, own):
+    hidden = total.shape[1]
+    whole = lambda: pl.BlockSpec(memory_space=pltpu.VMEM)
+    return pl.pallas_call(
+        functools.partial(finish_kernel, up_rows, own),
+        out_shape=tuple(jax.ShapeDtypeStruct((r, hidden), f32) for r in (up_rows, up_rows, own, 8)),
+        in_specs=[whole(), whole()],
+        out_specs=tuple(whole() for _ in range(4)),
+        name="finished",
+    )(apart, total)
 
 
 ALL = ("dp", "seq", "ffn")
@@ -790,10 +849,16 @@
 
     vec = jnp.stack([b_output, b_down, gain_attn, shift_attn, gain_ffn, shift_ffn, b_query, b_value])
     vec = jnp.pad(vec, ((0, 0), (0, width - own)))
+    seg = segment_ids[0].reshape(seq_n, rows)[order]
+    nblocks = seq_n * rows // BLOCK
+    flip = me.astype(jnp.int32) * (nblocks // seq_n)
+    tab = pair_table(random_blocks[0], global_blocks[0], flip, nblocks)
+    gl = global_blocks[0] ^ flip
     pack, rest = packed_weights(
         w_query, w_key, w_value, w_output, w_up, w_down, b_up[None], vec, dp_n, seq_n, ffn_n
     )
     lanes = pack.shape[4]
+    pack, seg, tab, gl = lax.optimization_barrier((pack, seg, tab, gl))
     pack = lax.all_to_all(
         pack.reshape(devices, own_pad + 8, lanes), ALL, split_axis=0, concat_axis=0, tiled=True
     )
@@ -804,12 +869,7 @@
     biases = biases.transpose(1, 0, 2).reshape(2, group).astype(f32)
     by_head = biases[1].reshape(heads, 1, HEAD_DIM)
     b_kv = jnp.concatenate([jnp.zeros_like(by_head), by_head], axis=1).reshape(1, heads * PAIR)
-    seg = segment_ids[0].reshape(seq_n, rows)[order]
-
-    nblocks = seq_n * rows // BLOCK
-    flip = me.astype(jnp.int32) * (nblocks // seq_n)
-    tab = pair_table(random_blocks[0], global_blocks[0], flip, nblocks)
-    gl = global_blocks[0] ^ flip
+
     ctx, (lse, lseg, k_all, v_all, q_all, mask_all) = attention_forward(
         tab, gl, near, seg, w_own, b_kv, biases[0][:, None]
     )
@@ -838,25 +898,25 @@
     small = jnp.concatenate([top, vec_grads], axis=2)
     payload = outer_products(
         me_ref, ctx_parts, normed_t, grad_ffn_t, grad_branch, grad_pre, hidden, small, slabs, slab_rows,
-        own if direct else 0,
+        own if direct else 0, APART if direct else 0,
     )
+    payload, apart = payload if direct else (payload[0], None)
     if not direct:
         grad_out = dot_nn(jnp.concatenate(ctx_parts, axis=0), grad_branch).astype(bf16)
         grad_out = grad_out.reshape(seq_n, group, width)[order].reshape(outer, ffn_n, own, width)
         payload = payload.reshape(ffn_n, 2, outer, up_rows, width).transpose(2, 0, 1, 3, 4)
         payload = jnp.concatenate([payload.reshape(outer, ffn_n, at, width), grad_out, small], axis=2)
         payload = jnp.pad(payload, ((0, 0), (0, 0), (0, -payload.shape[2] % 32), (0, 0)))
-    payload, do = lax.optimization_barrier((payload, do))
+    payload, apart, do = lax.optimization_barrier((payload, apart, do))
     total = lax.psum_scatter(payload.reshape(-1, width), ALL, scatter_dimension=0, tiled=True)
-    total = total.astype(f32)
-    out_up, out_down, out_output = total[:up_rows], total[up_rows:at], total[at : at + own]
-    out_bias_up = total[at + own]
-    out_vecs = total[at + own + 1 : at + own + 7, :own]
-
-    got = attention_backward(tab, gl, do, k_all, v_all, q_all, mask_all, lse, lseg, w_own)
-    dq, dkv, part_first = got[:3]
+    if direct:
+        apart = lax.all_to_all(
+            apart.reshape(devices, APART, width), ALL, split_axis=0, concat_axis=0, tiled=True
+        )
+
+    got = attention_backward(tab, gl, do, k_all, v_all, q_all, mask_all, seg, lse, lseg, w_own, grad_resid_one)
+    dq, dkv, grad_features = got[:3]
     part = [None] + list(got[3:])
-    grad_features = grad_resid_one + part_first
     bit = 1
     while bit < seq_n:
         for k in range(seq_n):
@@ -866,12 +926,21 @@
         bit *= 2
     grad_w = projection_gradients(near, dq, dkv, own, devices)
     grad_w, part = lax.optimization_barrier((grad_w, part[1:]))
+    grad_w, apart = lax.optimization_barrier((grad_w, apart))
     part = [None] + part
     bit = seq_n // 2
     while bit:
         grad_features = grad_features + flip_send(part[bit], "seq", bit).astype(f32)
         bit //= 2
     grad_w = lax.all_to_all(grad_w, ALL, split_axis=0, concat_axis=0, tiled=True)
+    if direct:
+        out_up, out_down, out_output, notes = finished(apart, total, up_rows, own)
+    else:
+        total = total.astype(f32)
+        out_up, out_down, out_output = total[:up_rows], total[up_rows:at], total[at : at + own]
+        notes = total[at + own : at + own + 8]
+    out_bias_up = notes[0]
+    out_vecs = notes[1:7, :own]
     out_query, out_key, out_value, col_sums = unpacked_gradients(
         grad_w.reshape(dp_n, seq_n, ffn_n, own_pad + 8, lanes), own, width
     )

time: 374 us -> 375 us (level)
  local copies, waits for them, and re-layouts: 32.8 us -> 24.8 us
  waiting for transfers between devices: 121 us -> 125 us
    ppermute x12, waiting for transfers between devices: 117 us -> 95.6 us  [flip_send(): return lax.ppermute(array, axis, [(i, i ^ bits) for i in range(count)])]
    all_to_all x0 -> x1, waiting for transfers between devices: none -> 16.8 us  [shards(): lax.all_to_all(apart.reshape(devices, APART, width), ALL, split_axis=0, c...]
    unnamed x46 -> x24, local copies, waits for them, and re-layouts: 11.6 us -> 4.24 us
    all_to_all x0 -> x1, starting transfers between devices: none -> 5.15 us  [shards(): lax.all_to_all(apart.reshape(devices, APART, width), ALL, split_axis=0, c...]
    pallas_call x1, Pallas kernels: 66 us -> 61.1 us  [attention_backward(): pl.pallas_call(functools.partial(backward_kernel, heads, chunks), out_sha...]
    pallas_call x1 -> x2, Pallas kernels: 16.3 us -> 21.2 us  [the longest x1 18.1 us: outer_products(): pl.pallas_call(functools.partial(outer_kernel, parts, up_rows, own, apart...]
    all_to_all x1, waiting for transfers between devices: 0.01 us -> 4.82 us  [shards(): lax.all_to_all(pack.reshape(devices, own_pad + 8, lanes), ALL, split_axis...]
    all_gather x1, waiting for transfers between devices: 3.27 us -> 7.9 us  [shards(): rest = lax.all_gather(rest, ALL, axis=0, tiled=False)]
  transfers between devices with their start and end apart: 16 -> 17, of which waited for: 6 -> 6; matrix products, arithmetic and copies ran while one was open for 8% -> 8% of each run, Pallas kernels for 34% -> 34%
where the time goes in v4:
time: 375 us; the launch traced here: 374 us
  Pallas kernels  169 us (45%)
  waiting for transfers between devices  125 us (33%)
  starting transfers between devices  25 us (7%)
  local copies, waits for them, and re-layouts  24.8 us (7%)
  other arithmetic  15.7 us (4%)
  between operations  14.4 us (4%)
    ppermute x12, waiting for transfers between devices, flip_send(): return lax.ppermute(array, axis, [(i, i ^ bits) for i in range(count)])  95.6 us
    pallas_call x1, Pallas kernels, attention_backward(): pl.pallas_call(functools.partial(backward_kernel, heads, chunks), out_sha...  61.1 us
    pallas_call x1, Pallas kernels, rows_chain(): pl.pallas_call(functools.partial(rows_kernel, parts, blocks, up_rows), gr...  38.2 us
    pallas_call x1, Pallas kernels, attention_forward(): pl.pallas_call(functools.partial(forward_kernel, heads, chunks), out_shap...  34.2 us
    pallas_call x1, Pallas kernels, outer_products(): pl.pallas_call(functools.partial(outer_kernel, parts, up_rows, own, apart...  18.1 us
    all_to_all x1, waiting for transfers between devices, shards(): lax.all_to_all(apart.reshape(devices, APART, width), ALL, split_axis=0, c...  16.8 us
    pallas_call x1, Pallas kernels, projection_gradients(): pl.pallas_call(functools.partial(weights_kernel, chunks, direct), out_sha...  10.2 us
    ppermute x12, starting transfers between devices, flip_send(): return lax.ppermute(array, axis, [(i, i ^ bits) for i in range(count)])  9.14 us
  transfers between devices with their start and end apart: 17, of which 6 were waited for; matrix products, arithmetic and copies ran while one was open for 8% of the time, Pallas kernels for 34%

profile of v4, /device:TPU:0, one launch (start us, length us, event | category | flops | bytes accessed | tf_op | source)
XLA Modules:
  0.0 374.2 jit_solution(11136653934533073090)
XLA Ops:
  9.9 2.3 packed_weights.1
  12.3 3.0 collective-permute-start.1
  26.8 4.9 %all-to-all-start = ((bf16[32,32,640]{2,1,0:T(8,128)(2,1)}), bf16[32,32,640]{2,1,0:T(8,128)(2,1)S(1)}, u32[]{:S(2)}, u32[]{:S(2)}) async-start(bf16[32,32,640]{2,1,0:T(8,128)(2,1)} %bitcast.23), calls=%async_computation | async-start | bytes 2621440 | tf_op jit(solution)/shard_map/all_to_all | solution.py:862
  32.1 40.5 %collective-permute-done.1.refs_2_ = bf16[1024,768]{1,0:T(8,128)(2,1)} collective-permute-done((bf16[1024,768]{1,0:T(8,128)(2,1)}, bf16[1024,768]{1,0:T(8,128)(2,1)}, u32[]{:S(2)}, u32[]{:S(2)}) %collective-permute-start.1) | collective-permute-done | bytes 1572896 | tf_op jit(solution)/shard_map/ppermute | solution.py:825
  72.6 4.8 %all-to-all-done = bf16[32,32,640]{2,1,0:T(8,128)(2,1)S(1)} async-done(((bf16[32,32,640]{2,1,0:T(8,128)(2,1)}), bf16[32,32,640]{2,1,0:T(8,128)(2,1)S(1)}, u32[]{:S(2)}, u32[]{:S(2)}) %all-to-all-start) | async-done | bytes 1310752 | tf_op jit(solution)/shard_map/all_to_all | solution.py:862
  80.0 34.2 %attention_forward.1 = (bf16[192,1024]{1,0:T(8,128)(2,1)}, bf16[192,1024]{1,0:T(8,128)(2,1)}, bf16[192,1024]{1,0:T(8,128)(2,1)}, bf16[192,1024]{1,0:T(8,128)(2,1...) custom-call(s32[960]{0:T(1024)} %reshape.380.tab_ref, ...), custom_call_target="tpu_custom_call" | custom-call | flops 12000000000 | bytes 16000000 | tf_op jit(solution)/shard_map/attention_forward/pallas_call | solution.py:237
  116.1 7.9 %all-gather.3.cloned.1.call-done = bf16[7168,768]{1,0:T(8,128)(2,1)} async-done(((bf16[224,768]{1,0:T(8,128)(2,1)}), bf16[7168,768]{1,0:T(8,128)(2,1)}) %all-gather.3.cloned.1.call-update) | async-done | bytes 11010064 | tf_op jit(solution)/shard_map/all_gather | solution.py:865
  124.0 2.4 slice.123
  129.5 4.4 %collective-permute-done.5.refs_3_ = bf16[192,1024]{1,0:T(8,128)(2,1)S(1)} collective-permute-done((bf16[192,1024]{1,0:T(8,128)(2,1)}, bf16[192,1024]{1,0:T(8,128)(2,1)S(1)}, u32[]{:S(2)}, u32[]{:S(2)}) %collective-permute-start.5) | collective-permute-done | bytes 393248 | tf_op jit(solution)/shard_map/ppermute | solution.py:825
  134.7 38.2 %rows_chain.1 = (bf16[1024,768]{1,0:T(8,128)(2,1)}, f32[1024,768]{1,0:T(8,128)}, bf16[4,1024,768]{2,1,0:T(8,128)(2,1)}, bf16[4,1024,768]{2,1,0:T(8,128)(2,1)}, b...) custom-call(s32[1]{0:T(128)} %bitcast.me_ref, ...), custom_call_target="tpu_custom_call" | custom-call | flops 22000001024 | bytes 40000000 | tf_op jit(solution)/shard_map/rows_chain/pallas_call | solution.py:703
  177.3 18.1 %outer_products.1 = (bf16[8,4,160,768]{3,2,1,0:T(8,128)(2,1)}, bf16[8,4,64,768]{3,2,1,0:T(8,128)(2,1)}) custom-call(s32[1]{0:T(128)} %bitcast.me_ref, bf16[192,1024]{1,0:T(8,128)(2,1)} %get-tuple-element.79.refs_0_, bf16[192,1024]{1,0:T(8,128)(2,1)} %copy-done.5, bf16[192,1024]{1,0:T(8,128)(2,1)} %copy-done.6, bf16[192,1024]{1,0:T(8,128)(2,1)} %copy-done.7, ...), custom_call_target="tpu_custom_call" | custom-call | flops 11000000512 | bytes 28000000 | tf_op jit(solution)/shard_map/outer_products/pallas_call | solution.py:771
  196.4 5.2 %all-to-all-start.1 = ((bf16[32,64,768]{2,1,0:T(8,128)(2,1)}), bf16[32,64,768]{2,1,0:T(8,128)(2,1)}, u32[]{:S(2)}, u32[]{:S(2)}) async-start(bf16[32,64,768]{2,1,0:T(8,128)(2,1)} %bitcast.34), calls=%async_computation.1 | async-start | bytes 6291456 | tf_op jit(solution)/shard_map/all_to_all | solution.py:913
  201.6 61.1 %attention_backward.1 = (bf16[4,192,1024]{2,1,0:T(8,128)(2,1)}, bf16[4,1024,384]{2,1,0:T(8,128)(2,1)}, f32[1024,768]{1,0:T(8,128)}, bf16[1024,768]{1,0:T(8,128)(...) custom-call(s32[960]{0:T(1024)} %reshape.380.tab_ref, s32[2]{0:T(128)} %xor_bitcast_fusion.2.gl_ref, ...), custom_call_target="tpu_custom_call" | custom-call | flops 30000001024 | bytes 24000000 | tf_op jit(solution)/shard_map/attention_backward/pallas_call | solution.py:410
  262.9 10.2 %projection_gradients.1 = (bf16[32,32,640]{2,1,0:T(8,128)(2,1)}, f32[8,640]{1,0:T(8,128)}) custom-call(bf16[1024,768]{1,0:T(8,128)(2,1)} %bitcast.92, bf16[1024,768]{1,0:T(8,128)(2,1)} %collective-permute-done.refs_1_, bf16[1024,768]{1,0:T(8,128)(2,1)} %collective-permute-done.1.refs_2_, bf16[1024,768]{1,0:T(8,128)(2,1)} %collective-permute-done.2.refs_3_, ...), custom_call_target="tpu_custom_call" | custom-call | flops 4000000000 | bytes 12000000 | tf_op jit(solution)/shard_map/projection_gradients/pallas_call | solution.py:550
  273.1 2.9 add_convert_fusion
  276.0 16.8 %all-to-all-done.1.apart_ref = bf16[32,64,768]{2,1,0:T(8,128)(2,1)} async-done(((bf16[32,64,768]{2,1,0:T(8,128)(2,1)}), bf16[32,64,768]{2,1,0:T(8,128)(2,1)}, u32[]{:S(2)}, u32[]{:S(2)}) %all-to-all-start.1) | async-done | bytes 3145760 | tf_op jit(solution)/shard_map/all_to_all | solution.py:913
  292.8 5.7 %all-to-all-start.2 = ((bf16[32,32,640]{2,1,0:T(8,128)(2,1)}), bf16[32,32,640]{2,1,0:T(8,128)(2,1)S(1)}, u32[]{:S(2)}, u32[]{:S(2)}) async-start(bf16[32,32,640]{2,1,0:T(8,128)(2,1)} %get-tuple-element.120), calls=%async_computation.2 | async-start | bytes 2621440 | tf_op jit(solution)/shard_map/all_to_all | solution.py:935
  298.5 1.8 collective-permute-start.10
  300.4 50.6 %collective-permute-done.10 = bf16[1024,768]{1,0:T(8,128)(2,1)} collective-permute-done((bf16[1024,768]{1,0:T(8,128)(2,1)}, bf16[1024,768]{1,0:T(8,128)(2,1)}, u32[]{:S(2)}, u32[]{:S(2)}) %collective-permute-start.10) | collective-permute-done | bytes 1572896 | tf_op jit(solution)/shard_map/ppermute | solution.py:825
  351.0 4.9 %add_bitcast_fusion = f32[1,1024,768]{2,1,0:T(8,128)} fusion(bf16[1024,768]{1,0:T(8,128)(2,1)} %collective-permute-done.11, f32[1024,768]{1,0:T(8,128)} %get-tuple-element.109, bf16[1024,768]{1,0:T(8,128)(2,1)} %collective-permute-done.10), kind=kLoop, calls=%fused_computation.3 | loop fusion | flops 3145728 | bytes 9437184 | tf_op jit(solution)/shard_map/broadcast_in_dim | solution.py:952
  357.1 2.2 unpacked_gradients.1
  361.5 3.1 finished.1
  364.6 1.3 slice_reduce_fusion.2
  365.9 1.4 slice_bitcast_fusion
  (101 shorter events, 31.8 us)
Async XLA Ops:
  7.2 19.1 %copy-start.3 = (s32[1,2]{1,0:T(1,128)S(1)}, s32[1,2]{1,0:T(1,128)}, u32[]{:S(2)}) copy-start(s32[1,2]{1,0:T(1,128)} %param.38) | copy-start | bytes 28
  7.2 17.2 %copy-start.2 = (s32[1,4096]{1,0:T(1,128)S(1)}, s32[1,4096]{1,0:T(1,128)}, u32[]{:S(2)}) copy-start(s32[1,4096]{1,0:T(1,128)} %param.36) | copy-start | bytes 49156
  7.2 116.8 %all-gather.3.cloned.1.call-start = ((), (), s32[]{:S(2)}) async-start(), calls=%async_computation.5 | async-start | bytes 11354112 | tf_op jit(solution)/shard_map/all_gather | solution.py:865
  12.3 60.3 %collective-permute-start.1 = (bf16[1024,768]{1,0:T(8,128)(2,1)}, bf16[1024,768]{1,0:T(8,128)(2,1)}, u32[]{:S(2)}, u32[]{:S(2)}) collective-permute-start(bf16[1024,768]{1,0:T(8,128)(2,1)} %bitcast.89), channel_id=1, source_target_pairs={{0,8},{4,12},{8,0},{12,4},{1,9},{5,13},{9,1},{13,5},{2,10},{6,14},... | collective-permute-start | bytes 4718600 | tf_op jit(solution)/shard_map/ppermute | solution.py:825
  23.0 8.7 %copy-start.4 = (bf16[1,1024,768]{2,1,0:T(8,128)(2,1)S(1)}, bf16[1,1024,768]{2,1,0:T(8,128)(2,1)}, u32[]{:S(2)}) copy-start(bf16[1,1024,768]{2,1,0:T(8,128)(2,1)} %param.20) | copy-start | bytes 4718596
  26.8 50.6 %all-to-all-start = ((bf16[32,32,640]{2,1,0:T(8,128)(2,1)}), bf16[32,32,640]{2,1,0:T(8,128)(2,1)S(1)}, u32[]{:S(2)}, u32[]{:S(2)}) async-start(bf16[32,32,640]{2,1,0:T(8,128)(2,1)} %bitcast.23), calls=%async_computation | async-start | bytes 2621440 | tf_op jit(solution)/shard_map/all_to_all | solution.py:862
  31.7 329.8 %reduce-scatter.2.cloned.1.call-start = ((), (), s32[]{:S(2)}) async-start(), calls=%async_computation.4 | async-start | bytes 8110080 | tf_op jit(solution)/shard_map/reduce_scatter | solution.py:911
  31.8 48.2 %collective-permute-start = (bf16[1024,768]{1,0:T(8,128)(2,1)S(1)}, bf16[1024,768]{1,0:T(8,128)(2,1)}, u32[]{:S(2)}, u32[]{:S(2)}) collective-permute-start(bf16[1024,768]{1,0:T(8,128)(2,1)S(1)} %bitcast.93), channel_id=1, source_target_pairs={{0,4},{4,0},{8,12},{12,8},{1,5},{5,1},{9,13},{13,9},{2,6},{6,2},{1... | collective-permute-start | bytes 4718600 | tf_op jit(solution)/shard_map/ppermute | solution.py:825
  72.6 7.4 %collective-permute-start.2 = (bf16[1024,768]{1,0:T(8,128)(2,1)}, bf16[1024,768]{1,0:T(8,128)(2,1)}, u32[]{:S(2)}, u32[]{:S(2)}) collective-permute-start(bf16[1024,768]{1,0:T(8,128)(2,1)} %collective-permute-done.1.refs_2_), channel_id=1, source_target_pairs={{0,4},{4,0},{8,12},{12,8},{1,5},{5,1},{9,13},{13,9},{2,6},{6,2},{1... | collective-permute-start | bytes 4718600 | tf_op jit(solution)/shard_map/ppermute | solution.py:825
  114.1 15.4 %collective-permute-start.3 = (bf16[192,1024]{1,0:T(8,128)(2,1)}, bf16[192,1024]{1,0:T(8,128)(2,1)S(1)}, u32[]{:S(2)}, u32[]{:S(2)}) collective-permute-start(bf16[192,1024]{1,0:T(8,128)(2,1)} %get-tuple-element.80), channel_id=1, source_target_pairs={{0,4},{4,0},{8,12},{12,8},{1,5},{5,1},{9,13},{13,9},{2,6},{6,2},{1... | collective-permute-start | bytes 1179656 | tf_op jit(solution)/shard_map/ppermute | solution.py:825
  114.2 15.3 %collective-permute-start.4 = (bf16[192,1024]{1,0:T(8,128)(2,1)}, bf16[192,1024]{1,0:T(8,128)(2,1)S(1)}, u32[]{:S(2)}, u32[]{:S(2)}) collective-permute-start(bf16[192,1024]{1,0:T(8,128)(2,1)} %get-tuple-element.81), channel_id=1, source_target_pairs={{0,8},{4,12},{8,0},{12,4},{1,9},{5,13},{9,1},{13,5},{2,10},{6,14},... | collective-permute-start | bytes 1179656 | tf_op jit(solution)/shard_map/ppermute | solution.py:825
  115.1 18.8 %collective-permute-start.5 = (bf16[192,1024]{1,0:T(8,128)(2,1)}, bf16[192,1024]{1,0:T(8,128)(2,1)S(1)}, u32[]{:S(2)}, u32[]{:S(2)}) collective-permute-start(bf16[192,1024]{1,0:T(8,128)(2,1)} %get-tuple-element.82), channel_id=1, source_target_pairs={{0,12},{4,8},{8,4},{12,0},{1,13},{5,9},{9,5},{13,1},{2,14},{6,10},... | collective-permute-start | bytes 1179656 | tf_op jit(solution)/shard_map/ppermute | solution.py:825
  129.5 4.4 %copy-start.5 = (bf16[192,1024]{1,0:T(8,128)(2,1)}, bf16[192,1024]{1,0:T(8,128)(2,1)S(1)}, u32[]{:S(2)}) copy-start(bf16[192,1024]{1,0:T(8,128)(2,1)S(1)} %collective-permute-done.3.refs_1_) | copy-start | bytes 1179652
  129.5 4.4 %copy-start.6 = (bf16[192,1024]{1,0:T(8,128)(2,1)}, bf16[192,1024]{1,0:T(8,128)(2,1)S(1)}, u32[]{:S(2)}) copy-start(bf16[192,1024]{1,0:T(8,128)(2,1)S(1)} %collective-permute-done.4.refs_2_) | copy-start | bytes 1179652
  174.5 20.9 %collective-permute-start.6 = (bf16[192,1024]{1,0:T(8,128)(2,1)}, bf16[192,1024]{1,0:T(8,128)(2,1)S(1)}, u32[]{:S(2)}, u32[]{:S(2)}) collective-permute-start(bf16[192,1024]{1,0:T(8,128)(2,1)} %get-tuple-element.95), channel_id=1, source_target_pairs={{0,4},{4,0},{8,12},{12,8},{1,5},{5,1},{9,13},{13,9},{2,6},{6,2},{1... | collective-permute-start | bytes 1179656 | tf_op jit(solution)/shard_map/ppermute | solution.py:825
  174.7 20.7 %collective-permute-start.7 = (bf16[192,1024]{1,0:T(8,128)(2,1)}, bf16[192,1024]{1,0:T(8,128)(2,1)S(1)}, u32[]{:S(2)}, u32[]{:S(2)}) collective-permute-start(bf16[192,1024]{1,0:T(8,128)(2,1)} %get-tuple-element.96), channel_id=1, source_target_pairs={{0,8},{4,12},{8,0},{12,4},{1,9},{5,13},{9,1},{13,5},{2,10},{6,14},... | collective-permute-start | bytes 1179656 | tf_op jit(solution)/shard_map/ppermute | solution.py:825
  175.3 20.1 %collective-permute-start.8 = (bf16[192,1024]{1,0:T(8,128)(2,1)}, bf16[192,1024]{1,0:T(8,128)(2,1)S(1)}, u32[]{:S(2)}, u32[]{:S(2)}) collective-permute-start(bf16[192,1024]{1,0:T(8,128)(2,1)} %get-tuple-element.97), channel_id=1, source_target_pairs={{0,12},{4,8},{8,4},{12,0},{1,13},{5,9},{9,5},{13,1},{2,14},{6,10},... | collective-permute-start | bytes 1179656 | tf_op jit(solution)/shard_map/ppermute | solution.py:825
  196.4 96.4 %all-to-all-start.1 = ((bf16[32,64,768]{2,1,0:T(8,128)(2,1)}), bf16[32,64,768]{2,1,0:T(8,128)(2,1)}, u32[]{:S(2)}, u32[]{:S(2)}) async-start(bf16[32,64,768]{2,1,0:T(8,128)(2,1)} %bitcast.34), calls=%async_computation.1 | async-start | bytes 6291456 | tf_op jit(solution)/shard_map/all_to_all | solution.py:913
  262.7 10.3 %collective-permute-start.9 = (bf16[1024,768]{1,0:T(8,128)(2,1)}, bf16[1024,768]{1,0:T(8,128)(2,1)}, u32[]{:S(2)}, u32[]{:S(2)}) collective-permute-start(bf16[1024,768]{1,0:T(8,128)(2,1)} %get-tuple-element.115), channel_id=1, source_target_pairs={{0,4},{4,0},{8,12},{12,8},{1,5},{5,1},{9,13},{13,9},{2,6},{6,2},{1... | collective-permute-start | bytes 4718600 | tf_op jit(solution)/shard_map/ppermute | solution.py:825
  262.9 10.2 %copy-start.1 = (bf16[1024,768]{1,0:T(8,128)(2,1)S(1)}, bf16[1024,768]{1,0:T(8,128)(2,1)}, u32[]{:S(2)}) copy-start(bf16[1024,768]{1,0:T(8,128)(2,1)} %get-tuple-element.114) | copy-start | bytes 4718596
  292.8 63.1 %all-to-all-start.2 = ((bf16[32,32,640]{2,1,0:T(8,128)(2,1)}), bf16[32,32,640]{2,1,0:T(8,128)(2,1)S(1)}, u32[]{:S(2)}, u32[]{:S(2)}) async-start(bf16[32,32,640]{2,1,0:T(8,128)(2,1)} %get-tuple-element.120), calls=%async_computation.2 | async-start | bytes 2621440 | tf_op jit(solution)/shard_map/all_to_all | solution.py:935
  298.5 52.5 %collective-permute-start.10 = (bf16[1024,768]{1,0:T(8,128)(2,1)}, bf16[1024,768]{1,0:T(8,128)(2,1)}, u32[]{:S(2)}, u32[]{:S(2)}) collective-permute-start(bf16[1024,768]{1,0:T(8,128)(2,1)} %add_convert_fusion), channel_id=1, source_target_pairs={{0,8},{4,12},{8,0},{12,4},{1,9},{5,13},{9,1},{13,5},{2,10},{6,14},... | collective-permute-start | bytes 4718600 | tf_op jit(solution)/shard_map/ppermute | solution.py:825
  300.4 50.6 %collective-permute-start.11 = (bf16[1024,768]{1,0:T(8,128)(2,1)}, bf16[1024,768]{1,0:T(8,128)(2,1)}, u32[]{:S(2)}, u32[]{:S(2)}) collective-permute-start(bf16[1024,768]{1,0:T(8,128)(2,1)} %get-tuple-element.117), channel_id=1, source_target_pairs={{0,4},{4,0},{8,12},{12,8},{1,5},{5,1},{9,13},{13,9},{2,6},{6,2},{1... | collective-permute-start | bytes 4718600 | tf_op jit(solution)/shard_map/ppermute | solution.py:825
  355.9 1.2 copy-start
  (4 other events, 3.4 us)
Sparse Core Ops, SparseCore 0:
  12.4 111.5 all-gather.2
  195.6 143.0 reduce-scatter.1

commit v5 on v4

--- a/solution.py
+++ b/solution.py
@@ -26,29 +26,22 @@
     return lax.dot_general(a, b, (((0,), (0,)), ((), ())), preferred_element_type=f32)
 
 
-def pair_table(rand_local, global_ids, flip, nblocks):
-    heads = rand_local.shape[0]
-    null = nblocks
-    first = (2 * jnp.arange(nblocks // 2, dtype=jnp.int32)) ^ flip
+def slots(rand_ref, glob_ref, flip, head, pair, nblocks):
+    first = (2 * pair) ^ flip
+
+    def row(block):
+        return pl.multiple_of(block * BLOCK, BLOCK)
 
     def near(block):
-        bad = (block < 0) | (block >= nblocks) | (block == global_ids[0]) | (block == global_ids[1])
-        return jnp.where(bad, null, block ^ flip)
-
-    rand_first = rand_local[:, first, :] ^ flip
-    rand_second = rand_local[:, first + 1, :] ^ flip
-    nears = jnp.stack([near(first), near(first + 1), near(first - 1), near(first + 2)], axis=1)
-    nears = jnp.broadcast_to(nears[None], (heads,) + nears.shape)
-    return jnp.concatenate(
-        [nears[:, :, 0:3], rand_first, nears[:, :, 3:4], rand_second], axis=2
-    ).astype(jnp.int32).reshape(-1)
-
-
-def slots(tab_ref, gl_ref, head, pair, npairs):
-    at = (head * npairs + pair) * 10
-    got = [pl.multiple_of(tab_ref[at + j] * BLOCK, BLOCK) for j in range(10)]
-    glob = [pl.multiple_of(gl_ref[j] * BLOCK, BLOCK) for j in range(2)]
-    return got[0:2] + glob, got[2:6], got[6:10]
+        bad = (block < 0) | (block >= nblocks) | (block == glob_ref[0, 0]) | (block == glob_ref[0, 1])
+        return row(jnp.where(bad, nblocks, block ^ flip))
+
+    def drawn(block):
+        at = (head * nblocks + block) * 3
+        return [row(rand_ref[at + j] ^ flip) for j in range(3)]
+
+    shared = [near(first), near(first + 1)] + [row(glob_ref[0, j] ^ flip) for j in range(2)]
+    return shared, [near(first - 1)] + drawn(first), [near(first + 2)] + drawn(first + 1)
 
 
 def stack_rows(ref, offsets, lanes):
@@ -63,8 +56,8 @@
 
 
 UNROLL = 4
-BACK_UNROLL = 4
-APART = 64
+BACK_UNROLL = 2
+APART = 32
 VMEM_BYTES = 62 << 20
 
 
@@ -76,21 +69,26 @@
     return jnp.concatenate([q_ref[h * BLOCK : (h + 1) * BLOCK, pl.ds(at, PAIR)], mask_ref[:, pl.ds(at, PAIR)]], axis=0)
 
 
-def global_queries(q_ref, mask_ref, h, gl_ref):
+def global_queries(q_ref, mask_ref, h, gl):
     return jnp.concatenate(
         [
-            global_columns(q_ref, slice(h * BLOCK, (h + 1) * BLOCK), gl_ref),
-            global_columns(mask_ref, slice(0, BLOCK), gl_ref),
+            global_columns(q_ref, slice(h * BLOCK, (h + 1) * BLOCK), gl),
+            global_columns(mask_ref, slice(0, BLOCK), gl),
         ],
         axis=0,
     ).astype(bf16)
 
 
-def global_columns(src_ref, rows, gl_ref):
+def placed(me_ref, glob_ref, nblocks, chunks):
+    flip = me_ref[0] * (nblocks // chunks)
+    return flip, [glob_ref[0, j] ^ flip for j in range(2)]
+
+
+def global_columns(src_ref, rows, gl):
     lane = lax.broadcasted_iota(jnp.int32, (1, PAIR), 1)
     parts = []
     for g in range(2):
-        block = gl_ref[g]
+        block = gl[g]
         at = pl.multiple_of((block // 2) * PAIR, PAIR)
         both = src_ref[rows, pl.ds(at, PAIR)].astype(f32)
         moved = pltpu.roll(both, BLOCK, 1)
@@ -98,19 +96,21 @@
     return jnp.where(lane < BLOCK, parts[0], parts[1])
 
 
-def put_global_columns(dst_ref, rows, gl_ref, value, per_chunk):
+def put_global_columns(dst_ref, rows, gl, value, per_chunk, low, high):
     lane = lax.broadcasted_iota(jnp.int32, (1, PAIR), 1)
     moved = pltpu.roll(value, BLOCK, 1)
     for g in range(2):
-        block = gl_ref[g]
-        pair = block // 2
-        half = block % 2
+        pair = gl[g] // 2
+        half = gl[g] % 2
         chunk = pair // per_chunk
-        at = pl.multiple_of((pair % per_chunk) * PAIR, PAIR)
-        src = jnp.where(half == g, value, moved)
-        old = dst_ref[chunk, rows, pl.ds(at, PAIR)].astype(f32)
-        new = jnp.where((lane >= BLOCK) == (half == 1), src, old)
-        dst_ref[chunk, rows, pl.ds(at, PAIR)] = new.astype(dst_ref.dtype)
+
+        @pl.when((chunk >= low) & (chunk < high))
+        def _():
+            at = pl.multiple_of((pair % per_chunk) * PAIR, PAIR)
+            src = jnp.where(half == g, value, moved)
+            old = dst_ref[chunk - low, rows, pl.ds(at, PAIR)].astype(f32)
+            new = jnp.where((lane >= BLOCK) == (half == 1), src, old)
+            dst_ref[chunk - low, rows, pl.ds(at, PAIR)] = new.astype(dst_ref.dtype)
 
 
 def project_rows(x, seg, w_ref, wq, bkv_ref, bq_ref, k_ref, v_ref, q_ref, mask_ref, at):
@@ -136,43 +136,22 @@
     return jnp.transpose(cols, (1, 0))[0 : heads * HEAD_DIM].astype(bf16)
 
 
-def forward_kernel(heads, chunks, tab_ref, gl_ref, *refs):
-    x_refs = refs[0:chunks]
-    seg_ref, w_ref, bkv_ref, bq_ref = refs[chunks : chunks + 4]
-    out_refs = refs[chunks + 4 : 2 * chunks + 4]
-    lse_ref, lseg_ref, k_sc, v_sc, q_sc, mask_sc, s_sc, out_ref = refs[2 * chunks + 4 :]
-    rows = x_refs[0].shape[0]
-    length = rows * chunks
-    npairs = length // PAIR
-    per_chunk = npairs // chunks
-    tile = 256
-    wq = query_weights(w_ref, heads)
-    for c in range(chunks):
-
-        @pl.loop(0, rows // tile)
-        def _(t):
-            at = pl.multiple_of(t * tile, tile)
-            project_rows(
-                x_refs[c][pl.ds(at, tile), :], seg_ref[c : c + 1, pl.ds(at, tile)], w_ref, wq, bkv_ref, bq_ref,
-                k_sc, v_sc, q_sc, mask_sc, pl.multiple_of(c * rows + t * tile, tile),
-            )
-
-    null_lane = lax.broadcasted_iota(jnp.int32, (BLOCK, heads * PAIR), 1) % PAIR
-    k_sc[pl.ds(length, BLOCK), :] = (null_lane == BLOCK + 16).astype(f32).astype(bf16)
-    v_sc[pl.ds(length, BLOCK), :] = jnp.zeros((BLOCK, heads * PAIR), bf16)
+def sparse_forward(heads, low, high, per_chunk, rand_ref, glob_ref, flip, k_ref, kv_ref, q_ref, mask_ref, out_ref, lse_ref):
+    nblocks = (k_ref.shape[0] - BLOCK) // BLOCK
     first, second = lane_halves(PAIR, bf16)
     lane = lax.broadcasted_iota(jnp.int32, (1, PAIR), 1)
 
-    def one_pair(pair):
-        chunk = pair // per_chunk
-        local = pl.multiple_of((pair % per_chunk) * PAIR, PAIR)
+    def one_pair(spot):
+        chunk = spot // per_chunk
+        local = pl.multiple_of((spot % per_chunk) * PAIR, PAIR)
+        pair = low * per_chunk + spot
         at = pl.multiple_of(pair * PAIR, PAIR)
         for h in range(heads):
-            shared, mine, other = slots(tab_ref, gl_ref, h, pair, npairs)
+            shared, mine, other = slots(rand_ref, glob_ref, flip, h, pair, nblocks)
             kl = head_lanes(h)
-            q = query_columns(q_sc, mask_sc, h, at)
-            s_sh = dot_nn(stack_rows(k_sc, shared, kl), q)
-            k_pr = jnp.concatenate([stack_rows(k_sc, mine, kl), stack_rows(k_sc, other, kl)], axis=1)
+            q = query_columns(q_ref, mask_ref, h, at)
+            s_sh = dot_nn(stack_rows(k_ref, shared, kl), q)
+            k_pr = jnp.concatenate([stack_rows(k_ref, mine, kl), stack_rows(k_ref, other, kl)], axis=1)
             s_pr = dot_nn(k_pr, jnp.concatenate([q * first, q * second], axis=0))
             peak = jnp.maximum(jnp.max(s_sh, axis=0, keepdims=True), jnp.max(s_pr, axis=0, keepdims=True))
             e_sh = jnp.exp(s_sh - peak)
@@ -181,20 +160,50 @@
             inv = 1.0 / total
             p_sh = (e_sh * inv).astype(bf16)
             p_pr = (e_pr * inv).astype(bf16)
-            v_pr = jnp.concatenate([stack_rows(v_sc, mine, kl), stack_rows(v_sc, other, kl)], axis=1)
-            o_sh = dot_tn(stack_rows(v_sc, shared, kl), p_sh)
+            v_pr = jnp.concatenate([stack_rows(kv_ref, mine, kl), stack_rows(kv_ref, other, kl)], axis=1)
+            o_sh = dot_tn(stack_rows(kv_ref, shared, kl), p_sh)
             o_pr = dot_tn(v_pr, p_pr)
             ctx = o_sh[BLOCK:PAIR] + jnp.where(lane < BLOCK, o_pr[BLOCK:PAIR], o_pr[PAIR + BLOCK : 2 * PAIR])
             out_ref[chunk, h * BLOCK : (h + 1) * BLOCK, pl.ds(local, PAIR)] = ctx.astype(bf16)
-            lse_ref[h, pl.ds(pair, 1), :] = peak + jnp.log(total)
-
-    @pl.loop(0, npairs // UNROLL)
+            lse_ref[h, pl.ds(spot, 1), :] = peak + jnp.log(total)
+
+    @pl.loop(0, (high - low) * per_chunk // UNROLL)
     def _(some):
         for i in range(UNROLL):
             one_pair(UNROLL * some + i)
 
+
+def forward_kernel(heads, chunks, me_ref, rand_ref, glob_ref, *refs):
+    x_refs = refs[0:chunks]
+    seg_ref, w_ref, bkv_ref, bq_ref = refs[chunks : chunks + 4]
+    far = chunks // 2
+    out_refs = refs[chunks + 4 : chunks + 4 + far]
+    lse_ref, lseg_ref, glob_ctx_ref, k_sc, v_sc, q_sc, mask_sc, s_sc, out_ref, seg_sc = refs[chunks + 4 + far :]
+    rows = x_refs[0].shape[0]
+    length = rows * chunks
+    per_chunk = length // PAIR // chunks
+    flip, gl = placed(me_ref, glob_ref, length // BLOCK, chunks)
+    tile = 256
+    wq = query_weights(w_ref, heads)
+    for c in range(chunks):
+        seg_sc[c : c + 1, :] = seg_ref[pl.ds(me_ref[0] ^ c, 1), :]
+    for c in range(chunks):
+
+        @pl.loop(0, rows // tile)
+        def _(t):
+            at = pl.multiple_of(t * tile, tile)
+            project_rows(
+                x_refs[c][pl.ds(at, tile), :], seg_sc[c : c + 1, pl.ds(at, tile)], w_ref, wq, bkv_ref, bq_ref,
+                k_sc, v_sc, q_sc, mask_sc, pl.multiple_of(c * rows + t * tile, tile),
+            )
+
+    null_lane = lax.broadcasted_iota(jnp.int32, (BLOCK, heads * PAIR), 1) % PAIR
+    k_sc[pl.ds(length, BLOCK), :] = (null_lane == BLOCK + 16).astype(f32).astype(bf16)
+    v_sc[pl.ds(length, BLOCK), :] = jnp.zeros((BLOCK, heads * PAIR), bf16)
+    sparse_forward(heads, far, chunks, per_chunk, rand_ref, glob_ref, flip, k_sc, v_sc, q_sc, mask_sc, out_ref, lse_ref)
+
     step = 512
-    queries = [global_queries(q_sc, mask_sc, h, gl_ref) for h in range(heads)]
+    queries = [global_queries(q_sc, mask_sc, h, gl) for h in range(heads)]
 
     def score(c, peaks):
         at = pl.multiple_of(c * step, step)
@@ -222,61 +231,107 @@
     for h in range(heads):
         total, ctx = sums[h]
         ctx = ctx[BLOCK:PAIR] * (1.0 / total)
-        put_global_columns(out_ref, slice(h * BLOCK, (h + 1) * BLOCK), gl_ref, ctx, per_chunk)
+        glob_ctx_ref[h] = ctx
+        put_global_columns(out_ref, slice(h * BLOCK, (h + 1) * BLOCK), gl, ctx, per_chunk, far, chunks)
         lseg_ref[h : h + 1, :] = peaks[h] + jnp.log(total)
-    for c in range(chunks):
+    for c in range(far):
         out_refs[c][...] = out_ref[c]
 
 
-def attention_forward(tab, gl, x, seg, w, b_kv, b_q):
+def attention_forward(me, rand, glob, x, seg, w, b_kv, b_q):
     chunks = len(x)
+    far = chunks // 2
     rows = x[0].shape[0]
     length = rows * chunks
     heads = b_q.shape[0] // HEAD_DIM
     whole = lambda: pl.BlockSpec(memory_space=pltpu.VMEM)
     got = pl.pallas_call(
         functools.partial(forward_kernel, heads, chunks),
-        out_shape=(jax.ShapeDtypeStruct((heads * HEAD_DIM, rows), bf16),) * chunks
+        out_shape=(jax.ShapeDtypeStruct((heads * HEAD_DIM, rows), bf16),) * far
         + (
-            jax.ShapeDtypeStruct((heads, length // PAIR, PAIR), f32),
+            jax.ShapeDtypeStruct((heads, length // PAIR // 2, PAIR), f32),
             jax.ShapeDtypeStruct((heads, PAIR), f32),
+            jax.ShapeDtypeStruct((heads, HEAD_DIM, PAIR), f32),
             jax.ShapeDtypeStruct((length + BLOCK, heads * PAIR), bf16),
             jax.ShapeDtypeStruct((length + BLOCK, heads * PAIR), bf16),
             jax.ShapeDtypeStruct((heads * HEAD_DIM, length), bf16),
             jax.ShapeDtypeStruct((BLOCK, length), bf16),
         ),
-        in_specs=[pl.BlockSpec(memory_space=pltpu.SMEM)] * 2 + [whole() for _ in range(chunks + 4)],
-        out_specs=tuple(whole() for _ in range(chunks + 6)),
+        in_specs=[pl.BlockSpec(memory_space=pltpu.SMEM)] * 3 + [whole() for _ in range(chunks + 4)],
+        out_specs=tuple(whole() for _ in range(far + 7)),
         scratch_shapes=[
             pltpu.VMEM((heads, length, PAIR), f32),
-            pltpu.VMEM((chunks, heads * HEAD_DIM, rows), bf16),
+            pltpu.VMEM((far, heads * HEAD_DIM, rows), bf16),
+            pltpu.VMEM((chunks, rows), jnp.int32),
         ],
         compiler_params=pltpu.CompilerParams(vmem_limit_bytes=VMEM_BYTES),
-        cost_estimate=pl.CostEstimate(flops=12_000_000_000, bytes_accessed=16_000_000, transcendentals=8_000_000),
+        cost_estimate=pl.CostEstimate(flops=10_000_000_000, bytes_accessed=16_000_000, transcendentals=6_000_000),
         name="attention_forward",
-    )(tab, gl, *x, seg, w, b_kv, b_q)
-    return got[:chunks], got[chunks:]
-
-
-def backward_kernel(heads, chunks, tab_ref, gl_ref, *refs):
+    )(me, rand, glob, *x, seg, w, b_kv, b_q)
+    return got[:far], got[far:]
+
+
+def near_kernel(heads, chunks, me_ref, rand_ref, glob_ref, k_ref, kv_ref, q_ref, mask_ref, glob_ctx_ref, *refs):
+    half = chunks // 2
+    out_refs = refs[:half]
+    lse_ref, out_ref = refs[half:]
+    length = q_ref.shape[1]
+    per_chunk = length // PAIR // chunks
+    flip, gl = placed(me_ref, glob_ref, length // BLOCK, chunks)
+    sparse_forward(heads, 0, half, per_chunk, rand_ref, glob_ref, flip, k_ref, kv_ref, q_ref, mask_ref, out_ref, lse_ref)
+    for h in range(heads):
+        put_global_columns(out_ref, slice(h * BLOCK, (h + 1) * BLOCK), gl, glob_ctx_ref[h], per_chunk, 0, half)
+    for c in range(half):
+        out_refs[c][...] = out_ref[c]
+
+
+def attention_near(me, rand, glob, k, kv, q, mask, glob_ctx, chunks):
+    heads = glob_ctx.shape[0]
+    half = chunks // 2
+    length = q.shape[1]
+    rows = length // chunks
+    whole = lambda: pl.BlockSpec(memory_space=pltpu.VMEM)
+    got = pl.pallas_call(
+        functools.partial(near_kernel, heads, chunks),
+        out_shape=(jax.ShapeDtypeStruct((heads * HEAD_DIM, rows), bf16),) * half
+        + (jax.ShapeDtypeStruct((heads, length // PAIR // 2, PAIR), f32),),
+        in_specs=[pl.BlockSpec(memory_space=pltpu.SMEM)] * 3 + [whole() for _ in range(5)],
+        out_specs=tuple(whole() for _ in range(half + 1)),
+        scratch_shapes=[pltpu.VMEM((half, heads * HEAD_DIM, rows), bf16)],
+        compiler_params=pltpu.CompilerParams(vmem_limit_bytes=VMEM_BYTES),
+        cost_estimate=pl.CostEstimate(flops=6_000_000_000, bytes_accessed=9_000_000, transcendentals=3_000_000),
+        name="attention_near",
+    )(me, rand, glob, k, kv, q, mask, glob_ctx)
+    return got[:half], got[half]
+
+
+def backward_kernel(heads, chunks, me_ref, rand_ref, glob_ref, *refs):
     do_refs = refs[:chunks]
-    (k_ref, kv_ref, q_ref, mask_ref, seg_ref, lse_ref, lseg_ref, w_ref, resid_ref, dq_ref, dkv_ref, first_ref) = refs[
-        chunks : chunks + 12
-    ]
-    part_refs = refs[chunks + 12 : 2 * chunks + 11]
-    do_sc, acc, p_sc, d_sc, seg_sc, line_sc = refs[2 * chunks + 11 :]
+    (k_ref, kv_ref, q_ref, mask_ref, seg_ref, lse_near_ref, lse_far_ref, lseg_ref, w_ref, resid_ref, dq_ref, dkv_ref,
+     first_ref) = refs[chunks : chunks + 13]
+    part_refs = refs[chunks + 13 : 2 * chunks + 12]
+    do_sc, acc, p_sc, d_sc, seg_sc, line_sc, lse_ref, row_sc = refs[2 * chunks + 12 :]
     rows = do_refs[0].shape[1]
     length = rows * chunks
     npairs = length // PAIR
     per_chunk = npairs // chunks
     scale = HEAD_DIM ** -0.5
+    flip, gl = placed(me_ref, glob_ref, length // BLOCK, chunks)
+    lse_ref[:, 0 : npairs // 2, :] = lse_near_ref[...]
+    lse_ref[:, npairs // 2 :, :] = lse_far_ref[...]
     for c in range(chunks):
         do_sc[:, c * rows : (c + 1) * rows] = do_refs[c][...]
-        for t in range(per_chunk):
-            line = seg_ref[c : c + 1, t * PAIR : (t + 1) * PAIR].astype(f32)
-            line_sc[c * per_chunk + t] = line
-            to = c * rows + t * PAIR
-            seg_sc[to : to + PAIR, :] = jnp.transpose(jnp.broadcast_to(line, (PAIR, PAIR)), (1, 0))
+        row_sc[c : c + 1, :] = seg_ref[pl.ds(me_ref[0] ^ c, 1), :].astype(f32)
+
+        @pl.loop(0, per_chunk // 4)
+        def _(some):
+            for i in range(4):
+                t = 4 * some + i
+                line = row_sc[c : c + 1, pl.ds(pl.multiple_of(t * PAIR, PAIR), PAIR)]
+                line_sc[c * per_chunk + t] = line
+                to = pl.multiple_of(c * rows + t * PAIR, PAIR)
+                seg_sc[pl.ds(to, PAIR), :] = jnp.transpose(jnp.broadcast_to(line, (PAIR, PAIR)), (1, 0))
+
     seg_sc[length : length + BLOCK, :] = jnp.full((BLOCK, PAIR), -1.0, f32)
     first2, second2 = lane_halves(2 * PAIR, bf16)
     ffirst, fsecond = lane_halves(PAIR, f32)
@@ -298,9 +353,9 @@
         return jnp.concatenate([top, jnp.concatenate([zeros, do], axis=1)], axis=0)
 
     step = 512
-    mask_glob = global_columns(mask_ref, slice(0, BLOCK), gl_ref).astype(bf16)
-    q_glob = [global_columns(q_ref, head_rows(h), gl_ref).astype(bf16) for h in range(heads)]
-    do_glob = [global_columns(do_sc, head_rows(h), gl_ref).astype(bf16) for h in range(heads)]
+    mask_glob = global_columns(mask_ref, slice(0, BLOCK), gl).astype(bf16)
+    q_glob = [global_columns(q_ref, head_rows(h), gl).astype(bf16) for h in range(heads)]
+    do_glob = [global_columns(do_sc, head_rows(h), gl).astype(bf16) for h in range(heads)]
 
     def weigh(c, deltas):
         at = pl.multiple_of(c * step, step)
@@ -336,13 +391,13 @@
         chunk = pair // per_chunk
         local = pl.multiple_of((pair % per_chunk) * PAIR, PAIR)
         at = pl.multiple_of(pair * PAIR, PAIR)
-        hit_first = (gl_ref[0] == 2 * pair) | (gl_ref[1] == 2 * pair)
-        hit_second = (gl_ref[0] == 2 * pair + 1) | (gl_ref[1] == 2 * pair + 1)
+        hit_first = (gl[0] == 2 * pair) | (gl[1] == 2 * pair)
+        hit_second = (gl[0] == 2 * pair + 1) | (gl[1] == 2 * pair + 1)
         shut = ffirst * jnp.where(hit_first, -MASKED, 0.0) + fsecond * jnp.where(hit_second, -MASKED, 0.0)
         every = slice(0, PAIR)
         for h in range(heads):
             kl = head_lanes(h)
-            shared, mine, other = slots(tab_ref, gl_ref, h, pair, npairs)
+            shared, mine, other = slots(rand_ref, glob_ref, flip, h, pair, length // BLOCK)
             q = q_ref[head_rows(h), pl.ds(at, PAIR)]
             do = do_sc[head_rows(h), pl.ds(at, PAIR)]
             lse = lse_ref[h, pl.ds(pair, 1), :] + shut
@@ -382,7 +437,7 @@
             one_pair(BACK_UNROLL * some + i)
 
     for h in range(heads):
-        put_global_columns(dq_ref, head_rows(h), gl_ref, dqs[h][0:BLOCK] * scale, per_chunk)
+        put_global_columns(dq_ref, head_rows(h), gl, dqs[h][0:BLOCK] * scale, per_chunk, 0, chunks)
         for c in range(chunks):
             dkv_ref[c, :, head_lanes(h)] = acc[h, pl.ds(c * rows, rows), :].astype(bf16)
     tile = 256
@@ -400,7 +455,7 @@
                 part_refs[c - 1][pl.ds(at, tile), :] = got.astype(bf16)
 
 
-def attention_backward(tab, gl, do, k, kv, q, mask, seg, lse, lseg, w, resid):
+def attention_backward(me, rand, glob, do, k, kv, q, mask, seg, lse_near, lse_far, lseg, w, resid):
     chunks = len(do)
     group, rows = do[0].shape
     heads = group // HEAD_DIM
@@ -415,7 +470,7 @@
             jax.ShapeDtypeStruct((rows, width), f32),
         )
         + (jax.ShapeDtypeStruct((rows, width), bf16),) * (chunks - 1),
-        in_specs=[pl.BlockSpec(memory_space=pltpu.SMEM)] * 2 + [whole() for _ in range(chunks + 9)],
+        in_specs=[pl.BlockSpec(memory_space=pltpu.SMEM)] * 3 + [whole() for _ in range(chunks + 10)],
         out_specs=tuple(whole() for _ in range(chunks + 2)),
         scratch_shapes=[
             pltpu.VMEM((group, length), bf16),
@@ -424,11 +479,13 @@
             pltpu.VMEM((heads, length, PAIR), f32),
             pltpu.VMEM((length + BLOCK, PAIR), f32),
             pltpu.VMEM((length // PAIR, 1, PAIR), f32),
+            pltpu.VMEM((heads, length // PAIR, PAIR), f32),
+            pltpu.VMEM((chunks, rows), f32),
         ],
         compiler_params=pltpu.CompilerParams(vmem_limit_bytes=VMEM_BYTES),
         cost_estimate=pl.CostEstimate(flops=30_000_000_000, bytes_accessed=24_000_000, transcendentals=8_000_000),
         name="attention_backward",
-    )(tab, gl, *do, k, kv, q, mask, seg, lse, lseg, w, resid)
+    )(me, rand, glob, *do, k, kv, q, mask, seg, lse_near, lse_far, lseg, w, resid)
 
 
 def round_up(value, to):
@@ -622,12 +679,12 @@
     )
 
 
-def rows_kernel(parts, blocks, up_rows, me_ref, *refs):
+def rows_kernel(parts, blocks, up_rows, own, me_ref, *refs):
     ctx_refs = refs[:parts]
     (x_ref, cot_ref, rest_ref, wo_ref, vec_ref, bup_ref, out_ref, resid_ref, hid_ref, pre_ref, nlt_ref, gft_ref,
      gb_ref) = refs[parts : parts + 13]
     do_refs = refs[parts + 13 : 2 * parts + 13]
-    sums_ref, gbup_ref, slope_sc = refs[2 * parts + 13 :]
+    sums_ref, gbup_ref, slope_sc, wo_sc, wide_sc = refs[2 * parts + 13 :]
     group = ctx_refs[0].shape[0]
     width = x_ref.shape[1]
 
@@ -644,18 +701,32 @@
     def _():
         sums_ref[...] = jnp.zeros_like(sums_ref)
         gbup_ref[...] = jnp.zeros_like(gbup_ref)
+        if own:
+            for o in range(rest_ref.shape[0]):
+                for f in range(blocks):
+                    to = (o * blocks + f) * own
+                    wide_sc[to : to + own, :] = rest_ref[o, f, 2 * up_rows : 2 * up_rows + own, :].astype(f32)
+            wo_sc[...] = wide_sc[...].astype(bf16)
+        else:
+            wo_sc[...] = wo_ref[...]
+
+    def bias_up(f):
+        if own:
+            row = rest_ref[0, f, 2 * up_rows + own : 2 * up_rows + own + 8, :].astype(f32)
+            return row[7:8, :]
+        return bup_ref[f : f + 1, :]
 
     ctx = jnp.concatenate([r[...] for r in ctx_refs], axis=0)
-    w_o = jnp.concatenate([wo_ref[own_rows(k), :] for k in range(parts)], axis=0)
+    w_o = jnp.concatenate([wo_sc[own_rows(k), :] for k in range(parts)], axis=0)
     resid_one = x_ref[...].astype(f32) + (dot_tn(ctx, w_o) + vec_ref[0:1, :])
     unit_one, scale_one = unit_rows(resid_one)
     normed_one = unit_one * vec_ref[2:3, :] + vec_ref[3:4, :]
     low = normed_one.astype(bf16)
     nlt_ref[...] = transposed(normed_one)
     total = normed_one + vec_ref[1:2, :]
-    pre = dot_nn(low, up(0)) + bup_ref[0:1, :]
+    pre = dot_nn(low, up(0)) + bias_up(0)
     for f in range(blocks):
-        later = dot_nn(low, up(f + 1)) + bup_ref[f + 1 : f + 2, :] if f + 1 < blocks else None
+        later = dot_nn(low, up(f + 1)) + bias_up(f + 1) if f + 1 < blocks else None
         phi = 0.5 + 0.5 * lax.erf(pre * (0.5 ** 0.5))
         slope_sc[f] = phi + pre * (jnp.exp(-0.5 * pre * pre) * 0.3989422804014327)
         hid = (pre * phi).astype(bf16)
@@ -690,7 +761,7 @@
         sums_ref[row : row + 1, :] += jnp.sum(value, axis=0, keepdims=True)
 
 
-def rows_chain(me, ctx_parts, x, cot, rest, up_rows, w_o, vecs, bias_up):
+def rows_chain(me, ctx_parts, x, cot, rest, up_rows, own, w_o, vecs, bias_up):
     parts = len(ctx_parts)
     group, rows = ctx_parts[0].shape
     width = x.shape[1]
@@ -701,7 +772,7 @@
     wide = pl.BlockSpec((width, tile), lambda i: (0, i))
     cube = pl.BlockSpec((blocks, tile, hidden), lambda i: (0, i, 0))
     return pl.pallas_call(
-        functools.partial(rows_kernel, parts, blocks, up_rows),
+        functools.partial(rows_kernel, parts, blocks, up_rows, own),
         grid=(rows // tile,),
         out_shape=(
             jax.ShapeDtypeStruct((rows, width), bf16),
@@ -722,7 +793,11 @@
         )
         + (pl.BlockSpec((group, tile), lambda i: (0, i)),) * parts
         + (pl.BlockSpec((8, width), lambda i: (0, 0)), pl.BlockSpec((8, hidden), lambda i: (0, 0))),
-        scratch_shapes=[pltpu.VMEM((blocks, tile, hidden), f32)],
+        scratch_shapes=[
+            pltpu.VMEM((blocks, tile, hidden), f32),
+            pltpu.VMEM((width, width), bf16),
+            pltpu.VMEM((width, width), f32),
+        ],
         compiler_params=pltpu.CompilerParams(vmem_limit_bytes=VMEM_BYTES),
         cost_estimate=pl.CostEstimate(flops=22_000_000_000, bytes_accessed=40_000_000, transcendentals=6_000_000),
         name="rows_chain",
@@ -731,14 +806,14 @@
 
 def outer_kernel(parts, up_rows, own, apart, me_ref, *refs):
     ctx_refs = refs[:parts]
-    nlt_ref, gft_ref, gb_ref, pre_ref, hid_ref, small_ref, out_ref = refs[parts : parts + 7]
+    nlt_ref, gft_ref, gb_ref, pre_ref, hid_ref, sums_ref, gbup_ref, out_ref = refs[parts : parts + 8]
     wo_sc = refs[-1]
     slabs, hidden = out_ref.shape[0], out_ref.shape[3]
     group = ctx_refs[0].shape[0]
     f = pl.program_id(0)
     up = dot_nn(nlt_ref[...], pre_ref[0]).astype(bf16).reshape(slabs, up_rows, hidden)
     if apart:
-        refs[parts + 7][:, 0, :, :] = up[:, 0:apart]
+        refs[parts + 8][:, 0, :, :] = up[:, 0:apart]
     out_ref[:, 0, 0 : up_rows - apart, :] = up[:, apart:]
     at = up_rows - apart
     down = dot_nn(gft_ref[...], hid_ref[0]).astype(bf16)
@@ -758,10 +833,12 @@
         for j in range(share):
             rows = pl.ds(pl.multiple_of(j * stride + f * own, 8), own)
             out_ref[(me_ref[0] ^ k) * share + j, 0, at : at + own, :] = wo_sc[k, rows, :].astype(bf16)
-    out_ref[:, 0, at + own :, :] = small_ref[:, 0]
-
-
-def outer_products(me, ctx_parts, nlt, gft, gb, pre, hid, small, slabs, up_rows, own, apart):
+    small = jnp.concatenate([gbup_ref[pl.ds(f, 1), :], sums_ref[0:7, :]], axis=0).astype(bf16)
+    for o in range(slabs):
+        out_ref[o, 0, at + own :, :] = small
+
+
+def outer_products(me, ctx_parts, nlt, gft, gb, pre, hid, sums, gbup, slabs, up_rows, own, apart):
     blocks, rows, hidden = pre.shape
     parts = len(ctx_parts)
     group = ctx_parts[0].shape[0]
@@ -780,14 +857,15 @@
             once(gb.shape),
             pl.BlockSpec((1, rows, hidden), lambda i: (i, 0, 0)),
             pl.BlockSpec((1, rows, hidden), lambda i: (i, 0, 0)),
-            pl.BlockSpec((small.shape[0], 1) + small.shape[2:], lambda i: (0, i, 0, 0)),
+            once(sums.shape),
+            once(gbup.shape),
         ],
         out_specs=tuple(pl.BlockSpec((slabs, 1, r, hidden), lambda i: (0, i, 0, 0)) for r in sizes),
         scratch_shapes=[pltpu.VMEM((parts, group, gb.shape[1]), f32)],
         compiler_params=pltpu.CompilerParams(vmem_limit_bytes=VMEM_BYTES),
         cost_estimate=pl.CostEstimate(flops=11_000_000_000, bytes_accessed=28_000_000, transcendentals=0),
         name="outer_products",
-    )(me, *ctx_parts, nlt, gft, gb, pre, hid, small)
+    )(me, *ctx_parts, nlt, gft, gb, pre, hid, sums, gbup)
 
 
 def finish_kernel(up_rows, own, apart_ref, total_ref, up_ref, down_ref, wo_ref, small_ref):
@@ -849,16 +927,13 @@
 
     vec = jnp.stack([b_output, b_down, gain_attn, shift_attn, gain_ffn, shift_ffn, b_query, b_value])
     vec = jnp.pad(vec, ((0, 0), (0, width - own)))
-    seg = segment_ids[0].reshape(seq_n, rows)[order]
-    nblocks = seq_n * rows // BLOCK
-    flip = me.astype(jnp.int32) * (nblocks // seq_n)
-    tab = pair_table(random_blocks[0], global_blocks[0], flip, nblocks)
-    gl = global_blocks[0] ^ flip
+    seg = segment_ids[0].reshape(seq_n, rows)
+    rand = random_blocks.reshape(-1)
     pack, rest = packed_weights(
         w_query, w_key, w_value, w_output, w_up, w_down, b_up[None], vec, dp_n, seq_n, ffn_n
     )
     lanes = pack.shape[4]
-    pack, seg, tab, gl = lax.optimization_barrier((pack, seg, tab, gl))
+    pack, seg, rand = lax.optimization_barrier((pack, seg, rand))
     pack = lax.all_to_all(
         pack.reshape(devices, own_pad + 8, lanes), ALL, split_axis=0, concat_axis=0, tiled=True
     )
@@ -870,40 +945,49 @@
     by_head = biases[1].reshape(heads, 1, HEAD_DIM)
     b_kv = jnp.concatenate([jnp.zeros_like(by_head), by_head], axis=1).reshape(1, heads * PAIR)
 
-    ctx, (lse, lseg, k_all, v_all, q_all, mask_all) = attention_forward(
-        tab, gl, near, seg, w_own, b_kv, biases[0][:, None]
+    far = seq_n // 2
+    ctx_far, (lse_far, lseg, glob_ctx, k_all, v_all, q_all, mask_all) = attention_forward(
+        me_ref, rand, global_blocks, near, seg, w_own, b_kv, biases[0][:, None]
     )
-    ctx_parts = [ctx[0]] + [flip_send(ctx[k], "seq", k) for k in range(1, seq_n)]
+    ctx_parts = [None] * far + [flip_send(ctx_far[k - far], "seq", k) for k in range(far, seq_n)]
+    ctx_near, lse_near = attention_near(
+        me_ref, rand, global_blocks, k_all, v_all, q_all, mask_all, glob_ctx, seq_n
+    )
+    ctx_parts[far:], ctx_parts[0] = lax.optimization_barrier((ctx_parts[far:], ctx_near[0]))
+    for k in range(1, far):
+        ctx_parts[k] = flip_send(ctx_near[k], "seq", k)
 
     up_rows = w_up.shape[0]
     at = 2 * up_rows
     rest = rest.reshape(outer, ffn_n, rest.shape[1], width)
     w_o = rest[:, :, at : at + own].reshape(width, width)
     bias_up = rest[0, :, at + own_pad + 7].astype(f32)
-    vecs = rest[:, :, at + own_pad :, :own].transpose(2, 0, 1, 3).reshape(8, width).astype(f32)
+    vecs = pack[:, own_pad:, :own].transpose(1, 0, 2).reshape(8, width).astype(f32)
     direct = up_rows % 16 == 0 and own % 8 == 0 and outer % seq_n == 0 and (outer // seq_n) * ffn_n * own == group
     if not direct:
         rest = rest[:, :, :at].reshape(outer, ffn_n, 2, up_rows, width).transpose(1, 2, 0, 3, 4)
         rest = rest.reshape(1, ffn_n, 2 * outer * up_rows, width)
     slabs, slab_rows = (outer, up_rows) if direct else (1, outer * up_rows)
 
-    got = rows_chain(me_ref, ctx_parts, features, cotangent[0], rest, slab_rows, w_o, vecs, bias_up)
+    got = rows_chain(
+        me_ref, ctx_parts, features, cotangent[0], rest, slab_rows, own if direct else 0,
+        jnp.zeros((8, PAIR), bf16) if direct else w_o, vecs, jnp.zeros((8, PAIR), f32) if direct else bias_up,
+    )
     out, grad_resid_one, hidden, grad_pre, normed_t, grad_ffn_t, grad_branch = got[:7]
     grad_ctx, (sums, grad_bias_up) = got[7 : 7 + seq_n], got[7 + seq_n :]
     do = [grad_ctx[0]] + [flip_send(grad_ctx[k], "seq", k) for k in range(1, seq_n)]
 
-    vec_grads = sums[:6].astype(bf16).reshape(6, outer, ffn_n, own).transpose(1, 2, 0, 3)
-    vec_grads = jnp.pad(vec_grads, ((0, 0), (0, 0), (0, 1), (0, width - own)))
-    top = jnp.broadcast_to(grad_bias_up[None, :ffn_n, None].astype(bf16), (outer, ffn_n, 1, width))
-    small = jnp.concatenate([top, vec_grads], axis=2)
     payload = outer_products(
-        me_ref, ctx_parts, normed_t, grad_ffn_t, grad_branch, grad_pre, hidden, small, slabs, slab_rows,
+        me_ref, ctx_parts, normed_t, grad_ffn_t, grad_branch, grad_pre, hidden, sums, grad_bias_up, slabs, slab_rows,
         own if direct else 0, APART if direct else 0,
     )
     payload, apart = payload if direct else (payload[0], None)
     if not direct:
         grad_out = dot_nn(jnp.concatenate(ctx_parts, axis=0), grad_branch).astype(bf16)
         grad_out = grad_out.reshape(seq_n, group, width)[order].reshape(outer, ffn_n, own, width)
+        top = jnp.broadcast_to(grad_bias_up[None, :ffn_n, None], (outer, ffn_n, 1, width))
+        small = jnp.concatenate([top, jnp.broadcast_to(sums[None, None, :7], (outer, ffn_n, 7, width))], axis=2)
+        small = small.astype(bf16)
         payload = payload.reshape(ffn_n, 2, outer, up_rows, width).transpose(2, 0, 1, 3, 4)
         payload = jnp.concatenate([payload.reshape(outer, ffn_n, at, width), grad_out, small], axis=2)
         payload = jnp.pad(payload, ((0, 0), (0, 0), (0, -payload.shape[2] % 32), (0, 0)))
@@ -914,7 +998,10 @@
             apart.reshape(devices, APART, width), ALL, split_axis=0, concat_axis=0, tiled=True
         )
 
-    got = attention_backward(tab, gl, do, k_all, v_all, q_all, mask_all, seg, lse, lseg, w_own, grad_resid_one)
+    got = attention_backward(
+        me_ref, rand, global_blocks, do, k_all, v_all, q_all, mask_all, seg, lse_near, lse_far, lseg, w_own,
+        grad_resid_one,
+    )
     dq, dkv, grad_features = got[:3]
     part = [None] + list(got[3:])
     bit = 1
@@ -933,6 +1020,7 @@
         grad_features = grad_features + flip_send(part[bit], "seq", bit).astype(f32)
         bit //= 2
     grad_w = lax.all_to_all(grad_w, ALL, split_axis=0, concat_axis=0, tiled=True)
+    grad_w, grad_features = lax.optimization_barrier((grad_w, grad_features))
     if direct:
         out_up, out_down, out_output, notes = finished(apart, total, up_rows, own)
     else:
@@ -940,7 +1028,7 @@
         out_up, out_down, out_output = total[:up_rows], total[up_rows:at], total[at : at + own]
         notes = total[at + own : at + own + 8]
     out_bias_up = notes[0]
-    out_vecs = notes[1:7, :own]
+    out_vecs = lax.dynamic_slice(notes, (1, here * own), (6, own))
     out_query, out_key, out_value, col_sums = unpacked_gradients(
         grad_w.reshape(dp_n, seq_n, ffn_n, own_pad + 8, lanes), own, width
     )

time: 375 us -> 354 us (0.944)
  waiting for transfers between devices: 125 us -> 113 us
  local copies, waits for them, and re-layouts: 24.8 us -> 16.8 us
  Pallas kernels: 169 us -> 175 us
  other arithmetic: 15.7 us -> 9.96 us
    all_to_all x1, waiting for transfers between devices: 16.8 us -> 0.01 us  [shards(): lax.all_to_all(apart.reshape(devices, APART, width), ALL, split_axis=0, c...]
    ppermute x12, waiting for transfers between devices: 95.6 us -> 108 us  [flip_send(): return lax.ppermute(array, axis, [(i, i ^ bits) for i in range(count)])]
    pallas_call x1 -> x2, Pallas kernels: 38.2 us -> 49.4 us  [the longest x1 37.7 us: rows_chain(): pl.pallas_call(functools.partial(rows_kernel, parts, blocks, up_rows, own...]
    all_gather x1, waiting for transfers between devices: 7.9 us -> 0.01 us  [shards(): rest = lax.all_gather(rest, ALL, axis=0, tiled=False)]
    pallas_call x1, Pallas kernels: 34.2 us -> 26.8 us  [attention_forward(): pl.pallas_call(functools.partial(forward_kernel, heads, chunks), out_shap...]
    slice x5 -> x0, local copies, waits for them, and re-layouts: 6.04 us -> none  [the longest x1 2.43 us: shards(): w_o = rest[:, :, at:at + own].reshape(width, width)]
    add x0 -> x1, other arithmetic: none -> 4.92 us  [shards(): grad_features = grad_features + flip_send(part[bit], 'seq', bit).astype(f32)]
    broadcast_in_dim x1 -> x0, other arithmetic: 4.9 us -> none  [shards(): grad_features[None]]
  transfers between devices with their start and end apart: 17 -> 17, of which waited for: 6 -> 4; matrix products, arithmetic and copies ran while one was open for 8% -> 5% of each run, Pallas kernels for 34% -> 37%
where the time goes in v5:
time: 354 us
  Pallas kernels  175 us (49%)
  waiting for transfers between devices  113 us (32%)
  starting transfers between devices  25.5 us (7%)
  local copies, waits for them, and re-layouts  16.8 us (5%)
  between operations  14.2 us (4%)
  other arithmetic  9.96 us (3%)
    ppermute x12, waiting for transfers between devices, flip_send(): return lax.ppermute(array, axis, [(i, i ^ bits) for i in range(count)])  108 us
    pallas_call x1, Pallas kernels, attention_backward(): pl.pallas_call(functools.partial(backward_kernel, heads, chunks), out_sha...  63.6 us
    pallas_call x1, Pallas kernels, rows_chain(): pl.pallas_call(functools.partial(rows_kernel, parts, blocks, up_rows, own...  37.7 us
    pallas_call x1, Pallas kernels, attention_forward(): pl.pallas_call(functools.partial(forward_kernel, heads, chunks), out_shap...  26.8 us
    pallas_call x1, Pallas kernels, outer_products(): pl.pallas_call(functools.partial(outer_kernel, parts, up_rows, own, apart...  17.7 us
    pallas_call x1, Pallas kernels, attention_near(): pl.pallas_call(functools.partial(near_kernel, heads, chunks), out_shape=(...  11.8 us
    pallas_call x1, Pallas kernels, projection_gradients(): pl.pallas_call(functools.partial(weights_kernel, chunks, direct), out_sha...  10.1 us
    ppermute x12, starting transfers between devices, flip_send(): return lax.ppermute(array, axis, [(i, i ^ bits) for i in range(count)])  9.7 us
  transfers between devices with their start and end apart: 17, of which 4 were waited for; matrix products, arithmetic and copies ran while one was open for 5% of the time, Pallas kernels for 37%

profile of v5, /device:TPU:0, one launch (start us, length us, event | category | flops | bytes accessed | tf_op | source)
XLA Modules:
  0.0 353.5 jit_solution(1796103280562595058)
XLA Ops:
  7.2 1.3 broadcast_in_dim.20.bup_ref
  9.9 2.3 packed_weights.1
  12.2 3.0 collective-permute-start.1
  17.3 1.4 reduce.17
  19.4 4.9 %all-to-all-start = ((bf16[32,32,640]{2,1,0:T(8,128)(2,1)}), bf16[32,32,640]{2,1,0:T(8,128)(2,1)S(1)}, u32[]{:S(2)}, u32[]{:S(2)}) async-start(bf16[32,32,640]{2,1,0:T(8,128)(2,1)} %bitcast.45), calls=%async_computation | async-start | bytes 2621440 | tf_op jit(solution)/shard_map/all_to_all | solution.py:937
  24.7 48.4 %collective-permute-done.1.refs_2_ = bf16[1024,768]{1,0:T(8,128)(2,1)} collective-permute-done((bf16[1024,768]{1,0:T(8,128)(2,1)}, bf16[1024,768]{1,0:T(8,128)(2,1)}, u32[]{:S(2)}, u32[]{:S(2)}) %collective-permute-start.1) | collective-permute-done | bytes 1572896 | tf_op jit(solution)/shard_map/ppermute | solution.py:903
  73.1 4.3 %all-to-all-done = bf16[32,32,640]{2,1,0:T(8,128)(2,1)S(1)} async-done(((bf16[32,32,640]{2,1,0:T(8,128)(2,1)}), bf16[32,32,640]{2,1,0:T(8,128)(2,1)S(1)}, u32[]{:S(2)}, u32[]{:S(2)}) %all-to-all-start) | async-done | bytes 1310752 | tf_op jit(solution)/shard_map/all_to_all | solution.py:937
  80.0 26.8 %attention_forward.1 = (bf16[192,1024]{1,0:T(8,128)(2,1)}, bf16[192,1024]{1,0:T(8,128)(2,1)}, f32[3,16,128]{2,1,0:T(8,128)}, f32[3,128]{1,0:T(4,128)}, f32[3,64,...) custom-call(s32[1]{0:T(128)} %bitcast.me_ref, ...), custom_call_target="tpu_custom_call" | custom-call | flops 10000000000 | bytes 16000000 | tf_op jit(solution)/shard_map/attention_forward/pallas_call | solution.py:248
  107.4 11.8 %attention_near.1 = (bf16[192,1024]{1,0:T(8,128)(2,1)}, bf16[192,1024]{1,0:T(8,128)(2,1)}, f32[3,16,128]{2,1,0:T(8,128)}) custom-call(s32[1]{0:T(128)} %bitcast.me_ref, s32[576]{0:T(1024)} %reshape.74.rand_ref, s32[1,2]{1,0:T(1,128)} %glob_ref.5, bf16[4160,384]{1,0:T(8,128)(2,1)} %get-tuple-element.86.k_ref.refs_4_, ...), custom_call_target="tpu_custom_call" | custom-call | flops 6000000000 | bytes 9000000 | tf_op jit(solution)/shard_map/attention_near/pallas_call | solution.py:294
  119.2 1.8 collective-permute-start.5
  121.8 4.5 %collective-permute-done.4.refs_3_ = bf16[192,1024]{1,0:T(8,128)(2,1)} collective-permute-done((bf16[192,1024]{1,0:T(8,128)(2,1)}, bf16[192,1024]{1,0:T(8,128)(2,1)}, u32[]{:S(2)}, u32[]{:S(2)}) %collective-permute-start.4) | collective-permute-done | bytes 393248 | tf_op jit(solution)/shard_map/ppermute | solution.py:903
  127.5 37.7 %rows_chain.1 = (bf16[1024,768]{1,0:T(8,128)(2,1)}, f32[1024,768]{1,0:T(8,128)}, bf16[4,1024,768]{2,1,0:T(8,128)(2,1)}, bf16[4,1024,768]{2,1,0:T(8,128)(2,1)}, b...) custom-call(s32[1]{0:T(128)} %bitcast.me_ref, ...), custom_call_target="tpu_custom_call" | custom-call | flops 22000001024 | bytes 40000000 | tf_op jit(solution)/shard_map/rows_chain/pallas_call | solution.py:774
  167.2 17.7 %outer_products.1 = (bf16[8,4,192,768]{3,2,1,0:T(8,128)(2,1)}, bf16[8,4,32,768]{3,2,1,0:T(8,128)(2,1)}) custom-call(s32[1]{0:T(128)} %bitcast.me_ref, bf16[192,1024]{1,0:T(8,128)(2,1)} %get-tuple-element.92.refs_0_, bf16[192,1024]{1,0:T(8,128)(2,1)} %collective-permute-done.5.refs_1_, bf16[192,1024]{1,0:T(8,128)(2,1)} %copy-done.2, ...), custom_call_target="tpu_custom_call" | custom-call | flops 11000000512 | bytes 28000000 | tf_op jit(solution)/shard_map/outer_products/pallas_call | solution.py:848
  186.0 5.1 %all-to-all-start.1 = ((bf16[32,32,768]{2,1,0:T(8,128)(2,1)}), bf16[32,32,768]{2,1,0:T(8,128)(2,1)S(1)}, u32[]{:S(2)}, u32[]{:S(2)}) async-start(bf16[32,32,768]{2,1,0:T(8,128)(2,1)} %bitcast.44), calls=%async_computation.1 | async-start | bytes 3145728 | tf_op jit(solution)/shard_map/all_to_all | solution.py:997
  191.1 63.6 %attention_backward.1 = (bf16[4,192,1024]{2,1,0:T(8,128)(2,1)}, bf16[4,1024,384]{2,1,0:T(8,128)(2,1)}, f32[1024,768]{1,0:T(8,128)}, bf16[1024,768]{1,0:T(8,128)(...) custom-call(s32[1]{0:T(128)} %bitcast.me_ref, s32[576]{0:T(1024)} %reshape.74.rand_ref, s32[1,2]{1,0:T(1,128)} %glob_ref.5, ...), custom_call_target="tpu_custom_call" | custom-call | flops 30000001024 | bytes 24000000 | tf_op jit(solution)/shard_map/attention_backward/pallas_call | solution.py:465
  254.8 10.1 %projection_gradients.1 = (bf16[32,32,640]{2,1,0:T(8,128)(2,1)}, f32[8,640]{1,0:T(8,128)}) custom-call(bf16[1024,768]{1,0:T(8,128)(2,1)} %bitcast.62, bf16[1024,768]{1,0:T(8,128)(2,1)} %collective-permute-done.refs_1_, bf16[1024,768]{1,0:T(8,128)(2,1)} %collective-permute-done.1.refs_2_, bf16[1024,768]{1,0:T(8,128)(2,1)} %collective-permute-done.2.refs_3_, ...), custom_call_target="tpu_custom_call" | custom-call | flops 4000000000 | bytes 12000000 | tf_op jit(solution)/shard_map/projection_gradients/pallas_call | solution.py:607
  264.9 3.5 %add_convert_fusion = bf16[1024,768]{1,0:T(8,128)(2,1)} fusion(bf16[1024,768]{1,0:T(8,128)(2,1)} %collective-permute-done.9, bf16[1024,768]{1,0:T(8,128)(2,1)} %get-tuple-element.123), kind=kLoop, calls=%fused_computation.1 | loop fusion | flops 3145728 | bytes 4718592 | tf_op jit(solution)/shard_map/convert_element_type | solution.py:1012
  268.5 5.6 %all-to-all-start.2 = ((bf16[32,32,640]{2,1,0:T(8,128)(2,1)}), bf16[32,32,640]{2,1,0:T(8,128)(2,1)S(1)}, u32[]{:S(2)}, u32[]{:S(2)}) async-start(bf16[32,32,640]{2,1,0:T(8,128)(2,1)} %get-tuple-element.127), calls=%async_computation.2 | async-start | bytes 2621440 | tf_op jit(solution)/shard_map/all_to_all | solution.py:1022
  274.1 1.8 collective-permute-start.10
  276.0 55.2 %collective-permute-done.10 = bf16[1024,768]{1,0:T(8,128)(2,1)} collective-permute-done((bf16[1024,768]{1,0:T(8,128)(2,1)}, bf16[1024,768]{1,0:T(8,128)(2,1)}, u32[]{:S(2)}, u32[]{:S(2)}) %collective-permute-start.10) | collective-permute-done | bytes 1572896 | tf_op jit(solution)/shard_map/ppermute | solution.py:903
  331.2 4.9 %convert_add_fusion = f32[1024,768]{1,0:T(8,128)} fusion(bf16[1024,768]{1,0:T(8,128)(2,1)} %collective-permute-done.11, f32[1024,768]{1,0:T(8,128)} %get-tuple-element.128, bf16[1024,768]{1,0:T(8,128)(2,1)} %collective-permute-done.10), kind=kLoop, calls=%fused_computation | loop fusion | flops 3145728 | bytes 9437184 | tf_op jit(solution)/shard_map/add | solution.py:1020
  337.2 2.2 unpacked_gradients.1
  341.6 2.4 finished.1
  344.0 1.3 slice_reduce_fusion.2
  (65 shorter events, 17.4 us)
Async XLA Ops:
  7.2 119.1 %all-gather.3.cloned.1.call-start = ((), (), s32[]{:S(2)}) async-start(), calls=%async_computation.5 | async-start | bytes 11354112 | tf_op jit(solution)/shard_map/all_gather | solution.py:940
  12.2 60.9 %collective-permute-start.1 = (bf16[1024,768]{1,0:T(8,128)(2,1)}, bf16[1024,768]{1,0:T(8,128)(2,1)}, u32[]{:S(2)}, u32[]{:S(2)}) collective-permute-start(bf16[1024,768]{1,0:T(8,128)(2,1)} %bitcast.58), channel_id=1, source_target_pairs={{0,8},{4,12},{8,0},{12,4},{1,9},{5,13},{9,1},{13,5},{2,10},{6,14},... | collective-permute-start | bytes 4718600 | tf_op jit(solution)/shard_map/ppermute | solution.py:903
  19.4 58.0 %all-to-all-start = ((bf16[32,32,640]{2,1,0:T(8,128)(2,1)}), bf16[32,32,640]{2,1,0:T(8,128)(2,1)S(1)}, u32[]{:S(2)}, u32[]{:S(2)}) async-start(bf16[32,32,640]{2,1,0:T(8,128)(2,1)} %bitcast.45), calls=%async_computation | async-start | bytes 2621440 | tf_op jit(solution)/shard_map/all_to_all | solution.py:937
  24.3 317.3 %reduce-scatter.2.cloned.1.call-start = ((), (), s32[]{:S(2)}) async-start(), calls=%async_computation.4 | async-start | bytes 9732096 | tf_op jit(solution)/shard_map/reduce_scatter | solution.py:995
  24.3 55.6 %collective-permute-start = (bf16[1024,768]{1,0:T(8,128)(2,1)}, bf16[1024,768]{1,0:T(8,128)(2,1)}, u32[]{:S(2)}, u32[]{:S(2)}) collective-permute-start(bf16[1024,768]{1,0:T(8,128)(2,1)} %bitcast.59), channel_id=1, source_target_pairs={{0,4},{4,0},{8,12},{12,8},{1,5},{5,1},{9,13},{13,9},{2,6},{6,2},{1... | collective-permute-start | bytes 4718600 | tf_op jit(solution)/shard_map/ppermute | solution.py:903
  73.1 6.9 %collective-permute-start.2 = (bf16[1024,768]{1,0:T(8,128)(2,1)}, bf16[1024,768]{1,0:T(8,128)(2,1)}, u32[]{:S(2)}, u32[]{:S(2)}) collective-permute-start(bf16[1024,768]{1,0:T(8,128)(2,1)} %collective-permute-done.1.refs_2_), channel_id=1, source_target_pairs={{0,4},{4,0},{8,12},{12,8},{1,5},{5,1},{9,13},{13,9},{2,6},{6,2},{1... | collective-permute-start | bytes 4718600 | tf_op jit(solution)/shard_map/ppermute | solution.py:903
  106.8 15.0 %collective-permute-start.3 = (bf16[192,1024]{1,0:T(8,128)(2,1)}, bf16[192,1024]{1,0:T(8,128)(2,1)S(1)}, u32[]{:S(2)}, u32[]{:S(2)}) collective-permute-start(bf16[192,1024]{1,0:T(8,128)(2,1)} %get-tuple-element.84), channel_id=1, source_target_pairs={{0,8},{4,12},{8,0},{12,4},{1,9},{5,13},{9,1},{13,5},{2,10},{6,14},... | collective-permute-start | bytes 1179656 | tf_op jit(solution)/shard_map/ppermute | solution.py:903
  107.4 18.9 %collective-permute-start.4 = (bf16[192,1024]{1,0:T(8,128)(2,1)}, bf16[192,1024]{1,0:T(8,128)(2,1)}, u32[]{:S(2)}, u32[]{:S(2)}) collective-permute-start(bf16[192,1024]{1,0:T(8,128)(2,1)} %get-tuple-element.85), channel_id=1, source_target_pairs={{0,12},{4,8},{8,4},{12,0},{1,13},{5,9},{9,5},{13,1},{2,14},{6,10},... | collective-permute-start | bytes 1179656 | tf_op jit(solution)/shard_map/ppermute | solution.py:903
  119.2 7.1 %collective-permute-start.5 = (bf16[192,1024]{1,0:T(8,128)(2,1)}, bf16[192,1024]{1,0:T(8,128)(2,1)}, u32[]{:S(2)}, u32[]{:S(2)}) collective-permute-start(bf16[192,1024]{1,0:T(8,128)(2,1)} %get-tuple-element.93), channel_id=1, source_target_pairs={{0,4},{4,0},{8,12},{12,8},{1,5},{5,1},{9,13},{13,9},{2,6},{6,2},{1... | collective-permute-start | bytes 1179656 | tf_op jit(solution)/shard_map/ppermute | solution.py:903
  121.8 5.7 %copy-start.2 = (bf16[192,1024]{1,0:T(8,128)(2,1)}, bf16[192,1024]{1,0:T(8,128)(2,1)S(1)}, u32[]{:S(2)}) copy-start(bf16[192,1024]{1,0:T(8,128)(2,1)S(1)} %collective-permute-done.3.refs_2_) | copy-start | bytes 1179652
  165.2 19.8 %collective-permute-start.6 = (bf16[192,1024]{1,0:T(8,128)(2,1)}, bf16[192,1024]{1,0:T(8,128)(2,1)S(1)}, u32[]{:S(2)}, u32[]{:S(2)}) collective-permute-start(bf16[192,1024]{1,0:T(8,128)(2,1)} %get-tuple-element.108), channel_id=1, source_target_pairs={{0,4},{4,0},{8,12},{12,8},{1,5},{5,1},{9,13},{13,9},{2,6},{6,2},{1... | collective-permute-start | bytes 1179656 | tf_op jit(solution)/shard_map/ppermute | solution.py:903
  165.8 19.2 %collective-permute-start.7 = (bf16[192,1024]{1,0:T(8,128)(2,1)}, bf16[192,1024]{1,0:T(8,128)(2,1)S(1)}, u32[]{:S(2)}, u32[]{:S(2)}) collective-permute-start(bf16[192,1024]{1,0:T(8,128)(2,1)} %get-tuple-element.109), channel_id=1, source_target_pairs={{0,8},{4,12},{8,0},{12,4},{1,9},{5,13},{9,1},{13,5},{2,10},{6,14},... | collective-permute-start | bytes 1179656 | tf_op jit(solution)/shard_map/ppermute | solution.py:903
  166.2 18.8 %collective-permute-start.8 = (bf16[192,1024]{1,0:T(8,128)(2,1)}, bf16[192,1024]{1,0:T(8,128)(2,1)S(1)}, u32[]{:S(2)}, u32[]{:S(2)}) collective-permute-start(bf16[192,1024]{1,0:T(8,128)(2,1)} %get-tuple-element.110), channel_id=1, source_target_pairs={{0,12},{4,8},{8,4},{12,0},{1,13},{5,9},{9,5},{13,1},{2,14},{6,10},... | collective-permute-start | bytes 1179656 | tf_op jit(solution)/shard_map/ppermute | solution.py:903
  185.0 0.8 copy-start.3
  185.0 0.9 copy-start.4
  185.0 1.0 copy-start.5
  186.0 82.5 %all-to-all-start.1 = ((bf16[32,32,768]{2,1,0:T(8,128)(2,1)}), bf16[32,32,768]{2,1,0:T(8,128)(2,1)S(1)}, u32[]{:S(2)}, u32[]{:S(2)}) async-start(bf16[32,32,768]{2,1,0:T(8,128)(2,1)} %bitcast.44), calls=%async_computation.1 | async-start | bytes 3145728 | tf_op jit(solution)/shard_map/all_to_all | solution.py:997
  254.8 10.2 %collective-permute-start.9 = (bf16[1024,768]{1,0:T(8,128)(2,1)}, bf16[1024,768]{1,0:T(8,128)(2,1)}, u32[]{:S(2)}, u32[]{:S(2)}) collective-permute-start(bf16[1024,768]{1,0:T(8,128)(2,1)} %get-tuple-element.124), channel_id=1, source_target_pairs={{0,4},{4,0},{8,12},{12,8},{1,5},{5,1},{9,13},{13,9},{2,6},{6,2},{1... | collective-permute-start | bytes 4718600 | tf_op jit(solution)/shard_map/ppermute | solution.py:903
  268.5 67.6 %copy-start = (bf16[32,32,768]{2,1,0:T(8,128)(2,1)}, bf16[32,32,768]{2,1,0:T(8,128)(2,1)S(1)}, u32[]{:S(2)}) copy-start(bf16[32,32,768]{2,1,0:T(8,128)(2,1)S(1)} %all-to-all-done.1.apart_ref) | copy-start | bytes 4718596
  268.5 67.6 %all-to-all-start.2 = ((bf16[32,32,640]{2,1,0:T(8,128)(2,1)}), bf16[32,32,640]{2,1,0:T(8,128)(2,1)S(1)}, u32[]{:S(2)}, u32[]{:S(2)}) async-start(bf16[32,32,640]{2,1,0:T(8,128)(2,1)} %get-tuple-element.127), calls=%async_computation.2 | async-start | bytes 2621440 | tf_op jit(solution)/shard_map/all_to_all | solution.py:1022
  274.1 57.0 %collective-permute-start.10 = (bf16[1024,768]{1,0:T(8,128)(2,1)}, bf16[1024,768]{1,0:T(8,128)(2,1)}, u32[]{:S(2)}, u32[]{:S(2)}) collective-permute-start(bf16[1024,768]{1,0:T(8,128)(2,1)} %add_convert_fusion), channel_id=1, source_target_pairs={{0,8},{4,12},{8,0},{12,4},{1,9},{5,13},{9,1},{13,5},{2,10},{6,14},... | collective-permute-start | bytes 4718600 | tf_op jit(solution)/shard_map/ppermute | solution.py:903
  276.0 55.2 %collective-permute-start.11 = (bf16[1024,768]{1,0:T(8,128)(2,1)}, bf16[1024,768]{1,0:T(8,128)(2,1)}, u32[]{:S(2)}, u32[]{:S(2)}) collective-permute-start(bf16[1024,768]{1,0:T(8,128)(2,1)} %get-tuple-element.130), channel_id=1, source_target_pairs={{0,4},{4,0},{8,12},{12,8},{1,5},{5,1},{9,13},{13,9},{2,6},{6,2},{1... | collective-permute-start | bytes 4718600 | tf_op jit(solution)/shard_map/ppermute | solution.py:903
  336.1 1.1 copy-start.1
Sparse Core Ops, SparseCore 0:
  12.4 113.2 all-gather.2
  185.1 149.7 reduce-scatter.1

commit v6 on v5

--- a/solution.py
+++ b/solution.py
@@ -57,7 +57,7 @@
 
 UNROLL = 4
 BACK_UNROLL = 2
-APART = 32
+APART = 48
 VMEM_BYTES = 62 << 20
 
 
@@ -563,38 +563,38 @@
 
 def weights_kernel(chunks, direct, *refs):
     x_refs = refs[:chunks]
-    dq_ref, dkv_ref, out_ref, sums_ref, acc = refs[chunks:]
-    group, rows = dq_ref.shape[1], dq_ref.shape[2]
+    dq_ref, dkv_ref, out_ref, sums_ref, acc, sum_sc = refs[chunks:]
+    group = dq_ref.shape[1]
     lanes = dkv_ref.shape[2]
-    ones = jnp.ones((8, rows), bf16)
-    sum_q = jnp.zeros((8, group), f32)
-    sum_kv = jnp.zeros((8, lanes), f32)
-    acc[lanes + group :, :] = jnp.zeros((acc.shape[0] - lanes - group, acc.shape[1]), f32)
-    for c in range(chunks):
-        x = x_refs[c][...]
-        got_kv = dot_tn(dkv_ref[c], x)
-        got_q = dot_nn(dq_ref[c], x)
-        if c == 0:
-            acc[0:lanes, :] = got_kv
-            acc[lanes : lanes + group, :] = got_q
+    full = acc.shape[0]
+    x = jnp.concatenate([r[...] for r in x_refs], axis=0)
+    dkv = jnp.concatenate([dkv_ref[c] for c in range(chunks)], axis=0)
+    dq = jnp.concatenate([dq_ref[c] for c in range(chunks)], axis=1)
+    ones = jnp.ones((8, x.shape[0]), bf16)
+
+    @pl.when(pl.program_id(0) == 0)
+    def _():
+        acc[...] = jnp.zeros_like(acc)
+        sum_sc[...] = jnp.zeros_like(sum_sc)
+
+    acc[0:lanes, :] += dot_tn(dkv, x)
+    acc[lanes : lanes + group, :] += dot_nn(dq, x)
+    sum_sc[:, 0:lanes] += dot_nn(ones, dkv)
+    sum_sc[:, lanes : lanes + group] += dot_nt(ones, dq)
+
+    @pl.when(pl.program_id(0) == pl.num_programs(0) - 1)
+    def _():
+        grad = jnp.transpose(acc[...], (1, 0))
+        sums_ref[...] = sum_sc[...]
+        if direct:
+            blocks, per, _ = out_ref.shape
+            own = per - 8
+            grad = grad.reshape(blocks, own, full)
+            for b in range(blocks):
+                out_ref[b, 0:own, :] = grad[b].astype(bf16)
+                out_ref[b, own:, :] = sum_sc[...].astype(bf16)
         else:
-            acc[0:lanes, :] += got_kv
-            acc[lanes : lanes + group, :] += got_q
-        sum_q = sum_q + dot_nt(ones, dq_ref[c])
-        sum_kv = sum_kv + dot_nn(ones, dkv_ref[c])
-    grad = jnp.transpose(acc[...], (1, 0))
-    blank = jnp.zeros((8, acc.shape[0] - lanes - group), f32)
-    sums = jnp.concatenate([sum_kv, sum_q, blank], axis=1)
-    sums_ref[...] = sums
-    if direct:
-        blocks, per, _ = out_ref.shape
-        own = per - 8
-        grad = grad.astype(f32).reshape(blocks, own, acc.shape[0])
-        for b in range(blocks):
-            out_ref[b, 0:own, :] = grad[b].astype(bf16)
-            out_ref[b, own:, :] = sums.astype(bf16)
-    else:
-        out_ref[...] = grad.astype(bf16)
+            out_ref[...] = grad.astype(bf16)
 
 
 def projection_gradients(x, dq, dkv, own, devices):
@@ -603,16 +603,22 @@
     lanes = dkv.shape[2]
     full = lanes + round_up(group, PAIR)
     direct = own % 8 == 0
-    whole = lambda: pl.BlockSpec(memory_space=pltpu.VMEM)
+    tile = 256
+    shape = (devices, own + 8, full) if direct else (width, full)
     out, sums = pl.pallas_call(
         functools.partial(weights_kernel, chunks, direct),
-        out_shape=(
-            jax.ShapeDtypeStruct((devices, own + 8, full) if direct else (width, full), bf16),
-            jax.ShapeDtypeStruct((8, full), f32),
+        grid=(rows // tile,),
+        out_shape=(jax.ShapeDtypeStruct(shape, bf16), jax.ShapeDtypeStruct((8, full), f32)),
+        in_specs=[pl.BlockSpec((tile, width), lambda i: (i, 0)) for _ in range(chunks)]
+        + [
+            pl.BlockSpec((chunks, group, tile), lambda i: (0, 0, i)),
+            pl.BlockSpec((chunks, tile, lanes), lambda i: (0, i, 0)),
+        ],
+        out_specs=(
+            pl.BlockSpec(shape, lambda i: (0,) * len(shape), pipeline_mode=pl.Buffered(1)),
+            pl.BlockSpec((8, full), lambda i: (0, 0)),
         ),
-        in_specs=[whole() for _ in range(chunks + 2)],
-        out_specs=(whole(), whole()),
-        scratch_shapes=[pltpu.VMEM((full, width), f32)],
+        scratch_shapes=[pltpu.VMEM((full, width), f32), pltpu.VMEM((8, full), f32)],
         compiler_params=pltpu.CompilerParams(vmem_limit_bytes=VMEM_BYTES),
         cost_estimate=pl.CostEstimate(flops=4_000_000_000, bytes_accessed=12_000_000, transcendentals=0),
         name="projection_gradients",
@@ -992,7 +998,7 @@
         payload = jnp.concatenate([payload.reshape(outer, ffn_n, at, width), grad_out, small], axis=2)
         payload = jnp.pad(payload, ((0, 0), (0, 0), (0, -payload.shape[2] % 32), (0, 0)))
     payload, apart, do = lax.optimization_barrier((payload, apart, do))
-    total = lax.psum_scatter(payload.reshape(-1, width), ALL, scatter_dimension=0, tiled=True)
+    total = lax.psum_scatter(payload.reshape(-1, width), ("dp", "seq"), scatter_dimension=0, tiled=True)
     if direct:
         apart = lax.all_to_all(
             apart.reshape(devices, APART, width), ALL, split_axis=0, concat_axis=0, tiled=True
@@ -1016,11 +1022,12 @@
     grad_w, apart = lax.optimization_barrier((grad_w, apart))
     part = [None] + part
     bit = seq_n // 2
+    part[bit], total = lax.optimization_barrier((part[bit], total))
+    total = lax.psum_scatter(total, "ffn", scatter_dimension=0, tiled=True)
     while bit:
         grad_features = grad_features + flip_send(part[bit], "seq", bit).astype(f32)
         bit //= 2
     grad_w = lax.all_to_all(grad_w, ALL, split_axis=0, concat_axis=0, tiled=True)
-    grad_w, grad_features = lax.optimization_barrier((grad_w, grad_features))
     if direct:
         out_up, out_down, out_output, notes = finished(apart, total, up_rows, own)
     else:

time: 354 us -> 347 us (0.980)
  waiting for transfers between devices: 113 us -> 103 us
    ppermute x12, waiting for transfers between devices: 108 us -> 52.9 us  [flip_send(): return lax.ppermute(array, axis, [(i, i ^ bits) for i in range(count)])]
    all_to_all x1, waiting for transfers between devices: 0.01 us -> 45.1 us  [shards(): lax.all_to_all(grad_w, ALL, split_axis=0, concat_axis=0, tiled=True)]
    add x1 -> x0, other arithmetic: 4.92 us -> none  [shards(): grad_features = grad_features + flip_send(part[bit], 'seq', bit).astype(f32)]
    broadcast_in_dim x0 -> x1, other arithmetic: none -> 4.9 us  [shards(): grad_features[None]]
  transfers between devices with their start and end apart: 17 -> 18, of which waited for: 4 -> 4; matrix products, arithmetic and copies ran while one was open for 5% -> 5% of each run, Pallas kernels for 37% -> 39%
where the time goes in v6:
time: 347 us; the launch traced here: 345 us
  Pallas kernels  176 us (51%)
  waiting for transfers between devices  103 us (30%)
  starting transfers between devices  25.7 us (7%)
  local copies, waits for them, and re-layouts  16.8 us (5%)
  between operations  13.9 us (4%)
  other arithmetic  9.34 us (3%)
    pallas_call x1, Pallas kernels, attention_backward(): pl.pallas_call(functools.partial(backward_kernel, heads, chunks), out_sha...  65.2 us
    ppermute x12, waiting for transfers between devices, flip_send(): return lax.ppermute(array, axis, [(i, i ^ bits) for i in range(count)])  52.9 us
    all_to_all x1, waiting for transfers between devices, shards(): lax.all_to_all(grad_w, ALL, split_axis=0, concat_axis=0, tiled=True)  45.1 us
    pallas_call x1, Pallas kernels, rows_chain(): pl.pallas_call(functools.partial(rows_kernel, parts, blocks, up_rows, own...  37.7 us
    pallas_call x1, Pallas kernels, attention_forward(): pl.pallas_call(functools.partial(forward_kernel, heads, chunks), out_shap...  26.8 us
    pallas_call x1, Pallas kernels, outer_products(): pl.pallas_call(functools.partial(outer_kernel, parts, up_rows, own, apart...  17.6 us
    pallas_call x1, Pallas kernels, attention_near(): pl.pallas_call(functools.partial(near_kernel, heads, chunks), out_shape=(...  11.8 us
    ppermute x12, starting transfers between devices, flip_send(): return lax.ppermute(array, axis, [(i, i ^ bits) for i in range(count)])  9.77 us
  transfers between devices with their start and end apart: 18, of which 4 were waited for; matrix products, arithmetic and copies ran while one was open for 5% of the time, Pallas kernels for 39%

profile of v6, /device:TPU:0, one launch (start us, length us, event | category | flops | bytes accessed | tf_op | source)
XLA Modules:
  0.0 344.7 jit_solution(17351917230996018606)
XLA Ops:
  7.2 1.3 broadcast_in_dim.20.bup_ref
  9.9 2.3 packed_weights.1
  12.2 3.0 collective-permute-start.1
  17.3 1.4 reduce.17
  19.4 4.9 %all-to-all-start = ((bf16[32,32,640]{2,1,0:T(8,128)(2,1)}), bf16[32,32,640]{2,1,0:T(8,128)(2,1)S(1)}, u32[]{:S(2)}, u32[]{:S(2)}) async-start(bf16[32,32,640]{2,1,0:T(8,128)(2,1)} %bitcast.44), calls=%async_computation | async-start | bytes 2621440 | tf_op jit(solution)/shard_map/all_to_all | solution.py:943
  24.7 48.4 %collective-permute-done.1.refs_2_ = bf16[1024,768]{1,0:T(8,128)(2,1)} collective-permute-done((bf16[1024,768]{1,0:T(8,128)(2,1)}, bf16[1024,768]{1,0:T(8,128)(2,1)}, u32[]{:S(2)}, u32[]{:S(2)}) %collective-permute-start.1) | collective-permute-done | bytes 1572896 | tf_op jit(solution)/shard_map/ppermute | solution.py:909
  73.1 4.3 %all-to-all-done = bf16[32,32,640]{2,1,0:T(8,128)(2,1)S(1)} async-done(((bf16[32,32,640]{2,1,0:T(8,128)(2,1)}), bf16[32,32,640]{2,1,0:T(8,128)(2,1)S(1)}, u32[]{:S(2)}, u32[]{:S(2)}) %all-to-all-start) | async-done | bytes 1310752 | tf_op jit(solution)/shard_map/all_to_all | solution.py:943
  80.0 26.8 %attention_forward.1 = (bf16[192,1024]{1,0:T(8,128)(2,1)}, bf16[192,1024]{1,0:T(8,128)(2,1)}, f32[3,16,128]{2,1,0:T(8,128)}, f32[3,128]{1,0:T(4,128)}, f32[3,64,...) custom-call(s32[1]{0:T(128)} %bitcast.me_ref, ...), custom_call_target="tpu_custom_call" | custom-call | flops 10000000000 | bytes 16000000 | tf_op jit(solution)/shard_map/attention_forward/pallas_call | solution.py:248
  107.4 11.8 %attention_near.1 = (bf16[192,1024]{1,0:T(8,128)(2,1)}, bf16[192,1024]{1,0:T(8,128)(2,1)}, f32[3,16,128]{2,1,0:T(8,128)}) custom-call(s32[1]{0:T(128)} %bitcast.me_ref, s32[576]{0:T(1024)} %reshape.74.rand_ref, s32[1,2]{1,0:T(1,128)} %glob_ref.5, bf16[4160,384]{1,0:T(8,128)(2,1)} %get-tuple-element.86.k_ref.refs_4_, ...), custom_call_target="tpu_custom_call" | custom-call | flops 6000000000 | bytes 9000000 | tf_op jit(solution)/shard_map/attention_near/pallas_call | solution.py:294
  119.3 1.8 collective-permute-start.5
  121.9 4.4 %collective-permute-done.4.refs_3_ = bf16[192,1024]{1,0:T(8,128)(2,1)} collective-permute-done((bf16[192,1024]{1,0:T(8,128)(2,1)}, bf16[192,1024]{1,0:T(8,128)(2,1)}, u32[]{:S(2)}, u32[]{:S(2)}) %collective-permute-start.4) | collective-permute-done | bytes 393248 | tf_op jit(solution)/shard_map/ppermute | solution.py:909
  127.5 37.7 %rows_chain.1 = (bf16[1024,768]{1,0:T(8,128)(2,1)}, f32[1024,768]{1,0:T(8,128)}, bf16[4,1024,768]{2,1,0:T(8,128)(2,1)}, bf16[4,1024,768]{2,1,0:T(8,128)(2,1)}, b...) custom-call(s32[1]{0:T(128)} %bitcast.me_ref, ...), custom_call_target="tpu_custom_call" | custom-call | flops 22000001024 | bytes 40000000 | tf_op jit(solution)/shard_map/rows_chain/pallas_call | solution.py:780
  167.2 17.6 %outer_products.1 = (bf16[8,4,176,768]{3,2,1,0:T(8,128)(2,1)}, bf16[8,4,48,768]{3,2,1,0:T(8,128)(2,1)}) custom-call(s32[1]{0:T(128)} %bitcast.me_ref, bf16[192,1024]{1,0:T(8,128)(2,1)} %get-tuple-element.92.refs_0_, bf16[192,1024]{1,0:T(8,128)(2,1)} %collective-permute-done.5.refs_1_, bf16[192,1024]{1,0:T(8,128)(2,1)} %copy-done.2, ...), custom_call_target="tpu_custom_call" | custom-call | flops 11000000512 | bytes 28000000 | tf_op jit(solution)/shard_map/outer_products/pallas_call | solution.py:854
  185.8 5.3 %all-to-all-start.1 = ((bf16[32,48,768]{2,1,0:T(8,128)(2,1)}), bf16[32,48,768]{2,1,0:T(8,128)(2,1)}, u32[]{:S(2)}, u32[]{:S(2)}) async-start(bf16[32,48,768]{2,1,0:T(8,128)(2,1)} %bitcast.19), calls=%async_computation.2 | async-start | bytes 4718592 | tf_op jit(solution)/shard_map/all_to_all | solution.py:1003
  191.1 65.2 %attention_backward.1 = (bf16[4,192,1024]{2,1,0:T(8,128)(2,1)}, bf16[4,1024,384]{2,1,0:T(8,128)(2,1)}, f32[1024,768]{1,0:T(8,128)}, bf16[1024,768]{1,0:T(8,128)(...) custom-call(s32[1]{0:T(128)} %bitcast.me_ref, s32[576]{0:T(1024)} %reshape.74.rand_ref, s32[1,2]{1,0:T(1,128)} %glob_ref.5, ...), custom_call_target="tpu_custom_call" | custom-call | flops 30000001024 | bytes 24000000 | tf_op jit(solution)/shard_map/attention_backward/pallas_call | solution.py:465
  256.3 9.7 %projection_gradients.1 = (bf16[32,32,640]{2,1,0:T(8,128)(2,1)}, f32[8,640]{1,0:T(8,128)}) custom-call(bf16[1024,768]{1,0:T(8,128)(2,1)} %bitcast.61, bf16[1024,768]{1,0:T(8,128)(2,1)} %collective-permute-done.refs_1_, bf16[1024,768]{1,0:T(8,128)(2,1)} %collective-permute-done.1.refs_2_, bf16[1024,768]{1,0:T(8,128)(2,1)} %collective-permute-done.2.refs_3_, ...), custom_call_target="tpu_custom_call" | custom-call | flops 4000000000 | bytes 12000000 | tf_op jit(solution)/shard_map/projection_gradients/pallas_call | solution.py:608
  266.0 2.9 add_convert_fusion
  268.9 5.6 %all-to-all-start.2 = ((bf16[32,32,640]{2,1,0:T(8,128)(2,1)}), bf16[32,32,640]{2,1,0:T(8,128)(2,1)S(1)}, u32[]{:S(2)}, u32[]{:S(2)}) async-start(bf16[32,32,640]{2,1,0:T(8,128)(2,1)} %get-tuple-element.132), calls=%async_computation.3 | async-start | bytes 2621440 | tf_op jit(solution)/shard_map/all_to_all | solution.py:1030
  275.6 1.7 collective-permute-start.10
  277.3 45.1 %all-to-all-done.2 = bf16[32,32,640]{2,1,0:T(8,128)(2,1)S(1)} async-done(((bf16[32,32,640]{2,1,0:T(8,128)(2,1)}), bf16[32,32,640]{2,1,0:T(8,128)(2,1)S(1)}, u32[]{:S(2)}, u32[]{:S(2)}) %all-to-all-start.2) | async-done | bytes 1310752 | tf_op jit(solution)/shard_map/all_to_all | solution.py:1030
  323.5 2.2 unpacked_gradients.1
  327.9 4.9 %add_bitcast_fusion = f32[1,1024,768]{2,1,0:T(8,128)} fusion(bf16[1024,768]{1,0:T(8,128)(2,1)} %collective-permute-done.11, f32[1024,768]{1,0:T(8,128)} %get-tuple-element.119, bf16[1024,768]{1,0:T(8,128)(2,1)} %collective-permute-done.10), kind=kLoop, calls=%fused_computation | loop fusion | flops 3145728 | bytes 9437184 | tf_op jit(solution)/shard_map/broadcast_in_dim | solution.py:1047
  332.8 2.7 finished.1
  335.6 1.3 slice_reduce_fusion.2
  (68 shorter events, 18.4 us)
Async XLA Ops:
  7.2 119.1 %all-gather.3.cloned.1.call-start = ((), (), s32[]{:S(2)}) async-start(), calls=%async_computation.7 | async-start | bytes 11354112 | tf_op jit(solution)/shard_map/all_gather | solution.py:946
  12.2 60.9 %collective-permute-start.1 = (bf16[1024,768]{1,0:T(8,128)(2,1)}, bf16[1024,768]{1,0:T(8,128)(2,1)}, u32[]{:S(2)}, u32[]{:S(2)}) collective-permute-start(bf16[1024,768]{1,0:T(8,128)(2,1)} %bitcast.57), channel_id=1, source_target_pairs={{0,8},{4,12},{8,0},{12,4},{1,9},{5,13},{9,1},{13,5},{2,10},{6,14},... | collective-permute-start | bytes 4718600 | tf_op jit(solution)/shard_map/ppermute | solution.py:909
  19.4 58.0 %all-to-all-start = ((bf16[32,32,640]{2,1,0:T(8,128)(2,1)}), bf16[32,32,640]{2,1,0:T(8,128)(2,1)S(1)}, u32[]{:S(2)}, u32[]{:S(2)}) async-start(bf16[32,32,640]{2,1,0:T(8,128)(2,1)} %bitcast.44), calls=%async_computation | async-start | bytes 2621440 | tf_op jit(solution)/shard_map/all_to_all | solution.py:943
  24.3 250.3 %reduce-scatter.3.cloned.1.call-start = ((), (), s32[]{:S(2)}) async-start(), calls=%async_computation.5 | async-start | bytes 9732096 | tf_op jit(solution)/shard_map/reduce_scatter | solution.py:1001
  24.3 55.7 %collective-permute-start = (bf16[1024,768]{1,0:T(8,128)(2,1)}, bf16[1024,768]{1,0:T(8,128)(2,1)}, u32[]{:S(2)}, u32[]{:S(2)}) collective-permute-start(bf16[1024,768]{1,0:T(8,128)(2,1)} %bitcast.58), channel_id=1, source_target_pairs={{0,4},{4,0},{8,12},{12,8},{1,5},{5,1},{9,13},{13,9},{2,6},{6,2},{1... | collective-permute-start | bytes 4718600 | tf_op jit(solution)/shard_map/ppermute | solution.py:909
  73.1 6.9 %collective-permute-start.2 = (bf16[1024,768]{1,0:T(8,128)(2,1)}, bf16[1024,768]{1,0:T(8,128)(2,1)}, u32[]{:S(2)}, u32[]{:S(2)}) collective-permute-start(bf16[1024,768]{1,0:T(8,128)(2,1)} %collective-permute-done.1.refs_2_), channel_id=1, source_target_pairs={{0,4},{4,0},{8,12},{12,8},{1,5},{5,1},{9,13},{13,9},{2,6},{6,2},{1... | collective-permute-start | bytes 4718600 | tf_op jit(solution)/shard_map/ppermute | solution.py:909
  106.8 15.1 %collective-permute-start.3 = (bf16[192,1024]{1,0:T(8,128)(2,1)}, bf16[192,1024]{1,0:T(8,128)(2,1)S(1)}, u32[]{:S(2)}, u32[]{:S(2)}) collective-permute-start(bf16[192,1024]{1,0:T(8,128)(2,1)} %get-tuple-element.84), channel_id=1, source_target_pairs={{0,8},{4,12},{8,0},{12,4},{1,9},{5,13},{9,1},{13,5},{2,10},{6,14},... | collective-permute-start | bytes 1179656 | tf_op jit(solution)/shard_map/ppermute | solution.py:909
  107.4 18.9 %collective-permute-start.4 = (bf16[192,1024]{1,0:T(8,128)(2,1)}, bf16[192,1024]{1,0:T(8,128)(2,1)}, u32[]{:S(2)}, u32[]{:S(2)}) collective-permute-start(bf16[192,1024]{1,0:T(8,128)(2,1)} %get-tuple-element.85), channel_id=1, source_target_pairs={{0,12},{4,8},{8,4},{12,0},{1,13},{5,9},{9,5},{13,1},{2,14},{6,10},... | collective-permute-start | bytes 1179656 | tf_op jit(solution)/shard_map/ppermute | solution.py:909
  119.3 7.0 %collective-permute-start.5 = (bf16[192,1024]{1,0:T(8,128)(2,1)}, bf16[192,1024]{1,0:T(8,128)(2,1)}, u32[]{:S(2)}, u32[]{:S(2)}) collective-permute-start(bf16[192,1024]{1,0:T(8,128)(2,1)} %get-tuple-element.93), channel_id=1, source_target_pairs={{0,4},{4,0},{8,12},{12,8},{1,5},{5,1},{9,13},{13,9},{2,6},{6,2},{1... | collective-permute-start | bytes 1179656 | tf_op jit(solution)/shard_map/ppermute | solution.py:909
  121.9 5.6 %copy-start.2 = (bf16[192,1024]{1,0:T(8,128)(2,1)}, bf16[192,1024]{1,0:T(8,128)(2,1)S(1)}, u32[]{:S(2)}) copy-start(bf16[192,1024]{1,0:T(8,128)(2,1)S(1)} %collective-permute-done.3.refs_2_) | copy-start | bytes 1179652
  165.2 19.6 %collective-permute-start.6 = (bf16[192,1024]{1,0:T(8,128)(2,1)}, bf16[192,1024]{1,0:T(8,128)(2,1)S(1)}, u32[]{:S(2)}, u32[]{:S(2)}) collective-permute-start(bf16[192,1024]{1,0:T(8,128)(2,1)} %get-tuple-element.108), channel_id=1, source_target_pairs={{0,4},{4,0},{8,12},{12,8},{1,5},{5,1},{9,13},{13,9},{2,6},{6,2},{1... | collective-permute-start | bytes 1179656 | tf_op jit(solution)/shard_map/ppermute | solution.py:909
  165.7 19.1 %collective-permute-start.7 = (bf16[192,1024]{1,0:T(8,128)(2,1)}, bf16[192,1024]{1,0:T(8,128)(2,1)S(1)}, u32[]{:S(2)}, u32[]{:S(2)}) collective-permute-start(bf16[192,1024]{1,0:T(8,128)(2,1)} %get-tuple-element.109), channel_id=1, source_target_pairs={{0,8},{4,12},{8,0},{12,4},{1,9},{5,13},{9,1},{13,5},{2,10},{6,14},... | collective-permute-start | bytes 1179656 | tf_op jit(solution)/shard_map/ppermute | solution.py:909
  166.2 18.6 %collective-permute-start.8 = (bf16[192,1024]{1,0:T(8,128)(2,1)}, bf16[192,1024]{1,0:T(8,128)(2,1)S(1)}, u32[]{:S(2)}, u32[]{:S(2)}) collective-permute-start(bf16[192,1024]{1,0:T(8,128)(2,1)} %get-tuple-element.110), channel_id=1, source_target_pairs={{0,12},{4,8},{8,4},{12,0},{1,13},{5,9},{9,5},{13,1},{2,14},{6,10},... | collective-permute-start | bytes 1179656 | tf_op jit(solution)/shard_map/ppermute | solution.py:909
  184.8 0.8 copy-start.3
  184.8 0.9 copy-start.4
  184.8 1.0 copy-start.5
  185.8 83.1 %all-to-all-start.1 = ((bf16[32,48,768]{2,1,0:T(8,128)(2,1)}), bf16[32,48,768]{2,1,0:T(8,128)(2,1)}, u32[]{:S(2)}, u32[]{:S(2)}) async-start(bf16[32,48,768]{2,1,0:T(8,128)(2,1)} %bitcast.19), calls=%async_computation.2 | async-start | bytes 4718592 | tf_op jit(solution)/shard_map/all_to_all | solution.py:1003
  256.3 9.7 %collective-permute-start.9 = (bf16[1024,768]{1,0:T(8,128)(2,1)}, bf16[1024,768]{1,0:T(8,128)(2,1)}, u32[]{:S(2)}, u32[]{:S(2)}) collective-permute-start(bf16[1024,768]{1,0:T(8,128)(2,1)} %get-tuple-element.125), channel_id=1, source_target_pairs={{0,4},{4,0},{8,12},{12,8},{1,5},{5,1},{9,13},{13,9},{2,6},{6,2},{1... | collective-permute-start | bytes 4718600 | tf_op jit(solution)/shard_map/ppermute | solution.py:909
  256.3 9.7 %copy-start.1 = (bf16[1024,768]{1,0:T(8,128)(2,1)S(1)}, bf16[1024,768]{1,0:T(8,128)(2,1)}, u32[]{:S(2)}) copy-start(bf16[1024,768]{1,0:T(8,128)(2,1)} %get-tuple-element.124) | copy-start | bytes 4718596
  268.9 53.5 %all-to-all-start.2 = ((bf16[32,32,640]{2,1,0:T(8,128)(2,1)}), bf16[32,32,640]{2,1,0:T(8,128)(2,1)S(1)}, u32[]{:S(2)}, u32[]{:S(2)}) async-start(bf16[32,32,640]{2,1,0:T(8,128)(2,1)} %get-tuple-element.132), calls=%async_computation.3 | async-start | bytes 2621440 | tf_op jit(solution)/shard_map/all_to_all | solution.py:1030
  274.5 58.3 %reduce-scatter.5.cloned.1.call-start = ((), (), s32[]{:S(2)}) async-start(), calls=%async_computation.6 | async-start | bytes 1351680 | tf_op jit(solution)/shard_map/reduce_scatter | solution.py:1026
  275.3 52.6 %collective-permute-start.11 = (bf16[1024,768]{1,0:T(8,128)(2,1)}, bf16[1024,768]{1,0:T(8,128)(2,1)}, u32[]{:S(2)}, u32[]{:S(2)}) collective-permute-start(bf16[1024,768]{1,0:T(8,128)(2,1)} %get-tuple-element.129), channel_id=1, source_target_pairs={{0,4},{4,0},{8,12},{12,8},{1,5},{5,1},{9,13},{13,9},{2,6},{6,2},{1... | collective-permute-start | bytes 4718600 | tf_op jit(solution)/shard_map/ppermute | solution.py:909
  275.6 52.3 %collective-permute-start.10 = (bf16[1024,768]{1,0:T(8,128)(2,1)}, bf16[1024,768]{1,0:T(8,128)(2,1)}, u32[]{:S(2)}, u32[]{:S(2)}) collective-permute-start(bf16[1024,768]{1,0:T(8,128)(2,1)} %add_convert_fusion), channel_id=1, source_target_pairs={{0,8},{4,12},{8,0},{12,4},{1,9},{5,13},{9,1},{13,5},{2,10},{6,14},... | collective-permute-start | bytes 4718600 | tf_op jit(solution)/shard_map/ppermute | solution.py:909
  322.4 1.1 copy-start
Sparse Core Ops, SparseCore 0:
  12.4 113.2 all-gather.2
  185.0 83.8 reduce-scatter.2
  277.8 41.2 reduce-scatter.4

commit v7 on v6

--- a/solution.py
+++ b/solution.py
@@ -56,8 +56,8 @@
 
 
 UNROLL = 4
-BACK_UNROLL = 2
-APART = 48
+BACK_UNROLL = 4
+APART = 0
 VMEM_BYTES = 62 << 20
 
 
@@ -874,31 +874,25 @@
     )(me, *ctx_parts, nlt, gft, gb, pre, hid, sums, gbup)
 
 
-def finish_kernel(up_rows, own, apart_ref, total_ref, up_ref, down_ref, wo_ref, small_ref):
-    apart = apart_ref.shape[1]
-    total = jnp.zeros(apart_ref.shape[1:], f32)
-    for d in range(apart_ref.shape[0]):
-        total = total + apart_ref[d].astype(f32)
-    up_ref[0:apart, :] = total
+def finish_kernel(up_rows, own, total_ref, up_ref, down_ref, wo_ref, small_ref):
     rest = total_ref[...].astype(f32)
-    at = up_rows - apart
-    up_ref[apart:, :] = rest[0:at]
-    down_ref[...] = rest[at : at + up_rows]
-    at += up_rows
+    up_ref[...] = rest[0:up_rows]
+    down_ref[...] = rest[up_rows : 2 * up_rows]
+    at = 2 * up_rows
     wo_ref[...] = rest[at : at + own]
     small_ref[...] = rest[at + own : at + own + 8]
 
 
-def finished(apart, total, up_rows, own):
+def finished(total, up_rows, own):
     hidden = total.shape[1]
     whole = lambda: pl.BlockSpec(memory_space=pltpu.VMEM)
     return pl.pallas_call(
         functools.partial(finish_kernel, up_rows, own),
         out_shape=tuple(jax.ShapeDtypeStruct((r, hidden), f32) for r in (up_rows, up_rows, own, 8)),
-        in_specs=[whole(), whole()],
+        in_specs=[whole()],
         out_specs=tuple(whole() for _ in range(4)),
         name="finished",
-    )(apart, total)
+    )(total)
 
 
 ALL = ("dp", "seq", "ffn")
@@ -987,7 +981,7 @@
         me_ref, ctx_parts, normed_t, grad_ffn_t, grad_branch, grad_pre, hidden, sums, grad_bias_up, slabs, slab_rows,
         own if direct else 0, APART if direct else 0,
     )
-    payload, apart = payload if direct else (payload[0], None)
+    payload, apart = payload if direct and APART else (payload[0], None)
     if not direct:
         grad_out = dot_nn(jnp.concatenate(ctx_parts, axis=0), grad_branch).astype(bf16)
         grad_out = grad_out.reshape(seq_n, group, width)[order].reshape(outer, ffn_n, own, width)
@@ -999,7 +993,7 @@
         payload = jnp.pad(payload, ((0, 0), (0, 0), (0, -payload.shape[2] % 32), (0, 0)))
     payload, apart, do = lax.optimization_barrier((payload, apart, do))
     total = lax.psum_scatter(payload.reshape(-1, width), ("dp", "seq"), scatter_dimension=0, tiled=True)
-    if direct:
+    if apart is not None:
         apart = lax.all_to_all(
             apart.reshape(devices, APART, width), ALL, split_axis=0, concat_axis=0, tiled=True
         )
@@ -1022,14 +1016,18 @@
     grad_w, apart = lax.optimization_barrier((grad_w, apart))
     part = [None] + part
     bit = seq_n // 2
-    part[bit], total = lax.optimization_barrier((part[bit], total))
+    first = flip_send(part[bit][: rows // 8], "seq", bit)
+    first, total = lax.optimization_barrier((first, total))
     total = lax.psum_scatter(total, "ffn", scatter_dimension=0, tiled=True)
+    second = flip_send(part[bit][rows // 8 :], "seq", bit)
+    grad_features = grad_features + jnp.concatenate([first, second], axis=0).astype(f32)
+    bit //= 2
     while bit:
         grad_features = grad_features + flip_send(part[bit], "seq", bit).astype(f32)
         bit //= 2
     grad_w = lax.all_to_all(grad_w, ALL, split_axis=0, concat_axis=0, tiled=True)
     if direct:
-        out_up, out_down, out_output, notes = finished(apart, total, up_rows, own)
+        out_up, out_down, out_output, notes = finished(total, up_rows, own)
     else:
         total = total.astype(f32)
         out_up, out_down, out_output = total[:up_rows], total[up_rows:at], total[at : at + own]

time: 347 us -> 335 us (0.965)
  starting transfers between devices: 25.7 us -> 20.7 us
  Pallas kernels: 176 us -> 172 us
    all_to_all x1, waiting for transfers between devices: 45.1 us -> 20.5 us  [shards(): lax.all_to_all(grad_w, ALL, split_axis=0, concat_axis=0, tiled=True)]
    ppermute x12 -> x13, waiting for transfers between devices: 52.9 us -> 77.5 us  [flip_send(): return lax.ppermute(array, axis, [(i, i ^ bits) for i in range(count)])]
    all_to_all x1 -> x0, starting transfers between devices: 5.27 us -> none  [shards(): lax.all_to_all(apart.reshape(devices, APART, width), ALL, split_axis=0, c...]
    ppermute x12 -> x13, starting transfers between devices: 9.77 us -> 10.9 us  [flip_send(): return lax.ppermute(array, axis, [(i, i ^ bits) for i in range(count)])]
  transfers between devices with their start and end apart: 18 -> 18, of which waited for: 4 -> 6; matrix products, arithmetic and copies ran while one was open for 5% -> 5% of each run, Pallas kernels for 39% -> 39%
where the time goes in v7:
time: 335 us
  Pallas kernels  172 us (51%)
  waiting for transfers between devices  102 us (30%)
  starting transfers between devices  20.7 us (6%)
  local copies, waits for them, and re-layouts  18 us (5%)
  between operations  13.9 us (4%)
  other arithmetic  8.13 us (2%)
    ppermute x13, waiting for transfers between devices, flip_send(): return lax.ppermute(array, axis, [(i, i ^ bits) for i in range(count)])  77.5 us
    pallas_call x1, Pallas kernels, attention_backward(): pl.pallas_call(functools.partial(backward_kernel, heads, chunks), out_sha...  61.8 us
    pallas_call x1, Pallas kernels, rows_chain(): pl.pallas_call(functools.partial(rows_kernel, parts, blocks, up_rows, own...  37.7 us
    pallas_call x1, Pallas kernels, attention_forward(): pl.pallas_call(functools.partial(forward_kernel, heads, chunks), out_shap...  26.8 us
    all_to_all x1, waiting for transfers between devices, shards(): lax.all_to_all(grad_w, ALL, split_axis=0, concat_axis=0, tiled=True)  20.5 us
    pallas_call x1, Pallas kernels, outer_products(): pl.pallas_call(functools.partial(outer_kernel, parts, up_rows, own, apart...  17.6 us
    pallas_call x1, Pallas kernels, attention_near(): pl.pallas_call(functools.partial(near_kernel, heads, chunks), out_shape=(...  11.8 us
    ppermute x13, starting transfers between devices, flip_send(): return lax.ppermute(array, axis, [(i, i ^ bits) for i in range(count)])  10.9 us
  transfers between devices with their start and end apart: 18, of which 6 were waited for; matrix products, arithmetic and copies ran while one was open for 5% of the time, Pallas kernels for 39%

profile of v7, /device:TPU:0, one launch (start us, length us, event | category | flops | bytes accessed | tf_op | source)
XLA Modules:
  0.0 334.6 jit_solution(1961537611560658604)
XLA Ops:
  9.9 2.3 packed_weights.1
  12.2 3.0 collective-permute-start.1
  17.3 1.4 reduce.17
  19.4 4.9 %all-to-all-start = ((bf16[32,32,640]{2,1,0:T(8,128)(2,1)}), bf16[32,32,640]{2,1,0:T(8,128)(2,1)S(1)}, u32[]{:S(2)}, u32[]{:S(2)}) async-start(bf16[32,32,640]{2,1,0:T(8,128)(2,1)} %bitcast.43), calls=%async_computation | async-start | bytes 2621440 | tf_op jit(solution)/shard_map/all_to_all | solution.py:937
  24.7 48.4 %collective-permute-done.1.refs_2_ = bf16[1024,768]{1,0:T(8,128)(2,1)} collective-permute-done((bf16[1024,768]{1,0:T(8,128)(2,1)}, bf16[1024,768]{1,0:T(8,128)(2,1)}, u32[]{:S(2)}, u32[]{:S(2)}) %collective-permute-start.1) | collective-permute-done | bytes 1572896 | tf_op jit(solution)/shard_map/ppermute | solution.py:903
  73.1 4.3 %all-to-all-done = bf16[32,32,640]{2,1,0:T(8,128)(2,1)S(1)} async-done(((bf16[32,32,640]{2,1,0:T(8,128)(2,1)}), bf16[32,32,640]{2,1,0:T(8,128)(2,1)S(1)}, u32[]{:S(2)}, u32[]{:S(2)}) %all-to-all-start) | async-done | bytes 1310752 | tf_op jit(solution)/shard_map/all_to_all | solution.py:937
  80.0 26.8 %attention_forward.1 = (bf16[192,1024]{1,0:T(8,128)(2,1)}, bf16[192,1024]{1,0:T(8,128)(2,1)}, f32[3,16,128]{2,1,0:T(8,128)}, f32[3,128]{1,0:T(4,128)}, f32[3,64,...) custom-call(s32[1]{0:T(128)} %bitcast.me_ref, ...), custom_call_target="tpu_custom_call" | custom-call | flops 10000000000 | bytes 16000000 | tf_op jit(solution)/shard_map/attention_forward/pallas_call | solution.py:248
  107.5 11.8 %attention_near.1 = (bf16[192,1024]{1,0:T(8,128)(2,1)}, bf16[192,1024]{1,0:T(8,128)(2,1)}, f32[3,16,128]{2,1,0:T(8,128)}) custom-call(s32[1]{0:T(128)} %bitcast.me_ref, s32[576]{0:T(1024)} %reshape.71.rand_ref, s32[1,2]{1,0:T(1,128)} %glob_ref.5, bf16[4160,384]{1,0:T(8,128)(2,1)} %get-tuple-element.81.k_ref.refs_4_, ...), custom_call_target="tpu_custom_call" | custom-call | flops 6000000000 | bytes 9000000 | tf_op jit(solution)/shard_map/attention_near/pallas_call | solution.py:294
  119.3 1.8 collective-permute-start.5
  121.9 4.5 %collective-permute-done.4.refs_3_ = bf16[192,1024]{1,0:T(8,128)(2,1)} collective-permute-done((bf16[192,1024]{1,0:T(8,128)(2,1)}, bf16[192,1024]{1,0:T(8,128)(2,1)}, u32[]{:S(2)}, u32[]{:S(2)}) %collective-permute-start.4) | collective-permute-done | bytes 393248 | tf_op jit(solution)/shard_map/ppermute | solution.py:903
  127.5 37.7 %rows_chain.1 = (bf16[1024,768]{1,0:T(8,128)(2,1)}, f32[1024,768]{1,0:T(8,128)}, bf16[4,1024,768]{2,1,0:T(8,128)(2,1)}, bf16[4,1024,768]{2,1,0:T(8,128)(2,1)}, b...) custom-call(s32[1]{0:T(128)} %bitcast.me_ref, ...), custom_call_target="tpu_custom_call" | custom-call | flops 22000001024 | bytes 40000000 | tf_op jit(solution)/shard_map/rows_chain/pallas_call | solution.py:780
  167.2 17.6 %outer_products.1 = bf16[8,4,224,768]{3,2,1,0:T(8,128)(2,1)} custom-call(s32[1]{0:T(128)} %bitcast.me_ref, bf16[192,1024]{1,0:T(8,128)(2,1)} %get-tuple-element.87.refs_0_, bf16[192,1024]{1,0:T(8,128)(2,1)} %collective-permute-done.5.refs_1_, bf16[192,1024]{1,0:T(8,128)(2,1)} %copy-done.2, bf16[192,1024]{1,0:T(8,128)(2,1)} %collective-permute-done.4.refs_3_, ...), custom_call_target="tpu_custom_call" | custom-call | flops 11000000512 | bytes 28000000 | tf_op jit(solution)/shard_map/outer_products/pallas_call | solution.py:854
  185.8 61.8 %attention_backward.1 = (bf16[4,192,1024]{2,1,0:T(8,128)(2,1)}, bf16[4,1024,384]{2,1,0:T(8,128)(2,1)}, f32[1024,768]{1,0:T(8,128)}, bf16[1024,768]{1,0:T(8,128)(...) custom-call(s32[1]{0:T(128)} %bitcast.me_ref, s32[576]{0:T(1024)} %reshape.71.rand_ref, s32[1,2]{1,0:T(1,128)} %glob_ref.5, ...), custom_call_target="tpu_custom_call" | custom-call | flops 30000001024 | bytes 24000000 | tf_op jit(solution)/shard_map/attention_backward/pallas_call | solution.py:465
  248.7 9.6 %projection_gradients.1 = (bf16[32,32,640]{2,1,0:T(8,128)(2,1)}, f32[8,640]{1,0:T(8,128)}) custom-call(bf16[1024,768]{1,0:T(8,128)(2,1)} %bitcast.60, bf16[1024,768]{1,0:T(8,128)(2,1)} %collective-permute-done.refs_1_, bf16[1024,768]{1,0:T(8,128)(2,1)} %collective-permute-done.1.refs_2_, bf16[1024,768]{1,0:T(8,128)(2,1)} %collective-permute-done.2.refs_3_, ...), custom_call_target="tpu_custom_call" | custom-call | flops 4000000000 | bytes 12000000 | tf_op jit(solution)/shard_map/projection_gradients/pallas_call | solution.py:608
  258.3 1.8 add_convert_fusion
  260.1 4.7 %all-to-all-start.1 = ((bf16[32,32,640]{2,1,0:T(8,128)(2,1)}), bf16[32,32,640]{2,1,0:T(8,128)(2,1)S(1)}, u32[]{:S(2)}, u32[]{:S(2)}) async-start(bf16[32,32,640]{2,1,0:T(8,128)(2,1)} %get-tuple-element.123), calls=%async_computation.2 | async-start | bytes 2621440 | tf_op jit(solution)/shard_map/all_to_all | solution.py:1028
  264.9 1.8 collective-permute-start.10
  266.7 15.0 %collective-permute-done.10 = bf16[128,768]{1,0:T(8,128)(2,1)S(1)} collective-permute-done((bf16[128,768]{1,0:T(8,128)(2,1)S(1)}, bf16[128,768]{1,0:T(8,128)(2,1)S(1)}, u32[]{:S(2)}, u32[]{:S(2)}) %collective-permute-start.10) | collective-permute-done | bytes 196640 | tf_op jit(solution)/shard_map/ppermute | solution.py:903
  283.1 20.5 %all-to-all-done.1 = bf16[32,32,640]{2,1,0:T(8,128)(2,1)S(1)} async-done(((bf16[32,32,640]{2,1,0:T(8,128)(2,1)}), bf16[32,32,640]{2,1,0:T(8,128)(2,1)S(1)}, u32[]{:S(2)}, u32[]{:S(2)}) %all-to-all-start.1) | async-done | bytes 1310752 | tf_op jit(solution)/shard_map/all_to_all | solution.py:1028
  304.7 2.2 unpacked_gradients.1
  309.1 9.6 %collective-permute-done.11 = bf16[896,768]{1,0:T(8,128)(2,1)} collective-permute-done((bf16[896,768]{1,0:T(8,128)(2,1)}, bf16[896,768]{1,0:T(8,128)(2,1)}, u32[]{:S(2)}, u32[]{:S(2)}) %collective-permute-start.11) | collective-permute-done | bytes 1376288 | tf_op jit(solution)/shard_map/ppermute | solution.py:903
  318.7 4.8 %add_bitcast_fusion = f32[1,1024,768]{2,1,0:T(8,128)} fusion(bf16[1024,768]{1,0:T(8,128)(2,1)} %collective-permute-done.12, f32[1024,768]{1,0:T(8,128)} %get-tuple-element.112, bf16[896,768]{1,0:T(8,128)(2,1)} %collective-permute-done.11, bf16[128,768]{1,0:T(8,128)(2,1)S(1)} %collective-permute-done.10), kind=kLoop, calls=%fused_computation | loop fusion | flops 5505024 | bytes 9437184 | tf_op jit(solution)/shard_map/broadcast_in_dim | solution.py:1045
  323.6 1.8 finished.1
  325.4 1.3 slice_reduce_fusion.2
  (70 shorter events, 21.2 us)
Async XLA Ops:
  7.2 119.1 %all-gather.3.cloned.1.call-start = ((), (), s32[]{:S(2)}) async-start(), calls=%async_computation.6 | async-start | bytes 11354112 | tf_op jit(solution)/shard_map/all_gather | solution.py:940
  12.2 60.9 %collective-permute-start.1 = (bf16[1024,768]{1,0:T(8,128)(2,1)}, bf16[1024,768]{1,0:T(8,128)(2,1)}, u32[]{:S(2)}, u32[]{:S(2)}) collective-permute-start(bf16[1024,768]{1,0:T(8,128)(2,1)} %bitcast.56), channel_id=1, source_target_pairs={{0,8},{4,12},{8,0},{12,4},{1,9},{5,13},{9,1},{13,5},{2,10},{6,14},... | collective-permute-start | bytes 4718600 | tf_op jit(solution)/shard_map/ppermute | solution.py:903
  19.4 58.0 %all-to-all-start = ((bf16[32,32,640]{2,1,0:T(8,128)(2,1)}), bf16[32,32,640]{2,1,0:T(8,128)(2,1)S(1)}, u32[]{:S(2)}, u32[]{:S(2)}) async-start(bf16[32,32,640]{2,1,0:T(8,128)(2,1)} %bitcast.43), calls=%async_computation | async-start | bytes 2621440 | tf_op jit(solution)/shard_map/all_to_all | solution.py:937
  24.3 257.4 %reduce-scatter.3.cloned.1.call-start = ((), (), s32[]{:S(2)}) async-start(), calls=%async_computation.4 | async-start | bytes 12386304 | tf_op jit(solution)/shard_map/reduce_scatter | solution.py:995
  24.3 55.7 %collective-permute-start = (bf16[1024,768]{1,0:T(8,128)(2,1)}, bf16[1024,768]{1,0:T(8,128)(2,1)}, u32[]{:S(2)}, u32[]{:S(2)}) collective-permute-start(bf16[1024,768]{1,0:T(8,128)(2,1)} %bitcast.57), channel_id=1, source_target_pairs={{0,4},{4,0},{8,12},{12,8},{1,5},{5,1},{9,13},{13,9},{2,6},{6,2},{1... | collective-permute-start | bytes 4718600 | tf_op jit(solution)/shard_map/ppermute | solution.py:903
  73.1 6.9 %collective-permute-start.2 = (bf16[1024,768]{1,0:T(8,128)(2,1)}, bf16[1024,768]{1,0:T(8,128)(2,1)}, u32[]{:S(2)}, u32[]{:S(2)}) collective-permute-start(bf16[1024,768]{1,0:T(8,128)(2,1)} %collective-permute-done.1.refs_2_), channel_id=1, source_target_pairs={{0,4},{4,0},{8,12},{12,8},{1,5},{5,1},{9,13},{13,9},{2,6},{6,2},{1... | collective-permute-start | bytes 4718600 | tf_op jit(solution)/shard_map/ppermute | solution.py:903
  106.8 15.1 %collective-permute-start.3 = (bf16[192,1024]{1,0:T(8,128)(2,1)}, bf16[192,1024]{1,0:T(8,128)(2,1)S(1)}, u32[]{:S(2)}, u32[]{:S(2)}) collective-permute-start(bf16[192,1024]{1,0:T(8,128)(2,1)} %get-tuple-element.79), channel_id=1, source_target_pairs={{0,8},{4,12},{8,0},{12,4},{1,9},{5,13},{9,1},{13,5},{2,10},{6,14},... | collective-permute-start | bytes 1179656 | tf_op jit(solution)/shard_map/ppermute | solution.py:903
  107.4 18.9 %collective-permute-start.4 = (bf16[192,1024]{1,0:T(8,128)(2,1)}, bf16[192,1024]{1,0:T(8,128)(2,1)}, u32[]{:S(2)}, u32[]{:S(2)}) collective-permute-start(bf16[192,1024]{1,0:T(8,128)(2,1)} %get-tuple-element.80), channel_id=1, source_target_pairs={{0,12},{4,8},{8,4},{12,0},{1,13},{5,9},{9,5},{13,1},{2,14},{6,10},... | collective-permute-start | bytes 1179656 | tf_op jit(solution)/shard_map/ppermute | solution.py:903
  119.3 7.1 %collective-permute-start.5 = (bf16[192,1024]{1,0:T(8,128)(2,1)}, bf16[192,1024]{1,0:T(8,128)(2,1)}, u32[]{:S(2)}, u32[]{:S(2)}) collective-permute-start(bf16[192,1024]{1,0:T(8,128)(2,1)} %get-tuple-element.88), channel_id=1, source_target_pairs={{0,4},{4,0},{8,12},{12,8},{1,5},{5,1},{9,13},{13,9},{2,6},{6,2},{1... | collective-permute-start | bytes 1179656 | tf_op jit(solution)/shard_map/ppermute | solution.py:903
  121.9 5.6 %copy-start.2 = (bf16[192,1024]{1,0:T(8,128)(2,1)}, bf16[192,1024]{1,0:T(8,128)(2,1)S(1)}, u32[]{:S(2)}) copy-start(bf16[192,1024]{1,0:T(8,128)(2,1)S(1)} %collective-permute-done.3.refs_2_) | copy-start | bytes 1179652
  165.2 19.6 %collective-permute-start.6 = (bf16[192,1024]{1,0:T(8,128)(2,1)}, bf16[192,1024]{1,0:T(8,128)(2,1)S(1)}, u32[]{:S(2)}, u32[]{:S(2)}) collective-permute-start(bf16[192,1024]{1,0:T(8,128)(2,1)} %get-tuple-element.101), channel_id=1, source_target_pairs={{0,4},{4,0},{8,12},{12,8},{1,5},{5,1},{9,13},{13,9},{2,6},{6,2},{1... | collective-permute-start | bytes 1179656 | tf_op jit(solution)/shard_map/ppermute | solution.py:903
  165.7 19.1 %collective-permute-start.7 = (bf16[192,1024]{1,0:T(8,128)(2,1)}, bf16[192,1024]{1,0:T(8,128)(2,1)S(1)}, u32[]{:S(2)}, u32[]{:S(2)}) collective-permute-start(bf16[192,1024]{1,0:T(8,128)(2,1)} %get-tuple-element.102), channel_id=1, source_target_pairs={{0,8},{4,12},{8,0},{12,4},{1,9},{5,13},{9,1},{13,5},{2,10},{6,14},... | collective-permute-start | bytes 1179656 | tf_op jit(solution)/shard_map/ppermute | solution.py:903
  166.2 18.6 %collective-permute-start.8 = (bf16[192,1024]{1,0:T(8,128)(2,1)}, bf16[192,1024]{1,0:T(8,128)(2,1)S(1)}, u32[]{:S(2)}, u32[]{:S(2)}) collective-permute-start(bf16[192,1024]{1,0:T(8,128)(2,1)} %get-tuple-element.103), channel_id=1, source_target_pairs={{0,12},{4,8},{8,4},{12,0},{1,13},{5,9},{9,5},{13,1},{2,14},{6,10},... | collective-permute-start | bytes 1179656 | tf_op jit(solution)/shard_map/ppermute | solution.py:903
  184.8 0.8 copy-start.3
  184.8 0.9 copy-start.4
  184.8 1.0 copy-start.5
  247.6 10.7 %collective-permute-start.9 = (bf16[1024,768]{1,0:T(8,128)(2,1)}, bf16[1024,768]{1,0:T(8,128)(2,1)}, u32[]{:S(2)}, u32[]{:S(2)}) collective-permute-start(bf16[1024,768]{1,0:T(8,128)(2,1)} %get-tuple-element.118), channel_id=1, source_target_pairs={{0,4},{4,0},{8,12},{12,8},{1,5},{5,1},{9,13},{13,9},{2,6},{6,2},{1... | collective-permute-start | bytes 4718600 | tf_op jit(solution)/shard_map/ppermute | solution.py:903
  248.7 9.6 %copy-start.1 = (bf16[1024,768]{1,0:T(8,128)(2,1)S(1)}, bf16[1024,768]{1,0:T(8,128)(2,1)}, u32[]{:S(2)}) copy-start(bf16[1024,768]{1,0:T(8,128)(2,1)} %get-tuple-element.117) | copy-start | bytes 4718596
  260.1 43.5 %all-to-all-start.1 = ((bf16[32,32,640]{2,1,0:T(8,128)(2,1)}), bf16[32,32,640]{2,1,0:T(8,128)(2,1)S(1)}, u32[]{:S(2)}, u32[]{:S(2)}) async-start(bf16[32,32,640]{2,1,0:T(8,128)(2,1)} %get-tuple-element.123), calls=%async_computation.2 | async-start | bytes 2621440 | tf_op jit(solution)/shard_map/all_to_all | solution.py:1028
  264.8 58.7 %reduce-scatter.5.cloned.1.call-start = ((), (), s32[]{:S(2)}) async-start(), calls=%async_computation.5 | async-start | bytes 1720320 | tf_op jit(solution)/shard_map/reduce_scatter | solution.py:1021
  264.9 16.8 %collective-permute-start.10 = (bf16[128,768]{1,0:T(8,128)(2,1)S(1)}, bf16[128,768]{1,0:T(8,128)(2,1)S(1)}, u32[]{:S(2)}, u32[]{:S(2)}) collective-permute-start(bf16[128,768]{1,0:T(8,128)(2,1)S(1)} %slice.62), channel_id=1, source_target_pairs={{0,8},{4,12},{8,0},{12,4},{1,9},{5,13},{9,1},{13,5},{2,10},{6,14},... | collective-permute-start | bytes 589832 | tf_op jit(solution)/shard_map/ppermute | solution.py:903
  281.7 37.0 %collective-permute-start.12 = (bf16[1024,768]{1,0:T(8,128)(2,1)}, bf16[1024,768]{1,0:T(8,128)(2,1)}, u32[]{:S(2)}, u32[]{:S(2)}) collective-permute-start(bf16[1024,768]{1,0:T(8,128)(2,1)} %get-tuple-element.122), channel_id=1, source_target_pairs={{0,4},{4,0},{8,12},{12,8},{1,5},{5,1},{9,13},{13,9},{2,6},{6,2},{1... | collective-permute-start | bytes 4718600 | tf_op jit(solution)/shard_map/ppermute | solution.py:903
  283.0 35.8 %collective-permute-start.11 = (bf16[896,768]{1,0:T(8,128)(2,1)}, bf16[896,768]{1,0:T(8,128)(2,1)}, u32[]{:S(2)}, u32[]{:S(2)}) collective-permute-start(bf16[896,768]{1,0:T(8,128)(2,1)} %slice.63), channel_id=1, source_target_pairs={{0,8},{4,12},{8,0},{12,4},{1,9},{5,13},{9,1},{13,5},{2,10},{6,14},... | collective-permute-start | bytes 4128776 | tf_op jit(solution)/shard_map/ppermute | solution.py:903
  303.6 1.1 copy-start
Sparse Core Ops, SparseCore 0:
  12.4 113.2 all-gather.2
  185.0 84.4 reduce-scatter.2
  281.9 36.9 reduce-scatter.4

commit v8 on v7

--- a/solution.py
+++ b/solution.py
@@ -1012,19 +1012,16 @@
                 part[k ^ bit] = (part[k ^ bit].astype(f32) + came).astype(bf16)
         bit *= 2
     grad_w = projection_gradients(near, dq, dkv, own, devices)
-    grad_w, part = lax.optimization_barrier((grad_w, part[1:]))
-    grad_w, apart = lax.optimization_barrier((grad_w, apart))
-    part = [None] + part
     bit = seq_n // 2
-    first = flip_send(part[bit][: rows // 8], "seq", bit)
-    first, total = lax.optimization_barrier((first, total))
+    lead = 192
+    first = flip_send(part[bit][:lead], "seq", bit)
+    grad_w, first = lax.optimization_barrier((grad_w, first))
+    second = flip_send(part[bit][lead:], "seq", bit)
+    extra = [flip_send(part[k], "seq", k) for k in range(1, bit) if k & (k - 1) == 0]
+    extra[0], total = lax.optimization_barrier((extra[0], total))
     total = lax.psum_scatter(total, "ffn", scatter_dimension=0, tiled=True)
-    second = flip_send(part[bit][rows // 8 :], "seq", bit)
-    grad_features = grad_features + jnp.concatenate([first, second], axis=0).astype(f32)
-    bit //= 2
-    while bit:
-        grad_features = grad_features + flip_send(part[bit], "seq", bit).astype(f32)
-        bit //= 2
+    for piece in [jnp.concatenate([first, second], axis=0)] + extra:
+        grad_features = grad_features + piece.astype(f32)
     grad_w = lax.all_to_all(grad_w, ALL, split_axis=0, concat_axis=0, tiled=True)
     if direct:
         out_up, out_down, out_output, notes = finished(total, up_rows, own)

time: 335 us -> 350 us (1.045)
  waiting for transfers between devices: 102 us -> 116 us
    all_to_all x1, waiting for transfers between devices: 20.5 us -> 47 us  [shards(): lax.all_to_all(grad_w, ALL, split_axis=0, concat_axis=0, tiled=True)]
    ppermute x13, waiting for transfers between devices: 77.5 us -> 64.3 us  [flip_send(): return lax.ppermute(array, axis, [(i, i ^ bits) for i in range(count)])]
  transfers between devices with their start and end apart: 18 -> 18, of which waited for: 6 -> 6; matrix products, arithmetic and copies ran while one was open for 5% -> 5% of each run, Pallas kernels for 39% -> 37%
where the time goes in v8:
time: 350 us; the launch traced here: 347 us
  Pallas kernels  172 us (49%)
  waiting for transfers between devices  116 us (33%)
  starting transfers between devices  20.2 us (6%)
  local copies, waits for them, and re-layouts  17.6 us (5%)
  between operations  13.9 us (4%)
  other arithmetic  7.81 us (2%)
    ppermute x13, waiting for transfers between devices, flip_send(): return lax.ppermute(array, axis, [(i, i ^ bits) for i in range(count)])  64.3 us
    pallas_call x1, Pallas kernels, attention_backward(): pl.pallas_call(functools.partial(backward_kernel, heads, chunks), out_sha...  61.8 us
    all_to_all x1, waiting for transfers between devices, shards(): lax.all_to_all(grad_w, ALL, split_axis=0, concat_axis=0, tiled=True)  47 us
    pallas_call x1, Pallas kernels, rows_chain(): pl.pallas_call(functools.partial(rows_kernel, parts, blocks, up_rows, own...  37.7 us
    pallas_call x1, Pallas kernels, attention_forward(): pl.pallas_call(functools.partial(forward_kernel, heads, chunks), out_shap...  26.8 us
    pallas_call x1, Pallas kernels, outer_products(): pl.pallas_call(functools.partial(outer_kernel, parts, up_rows, own, apart...  17.6 us
    pallas_call x1, Pallas kernels, attention_near(): pl.pallas_call(functools.partial(near_kernel, heads, chunks), out_shape=(...  11.8 us
    ppermute x13, starting transfers between devices, flip_send(): return lax.ppermute(array, axis, [(i, i ^ bits) for i in range(count)])  10.6 us
  transfers between devices with their start and end apart: 18, of which 6 were waited for; matrix products, arithmetic and copies ran while one was open for 5% of the time, Pallas kernels for 37%

profile of v8, /device:TPU:0, one launch (start us, length us, event | category | flops | bytes accessed | tf_op | source)
XLA Modules:
  0.0 347.2 jit_solution(6207372158010562696)
XLA Ops:
  9.9 2.3 packed_weights.1
  12.2 3.0 collective-permute-start.1
  17.3 1.4 reduce.17
  19.4 4.9 %all-to-all-start = ((bf16[32,32,640]{2,1,0:T(8,128)(2,1)}), bf16[32,32,640]{2,1,0:T(8,128)(2,1)S(1)}, u32[]{:S(2)}, u32[]{:S(2)}) async-start(bf16[32,32,640]{2,1,0:T(8,128)(2,1)} %bitcast.42), calls=%async_computation | async-start | bytes 2621440 | tf_op jit(solution)/shard_map/all_to_all | solution.py:937
  24.7 48.4 %collective-permute-done.1.refs_2_ = bf16[1024,768]{1,0:T(8,128)(2,1)} collective-permute-done((bf16[1024,768]{1,0:T(8,128)(2,1)}, bf16[1024,768]{1,0:T(8,128)(2,1)}, u32[]{:S(2)}, u32[]{:S(2)}) %collective-permute-start.1) | collective-permute-done | bytes 1572896 | tf_op jit(solution)/shard_map/ppermute | solution.py:903
  73.1 4.3 %all-to-all-done = bf16[32,32,640]{2,1,0:T(8,128)(2,1)S(1)} async-done(((bf16[32,32,640]{2,1,0:T(8,128)(2,1)}), bf16[32,32,640]{2,1,0:T(8,128)(2,1)S(1)}, u32[]{:S(2)}, u32[]{:S(2)}) %all-to-all-start) | async-done | bytes 1310752 | tf_op jit(solution)/shard_map/all_to_all | solution.py:937
  80.0 26.8 %attention_forward.1 = (bf16[192,1024]{1,0:T(8,128)(2,1)}, bf16[192,1024]{1,0:T(8,128)(2,1)}, f32[3,16,128]{2,1,0:T(8,128)}, f32[3,128]{1,0:T(4,128)}, f32[3,64,...) custom-call(s32[1]{0:T(128)} %bitcast.me_ref, ...), custom_call_target="tpu_custom_call" | custom-call | flops 10000000000 | bytes 16000000 | tf_op jit(solution)/shard_map/attention_forward/pallas_call | solution.py:248
  107.4 11.8 %attention_near.1 = (bf16[192,1024]{1,0:T(8,128)(2,1)}, bf16[192,1024]{1,0:T(8,128)(2,1)}, f32[3,16,128]{2,1,0:T(8,128)}) custom-call(s32[1]{0:T(128)} %bitcast.me_ref, s32[576]{0:T(1024)} %reshape.71.rand_ref, s32[1,2]{1,0:T(1,128)} %glob_ref.5, bf16[4160,384]{1,0:T(8,128)(2,1)} %get-tuple-element.80.k_ref.refs_4_, ...), custom_call_target="tpu_custom_call" | custom-call | flops 6000000000 | bytes 9000000 | tf_op jit(solution)/shard_map/attention_near/pallas_call | solution.py:294
  119.3 1.8 collective-permute-start.5
  121.8 4.5 %collective-permute-done.4.refs_3_ = bf16[192,1024]{1,0:T(8,128)(2,1)} collective-permute-done((bf16[192,1024]{1,0:T(8,128)(2,1)}, bf16[192,1024]{1,0:T(8,128)(2,1)}, u32[]{:S(2)}, u32[]{:S(2)}) %collective-permute-start.4) | collective-permute-done | bytes 393248 | tf_op jit(solution)/shard_map/ppermute | solution.py:903
  127.5 37.7 %rows_chain.1 = (bf16[1024,768]{1,0:T(8,128)(2,1)}, f32[1024,768]{1,0:T(8,128)}, bf16[4,1024,768]{2,1,0:T(8,128)(2,1)}, bf16[4,1024,768]{2,1,0:T(8,128)(2,1)}, b...) custom-call(s32[1]{0:T(128)} %bitcast.me_ref, ...), custom_call_target="tpu_custom_call" | custom-call | flops 22000001024 | bytes 40000000 | tf_op jit(solution)/shard_map/rows_chain/pallas_call | solution.py:780
  167.2 17.6 %outer_products.1 = bf16[8,4,224,768]{3,2,1,0:T(8,128)(2,1)} custom-call(s32[1]{0:T(128)} %bitcast.me_ref, bf16[192,1024]{1,0:T(8,128)(2,1)} %get-tuple-element.86.refs_0_, bf16[192,1024]{1,0:T(8,128)(2,1)} %collective-permute-done.5.refs_1_, bf16[192,1024]{1,0:T(8,128)(2,1)} %copy-done, bf16[192,1024]{1,0:T(8,128)(2,1)} %collective-permute-done.4.refs_3_, ...), custom_call_target="tpu_custom_call" | custom-call | flops 11000000512 | bytes 28000000 | tf_op jit(solution)/shard_map/outer_products/pallas_call | solution.py:854
  185.8 61.8 %attention_backward.1 = (bf16[4,192,1024]{2,1,0:T(8,128)(2,1)}, bf16[4,1024,384]{2,1,0:T(8,128)(2,1)}, f32[1024,768]{1,0:T(8,128)}, bf16[1024,768]{1,0:T(8,128)(...) custom-call(s32[1]{0:T(128)} %bitcast.me_ref, s32[576]{0:T(1024)} %reshape.71.rand_ref, s32[1,2]{1,0:T(1,128)} %glob_ref.5, ...), custom_call_target="tpu_custom_call" | custom-call | flops 30000001024 | bytes 24000000 | tf_op jit(solution)/shard_map/attention_backward/pallas_call | solution.py:465
  248.8 4.7 %collective-permute-done.9 = bf16[1024,768]{1,0:T(8,128)(2,1)S(1)} collective-permute-done((bf16[1024,768]{1,0:T(8,128)(2,1)}, bf16[1024,768]{1,0:T(8,128)(2,1)S(1)}, u32[]{:S(2)}, u32[]{:S(2)}) %collective-permute-start.9) | collective-permute-done | bytes 1572896 | tf_op jit(solution)/shard_map/ppermute | solution.py:903
  253.5 1.9 add_convert_fusion
  256.1 9.5 %projection_gradients.1 = (bf16[32,32,640]{2,1,0:T(8,128)(2,1)}, f32[8,640]{1,0:T(8,128)}) custom-call(bf16[1024,768]{1,0:T(8,128)(2,1)} %bitcast.59, bf16[1024,768]{1,0:T(8,128)(2,1)} %collective-permute-done.refs_1_, bf16[1024,768]{1,0:T(8,128)(2,1)} %collective-permute-done.1.refs_2_, bf16[1024,768]{1,0:T(8,128)(2,1)} %collective-permute-done.2.refs_3_, ...), custom_call_target="tpu_custom_call" | custom-call | flops 4000000000 | bytes 12000000 | tf_op jit(solution)/shard_map/projection_gradients/pallas_call | solution.py:608
  265.6 6.7 %collective-permute-done.10 = bf16[192,768]{1,0:T(8,128)(2,1)S(1)} collective-permute-done((bf16[192,768]{1,0:T(8,128)(2,1)}, bf16[192,768]{1,0:T(8,128)(2,1)S(1)}, u32[]{:S(2)}, u32[]{:S(2)}) %collective-permute-start.10) | collective-permute-done | bytes 294944 | tf_op jit(solution)/shard_map/ppermute | solution.py:903
  272.3 4.5 %all-to-all-start.1 = ((bf16[32,32,640]{2,1,0:T(8,128)(2,1)}), bf16[32,32,640]{2,1,0:T(8,128)(2,1)}, u32[]{:S(2)}, u32[]{:S(2)}) async-start(bf16[32,32,640]{2,1,0:T(8,128)(2,1)} %get-tuple-element.121), calls=%async_computation.2 | async-start | bytes 2621440 | tf_op jit(solution)/shard_map/all_to_all | solution.py:1025
  278.7 1.7 collective-permute-start.11
  280.4 47.0 %all-to-all-done.1 = bf16[32,32,640]{2,1,0:T(8,128)(2,1)} async-done(((bf16[32,32,640]{2,1,0:T(8,128)(2,1)}), bf16[32,32,640]{2,1,0:T(8,128)(2,1)}, u32[]{:S(2)}, u32[]{:S(2)}) %all-to-all-start.1) | async-done | bytes 1310752 | tf_op jit(solution)/shard_map/all_to_all | solution.py:1025
  327.3 2.2 unpacked_gradients.1
  331.8 4.4 %add_bitcast_fusion = f32[1,1024,768]{2,1,0:T(8,128)} fusion(bf16[1024,768]{1,0:T(8,128)(2,1)} %collective-permute-done.12, f32[1024,768]{1,0:T(8,128)} %get-tuple-element.111, bf16[832,768]{1,0:T(8,128)(2,1)S(1)} %collective-permute-done.11, bf16[192,768]{1,0:T(8,128)(2,1)S(1)} %collective-permute-done.10), kind=kLoop, calls=%fused_computation | loop fusion | flops 5505024 | bytes 9437184 | tf_op jit(solution)/shard_map/broadcast_in_dim | solution.py:1042
  336.2 1.8 finished.1
  338.1 1.3 slice_reduce_fusion.2
  (66 shorter events, 21.2 us)
Async XLA Ops:
  7.2 119.1 %all-gather.3.cloned.1.call-start = ((), (), s32[]{:S(2)}) async-start(), calls=%async_computation.6 | async-start | bytes 11354112 | tf_op jit(solution)/shard_map/all_gather | solution.py:940
  12.2 60.9 %collective-permute-start.1 = (bf16[1024,768]{1,0:T(8,128)(2,1)}, bf16[1024,768]{1,0:T(8,128)(2,1)}, u32[]{:S(2)}, u32[]{:S(2)}) collective-permute-start(bf16[1024,768]{1,0:T(8,128)(2,1)} %bitcast.55), channel_id=1, source_target_pairs={{0,8},{4,12},{8,0},{12,4},{1,9},{5,13},{9,1},{13,5},{2,10},{6,14},... | collective-permute-start | bytes 4718600 | tf_op jit(solution)/shard_map/ppermute | solution.py:903
  19.4 58.0 %all-to-all-start = ((bf16[32,32,640]{2,1,0:T(8,128)(2,1)}), bf16[32,32,640]{2,1,0:T(8,128)(2,1)S(1)}, u32[]{:S(2)}, u32[]{:S(2)}) async-start(bf16[32,32,640]{2,1,0:T(8,128)(2,1)} %bitcast.42), calls=%async_computation | async-start | bytes 2621440 | tf_op jit(solution)/shard_map/all_to_all | solution.py:937
  24.3 252.6 %reduce-scatter.3.cloned.1.call-start = ((), (), s32[]{:S(2)}) async-start(), calls=%async_computation.4 | async-start | bytes 12386304 | tf_op jit(solution)/shard_map/reduce_scatter | solution.py:995
  24.3 55.7 %collective-permute-start = (bf16[1024,768]{1,0:T(8,128)(2,1)}, bf16[1024,768]{1,0:T(8,128)(2,1)}, u32[]{:S(2)}, u32[]{:S(2)}) collective-permute-start(bf16[1024,768]{1,0:T(8,128)(2,1)} %bitcast.56), channel_id=1, source_target_pairs={{0,4},{4,0},{8,12},{12,8},{1,5},{5,1},{9,13},{13,9},{2,6},{6,2},{1... | collective-permute-start | bytes 4718600 | tf_op jit(solution)/shard_map/ppermute | solution.py:903
  73.1 6.9 %collective-permute-start.2 = (bf16[1024,768]{1,0:T(8,128)(2,1)}, bf16[1024,768]{1,0:T(8,128)(2,1)}, u32[]{:S(2)}, u32[]{:S(2)}) collective-permute-start(bf16[1024,768]{1,0:T(8,128)(2,1)} %collective-permute-done.1.refs_2_), channel_id=1, source_target_pairs={{0,4},{4,0},{8,12},{12,8},{1,5},{5,1},{9,13},{13,9},{2,6},{6,2},{1... | collective-permute-start | bytes 4718600 | tf_op jit(solution)/shard_map/ppermute | solution.py:903
  106.8 15.0 %collective-permute-start.3 = (bf16[192,1024]{1,0:T(8,128)(2,1)}, bf16[192,1024]{1,0:T(8,128)(2,1)S(1)}, u32[]{:S(2)}, u32[]{:S(2)}) collective-permute-start(bf16[192,1024]{1,0:T(8,128)(2,1)} %get-tuple-element.78), channel_id=1, source_target_pairs={{0,8},{4,12},{8,0},{12,4},{1,9},{5,13},{9,1},{13,5},{2,10},{6,14},... | collective-permute-start | bytes 1179656 | tf_op jit(solution)/shard_map/ppermute | solution.py:903
  107.4 18.9 %collective-permute-start.4 = (bf16[192,1024]{1,0:T(8,128)(2,1)}, bf16[192,1024]{1,0:T(8,128)(2,1)}, u32[]{:S(2)}, u32[]{:S(2)}) collective-permute-start(bf16[192,1024]{1,0:T(8,128)(2,1)} %get-tuple-element.79), channel_id=1, source_target_pairs={{0,12},{4,8},{8,4},{12,0},{1,13},{5,9},{9,5},{13,1},{2,14},{6,10},... | collective-permute-start | bytes 1179656 | tf_op jit(solution)/shard_map/ppermute | solution.py:903
  119.3 7.1 %collective-permute-start.5 = (bf16[192,1024]{1,0:T(8,128)(2,1)}, bf16[192,1024]{1,0:T(8,128)(2,1)}, u32[]{:S(2)}, u32[]{:S(2)}) collective-permute-start(bf16[192,1024]{1,0:T(8,128)(2,1)} %get-tuple-element.87), channel_id=1, source_target_pairs={{0,4},{4,0},{8,12},{12,8},{1,5},{5,1},{9,13},{13,9},{2,6},{6,2},{1... | collective-permute-start | bytes 1179656 | tf_op jit(solution)/shard_map/ppermute | solution.py:903
  121.8 5.7 %copy-start = (bf16[192,1024]{1,0:T(8,128)(2,1)}, bf16[192,1024]{1,0:T(8,128)(2,1)S(1)}, u32[]{:S(2)}) copy-start(bf16[192,1024]{1,0:T(8,128)(2,1)S(1)} %collective-permute-done.3.refs_2_) | copy-start | bytes 1179652
  165.2 19.6 %collective-permute-start.6 = (bf16[192,1024]{1,0:T(8,128)(2,1)}, bf16[192,1024]{1,0:T(8,128)(2,1)S(1)}, u32[]{:S(2)}, u32[]{:S(2)}) collective-permute-start(bf16[192,1024]{1,0:T(8,128)(2,1)} %get-tuple-element.100), channel_id=1, source_target_pairs={{0,4},{4,0},{8,12},{12,8},{1,5},{5,1},{9,13},{13,9},{2,6},{6,2},{1... | collective-permute-start | bytes 1179656 | tf_op jit(solution)/shard_map/ppermute | solution.py:903
  165.7 19.1 %collective-permute-start.7 = (bf16[192,1024]{1,0:T(8,128)(2,1)}, bf16[192,1024]{1,0:T(8,128)(2,1)S(1)}, u32[]{:S(2)}, u32[]{:S(2)}) collective-permute-start(bf16[192,1024]{1,0:T(8,128)(2,1)} %get-tuple-element.101), channel_id=1, source_target_pairs={{0,8},{4,12},{8,0},{12,4},{1,9},{5,13},{9,1},{13,5},{2,10},{6,14},... | collective-permute-start | bytes 1179656 | tf_op jit(solution)/shard_map/ppermute | solution.py:903
  166.3 18.6 %collective-permute-start.8 = (bf16[192,1024]{1,0:T(8,128)(2,1)}, bf16[192,1024]{1,0:T(8,128)(2,1)S(1)}, u32[]{:S(2)}, u32[]{:S(2)}) collective-permute-start(bf16[192,1024]{1,0:T(8,128)(2,1)} %get-tuple-element.102), channel_id=1, source_target_pairs={{0,12},{4,8},{8,4},{12,0},{1,13},{5,9},{9,5},{13,1},{2,14},{6,10},... | collective-permute-start | bytes 1179656 | tf_op jit(solution)/shard_map/ppermute | solution.py:903
  184.8 0.7 copy-start.1
  184.8 0.8 copy-start.2
  184.8 1.0 copy-start.3
  247.6 5.8 %collective-permute-start.9 = (bf16[1024,768]{1,0:T(8,128)(2,1)}, bf16[1024,768]{1,0:T(8,128)(2,1)S(1)}, u32[]{:S(2)}, u32[]{:S(2)}) collective-permute-start(bf16[1024,768]{1,0:T(8,128)(2,1)} %get-tuple-element.116), channel_id=1, source_target_pairs={{0,4},{4,0},{8,12},{12,8},{1,5},{5,1},{9,13},{13,9},{2,6},{6,2},{1... | collective-permute-start | bytes 4718600 | tf_op jit(solution)/shard_map/ppermute | solution.py:903
  248.7 28.1 %collective-permute-start.12 = (bf16[1024,768]{1,0:T(8,128)(2,1)}, bf16[1024,768]{1,0:T(8,128)(2,1)}, u32[]{:S(2)}, u32[]{:S(2)}) collective-permute-start(bf16[1024,768]{1,0:T(8,128)(2,1)} %get-tuple-element.118), channel_id=1, source_target_pairs={{0,4},{4,0},{8,12},{12,8},{1,5},{5,1},{9,13},{13,9},{2,6},{6,2},{1... | collective-permute-start | bytes 4718600 | tf_op jit(solution)/shard_map/ppermute | solution.py:903
  256.1 16.2 %collective-permute-start.10 = (bf16[192,768]{1,0:T(8,128)(2,1)}, bf16[192,768]{1,0:T(8,128)(2,1)S(1)}, u32[]{:S(2)}, u32[]{:S(2)}) collective-permute-start(bf16[192,768]{1,0:T(8,128)(2,1)} %slice.80), channel_id=1, source_target_pairs={{0,8},{4,12},{8,0},{12,4},{1,9},{5,13},{9,1},{13,5},{2,10},{6,14},... | collective-permute-start | bytes 884744 | tf_op jit(solution)/shard_map/ppermute | solution.py:903
  272.3 55.1 %all-to-all-start.1 = ((bf16[32,32,640]{2,1,0:T(8,128)(2,1)}), bf16[32,32,640]{2,1,0:T(8,128)(2,1)}, u32[]{:S(2)}, u32[]{:S(2)}) async-start(bf16[32,32,640]{2,1,0:T(8,128)(2,1)} %get-tuple-element.121), calls=%async_computation.2 | async-start | bytes 2621440 | tf_op jit(solution)/shard_map/all_to_all | solution.py:1025
  276.8 59.4 %reduce-scatter.5.cloned.1.call-start = ((), (), s32[]{:S(2)}) async-start(), calls=%async_computation.5 | async-start | bytes 1720320 | tf_op jit(solution)/shard_map/reduce_scatter | solution.py:1022
  278.7 53.1 %collective-permute-start.11 = (bf16[832,768]{1,0:T(8,128)(2,1)}, bf16[832,768]{1,0:T(8,128)(2,1)S(1)}, u32[]{:S(2)}, u32[]{:S(2)}) collective-permute-start(bf16[832,768]{1,0:T(8,128)(2,1)} %slice.81), channel_id=1, source_target_pairs={{0,8},{4,12},{8,0},{12,4},{1,9},{5,13},{9,1},{13,5},{2,10},{6,14},... | collective-permute-start | bytes 3833864 | tf_op jit(solution)/shard_map/ppermute | solution.py:903
Sparse Core Ops, SparseCore 0:
  12.4 113.2 all-gather.2
  185.0 90.5 reduce-scatter.2
  279.9 47.9 reduce-scatter.4

commit v9 on v7

--- a/solution.py
+++ b/solution.py
@@ -513,23 +513,17 @@
             for h in range(heads)
         ]
         for h in range(0, heads, 2):
-            second = half_columns(wq_ref, s * heads + h + 1, 1) if h + 1 < heads else jnp.zeros((own, PAIR), f32)
+            second = half_columns(wq_ref, s * heads + h + 1, 1) if h + 1 < heads else vec_ref[...].astype(f32)
             pieces.append(two_halves(half_columns(wq_ref, s * heads + h, 0), second))
         piece = jnp.concatenate(pieces, axis=1).astype(bf16)
-        notes = jnp.concatenate([vec_ref[...], jnp.zeros((8, piece.shape[1] - width), bf16)], axis=1) if (
-            piece.shape[1] > width
-        ) else vec_ref[:, 0 : piece.shape[1]]
         for b in range(blocks):
             for i in range(inner):
-                pack_ref[b, s, i, 0:own, :] = piece
-                pack_ref[b, s, i, own : own + 8, :] = notes
+                pack_ref[b, s, i] = piece
     u = up_ref.shape[0]
     rest_ref[0:u, :] = up_ref[...]
     rest_ref[u : 2 * u, :] = down_ref[...]
     rest_ref[2 * u : 2 * u + own, :] = wo_ref[...]
-    row = lax.broadcasted_iota(jnp.int32, (8, 1), 0)
-    block = jnp.where(row == 7, bup_ref[...].astype(f32), vec_ref[...].astype(f32))
-    rest_ref[2 * u + own : 2 * u + own + 8, :] = block.astype(bf16)
+    rest_ref[2 * u + own : 2 * u + own + 8, :] = jnp.broadcast_to(bup_ref[...], (8, width))
 
 
 def packed_weights(w_q, w_k, w_v, w_o, w_up, w_down, b_up, vec, dp_n, seq_n, ffn_n):
@@ -541,18 +535,17 @@
         group = heads * HEAD_DIM
         cols = lambda w: w.reshape(own, seq_n, heads, HEAD_DIM).transpose(1, 0, 2, 3)
         kv = jnp.stack([cols(w_k), cols(w_v)], axis=3).reshape(seq_n, own, 2 * group)
-        piece = jnp.concatenate([kv, cols(w_q).reshape(seq_n, own, group)], axis=2)
-        piece = jnp.pad(piece, ((0, 0), (0, round_up(own, 8) - own), (0, lanes - 3 * group)))
-        notes = jnp.broadcast_to(vec[None, :, :lanes], (seq_n, 8, lanes))
-        piece = jnp.concatenate([piece, notes], axis=1)
+        notes = jnp.broadcast_to(vec[None, :, HEAD_DIM:], (seq_n, own, PAIR - HEAD_DIM))
+        piece = jnp.concatenate([kv, cols(w_q).reshape(seq_n, own, group), notes], axis=2)
+        piece = jnp.pad(piece, ((0, 0), (0, round_up(own, 8) - own), (0, 0)))
         pack = jnp.broadcast_to(piece[None, :, None], (dp_n, seq_n, ffn_n) + piece.shape[1:])
         w_o = jnp.pad(w_o, ((0, round_up(own, 8) - own), (0, 0)))
-        return pack, jnp.concatenate([w_up, w_down, w_o, vec[:7], b_up], axis=0)
+        return pack, jnp.concatenate([w_up, w_down, w_o, jnp.broadcast_to(b_up, (8, width))], axis=0)
     whole = lambda: pl.BlockSpec(memory_space=pltpu.VMEM)
     return pl.pallas_call(
         functools.partial(pack_kernel, seq_n),
         out_shape=(
-            jax.ShapeDtypeStruct((dp_n, seq_n, ffn_n, own + 8, lanes), bf16),
+            jax.ShapeDtypeStruct((dp_n, seq_n, ffn_n, own, lanes), bf16),
             jax.ShapeDtypeStruct((2 * u + own + 8, width), bf16),
         ),
         in_specs=[whole() for _ in range(8)],
@@ -563,10 +556,10 @@
 
 def weights_kernel(chunks, direct, *refs):
     x_refs = refs[:chunks]
-    dq_ref, dkv_ref, out_ref, sums_ref, acc, sum_sc = refs[chunks:]
+    dq_ref, dkv_ref, out_ref, acc, sum_sc = refs[chunks:]
     group = dq_ref.shape[1]
     lanes = dkv_ref.shape[2]
-    full = acc.shape[0]
+    full, width = acc.shape
     x = jnp.concatenate([r[...] for r in x_refs], axis=0)
     dkv = jnp.concatenate([dkv_ref[c] for c in range(chunks)], axis=0)
     dq = jnp.concatenate([dq_ref[c] for c in range(chunks)], axis=1)
@@ -584,15 +577,21 @@
 
     @pl.when(pl.program_id(0) == pl.num_programs(0) - 1)
     def _():
+        lane = lax.broadcasted_iota(jnp.int32, (full, width), 0)
+        spot = lax.broadcasted_iota(jnp.int32, (full, width), 1) % group
+        pick_q = lane - lanes == spot
+        pick_v = (lane < lanes) & (lane % PAIR >= BLOCK) & (lane // PAIR * BLOCK + lane % BLOCK == spot)
+        sums = sum_sc[...].astype(bf16)
+        row = lax.broadcasted_iota(jnp.int32, (8, width), 0)
+        of_q = dot_nn(sums, pick_q.astype(f32).astype(bf16))
+        of_v = dot_nn(sums, pick_v.astype(f32).astype(bf16))
+        acc[lanes + group : lanes + group + 8, :] = jnp.where(row == 0, of_q, of_v)
         grad = jnp.transpose(acc[...], (1, 0))
-        sums_ref[...] = sum_sc[...]
         if direct:
-            blocks, per, _ = out_ref.shape
-            own = per - 8
+            blocks, own, _ = out_ref.shape
             grad = grad.reshape(blocks, own, full)
             for b in range(blocks):
-                out_ref[b, 0:own, :] = grad[b].astype(bf16)
-                out_ref[b, own:, :] = sum_sc[...].astype(bf16)
+                out_ref[b] = grad[b].astype(bf16)
         else:
             out_ref[...] = grad.astype(bf16)
 
@@ -604,20 +603,17 @@
     full = lanes + round_up(group, PAIR)
     direct = own % 8 == 0
     tile = 256
-    shape = (devices, own + 8, full) if direct else (width, full)
-    out, sums = pl.pallas_call(
+    shape = (devices, own, full) if direct else (width, full)
+    out = pl.pallas_call(
         functools.partial(weights_kernel, chunks, direct),
         grid=(rows // tile,),
-        out_shape=(jax.ShapeDtypeStruct(shape, bf16), jax.ShapeDtypeStruct((8, full), f32)),
+        out_shape=jax.ShapeDtypeStruct(shape, bf16),
         in_specs=[pl.BlockSpec((tile, width), lambda i: (i, 0)) for _ in range(chunks)]
         + [
             pl.BlockSpec((chunks, group, tile), lambda i: (0, 0, i)),
             pl.BlockSpec((chunks, tile, lanes), lambda i: (0, i, 0)),
         ],
-        out_specs=(
-            pl.BlockSpec(shape, lambda i: (0,) * len(shape), pipeline_mode=pl.Buffered(1)),
-            pl.BlockSpec((8, full), lambda i: (0, 0)),
-        ),
+        out_specs=pl.BlockSpec(shape, lambda i: (0,) * len(shape), pipeline_mode=pl.Buffered(1)),
         scratch_shapes=[pltpu.VMEM((full, width), f32), pltpu.VMEM((8, full), f32)],
         compiler_params=pltpu.CompilerParams(vmem_limit_bytes=VMEM_BYTES),
         cost_estimate=pl.CostEstimate(flops=4_000_000_000, bytes_accessed=12_000_000, transcendentals=0),
@@ -625,7 +621,6 @@
     )(*x, dq, dkv)
     if not direct:
         out = jnp.pad(out.reshape(devices, own, full), ((0, 0), (0, round_up(own, 8) - own), (0, 0)))
-        out = jnp.concatenate([out, jnp.broadcast_to(sums[None].astype(bf16), (devices, 8, full))], axis=1)
     return out
 
 
@@ -639,7 +634,7 @@
             for f in range(ffn_n):
                 total = total + got_ref[d, s, f].astype(f32)
         tot[s] = total
-        sums_ref[s : s + 1, :] = total[per - 8 : per - 7, :]
+        sums_ref[s] = total[:, full - PAIR :]
     for w in range(width // PAIR):
         spots = [((2 * w + i) // heads, (2 * w + i) % heads) for i in range(2)]
         cols = slice(w * PAIR, (w + 1) * PAIR)
@@ -657,7 +652,7 @@
     whole = lambda: pl.BlockSpec(memory_space=pltpu.VMEM)
     return pl.pallas_call(
         functools.partial(unpack_kernel, own),
-        out_shape=(jax.ShapeDtypeStruct((own, width), f32),) * 3 + (jax.ShapeDtypeStruct((seq_n, full), f32),),
+        out_shape=(jax.ShapeDtypeStruct((own, width), f32),) * 3 + (jax.ShapeDtypeStruct((seq_n, per, PAIR), f32),),
         in_specs=[whole()],
         out_specs=tuple(whole() for _ in range(4)),
         scratch_shapes=[pltpu.VMEM((seq_n, per, full), f32)],
@@ -925,8 +920,8 @@
         bit = k & -k
         near[k] = flip_send(features if bit == k else near[k ^ bit], "seq", bit)
 
-    vec = jnp.stack([b_output, b_down, gain_attn, shift_attn, gain_ffn, shift_ffn, b_query, b_value])
-    vec = jnp.pad(vec, ((0, 0), (0, width - own)))
+    vec = jnp.stack([b_output, b_down, gain_attn, shift_attn, gain_ffn, shift_ffn, b_query, b_value], axis=1)
+    vec = jnp.pad(vec, ((0, 0), (HEAD_DIM, PAIR - HEAD_DIM - 8)))
     seg = segment_ids[0].reshape(seq_n, rows)
     rand = random_blocks.reshape(-1)
     pack, rest = packed_weights(
@@ -935,13 +930,13 @@
     lanes = pack.shape[4]
     pack, seg, rand = lax.optimization_barrier((pack, seg, rand))
     pack = lax.all_to_all(
-        pack.reshape(devices, own_pad + 8, lanes), ALL, split_axis=0, concat_axis=0, tiled=True
+        pack.reshape(devices, own_pad, lanes), ALL, split_axis=0, concat_axis=0, tiled=True
     )
     rest = lax.all_gather(rest, ALL, axis=0, tiled=False)
     w_own = pack[:, :own].reshape(width, lanes)
     share = devices // seq_n
-    biases = lax.dynamic_slice(pack, (share * me, own_pad + 6, 0), (share, 2, own))
-    biases = biases.transpose(1, 0, 2).reshape(2, group).astype(f32)
+    vecs = w_own[:, lanes - HEAD_DIM : lanes - HEAD_DIM + 8].astype(f32).T
+    biases = lax.dynamic_slice(vecs, (6, me * group), (2, group))
     by_head = biases[1].reshape(heads, 1, HEAD_DIM)
     b_kv = jnp.concatenate([jnp.zeros_like(by_head), by_head], axis=1).reshape(1, heads * PAIR)
 
@@ -962,7 +957,6 @@
     rest = rest.reshape(outer, ffn_n, rest.shape[1], width)
     w_o = rest[:, :, at : at + own].reshape(width, width)
     bias_up = rest[0, :, at + own_pad + 7].astype(f32)
-    vecs = pack[:, own_pad:, :own].transpose(1, 0, 2).reshape(8, width).astype(f32)
     direct = up_rows % 16 == 0 and own % 8 == 0 and outer % seq_n == 0 and (outer // seq_n) * ffn_n * own == group
     if not direct:
         rest = rest[:, :, :at].reshape(outer, ffn_n, 2, up_rows, width).transpose(1, 2, 0, 3, 4)
@@ -1035,11 +1029,10 @@
     out_bias_up = notes[0]
     out_vecs = lax.dynamic_slice(notes, (1, here * own), (6, own))
     out_query, out_key, out_value, col_sums = unpacked_gradients(
-        grad_w.reshape(dp_n, seq_n, ffn_n, own_pad + 8, lanes), own, width
+        grad_w.reshape(dp_n, seq_n, ffn_n, own_pad, lanes), own, width
     )
-    row = lax.dynamic_index_in_dim(col_sums, here // share, keepdims=False)
-    row = jnp.stack([row[heads * PAIR : heads * PAIR + group], row[: heads * PAIR].reshape(heads, 2, HEAD_DIM)[:, 1].reshape(group)])
-    out_b = lax.dynamic_slice(row, (0, here % share * own), (2, own))
+    col = lax.dynamic_index_in_dim(col_sums, here // share, keepdims=False)[:own, HEAD_DIM : HEAD_DIM + 2]
+    out_b = [col[:, 0], col[:, 1]]
     return (
         out[None],
         grad_features[None],

time: 335 us -> 342 us (1.021)
  waiting for transfers between devices: 102 us -> 109 us
    all_to_all x1, waiting for transfers between devices: 20.5 us -> 39.1 us  [shards(): lax.all_to_all(grad_w, ALL, split_axis=0, concat_axis=0, tiled=True)]
    ppermute x13, waiting for transfers between devices: 77.5 us -> 62 us  [flip_send(): return lax.ppermute(array, axis, [(i, i ^ bits) for i in range(count)])]
  transfers between devices with their start and end apart: 18 -> 18, of which waited for: 6 -> 8; matrix products, arithmetic and copies ran while one was open for 5% -> 5% of each run, Pallas kernels for 39% -> 39%
where the time goes in v9:
time: 342 us; the launch traced here: 339 us
  Pallas kernels  172 us (50%)
  waiting for transfers between devices  109 us (32%)
  starting transfers between devices  20 us (6%)
  local copies, waits for them, and re-layouts  16.2 us (5%)
  between operations  13.9 us (4%)
  other arithmetic  8.15 us (2%)
    pallas_call x1, Pallas kernels, attention_backward(): pl.pallas_call(functools.partial(backward_kernel, heads, chunks), out_sha...  62.3 us
    ppermute x13, waiting for transfers between devices, flip_send(): return lax.ppermute(array, axis, [(i, i ^ bits) for i in range(count)])  62 us
    all_to_all x1, waiting for transfers between devices, shards(): lax.all_to_all(grad_w, ALL, split_axis=0, concat_axis=0, tiled=True)  39.1 us
    pallas_call x1, Pallas kernels, rows_chain(): pl.pallas_call(functools.partial(rows_kernel, parts, blocks, up_rows, own...  37.8 us
    pallas_call x1, Pallas kernels, attention_forward(): pl.pallas_call(functools.partial(forward_kernel, heads, chunks), out_shap...  26.8 us
    pallas_call x1, Pallas kernels, outer_products(): pl.pallas_call(functools.partial(outer_kernel, parts, up_rows, own, apart...  17.6 us
    pallas_call x1, Pallas kernels, attention_near(): pl.pallas_call(functools.partial(near_kernel, heads, chunks), out_shape=(...  11.9 us
    pallas_call x1, Pallas kernels, projection_gradients(): pl.pallas_call(functools.partial(weights_kernel, chunks, direct), grid=(r...  10.1 us
  transfers between devices with their start and end apart: 18, of which 8 were waited for; matrix products, arithmetic and copies ran while one was open for 5% of the time, Pallas kernels for 39%

profile of v9, /device:TPU:0, one launch (start us, length us, event | category | flops | bytes accessed | tf_op | source)
XLA Modules:
  0.0 339.3 jit_solution(5561677876809561301)
XLA Ops:
  10.1 2.2 packed_weights.1
  12.3 3.0 collective-permute-start.1
  17.4 1.4 reduce.11
  19.4 4.9 %all-to-all-start = ((bf16[32,24,640]{2,1,0:T(8,128)(2,1)}), bf16[32,24,640]{2,1,0:T(8,128)(2,1)S(1)}, u32[]{:S(2)}, u32[]{:S(2)}) async-start(bf16[32,24,640]{2,1,0:T(8,128)(2,1)} %bitcast.46), calls=%async_computation | async-start | bytes 1966080 | tf_op jit(solution)/shard_map/all_to_all | solution.py:932
  24.7 44.4 %collective-permute-done.1.refs_2_ = bf16[1024,768]{1,0:T(8,128)(2,1)} collective-permute-done((bf16[1024,768]{1,0:T(8,128)(2,1)}, bf16[1024,768]{1,0:T(8,128)(2,1)}, u32[]{:S(2)}, u32[]{:S(2)}) %collective-permute-start.1) | collective-permute-done | bytes 1572896 | tf_op jit(solution)/shard_map/ppermute | solution.py:898
  69.0 4.8 %all-to-all-done = bf16[32,24,640]{2,1,0:T(8,128)(2,1)S(1)} async-done(((bf16[32,24,640]{2,1,0:T(8,128)(2,1)}), bf16[32,24,640]{2,1,0:T(8,128)(2,1)S(1)}, u32[]{:S(2)}, u32[]{:S(2)}) %all-to-all-start) | async-done | bytes 983072 | tf_op jit(solution)/shard_map/all_to_all | solution.py:932
  75.6 26.8 %attention_forward.1 = (bf16[192,1024]{1,0:T(8,128)(2,1)}, bf16[192,1024]{1,0:T(8,128)(2,1)}, f32[3,16,128]{2,1,0:T(8,128)}, f32[3,128]{1,0:T(4,128)}, f32[3,64,...) custom-call(s32[1]{0:T(128)} %bitcast.me_ref, ...), custom_call_target="tpu_custom_call" | custom-call | flops 10000000000 | bytes 16000000 | tf_op jit(solution)/shard_map/attention_forward/pallas_call | solution.py:248
  103.2 11.9 %attention_near.1 = (bf16[192,1024]{1,0:T(8,128)(2,1)}, bf16[192,1024]{1,0:T(8,128)(2,1)}, f32[3,16,128]{2,1,0:T(8,128)}) custom-call(s32[1]{0:T(128)} %bitcast.me_ref, s32[576]{0:T(1024)} %reshape.55.rand_ref, s32[1,2]{1,0:T(1,128)} %glob_ref.5, bf16[4160,384]{1,0:T(8,128)(2,1)} %get-tuple-element.80.k_ref.refs_4_, ...), custom_call_target="tpu_custom_call" | custom-call | flops 6000000000 | bytes 9000000 | tf_op jit(solution)/shard_map/attention_near/pallas_call | solution.py:294
  115.1 1.4 collective-permute-start.5
  117.2 7.0 %collective-permute-done.4.refs_3_ = bf16[192,1024]{1,0:T(8,128)(2,1)S(1)} collective-permute-done((bf16[192,1024]{1,0:T(8,128)(2,1)}, bf16[192,1024]{1,0:T(8,128)(2,1)S(1)}, u32[]{:S(2)}, u32[]{:S(2)}) %collective-permute-start.4) | collective-permute-done | bytes 393248 | tf_op jit(solution)/shard_map/ppermute | solution.py:898
  124.3 1.6 all-gather.3.cloned.1.call-done
  127.1 37.8 %rows_chain.1 = (bf16[1024,768]{1,0:T(8,128)(2,1)}, f32[1024,768]{1,0:T(8,128)}, bf16[4,1024,768]{2,1,0:T(8,128)(2,1)}, bf16[4,1024,768]{2,1,0:T(8,128)(2,1)}, b...) custom-call(s32[1]{0:T(128)} %bitcast.me_ref, ...), custom_call_target="tpu_custom_call" | custom-call | flops 22000001024 | bytes 40000000 | tf_op jit(solution)/shard_map/rows_chain/pallas_call | solution.py:775
  165.1 1.7 collective-permute-start.8
  166.8 17.6 %outer_products.1 = bf16[8,4,224,768]{3,2,1,0:T(8,128)(2,1)} custom-call(s32[1]{0:T(128)} %bitcast.me_ref, bf16[192,1024]{1,0:T(8,128)(2,1)} %get-tuple-element.86.refs_0_, bf16[192,1024]{1,0:T(8,128)(2,1)} %copy-done.7, bf16[192,1024]{1,0:T(8,128)(2,1)} %copy-done.3, bf16[192,1024]{1,0:T(8,128)(2,1)} %copy-done.4, ...), custom_call_target="tpu_custom_call" | custom-call | flops 11000000512 | bytes 28000000 | tf_op jit(solution)/shard_map/outer_products/pallas_call | solution.py:849
  185.5 62.3 %attention_backward.1 = (bf16[4,192,1024]{2,1,0:T(8,128)(2,1)}, bf16[4,1024,384]{2,1,0:T(8,128)(2,1)}, f32[1024,768]{1,0:T(8,128)}, bf16[1024,768]{1,0:T(8,128)(...) custom-call(s32[1]{0:T(128)} %bitcast.me_ref, s32[576]{0:T(1024)} %reshape.55.rand_ref, s32[1,2]{1,0:T(1,128)} %glob_ref.5, ...), custom_call_target="tpu_custom_call" | custom-call | flops 30000001024 | bytes 24000000 | tf_op jit(solution)/shard_map/attention_backward/pallas_call | solution.py:465
  248.1 10.1 %projection_gradients.1 = bf16[32,24,640]{2,1,0:T(8,128)(2,1)} custom-call(bf16[1024,768]{1,0:T(8,128)(2,1)} %bitcast.9.refs_0_.refs_4_, bf16[1024,768]{1,0:T(8,128)(2,1)} %collective-permute-done.refs_1_, bf16[1024,768]{1,0:T(8,128)(2,1)} %collective-permute-done.1.refs_2_, bf16[1024,768]{1,0:T(8,128)(2,1)} %collective-permute-done.2.refs_3_, ...), custom_call_target="tpu_custom_call" | custom-call | flops 4000000000 | bytes 12000000 | tf_op jit(solution)/shard_map/projection_gradients/pallas_call | solution.py:607
  258.2 1.8 add_convert_fusion
  260.1 10.5 %collective-permute-done.10 = bf16[128,768]{1,0:T(8,128)(2,1)S(1)} collective-permute-done((bf16[128,768]{1,0:T(8,128)(2,1)S(1)}, bf16[128,768]{1,0:T(8,128)(2,1)S(1)}, u32[]{:S(2)}, u32[]{:S(2)}) %collective-permute-start.10) | collective-permute-done | bytes 196640 | tf_op jit(solution)/shard_map/ppermute | solution.py:898
  271.7 5.2 %all-to-all-start.1 = ((bf16[32,24,640]{2,1,0:T(8,128)(2,1)}), bf16[32,24,640]{2,1,0:T(8,128)(2,1)S(1)}, u32[]{:S(2)}, u32[]{:S(2)}) async-start(bf16[32,24,640]{2,1,0:T(8,128)(2,1)} %projection_gradients.1), calls=%async_computation.2 | async-start | bytes 1966080 | tf_op jit(solution)/shard_map/all_to_all | solution.py:1022
  278.3 1.7 collective-permute-start.11
  280.0 39.1 %all-to-all-done.1 = bf16[32,24,640]{2,1,0:T(8,128)(2,1)S(1)} async-done(((bf16[32,24,640]{2,1,0:T(8,128)(2,1)}), bf16[32,24,640]{2,1,0:T(8,128)(2,1)S(1)}, u32[]{:S(2)}, u32[]{:S(2)}) %all-to-all-start.1) | async-done | bytes 983072 | tf_op jit(solution)/shard_map/all_to_all | solution.py:1022
  320.0 2.0 unpacked_gradients.1
  323.5 4.8 %add_bitcast_fusion = f32[1,1024,768]{2,1,0:T(8,128)} fusion(bf16[1024,768]{1,0:T(8,128)(2,1)} %collective-permute-done.12, f32[1024,768]{1,0:T(8,128)} %get-tuple-element.111, bf16[896,768]{1,0:T(8,128)(2,1)} %collective-permute-done.11, bf16[128,768]{1,0:T(8,128)(2,1)S(1)} %collective-permute-done.10), kind=kLoop, calls=%fused_computation | loop fusion | flops 5505024 | bytes 9437184 | tf_op jit(solution)/shard_map/broadcast_in_dim | solution.py:1038
  328.3 1.8 finished.1
  (69 shorter events, 19.6 us)
Async XLA Ops:
  7.2 118.7 %all-gather.3.cloned.1.call-start = ((), (), s32[]{:S(2)}) async-start(), calls=%async_computation.6 | async-start | bytes 11354112 | tf_op jit(solution)/shard_map/all_gather | solution.py:935
  12.3 56.8 %collective-permute-start.1 = (bf16[1024,768]{1,0:T(8,128)(2,1)}, bf16[1024,768]{1,0:T(8,128)(2,1)}, u32[]{:S(2)}, u32[]{:S(2)}) collective-permute-start(bf16[1024,768]{1,0:T(8,128)(2,1)} %bitcast.9.refs_0_.refs_4_), channel_id=1, source_target_pairs={{0,8},{4,12},{8,0},{12,4},{1,9},{5,13},{9,1},{13,5},{2,10},{6,14},... | collective-permute-start | bytes 4718600 | tf_op jit(solution)/shard_map/ppermute | solution.py:898
  19.4 54.5 %all-to-all-start = ((bf16[32,24,640]{2,1,0:T(8,128)(2,1)}), bf16[32,24,640]{2,1,0:T(8,128)(2,1)S(1)}, u32[]{:S(2)}, u32[]{:S(2)}) async-start(bf16[32,24,640]{2,1,0:T(8,128)(2,1)} %bitcast.46), calls=%async_computation | async-start | bytes 1966080 | tf_op jit(solution)/shard_map/all_to_all | solution.py:932
  24.3 247.3 %reduce-scatter.3.cloned.1.call-start = ((), (), s32[]{:S(2)}) async-start(), calls=%async_computation.4 | async-start | bytes 12386304 | tf_op jit(solution)/shard_map/reduce_scatter | solution.py:989
  24.4 51.2 %collective-permute-start = (bf16[1024,768]{1,0:T(8,128)(2,1)}, bf16[1024,768]{1,0:T(8,128)(2,1)}, u32[]{:S(2)}, u32[]{:S(2)}) collective-permute-start(bf16[1024,768]{1,0:T(8,128)(2,1)} %bitcast.9.refs_0_.refs_4_), channel_id=1, source_target_pairs={{0,4},{4,0},{8,12},{12,8},{1,5},{5,1},{9,13},{13,9},{2,6},{6,2},{1... | collective-permute-start | bytes 4718600 | tf_op jit(solution)/shard_map/ppermute | solution.py:898
  69.0 6.6 %collective-permute-start.2 = (bf16[1024,768]{1,0:T(8,128)(2,1)}, bf16[1024,768]{1,0:T(8,128)(2,1)}, u32[]{:S(2)}, u32[]{:S(2)}) collective-permute-start(bf16[1024,768]{1,0:T(8,128)(2,1)} %collective-permute-done.1.refs_2_), channel_id=1, source_target_pairs={{0,4},{4,0},{8,12},{12,8},{1,5},{5,1},{9,13},{13,9},{2,6},{6,2},{1... | collective-permute-start | bytes 4718600 | tf_op jit(solution)/shard_map/ppermute | solution.py:898
  73.9 1.7 copy-start.2
  102.4 14.8 %collective-permute-start.3 = (bf16[192,1024]{1,0:T(8,128)(2,1)}, bf16[192,1024]{1,0:T(8,128)(2,1)S(1)}, u32[]{:S(2)}, u32[]{:S(2)}) collective-permute-start(bf16[192,1024]{1,0:T(8,128)(2,1)} %get-tuple-element.78), channel_id=1, source_target_pairs={{0,8},{4,12},{8,0},{12,4},{1,9},{5,13},{9,1},{13,5},{2,10},{6,14},... | collective-permute-start | bytes 1179656 | tf_op jit(solution)/shard_map/ppermute | solution.py:898
  103.0 21.2 %collective-permute-start.4 = (bf16[192,1024]{1,0:T(8,128)(2,1)}, bf16[192,1024]{1,0:T(8,128)(2,1)S(1)}, u32[]{:S(2)}, u32[]{:S(2)}) collective-permute-start(bf16[192,1024]{1,0:T(8,128)(2,1)} %get-tuple-element.79), channel_id=1, source_target_pairs={{0,12},{4,8},{8,4},{12,0},{1,13},{5,9},{9,5},{13,1},{2,14},{6,10},... | collective-permute-start | bytes 1179656 | tf_op jit(solution)/shard_map/ppermute | solution.py:898
  115.1 9.2 %collective-permute-start.5 = (bf16[192,1024]{1,0:T(8,128)(2,1)}, bf16[192,1024]{1,0:T(8,128)(2,1)S(1)}, u32[]{:S(2)}, u32[]{:S(2)}) collective-permute-start(bf16[192,1024]{1,0:T(8,128)(2,1)} %get-tuple-element.87), channel_id=1, source_target_pairs={{0,4},{4,0},{8,12},{12,8},{1,5},{5,1},{9,13},{13,9},{2,6},{6,2},{1... | collective-permute-start | bytes 1179656 | tf_op jit(solution)/shard_map/ppermute | solution.py:898
  117.2 9.9 %copy-start.3 = (bf16[192,1024]{1,0:T(8,128)(2,1)}, bf16[192,1024]{1,0:T(8,128)(2,1)S(1)}, u32[]{:S(2)}) copy-start(bf16[192,1024]{1,0:T(8,128)(2,1)S(1)} %collective-permute-done.3.refs_2_) | copy-start | bytes 1179652
  124.2 2.8 copy-start.4
  124.3 2.8 copy-start.7
  164.9 19.6 %collective-permute-start.6 = (bf16[192,1024]{1,0:T(8,128)(2,1)}, bf16[192,1024]{1,0:T(8,128)(2,1)S(1)}, u32[]{:S(2)}, u32[]{:S(2)}) collective-permute-start(bf16[192,1024]{1,0:T(8,128)(2,1)} %get-tuple-element.100), channel_id=1, source_target_pairs={{0,4},{4,0},{8,12},{12,8},{1,5},{5,1},{9,13},{13,9},{2,6},{6,2},{1... | collective-permute-start | bytes 1179656 | tf_op jit(solution)/shard_map/ppermute | solution.py:898
  165.1 19.4 %collective-permute-start.7 = (bf16[192,1024]{1,0:T(8,128)(2,1)}, bf16[192,1024]{1,0:T(8,128)(2,1)S(1)}, u32[]{:S(2)}, u32[]{:S(2)}) collective-permute-start(bf16[192,1024]{1,0:T(8,128)(2,1)} %get-tuple-element.101), channel_id=1, source_target_pairs={{0,8},{4,12},{8,0},{12,4},{1,9},{5,13},{9,1},{13,5},{2,10},{6,14},... | collective-permute-start | bytes 1179656 | tf_op jit(solution)/shard_map/ppermute | solution.py:898
  165.1 19.5 %collective-permute-start.8 = (bf16[192,1024]{1,0:T(8,128)(2,1)}, bf16[192,1024]{1,0:T(8,128)(2,1)S(1)}, u32[]{:S(2)}, u32[]{:S(2)}) collective-permute-start(bf16[192,1024]{1,0:T(8,128)(2,1)} %get-tuple-element.102), channel_id=1, source_target_pairs={{0,12},{4,8},{8,4},{12,0},{1,13},{5,9},{9,5},{13,1},{2,14},{6,10},... | collective-permute-start | bytes 1179656 | tf_op jit(solution)/shard_map/ppermute | solution.py:898
  185.5 142.9 %reduce-scatter.5.cloned.1.call-start = ((), (), s32[]{:S(2)}) async-start(), calls=%async_computation.5 | async-start | bytes 1720320 | tf_op jit(solution)/shard_map/reduce_scatter | solution.py:1015
  247.7 10.4 %collective-permute-start.9 = (bf16[1024,768]{1,0:T(8,128)(2,1)}, bf16[1024,768]{1,0:T(8,128)(2,1)}, u32[]{:S(2)}, u32[]{:S(2)}) collective-permute-start(bf16[1024,768]{1,0:T(8,128)(2,1)} %get-tuple-element.116), channel_id=1, source_target_pairs={{0,4},{4,0},{8,12},{12,8},{1,5},{5,1},{9,13},{13,9},{2,6},{6,2},{1... | collective-permute-start | bytes 4718600 | tf_op jit(solution)/shard_map/ppermute | solution.py:898
  248.1 10.1 %copy-start.1 = (bf16[1024,768]{1,0:T(8,128)(2,1)S(1)}, bf16[1024,768]{1,0:T(8,128)(2,1)}, u32[]{:S(2)}) copy-start(bf16[1024,768]{1,0:T(8,128)(2,1)} %get-tuple-element.115) | copy-start | bytes 4718596
  260.0 10.6 %collective-permute-start.10 = (bf16[128,768]{1,0:T(8,128)(2,1)S(1)}, bf16[128,768]{1,0:T(8,128)(2,1)S(1)}, u32[]{:S(2)}, u32[]{:S(2)}) collective-permute-start(bf16[128,768]{1,0:T(8,128)(2,1)S(1)} %slice.48), channel_id=1, source_target_pairs={{0,8},{4,12},{8,0},{12,4},{1,9},{5,13},{9,1},{13,5},{2,10},{6,14},... | collective-permute-start | bytes 589832 | tf_op jit(solution)/shard_map/ppermute | solution.py:898
  271.7 47.4 %all-to-all-start.1 = ((bf16[32,24,640]{2,1,0:T(8,128)(2,1)}), bf16[32,24,640]{2,1,0:T(8,128)(2,1)S(1)}, u32[]{:S(2)}, u32[]{:S(2)}) async-start(bf16[32,24,640]{2,1,0:T(8,128)(2,1)} %projection_gradients.1), calls=%async_computation.2 | async-start | bytes 1966080 | tf_op jit(solution)/shard_map/all_to_all | solution.py:1022
  276.8 46.6 %collective-permute-start.12 = (bf16[1024,768]{1,0:T(8,128)(2,1)}, bf16[1024,768]{1,0:T(8,128)(2,1)}, u32[]{:S(2)}, u32[]{:S(2)}) collective-permute-start(bf16[1024,768]{1,0:T(8,128)(2,1)} %get-tuple-element.120), channel_id=1, source_target_pairs={{0,4},{4,0},{8,12},{12,8},{1,5},{5,1},{9,13},{13,9},{2,6},{6,2},{1... | collective-permute-start | bytes 4718600 | tf_op jit(solution)/shard_map/ppermute | solution.py:898
  278.3 45.2 %collective-permute-start.11 = (bf16[896,768]{1,0:T(8,128)(2,1)}, bf16[896,768]{1,0:T(8,128)(2,1)}, u32[]{:S(2)}, u32[]{:S(2)}) collective-permute-start(bf16[896,768]{1,0:T(8,128)(2,1)} %slice.49), channel_id=1, source_target_pairs={{0,8},{4,12},{8,0},{12,4},{1,9},{5,13},{9,1},{13,5},{2,10},{6,14},... | collective-permute-start | bytes 4128776 | tf_op jit(solution)/shard_map/ppermute | solution.py:898
  319.1 1.0 copy-start
  (3 other events, 2.6 us)
Sparse Core Ops, SparseCore 0:
  12.4 113.4 all-gather.2
  184.7 86.9 reduce-scatter.2
  274.0 48.5 reduce-scatter.4

commit v10 on v9

--- a/solution.py
+++ b/solution.py
@@ -657,6 +657,7 @@
         out_specs=tuple(whole() for _ in range(4)),
         scratch_shapes=[pltpu.VMEM((seq_n, per, full), f32)],
         compiler_params=pltpu.CompilerParams(vmem_limit_bytes=VMEM_BYTES),
+        cost_estimate=pl.CostEstimate(flops=40_000_000_000, bytes_accessed=3_000_000, transcendentals=0),
         name="unpacked_gradients",
     )(got)
 
@@ -1010,12 +1011,8 @@
     grad_w, apart = lax.optimization_barrier((grad_w, apart))
     part = [None] + part
     bit = seq_n // 2
-    first = flip_send(part[bit][: rows // 8], "seq", bit)
-    first, total = lax.optimization_barrier((first, total))
+    part[bit], total = lax.optimization_barrier((part[bit], total))
     total = lax.psum_scatter(total, "ffn", scatter_dimension=0, tiled=True)
-    second = flip_send(part[bit][rows // 8 :], "seq", bit)
-    grad_features = grad_features + jnp.concatenate([first, second], axis=0).astype(f32)
-    bit //= 2
     while bit:
         grad_features = grad_features + flip_send(part[bit], "seq", bit).astype(f32)
         bit //= 2

time: 342 us -> 328 us (0.959)
  waiting for transfers between devices: 109 us -> 99.9 us
    all_to_all x1, waiting for transfers between devices: 39.1 us -> 33.8 us  [shards(): lax.all_to_all(grad_w, ALL, split_axis=0, concat_axis=0, tiled=True)]
    ppermute x13 -> x12, waiting for transfers between devices: 62 us -> 56.8 us  [flip_send(): return lax.ppermute(array, axis, [(i, i ^ bits) for i in range(count)])]
    ppermute x13 -> x12, starting transfers between devices: 9.83 us -> 9.39 us  [flip_send(): return lax.ppermute(array, axis, [(i, i ^ bits) for i in range(count)])]
  transfers between devices with their start and end apart: 18 -> 17, of which waited for: 8 -> 7; matrix products, arithmetic and copies ran while one was open for 5% -> 5% of each run, Pallas kernels for 39% -> 40%
where the time goes in v10:
time: 328 us; the launch traced here: 327 us
  Pallas kernels  173 us (53%)
  waiting for transfers between devices  99.9 us (30%)
  starting transfers between devices  17.8 us (5%)
  local copies, waits for them, and re-layouts  14 us (4%)
  between operations  13.9 us (4%)
  other arithmetic  8.88 us (3%)
    pallas_call x1, Pallas kernels, attention_backward(): pl.pallas_call(functools.partial(backward_kernel, heads, chunks), out_sha...  62.4 us
    ppermute x12, waiting for transfers between devices, flip_send(): return lax.ppermute(array, axis, [(i, i ^ bits) for i in range(count)])  56.8 us
    pallas_call x1, Pallas kernels, rows_chain(): pl.pallas_call(functools.partial(rows_kernel, parts, blocks, up_rows, own...  37.8 us
    all_to_all x1, waiting for transfers between devices, shards(): lax.all_to_all(grad_w, ALL, split_axis=0, concat_axis=0, tiled=True)  33.8 us
    pallas_call x1, Pallas kernels, attention_forward(): pl.pallas_call(functools.partial(forward_kernel, heads, chunks), out_shap...  26.8 us
    pallas_call x1, Pallas kernels, outer_products(): pl.pallas_call(functools.partial(outer_kernel, parts, up_rows, own, apart...  17.6 us
    pallas_call x1, Pallas kernels, attention_near(): pl.pallas_call(functools.partial(near_kernel, heads, chunks), out_shape=(...  11.9 us
    pallas_call x1, Pallas kernels, projection_gradients(): pl.pallas_call(functools.partial(weights_kernel, chunks, direct), grid=(r...  10.3 us
  transfers between devices with their start and end apart: 17, of which 7 were waited for; matrix products, arithmetic and copies ran while one was open for 5% of the time, Pallas kernels for 40%

profile of v10, /device:TPU:0, one launch (start us, length us, event | category | flops | bytes accessed | tf_op | source)
XLA Modules:
  0.0 327.4 jit_solution(6401006320017729878)
XLA Ops:
  10.1 2.2 packed_weights.1
  12.3 3.0 collective-permute-start.1
  17.4 1.4 reduce.11
  19.4 4.9 %all-to-all-start = ((bf16[32,24,640]{2,1,0:T(8,128)(2,1)}), bf16[32,24,640]{2,1,0:T(8,128)(2,1)S(1)}, u32[]{:S(2)}, u32[]{:S(2)}) async-start(bf16[32,24,640]{2,1,0:T(8,128)(2,1)} %bitcast.45), calls=%async_computation | async-start | bytes 1966080 | tf_op jit(solution)/shard_map/all_to_all | solution.py:933
  24.7 44.4 %collective-permute-done.1.refs_2_ = bf16[1024,768]{1,0:T(8,128)(2,1)} collective-permute-done((bf16[1024,768]{1,0:T(8,128)(2,1)}, bf16[1024,768]{1,0:T(8,128)(2,1)}, u32[]{:S(2)}, u32[]{:S(2)}) %collective-permute-start.1) | collective-permute-done | bytes 1572896 | tf_op jit(solution)/shard_map/ppermute | solution.py:899
  69.1 4.8 %all-to-all-done = bf16[32,24,640]{2,1,0:T(8,128)(2,1)S(1)} async-done(((bf16[32,24,640]{2,1,0:T(8,128)(2,1)}), bf16[32,24,640]{2,1,0:T(8,128)(2,1)S(1)}, u32[]{:S(2)}, u32[]{:S(2)}) %all-to-all-start) | async-done | bytes 983072 | tf_op jit(solution)/shard_map/all_to_all | solution.py:933
  75.6 26.8 %attention_forward.1 = (bf16[192,1024]{1,0:T(8,128)(2,1)}, bf16[192,1024]{1,0:T(8,128)(2,1)}, f32[3,16,128]{2,1,0:T(8,128)}, f32[3,128]{1,0:T(4,128)}, f32[3,64,...) custom-call(s32[1]{0:T(128)} %bitcast.me_ref, ...), custom_call_target="tpu_custom_call" | custom-call | flops 10000000000 | bytes 16000000 | tf_op jit(solution)/shard_map/attention_forward/pallas_call | solution.py:248
  103.2 11.9 %attention_near.1 = (bf16[192,1024]{1,0:T(8,128)(2,1)}, bf16[192,1024]{1,0:T(8,128)(2,1)}, f32[3,16,128]{2,1,0:T(8,128)}) custom-call(s32[1]{0:T(128)} %bitcast.me_ref, s32[576]{0:T(1024)} %reshape.55.rand_ref, s32[1,2]{1,0:T(1,128)} %glob_ref.5, bf16[4160,384]{1,0:T(8,128)(2,1)} %get-tuple-element.80.k_ref.refs_4_, ...), custom_call_target="tpu_custom_call" | custom-call | flops 6000000000 | bytes 9000000 | tf_op jit(solution)/shard_map/attention_near/pallas_call | solution.py:294
  115.1 1.4 collective-permute-start.5
  117.2 7.0 %collective-permute-done.4.refs_3_ = bf16[192,1024]{1,0:T(8,128)(2,1)S(1)} collective-permute-done((bf16[192,1024]{1,0:T(8,128)(2,1)}, bf16[192,1024]{1,0:T(8,128)(2,1)S(1)}, u32[]{:S(2)}, u32[]{:S(2)}) %collective-permute-start.4) | collective-permute-done | bytes 393248 | tf_op jit(solution)/shard_map/ppermute | solution.py:899
  124.3 1.6 all-gather.3.cloned.1.call-done
  127.1 37.8 %rows_chain.1 = (bf16[1024,768]{1,0:T(8,128)(2,1)}, f32[1024,768]{1,0:T(8,128)}, bf16[4,1024,768]{2,1,0:T(8,128)(2,1)}, bf16[4,1024,768]{2,1,0:T(8,128)(2,1)}, b...) custom-call(s32[1]{0:T(128)} %bitcast.me_ref, ...), custom_call_target="tpu_custom_call" | custom-call | flops 22000001024 | bytes 40000000 | tf_op jit(solution)/shard_map/rows_chain/pallas_call | solution.py:776
  165.1 1.7 collective-permute-start.8
  166.8 17.6 %outer_products.1 = bf16[8,4,224,768]{3,2,1,0:T(8,128)(2,1)} custom-call(s32[1]{0:T(128)} %bitcast.me_ref, bf16[192,1024]{1,0:T(8,128)(2,1)} %get-tuple-element.86.refs_0_, bf16[192,1024]{1,0:T(8,128)(2,1)} %copy-done.6, bf16[192,1024]{1,0:T(8,128)(2,1)} %copy-done.2, bf16[192,1024]{1,0:T(8,128)(2,1)} %copy-done.3, ...), custom_call_target="tpu_custom_call" | custom-call | flops 11000000512 | bytes 28000000 | tf_op jit(solution)/shard_map/outer_products/pallas_call | solution.py:850
  185.5 62.4 %attention_backward.1 = (bf16[4,192,1024]{2,1,0:T(8,128)(2,1)}, bf16[4,1024,384]{2,1,0:T(8,128)(2,1)}, f32[1024,768]{1,0:T(8,128)}, bf16[1024,768]{1,0:T(8,128)(...) custom-call(s32[1]{0:T(128)} %bitcast.me_ref, s32[576]{0:T(1024)} %reshape.55.rand_ref, s32[1,2]{1,0:T(1,128)} %glob_ref.5, ...), custom_call_target="tpu_custom_call" | custom-call | flops 30000001024 | bytes 24000000 | tf_op jit(solution)/shard_map/attention_backward/pallas_call | solution.py:465
  248.3 10.3 %projection_gradients.1 = bf16[32,24,640]{2,1,0:T(8,128)(2,1)} custom-call(bf16[1024,768]{1,0:T(8,128)(2,1)} %bitcast.60, bf16[1024,768]{1,0:T(8,128)(2,1)} %collective-permute-done.refs_1_, bf16[1024,768]{1,0:T(8,128)(2,1)} %collective-permute-done.1.refs_2_, bf16[1024,768]{1,0:T(8,128)(2,1)} %collective-permute-done.2.refs_3_, ...), custom_call_target="tpu_custom_call" | custom-call | flops 4000000000 | bytes 12000000 | tf_op jit(solution)/shard_map/projection_gradients/pallas_call | solution.py:607
  258.7 2.9 add_convert_fusion
  261.6 3.4 %all-to-all-start.1 = ((bf16[32,24,640]{2,1,0:T(8,128)(2,1)}), bf16[32,24,640]{2,1,0:T(8,128)(2,1)}, u32[]{:S(2)}, u32[]{:S(2)}) async-start(bf16[32,24,640]{2,1,0:T(8,128)(2,1)} %projection_gradients.1), calls=%async_computation.2 | async-start | bytes 1966080 | tf_op jit(solution)/shard_map/all_to_all | solution.py:1019
  265.2 2.8 reduce-scatter.3.cloned.1.call-done
  269.4 33.8 %all-to-all-done.1 = bf16[32,24,640]{2,1,0:T(8,128)(2,1)} async-done(((bf16[32,24,640]{2,1,0:T(8,128)(2,1)}), bf16[32,24,640]{2,1,0:T(8,128)(2,1)}, u32[]{:S(2)}, u32[]{:S(2)}) %all-to-all-start.1) | async-done | bytes 983072 | tf_op jit(solution)/shard_map/all_to_all | solution.py:1019
  303.2 2.0 unpacked_gradients.1
  306.6 5.4 %collective-permute-done.10 = bf16[1024,768]{1,0:T(8,128)(2,1)} collective-permute-done((bf16[1024,768]{1,0:T(8,128)(2,1)}, bf16[1024,768]{1,0:T(8,128)(2,1)}, u32[]{:S(2)}, u32[]{:S(2)}) %collective-permute-start.10) | collective-permute-done | bytes 1572896 | tf_op jit(solution)/shard_map/ppermute | solution.py:899
  312.0 4.4 %add_bitcast_fusion = f32[1,1024,768]{2,1,0:T(8,128)} fusion(bf16[1024,768]{1,0:T(8,128)(2,1)S(1)} %collective-permute-done.11, f32[1024,768]{1,0:T(8,128)} %get-tuple-element.111, bf16[1024,768]{1,0:T(8,128)(2,1)} %collective-permute-done.10), kind=kLoop, calls=%fused_computation | loop fusion | flops 3145728 | bytes 9437184 | tf_op jit(solution)/shard_map/broadcast_in_dim | solution.py:1035
  316.4 1.8 finished.1
  (63 shorter events, 17.7 us)
Async XLA Ops:
  7.2 118.7 %all-gather.3.cloned.1.call-start = ((), (), s32[]{:S(2)}) async-start(), calls=%async_computation.6 | async-start | bytes 11354112 | tf_op jit(solution)/shard_map/all_gather | solution.py:936
  12.3 56.8 %collective-permute-start.1 = (bf16[1024,768]{1,0:T(8,128)(2,1)}, bf16[1024,768]{1,0:T(8,128)(2,1)}, u32[]{:S(2)}, u32[]{:S(2)}) collective-permute-start(bf16[1024,768]{1,0:T(8,128)(2,1)} %bitcast.56), channel_id=1, source_target_pairs={{0,8},{4,12},{8,0},{12,4},{1,9},{5,13},{9,1},{13,5},{2,10},{6,14},... | collective-permute-start | bytes 4718600 | tf_op jit(solution)/shard_map/ppermute | solution.py:899
  19.4 54.5 %all-to-all-start = ((bf16[32,24,640]{2,1,0:T(8,128)(2,1)}), bf16[32,24,640]{2,1,0:T(8,128)(2,1)S(1)}, u32[]{:S(2)}, u32[]{:S(2)}) async-start(bf16[32,24,640]{2,1,0:T(8,128)(2,1)} %bitcast.45), calls=%async_computation | async-start | bytes 1966080 | tf_op jit(solution)/shard_map/all_to_all | solution.py:933
  24.3 243.7 %reduce-scatter.3.cloned.1.call-start = ((), (), s32[]{:S(2)}) async-start(), calls=%async_computation.4 | async-start | bytes 12386304 | tf_op jit(solution)/shard_map/reduce_scatter | solution.py:990
  24.4 51.2 %collective-permute-start = (bf16[1024,768]{1,0:T(8,128)(2,1)}, bf16[1024,768]{1,0:T(8,128)(2,1)}, u32[]{:S(2)}, u32[]{:S(2)}) collective-permute-start(bf16[1024,768]{1,0:T(8,128)(2,1)} %bitcast.57), channel_id=1, source_target_pairs={{0,4},{4,0},{8,12},{12,8},{1,5},{5,1},{9,13},{13,9},{2,6},{6,2},{1... | collective-permute-start | bytes 4718600 | tf_op jit(solution)/shard_map/ppermute | solution.py:899
  69.1 6.6 %collective-permute-start.2 = (bf16[1024,768]{1,0:T(8,128)(2,1)}, bf16[1024,768]{1,0:T(8,128)(2,1)}, u32[]{:S(2)}, u32[]{:S(2)}) collective-permute-start(bf16[1024,768]{1,0:T(8,128)(2,1)} %collective-permute-done.1.refs_2_), channel_id=1, source_target_pairs={{0,4},{4,0},{8,12},{12,8},{1,5},{5,1},{9,13},{13,9},{2,6},{6,2},{1... | collective-permute-start | bytes 4718600 | tf_op jit(solution)/shard_map/ppermute | solution.py:899
  73.9 1.7 copy-start.1
  102.4 14.8 %collective-permute-start.3 = (bf16[192,1024]{1,0:T(8,128)(2,1)}, bf16[192,1024]{1,0:T(8,128)(2,1)S(1)}, u32[]{:S(2)}, u32[]{:S(2)}) collective-permute-start(bf16[192,1024]{1,0:T(8,128)(2,1)} %get-tuple-element.78), channel_id=1, source_target_pairs={{0,8},{4,12},{8,0},{12,4},{1,9},{5,13},{9,1},{13,5},{2,10},{6,14},... | collective-permute-start | bytes 1179656 | tf_op jit(solution)/shard_map/ppermute | solution.py:899
  103.0 21.2 %collective-permute-start.4 = (bf16[192,1024]{1,0:T(8,128)(2,1)}, bf16[192,1024]{1,0:T(8,128)(2,1)S(1)}, u32[]{:S(2)}, u32[]{:S(2)}) collective-permute-start(bf16[192,1024]{1,0:T(8,128)(2,1)} %get-tuple-element.79), channel_id=1, source_target_pairs={{0,12},{4,8},{8,4},{12,0},{1,13},{5,9},{9,5},{13,1},{2,14},{6,10},... | collective-permute-start | bytes 1179656 | tf_op jit(solution)/shard_map/ppermute | solution.py:899
  115.1 9.2 %collective-permute-start.5 = (bf16[192,1024]{1,0:T(8,128)(2,1)}, bf16[192,1024]{1,0:T(8,128)(2,1)S(1)}, u32[]{:S(2)}, u32[]{:S(2)}) collective-permute-start(bf16[192,1024]{1,0:T(8,128)(2,1)} %get-tuple-element.87), channel_id=1, source_target_pairs={{0,4},{4,0},{8,12},{12,8},{1,5},{5,1},{9,13},{13,9},{2,6},{6,2},{1... | collective-permute-start | bytes 1179656 | tf_op jit(solution)/shard_map/ppermute | solution.py:899
  117.2 9.9 %copy-start.2 = (bf16[192,1024]{1,0:T(8,128)(2,1)}, bf16[192,1024]{1,0:T(8,128)(2,1)S(1)}, u32[]{:S(2)}) copy-start(bf16[192,1024]{1,0:T(8,128)(2,1)S(1)} %collective-permute-done.3.refs_2_) | copy-start | bytes 1179652
  124.2 2.8 copy-start.3
  124.3 2.8 copy-start.6
  164.8 19.6 %collective-permute-start.6 = (bf16[192,1024]{1,0:T(8,128)(2,1)}, bf16[192,1024]{1,0:T(8,128)(2,1)S(1)}, u32[]{:S(2)}, u32[]{:S(2)}) collective-permute-start(bf16[192,1024]{1,0:T(8,128)(2,1)} %get-tuple-element.100), channel_id=1, source_target_pairs={{0,4},{4,0},{8,12},{12,8},{1,5},{5,1},{9,13},{13,9},{2,6},{6,2},{1... | collective-permute-start | bytes 1179656 | tf_op jit(solution)/shard_map/ppermute | solution.py:899
  165.1 19.3 %collective-permute-start.7 = (bf16[192,1024]{1,0:T(8,128)(2,1)}, bf16[192,1024]{1,0:T(8,128)(2,1)S(1)}, u32[]{:S(2)}, u32[]{:S(2)}) collective-permute-start(bf16[192,1024]{1,0:T(8,128)(2,1)} %get-tuple-element.101), channel_id=1, source_target_pairs={{0,8},{4,12},{8,0},{12,4},{1,9},{5,13},{9,1},{13,5},{2,10},{6,14},... | collective-permute-start | bytes 1179656 | tf_op jit(solution)/shard_map/ppermute | solution.py:899
  165.1 19.4 %collective-permute-start.8 = (bf16[192,1024]{1,0:T(8,128)(2,1)}, bf16[192,1024]{1,0:T(8,128)(2,1)S(1)}, u32[]{:S(2)}, u32[]{:S(2)}) collective-permute-start(bf16[192,1024]{1,0:T(8,128)(2,1)} %get-tuple-element.102), channel_id=1, source_target_pairs={{0,12},{4,8},{8,4},{12,0},{1,13},{5,9},{9,5},{13,1},{2,14},{6,10},... | collective-permute-start | bytes 1179656 | tf_op jit(solution)/shard_map/ppermute | solution.py:899
  184.4 0.9 copy-start.5
  184.5 1.0 copy-start.7
  247.9 10.8 %collective-permute-start.9 = (bf16[1024,768]{1,0:T(8,128)(2,1)}, bf16[1024,768]{1,0:T(8,128)(2,1)}, u32[]{:S(2)}, u32[]{:S(2)}) collective-permute-start(bf16[1024,768]{1,0:T(8,128)(2,1)} %get-tuple-element.116), channel_id=1, source_target_pairs={{0,4},{4,0},{8,12},{12,8},{1,5},{5,1},{9,13},{13,9},{2,6},{6,2},{1... | collective-permute-start | bytes 4718600 | tf_op jit(solution)/shard_map/ppermute | solution.py:899
  248.3 10.3 %copy-start = (bf16[1024,768]{1,0:T(8,128)(2,1)S(1)}, bf16[1024,768]{1,0:T(8,128)(2,1)}, u32[]{:S(2)}) copy-start(bf16[1024,768]{1,0:T(8,128)(2,1)} %get-tuple-element.115) | copy-start | bytes 4718596
  261.6 41.6 %all-to-all-start.1 = ((bf16[32,24,640]{2,1,0:T(8,128)(2,1)}), bf16[32,24,640]{2,1,0:T(8,128)(2,1)}, u32[]{:S(2)}, u32[]{:S(2)}) async-start(bf16[32,24,640]{2,1,0:T(8,128)(2,1)} %projection_gradients.1), calls=%async_computation.2 | async-start | bytes 1966080 | tf_op jit(solution)/shard_map/all_to_all | solution.py:1019
  265.0 51.5 %reduce-scatter.5.cloned.1.call-start = ((), (), s32[]{:S(2)}) async-start(), calls=%async_computation.5 | async-start | bytes 1720320 | tf_op jit(solution)/shard_map/reduce_scatter | solution.py:1015
  265.0 41.6 %collective-permute-start.11 = (bf16[1024,768]{1,0:T(8,128)(2,1)}, bf16[1024,768]{1,0:T(8,128)(2,1)S(1)}, u32[]{:S(2)}, u32[]{:S(2)}) collective-permute-start(bf16[1024,768]{1,0:T(8,128)(2,1)} %get-tuple-element.120), channel_id=1, source_target_pairs={{0,4},{4,0},{8,12},{12,8},{1,5},{5,1},{9,13},{13,9},{2,6},{6,2},{1... | collective-permute-start | bytes 4718600 | tf_op jit(solution)/shard_map/ppermute | solution.py:899
  268.0 44.0 %collective-permute-start.10 = (bf16[1024,768]{1,0:T(8,128)(2,1)}, bf16[1024,768]{1,0:T(8,128)(2,1)}, u32[]{:S(2)}, u32[]{:S(2)}) collective-permute-start(bf16[1024,768]{1,0:T(8,128)(2,1)} %add_convert_fusion), channel_id=1, source_target_pairs={{0,8},{4,12},{8,0},{12,4},{1,9},{5,13},{9,1},{13,5},{2,10},{6,14},... | collective-permute-start | bytes 4718600 | tf_op jit(solution)/shard_map/ppermute | solution.py:899
  (1 other events, 0.8 us)
Sparse Core Ops, SparseCore 0:
  12.4 113.4 all-gather.2
  184.6 83.3 reduce-scatter.2
  270.3 41.4 reduce-scatter.4

commit v11 on v10

--- a/solution.py
+++ b/solution.py
@@ -178,7 +178,9 @@
     seg_ref, w_ref, bkv_ref, bq_ref = refs[chunks : chunks + 4]
     far = chunks // 2
     out_refs = refs[chunks + 4 : chunks + 4 + far]
-    lse_ref, lseg_ref, glob_ctx_ref, k_sc, v_sc, q_sc, mask_sc, s_sc, out_ref, seg_sc = refs[chunks + 4 + far :]
+    lse_ref, lseg_ref, glob_ctx_ref = refs[chunks + 4 + far : chunks + 7 + far]
+    saved_refs = refs[chunks + 7 + far : chunks + 11 + far]
+    s_sc, out_ref, seg_sc, k_sc, v_sc, q_sc, mask_sc, sems = refs[chunks + 11 + far :]
     rows = x_refs[0].shape[0]
     length = rows * chunks
     per_chunk = length // PAIR // chunks
@@ -200,6 +202,12 @@
     null_lane = lax.broadcasted_iota(jnp.int32, (BLOCK, heads * PAIR), 1) % PAIR
     k_sc[pl.ds(length, BLOCK), :] = (null_lane == BLOCK + 16).astype(f32).astype(bf16)
     v_sc[pl.ds(length, BLOCK), :] = jnp.zeros((BLOCK, heads * PAIR), bf16)
+    saves = [
+        pltpu.make_async_copy(src, dst, sems.at[i])
+        for i, (src, dst) in enumerate(zip((k_sc, v_sc, q_sc, mask_sc), saved_refs))
+    ]
+    for save in saves:
+        save.start()
     sparse_forward(heads, far, chunks, per_chunk, rand_ref, glob_ref, flip, k_sc, v_sc, q_sc, mask_sc, out_ref, lse_ref)
 
     step = 512
@@ -236,6 +244,8 @@
         lseg_ref[h : h + 1, :] = peaks[h] + jnp.log(total)
     for c in range(far):
         out_refs[c][...] = out_ref[c]
+    for save in saves:
+        save.wait()
 
 
 def attention_forward(me, rand, glob, x, seg, w, b_kv, b_q):
@@ -258,11 +268,16 @@
             jax.ShapeDtypeStruct((BLOCK, length), bf16),
         ),
         in_specs=[pl.BlockSpec(memory_space=pltpu.SMEM)] * 3 + [whole() for _ in range(chunks + 4)],
-        out_specs=tuple(whole() for _ in range(far + 7)),
+        out_specs=tuple([whole() for _ in range(far + 3)] + [pl.BlockSpec(memory_space=pl.ANY)] * 4),
         scratch_shapes=[
             pltpu.VMEM((heads, length, PAIR), f32),
             pltpu.VMEM((far, heads * HEAD_DIM, rows), bf16),
             pltpu.VMEM((chunks, rows), jnp.int32),
+            pltpu.VMEM((length + BLOCK, heads * PAIR), bf16),
+            pltpu.VMEM((length + BLOCK, heads * PAIR), bf16),
+            pltpu.VMEM((heads * HEAD_DIM, length), bf16),
+            pltpu.VMEM((BLOCK, length), bf16),
+            pltpu.SemaphoreType.DMA((4,)),
         ],
         compiler_params=pltpu.CompilerParams(vmem_limit_bytes=VMEM_BYTES),
         cost_estimate=pl.CostEstimate(flops=10_000_000_000, bytes_accessed=16_000_000, transcendentals=6_000_000),
@@ -307,10 +322,12 @@
 
 def backward_kernel(heads, chunks, me_ref, rand_ref, glob_ref, *refs):
     do_refs = refs[:chunks]
-    (k_ref, kv_ref, q_ref, mask_ref, seg_ref, lse_near_ref, lse_far_ref, lseg_ref, w_ref, resid_ref, dq_ref, dkv_ref,
+    (k_ref, kv_ref, q_ref, mask_ref, seg_ref, lse_near_ref, lse_far_ref, lseg_ref, w_ref, resid_hbm, dq_hbm, dkv_hbm,
      first_ref) = refs[chunks : chunks + 13]
     part_refs = refs[chunks + 13 : 2 * chunks + 12]
-    do_sc, acc, p_sc, d_sc, seg_sc, line_sc, lse_ref, row_sc = refs[2 * chunks + 12 :]
+    (do_sc, acc, p_sc, d_sc, seg_sc, line_sc, lse_ref, row_sc, resid_ref, dq_ref, dkv_ref, sems) = refs[2 * chunks + 12 :]
+    fetch = pltpu.make_async_copy(resid_hbm, resid_ref, sems.at[0])
+    fetch.start()
     rows = do_refs[0].shape[1]
     length = rows * chunks
     npairs = length // PAIR
@@ -440,6 +457,13 @@
         put_global_columns(dq_ref, head_rows(h), gl, dqs[h][0:BLOCK] * scale, per_chunk, 0, chunks)
         for c in range(chunks):
             dkv_ref[c, :, head_lanes(h)] = acc[h, pl.ds(c * rows, rows), :].astype(bf16)
+    saves = [
+        pltpu.make_async_copy(dq_ref, dq_hbm, sems.at[1]),
+        pltpu.make_async_copy(dkv_ref, dkv_hbm, sems.at[2]),
+    ]
+    for save in saves:
+        save.start()
+    fetch.wait()
     tile = 256
     wq = query_weights(w_ref, heads)
     for c in range(chunks):
@@ -453,6 +477,8 @@
                 first_ref[pl.ds(at, tile), :] = resid_ref[pl.ds(at, tile), :] + got
             else:
                 part_refs[c - 1][pl.ds(at, tile), :] = got.astype(bf16)
+    for save in saves:
+        save.wait()
 
 
 def attention_backward(me, rand, glob, do, k, kv, q, mask, seg, lse_near, lse_far, lseg, w, resid):
@@ -470,8 +496,10 @@
             jax.ShapeDtypeStruct((rows, width), f32),
         )
         + (jax.ShapeDtypeStruct((rows, width), bf16),) * (chunks - 1),
-        in_specs=[pl.BlockSpec(memory_space=pltpu.SMEM)] * 3 + [whole() for _ in range(chunks + 10)],
-        out_specs=tuple(whole() for _ in range(chunks + 2)),
+        in_specs=[pl.BlockSpec(memory_space=pltpu.SMEM)] * 3
+        + [whole() for _ in range(chunks + 9)]
+        + [pl.BlockSpec(memory_space=pl.ANY)],
+        out_specs=tuple([pl.BlockSpec(memory_space=pl.ANY)] * 2 + [whole() for _ in range(chunks)]),
         scratch_shapes=[
             pltpu.VMEM((group, length), bf16),
             pltpu.VMEM((heads, length + BLOCK, PAIR), f32),
@@ -481,6 +509,10 @@
             pltpu.VMEM((length // PAIR, 1, PAIR), f32),
             pltpu.VMEM((heads, length // PAIR, PAIR), f32),
             pltpu.VMEM((chunks, rows), f32),
+            pltpu.VMEM((rows, width), f32),
+            pltpu.VMEM((chunks, group, rows), bf16),
+            pltpu.VMEM((chunks, rows, heads * PAIR), bf16),
+            pltpu.SemaphoreType.DMA((3,)),
         ],
         compiler_params=pltpu.CompilerParams(vmem_limit_bytes=VMEM_BYTES),
         cost_estimate=pl.CostEstimate(flops=30_000_000_000, bytes_accessed=24_000_000, transcendentals=8_000_000),
@@ -503,7 +535,7 @@
     return jnp.where(lane < BLOCK, first, second)
 
 
-def pack_kernel(seq_n, wq_ref, wk_ref, wv_ref, wo_ref, up_ref, down_ref, bup_ref, vec_ref, pack_ref, rest_ref):
+def pack_kernel(seq_n, wq_ref, wk_ref, wv_ref, vec_ref, pack_ref):
     own, width = wq_ref.shape
     heads = width // HEAD_DIM // seq_n
     blocks, inner = pack_ref.shape[0], pack_ref.shape[2]
@@ -519,6 +551,10 @@
         for b in range(blocks):
             for i in range(inner):
                 pack_ref[b, s, i] = piece
+
+
+def rest_kernel(wo_ref, up_ref, down_ref, bup_ref, rest_ref):
+    own, width = wo_ref.shape
     u = up_ref.shape[0]
     rest_ref[0:u, :] = up_ref[...]
     rest_ref[u : 2 * u, :] = down_ref[...]
@@ -542,16 +578,21 @@
         w_o = jnp.pad(w_o, ((0, round_up(own, 8) - own), (0, 0)))
         return pack, jnp.concatenate([w_up, w_down, w_o, jnp.broadcast_to(b_up, (8, width))], axis=0)
     whole = lambda: pl.BlockSpec(memory_space=pltpu.VMEM)
-    return pl.pallas_call(
+    rest = pl.pallas_call(
+        rest_kernel,
+        out_shape=jax.ShapeDtypeStruct((2 * u + own + 8, width), bf16),
+        in_specs=[whole() for _ in range(4)],
+        out_specs=whole(),
+        name="rest_weights",
+    )(w_o, w_up, w_down, b_up)
+    pack = pl.pallas_call(
         functools.partial(pack_kernel, seq_n),
-        out_shape=(
-            jax.ShapeDtypeStruct((dp_n, seq_n, ffn_n, own, lanes), bf16),
-            jax.ShapeDtypeStruct((2 * u + own + 8, width), bf16),
-        ),
-        in_specs=[whole() for _ in range(8)],
-        out_specs=(whole(), whole()),
+        out_shape=jax.ShapeDtypeStruct((dp_n, seq_n, ffn_n, own, lanes), bf16),
+        in_specs=[whole() for _ in range(4)],
+        out_specs=whole(),
         name="packed_weights",
-    )(w_q, w_k, w_v, w_o, w_up, w_down, b_up, vec)
+    )(w_q, w_k, w_v, vec)
+    return pack, rest
 
 
 def weights_kernel(chunks, direct, *refs):
@@ -966,7 +1007,7 @@
 
     got = rows_chain(
         me_ref, ctx_parts, features, cotangent[0], rest, slab_rows, own if direct else 0,
-        jnp.zeros((8, PAIR), bf16) if direct else w_o, vecs, jnp.zeros((8, PAIR), f32) if direct else bias_up,
+        vecs if direct else w_o, vecs, vecs if direct else bias_up,
     )
     out, grad_resid_one, hidden, grad_pre, normed_t, grad_ffn_t, grad_branch = got[:7]
     grad_ctx, (sums, grad_bias_up) = got[7 : 7 + seq_n], got[7 + seq_n :]

time: 328 us -> 324 us (0.988)
  Pallas kernels: 173 us -> 169 us
    all_to_all x1, waiting for transfers between devices: 33.8 us -> 25.7 us  [shards(): lax.all_to_all(grad_w, ALL, split_axis=0, concat_axis=0, tiled=True)]
    ppermute x12, waiting for transfers between devices: 56.8 us -> 60.8 us  [flip_send(): return lax.ppermute(array, axis, [(i, i ^ bits) for i in range(count)])]
    reduce_scatter x1, waiting for transfers between devices: 2.76 us -> 6.11 us  [shards(): lax.psum_scatter(payload.reshape(-1, width), ('dp', 'seq'), scatter_dimen...]
  transfers between devices with their start and end apart: 17 -> 17, of which waited for: 7 -> 8; matrix products, arithmetic and copies ran while one was open for 5% -> 5% of each run, Pallas kernels for 40% -> 39%
where the time goes in v11:
time: 324 us; the launch traced here: 323 us
  Pallas kernels  169 us (52%)
  waiting for transfers between devices  99.4 us (31%)
  starting transfers between devices  19.4 us (6%)
  between operations  13.9 us (4%)
  local copies, waits for them, and re-layouts  12.9 us (4%)
  other arithmetic  8.93 us (3%)
    ppermute x12, waiting for transfers between devices, flip_send(): return lax.ppermute(array, axis, [(i, i ^ bits) for i in range(count)])  60.8 us
    pallas_call x1, Pallas kernels, attention_backward(): pl.pallas_call(functools.partial(backward_kernel, heads, chunks), out_sha...  60.4 us
    pallas_call x1, Pallas kernels, rows_chain(): pl.pallas_call(functools.partial(rows_kernel, parts, blocks, up_rows, own...  37.9 us
    all_to_all x1, waiting for transfers between devices, shards(): lax.all_to_all(grad_w, ALL, split_axis=0, concat_axis=0, tiled=True)  25.7 us
    pallas_call x1, Pallas kernels, attention_forward(): pl.pallas_call(functools.partial(forward_kernel, heads, chunks), out_shap...  23.8 us
    pallas_call x1, Pallas kernels, outer_products(): pl.pallas_call(functools.partial(outer_kernel, parts, up_rows, own, apart...  17.7 us
    pallas_call x1, Pallas kernels, attention_near(): pl.pallas_call(functools.partial(near_kernel, heads, chunks), out_shape=(...  11.9 us
    ppermute x12, starting transfers between devices, flip_send(): return lax.ppermute(array, axis, [(i, i ^ bits) for i in range(count)])  11 us
  transfers between devices with their start and end apart: 17, of which 8 were waited for; matrix products, arithmetic and copies ran while one was open for 5% of the time, Pallas kernels for 39%

profile of v11, /device:TPU:0, one launch (start us, length us, event | category | flops | bytes accessed | tf_op | source)
XLA Modules:
  0.0 323.3 jit_solution(12401141069149295542)
XLA Ops:
  8.5 1.8 rest_weights.1
  10.3 3.0 collective-permute-start.1
  19.0 1.9 packed_weights.1
  20.9 4.9 %all-to-all-start = ((bf16[32,24,640]{2,1,0:T(8,128)(2,1)}), bf16[32,24,640]{2,1,0:T(8,128)(2,1)S(1)}, u32[]{:S(2)}, u32[]{:S(2)}) async-start(bf16[32,24,640]{2,1,0:T(8,128)(2,1)} %bitcast.42), calls=%async_computation | async-start | bytes 1966080 | tf_op jit(solution)/shard_map/all_to_all | solution.py:974
  26.2 42.3 %collective-permute-done.1.refs_2_ = bf16[1024,768]{1,0:T(8,128)(2,1)} collective-permute-done((bf16[1024,768]{1,0:T(8,128)(2,1)}, bf16[1024,768]{1,0:T(8,128)(2,1)}, u32[]{:S(2)}, u32[]{:S(2)}) %collective-permute-start.1) | collective-permute-done | bytes 1572896 | tf_op jit(solution)/shard_map/ppermute | solution.py:940
  68.5 3.4 %all-to-all-done = bf16[32,24,640]{2,1,0:T(8,128)(2,1)S(1)} async-done(((bf16[32,24,640]{2,1,0:T(8,128)(2,1)}), bf16[32,24,640]{2,1,0:T(8,128)(2,1)S(1)}, u32[]{:S(2)}, u32[]{:S(2)}) %all-to-all-start) | async-done | bytes 983072 | tf_op jit(solution)/shard_map/all_to_all | solution.py:974
  73.6 23.8 %attention_forward.1 = (bf16[192,1024]{1,0:T(8,128)(2,1)}, bf16[192,1024]{1,0:T(8,128)(2,1)}, f32[3,16,128]{2,1,0:T(8,128)}, f32[3,128]{1,0:T(4,128)}, f32[3,64,...) custom-call(s32[1]{0:T(128)} %bitcast.me_ref, ...), custom_call_target="tpu_custom_call" | custom-call | flops 10000000000 | bytes 16000000 | tf_op jit(solution)/shard_map/attention_forward/pallas_call | solution.py:258
  98.6 11.9 %attention_near.1 = (bf16[192,1024]{1,0:T(8,128)(2,1)}, bf16[192,1024]{1,0:T(8,128)(2,1)}, f32[3,16,128]{2,1,0:T(8,128)}) custom-call(s32[1]{0:T(128)} %bitcast.me_ref, s32[576]{0:T(1024)} %reshape.55.rand_ref, s32[1,2]{1,0:T(1,128)} %glob_ref.5, bf16[4160,384]{1,0:T(8,128)(2,1)} %get-tuple-element.77.k_ref.refs_4_, ...), custom_call_target="tpu_custom_call" | custom-call | flops 6000000000 | bytes 9000000 | tf_op jit(solution)/shard_map/attention_near/pallas_call | solution.py:309
  113.7 7.4 %collective-permute-done.4.refs_3_ = bf16[192,1024]{1,0:T(8,128)(2,1)S(1)} collective-permute-done((bf16[192,1024]{1,0:T(8,128)(2,1)}, bf16[192,1024]{1,0:T(8,128)(2,1)S(1)}, u32[]{:S(2)}, u32[]{:S(2)}) %collective-permute-start.4) | collective-permute-done | bytes 393248 | tf_op jit(solution)/shard_map/ppermute | solution.py:940
  121.1 3.2 %all-gather.3.cloned.1.call-done = bf16[7168,768]{1,0:T(8,128)(2,1)} async-done(((bf16[224,768]{1,0:T(8,128)(2,1)}), bf16[7168,768]{1,0:T(8,128)(2,1)}) %all-gather.3.cloned.1.call-update) | async-done | bytes 11010064 | tf_op jit(solution)/shard_map/all_gather | solution.py:977
  124.4 37.9 %rows_chain.1 = (bf16[1024,768]{1,0:T(8,128)(2,1)}, f32[1024,768]{1,0:T(8,128)}, bf16[4,1024,768]{2,1,0:T(8,128)(2,1)}, bf16[4,1024,768]{2,1,0:T(8,128)(2,1)}, b...) custom-call(s32[1]{0:T(128)} %bitcast.me_ref, ...), custom_call_target="tpu_custom_call" | custom-call | flops 22000001024 | bytes 40000000 | tf_op jit(solution)/shard_map/rows_chain/pallas_call | solution.py:817
  162.6 1.6 collective-permute-start.8
  164.2 17.7 %outer_products.1 = bf16[8,4,224,768]{3,2,1,0:T(8,128)(2,1)} custom-call(s32[1]{0:T(128)} %bitcast.me_ref, bf16[192,1024]{1,0:T(8,128)(2,1)} %get-tuple-element.83.refs_0_, bf16[192,1024]{1,0:T(8,128)(2,1)} %copy-done.7, bf16[192,1024]{1,0:T(8,128)(2,1)} %copy-done.2, bf16[192,1024]{1,0:T(8,128)(2,1)} %copy-done.4, ...), custom_call_target="tpu_custom_call" | custom-call | flops 11000000512 | bytes 28000000 | tf_op jit(solution)/shard_map/outer_products/pallas_call | solution.py:891
  183.0 60.4 %attention_backward.1 = (bf16[4,192,1024]{2,1,0:T(8,128)(2,1)}, bf16[4,1024,384]{2,1,0:T(8,128)(2,1)}, f32[1024,768]{1,0:T(8,128)}, bf16[1024,768]{1,0:T(8,128)(...) custom-call(s32[1]{0:T(128)} %bitcast.me_ref, s32[576]{0:T(1024)} %reshape.55.rand_ref, s32[1,2]{1,0:T(1,128)} %glob_ref.5, ...), custom_call_target="tpu_custom_call" | custom-call | flops 30000001024 | bytes 24000000 | tf_op jit(solution)/shard_map/attention_backward/pallas_call | solution.py:491
  244.1 9.6 %projection_gradients.1 = bf16[32,24,640]{2,1,0:T(8,128)(2,1)} custom-call(bf16[1024,768]{1,0:T(8,128)(2,1)} %bitcast.9.refs_0_.refs_4_, bf16[1024,768]{1,0:T(8,128)(2,1)} %collective-permute-done.refs_1_, bf16[1024,768]{1,0:T(8,128)(2,1)} %collective-permute-done.1.refs_2_, bf16[1024,768]{1,0:T(8,128)(2,1)} %collective-permute-done.2.refs_3_, ...), custom_call_target="tpu_custom_call" | custom-call | flops 4000000000 | bytes 12000000 | tf_op jit(solution)/shard_map/projection_gradients/pallas_call | solution.py:648
  253.7 3.0 add_convert_fusion
  256.7 3.4 %all-to-all-start.1 = ((bf16[32,24,640]{2,1,0:T(8,128)(2,1)}), bf16[32,24,640]{2,1,0:T(8,128)(2,1)}, u32[]{:S(2)}, u32[]{:S(2)}) async-start(bf16[32,24,640]{2,1,0:T(8,128)(2,1)} %projection_gradients.1), calls=%async_computation.2 | async-start | bytes 1966080 | tf_op jit(solution)/shard_map/all_to_all | solution.py:1060
  260.3 6.1 %reduce-scatter.3.cloned.1.call-done = bf16[896,768]{1,0:T(8,128)(2,1)} async-done(((bf16[7168,768]{1,0:T(8,128)(2,1)}), bf16[896,768]{1,0:T(8,128)(2,1)}) %reduce-scatter.3.cloned.1.call-update) | async-done | bytes 1376272 | tf_op jit(solution)/shard_map/reduce_scatter | solution.py:1031
  266.4 2.7 collective-permute-start.10
  269.1 25.7 %all-to-all-done.1 = bf16[32,24,640]{2,1,0:T(8,128)(2,1)} async-done(((bf16[32,24,640]{2,1,0:T(8,128)(2,1)}), bf16[32,24,640]{2,1,0:T(8,128)(2,1)}, u32[]{:S(2)}, u32[]{:S(2)}) %all-to-all-start.1) | async-done | bytes 983072 | tf_op jit(solution)/shard_map/all_to_all | solution.py:1060
  294.8 2.0 unpacked_gradients.1
  298.3 9.6 %collective-permute-done.10 = bf16[1024,768]{1,0:T(8,128)(2,1)} collective-permute-done((bf16[1024,768]{1,0:T(8,128)(2,1)}, bf16[1024,768]{1,0:T(8,128)(2,1)}, u32[]{:S(2)}, u32[]{:S(2)}) %collective-permute-start.10) | collective-permute-done | bytes 1572896 | tf_op jit(solution)/shard_map/ppermute | solution.py:940
  307.9 4.4 %add_bitcast_fusion = f32[1,1024,768]{2,1,0:T(8,128)} fusion(bf16[1024,768]{1,0:T(8,128)(2,1)S(1)} %collective-permute-done.11, f32[1024,768]{1,0:T(8,128)} %get-tuple-element.107, bf16[1024,768]{1,0:T(8,128)(2,1)} %collective-permute-done.10), kind=kLoop, calls=%fused_computation | loop fusion | flops 3145728 | bytes 9437184 | tf_op jit(solution)/shard_map/broadcast_in_dim | solution.py:1076
  312.3 1.8 finished.1
  (62 shorter events, 19.8 us)
Async XLA Ops:
  7.2 117.2 %all-gather.3.cloned.1.call-start = ((), (), s32[]{:S(2)}) async-start(), calls=%async_computation.6 | async-start | bytes 11354112 | tf_op jit(solution)/shard_map/all_gather | solution.py:977
  10.3 58.2 %collective-permute-start.1 = (bf16[1024,768]{1,0:T(8,128)(2,1)}, bf16[1024,768]{1,0:T(8,128)(2,1)}, u32[]{:S(2)}, u32[]{:S(2)}) collective-permute-start(bf16[1024,768]{1,0:T(8,128)(2,1)} %bitcast.9.refs_0_.refs_4_), channel_id=1, source_target_pairs={{0,8},{4,12},{8,0},{12,4},{1,9},{5,13},{9,1},{13,5},{2,10},{6,14},... | collective-permute-start | bytes 4718600 | tf_op jit(solution)/shard_map/ppermute | solution.py:940
  20.9 51.1 %all-to-all-start = ((bf16[32,24,640]{2,1,0:T(8,128)(2,1)}), bf16[32,24,640]{2,1,0:T(8,128)(2,1)S(1)}, u32[]{:S(2)}, u32[]{:S(2)}) async-start(bf16[32,24,640]{2,1,0:T(8,128)(2,1)} %bitcast.42), calls=%async_computation | async-start | bytes 1966080 | tf_op jit(solution)/shard_map/all_to_all | solution.py:974
  25.8 240.6 %reduce-scatter.3.cloned.1.call-start = ((), (), s32[]{:S(2)}) async-start(), calls=%async_computation.4 | async-start | bytes 12386304 | tf_op jit(solution)/shard_map/reduce_scatter | solution.py:1031
  25.8 47.8 %collective-permute-start = (bf16[1024,768]{1,0:T(8,128)(2,1)}, bf16[1024,768]{1,0:T(8,128)(2,1)}, u32[]{:S(2)}, u32[]{:S(2)}) collective-permute-start(bf16[1024,768]{1,0:T(8,128)(2,1)} %bitcast.9.refs_0_.refs_4_), channel_id=1, source_target_pairs={{0,4},{4,0},{8,12},{12,8},{1,5},{5,1},{9,13},{13,9},{2,6},{6,2},{1... | collective-permute-start | bytes 4718600 | tf_op jit(solution)/shard_map/ppermute | solution.py:940
  68.5 5.1 %collective-permute-start.2 = (bf16[1024,768]{1,0:T(8,128)(2,1)}, bf16[1024,768]{1,0:T(8,128)(2,1)}, u32[]{:S(2)}, u32[]{:S(2)}) collective-permute-start(bf16[1024,768]{1,0:T(8,128)(2,1)} %collective-permute-done.1.refs_2_), channel_id=1, source_target_pairs={{0,4},{4,0},{8,12},{12,8},{1,5},{5,1},{9,13},{13,9},{2,6},{6,2},{1... | collective-permute-start | bytes 4718600 | tf_op jit(solution)/shard_map/ppermute | solution.py:940
  71.9 1.7 copy-start.1
  97.5 16.3 %collective-permute-start.3 = (bf16[192,1024]{1,0:T(8,128)(2,1)}, bf16[192,1024]{1,0:T(8,128)(2,1)S(1)}, u32[]{:S(2)}, u32[]{:S(2)}) collective-permute-start(bf16[192,1024]{1,0:T(8,128)(2,1)} %get-tuple-element.75), channel_id=1, source_target_pairs={{0,8},{4,12},{8,0},{12,4},{1,9},{5,13},{9,1},{13,5},{2,10},{6,14},... | collective-permute-start | bytes 1179656 | tf_op jit(solution)/shard_map/ppermute | solution.py:940
  98.6 22.6 %collective-permute-start.4 = (bf16[192,1024]{1,0:T(8,128)(2,1)}, bf16[192,1024]{1,0:T(8,128)(2,1)S(1)}, u32[]{:S(2)}, u32[]{:S(2)}) collective-permute-start(bf16[192,1024]{1,0:T(8,128)(2,1)} %get-tuple-element.76), channel_id=1, source_target_pairs={{0,12},{4,8},{8,4},{12,0},{1,13},{5,9},{9,5},{13,1},{2,14},{6,10},... | collective-permute-start | bytes 1179656 | tf_op jit(solution)/shard_map/ppermute | solution.py:940
  110.5 10.7 %collective-permute-start.5 = (bf16[192,1024]{1,0:T(8,128)(2,1)}, bf16[192,1024]{1,0:T(8,128)(2,1)S(1)}, u32[]{:S(2)}, u32[]{:S(2)}) collective-permute-start(bf16[192,1024]{1,0:T(8,128)(2,1)} %get-tuple-element.84), channel_id=1, source_target_pairs={{0,4},{4,0},{8,12},{12,8},{1,5},{5,1},{9,13},{13,9},{2,6},{6,2},{1... | collective-permute-start | bytes 1179656 | tf_op jit(solution)/shard_map/ppermute | solution.py:940
  113.7 10.7 %copy-start.2 = (bf16[192,1024]{1,0:T(8,128)(2,1)}, bf16[192,1024]{1,0:T(8,128)(2,1)S(1)}, u32[]{:S(2)}) copy-start(bf16[192,1024]{1,0:T(8,128)(2,1)S(1)} %collective-permute-done.3.refs_2_) | copy-start | bytes 1179652
  121.1 3.3 %copy-start.4 = (bf16[192,1024]{1,0:T(8,128)(2,1)}, bf16[192,1024]{1,0:T(8,128)(2,1)S(1)}, u32[]{:S(2)}) copy-start(bf16[192,1024]{1,0:T(8,128)(2,1)S(1)} %collective-permute-done.4.refs_3_) | copy-start | bytes 1179652
  121.1 3.3 %copy-start.7 = (bf16[192,1024]{1,0:T(8,128)(2,1)}, bf16[192,1024]{1,0:T(8,128)(2,1)S(1)}, u32[]{:S(2)}) copy-start(bf16[192,1024]{1,0:T(8,128)(2,1)S(1)} %collective-permute-done.5.refs_1_) | copy-start | bytes 1179652
  162.3 19.6 %collective-permute-start.6 = (bf16[192,1024]{1,0:T(8,128)(2,1)}, bf16[192,1024]{1,0:T(8,128)(2,1)S(1)}, u32[]{:S(2)}, u32[]{:S(2)}) collective-permute-start(bf16[192,1024]{1,0:T(8,128)(2,1)} %get-tuple-element.96), channel_id=1, source_target_pairs={{0,4},{4,0},{8,12},{12,8},{1,5},{5,1},{9,13},{13,9},{2,6},{6,2},{1... | collective-permute-start | bytes 1179656 | tf_op jit(solution)/shard_map/ppermute | solution.py:940
  162.6 19.3 %collective-permute-start.7 = (bf16[192,1024]{1,0:T(8,128)(2,1)}, bf16[192,1024]{1,0:T(8,128)(2,1)S(1)}, u32[]{:S(2)}, u32[]{:S(2)}) collective-permute-start(bf16[192,1024]{1,0:T(8,128)(2,1)} %get-tuple-element.97), channel_id=1, source_target_pairs={{0,8},{4,12},{8,0},{12,4},{1,9},{5,13},{9,1},{13,5},{2,10},{6,14},... | collective-permute-start | bytes 1179656 | tf_op jit(solution)/shard_map/ppermute | solution.py:940
  162.6 19.3 %collective-permute-start.8 = (bf16[192,1024]{1,0:T(8,128)(2,1)}, bf16[192,1024]{1,0:T(8,128)(2,1)S(1)}, u32[]{:S(2)}, u32[]{:S(2)}) collective-permute-start(bf16[192,1024]{1,0:T(8,128)(2,1)} %get-tuple-element.98), channel_id=1, source_target_pairs={{0,12},{4,8},{8,4},{12,0},{1,13},{5,9},{9,5},{13,1},{2,14},{6,10},... | collective-permute-start | bytes 1179656 | tf_op jit(solution)/shard_map/ppermute | solution.py:940
  181.9 0.9 copy-start.5
  182.0 1.0 copy-start.6
  243.4 10.3 %collective-permute-start.9 = (bf16[1024,768]{1,0:T(8,128)(2,1)}, bf16[1024,768]{1,0:T(8,128)(2,1)}, u32[]{:S(2)}, u32[]{:S(2)}) collective-permute-start(bf16[1024,768]{1,0:T(8,128)(2,1)} %get-tuple-element.112), channel_id=1, source_target_pairs={{0,4},{4,0},{8,12},{12,8},{1,5},{5,1},{9,13},{13,9},{2,6},{6,2},{1... | collective-permute-start | bytes 4718600 | tf_op jit(solution)/shard_map/ppermute | solution.py:940
  244.1 9.6 %copy-start = (bf16[1024,768]{1,0:T(8,128)(2,1)S(1)}, bf16[1024,768]{1,0:T(8,128)(2,1)}, u32[]{:S(2)}) copy-start(bf16[1024,768]{1,0:T(8,128)(2,1)} %get-tuple-element.111) | copy-start | bytes 4718596
  256.7 38.1 %all-to-all-start.1 = ((bf16[32,24,640]{2,1,0:T(8,128)(2,1)}), bf16[32,24,640]{2,1,0:T(8,128)(2,1)}, u32[]{:S(2)}, u32[]{:S(2)}) async-start(bf16[32,24,640]{2,1,0:T(8,128)(2,1)} %projection_gradients.1), calls=%async_computation.2 | async-start | bytes 1966080 | tf_op jit(solution)/shard_map/all_to_all | solution.py:1060
  260.1 52.3 %reduce-scatter.5.cloned.1.call-start = ((), (), s32[]{:S(2)}) async-start(), calls=%async_computation.5 | async-start | bytes 1720320 | tf_op jit(solution)/shard_map/reduce_scatter | solution.py:1056
  260.2 38.1 %collective-permute-start.11 = (bf16[1024,768]{1,0:T(8,128)(2,1)}, bf16[1024,768]{1,0:T(8,128)(2,1)S(1)}, u32[]{:S(2)}, u32[]{:S(2)}) collective-permute-start(bf16[1024,768]{1,0:T(8,128)(2,1)} %get-tuple-element.116), channel_id=1, source_target_pairs={{0,4},{4,0},{8,12},{12,8},{1,5},{5,1},{9,13},{13,9},{2,6},{6,2},{1... | collective-permute-start | bytes 4718600 | tf_op jit(solution)/shard_map/ppermute | solution.py:940
  266.4 41.5 %collective-permute-start.10 = (bf16[1024,768]{1,0:T(8,128)(2,1)}, bf16[1024,768]{1,0:T(8,128)(2,1)}, u32[]{:S(2)}, u32[]{:S(2)}) collective-permute-start(bf16[1024,768]{1,0:T(8,128)(2,1)} %add_convert_fusion), channel_id=1, source_target_pairs={{0,8},{4,12},{8,0},{12,4},{1,9},{5,13},{9,1},{13,5},{2,10},{6,14},... | collective-permute-start | bytes 4718600 | tf_op jit(solution)/shard_map/ppermute | solution.py:940
  (1 other events, 0.8 us)
Sparse Core Ops, SparseCore 0:
  10.8 113.5 all-gather.2
  182.1 84.2 reduce-scatter.2
  269.2 37.6 reduce-scatter.4

commit v12 on v11

--- a/solution.py
+++ b/solution.py
@@ -535,7 +535,7 @@
     return jnp.where(lane < BLOCK, first, second)
 
 
-def pack_kernel(seq_n, wq_ref, wk_ref, wv_ref, vec_ref, pack_ref):
+def pack_kernel(seq_n, wq_ref, wk_ref, wv_ref, vec_ref, more_ref, pack_ref):
     own, width = wq_ref.shape
     heads = width // HEAD_DIM // seq_n
     blocks, inner = pack_ref.shape[0], pack_ref.shape[2]
@@ -545,7 +545,9 @@
             for h in range(heads)
         ]
         for h in range(0, heads, 2):
-            second = half_columns(wq_ref, s * heads + h + 1, 1) if h + 1 < heads else vec_ref[...].astype(f32)
+            second = half_columns(wq_ref, s * heads + h + 1, 1) if h + 1 < heads else (
+                vec_ref[...].astype(f32) + more_ref[...].astype(f32)
+            )
             pieces.append(two_halves(half_columns(wq_ref, s * heads + h, 0), second))
         piece = jnp.concatenate(pieces, axis=1).astype(bf16)
         for b in range(blocks):
@@ -553,16 +555,15 @@
                 pack_ref[b, s, i] = piece
 
 
-def rest_kernel(wo_ref, up_ref, down_ref, bup_ref, rest_ref):
-    own, width = wo_ref.shape
+def rest_kernel(wo_ref, up_ref, down_ref, rest_ref):
+    own = wo_ref.shape[0]
     u = up_ref.shape[0]
     rest_ref[0:u, :] = up_ref[...]
     rest_ref[u : 2 * u, :] = down_ref[...]
     rest_ref[2 * u : 2 * u + own, :] = wo_ref[...]
-    rest_ref[2 * u + own : 2 * u + own + 8, :] = jnp.broadcast_to(bup_ref[...], (8, width))
-
-
-def packed_weights(w_q, w_k, w_v, w_o, w_up, w_down, b_up, vec, dp_n, seq_n, ffn_n):
+
+
+def packed_weights(w_q, w_k, w_v, w_o, w_up, w_down, vec, more, dp_n, seq_n, ffn_n):
     own, width = w_q.shape
     heads = width // HEAD_DIM // seq_n
     lanes = heads * PAIR + round_up(heads * HEAD_DIM, PAIR)
@@ -571,27 +572,27 @@
         group = heads * HEAD_DIM
         cols = lambda w: w.reshape(own, seq_n, heads, HEAD_DIM).transpose(1, 0, 2, 3)
         kv = jnp.stack([cols(w_k), cols(w_v)], axis=3).reshape(seq_n, own, 2 * group)
-        notes = jnp.broadcast_to(vec[None, :, HEAD_DIM:], (seq_n, own, PAIR - HEAD_DIM))
+        notes = jnp.broadcast_to((vec + more)[None, :, HEAD_DIM:], (seq_n, own, PAIR - HEAD_DIM))
         piece = jnp.concatenate([kv, cols(w_q).reshape(seq_n, own, group), notes], axis=2)
         piece = jnp.pad(piece, ((0, 0), (0, round_up(own, 8) - own), (0, 0)))
         pack = jnp.broadcast_to(piece[None, :, None], (dp_n, seq_n, ffn_n) + piece.shape[1:])
         w_o = jnp.pad(w_o, ((0, round_up(own, 8) - own), (0, 0)))
-        return pack, jnp.concatenate([w_up, w_down, w_o, jnp.broadcast_to(b_up, (8, width))], axis=0)
+        return pack, jnp.concatenate([w_up, w_down, w_o], axis=0)
     whole = lambda: pl.BlockSpec(memory_space=pltpu.VMEM)
     rest = pl.pallas_call(
         rest_kernel,
-        out_shape=jax.ShapeDtypeStruct((2 * u + own + 8, width), bf16),
-        in_specs=[whole() for _ in range(4)],
+        out_shape=jax.ShapeDtypeStruct((2 * u + own, width), bf16),
+        in_specs=[whole() for _ in range(3)],
         out_specs=whole(),
         name="rest_weights",
-    )(w_o, w_up, w_down, b_up)
+    )(w_o, w_up, w_down)
     pack = pl.pallas_call(
         functools.partial(pack_kernel, seq_n),
         out_shape=jax.ShapeDtypeStruct((dp_n, seq_n, ffn_n, own, lanes), bf16),
-        in_specs=[whole() for _ in range(4)],
+        in_specs=[whole() for _ in range(5)],
         out_specs=whole(),
         name="packed_weights",
-    )(w_q, w_k, w_v, vec)
+    )(w_q, w_k, w_v, vec, more)
     return pack, rest
 
 
@@ -754,9 +755,6 @@
             wo_sc[...] = wo_ref[...]
 
     def bias_up(f):
-        if own:
-            row = rest_ref[0, f, 2 * up_rows + own : 2 * up_rows + own + 8, :].astype(f32)
-            return row[7:8, :]
         return bup_ref[f : f + 1, :]
 
     ctx = jnp.concatenate([r[...] for r in ctx_refs], axis=0)
@@ -928,10 +926,35 @@
         out_shape=tuple(jax.ShapeDtypeStruct((r, hidden), f32) for r in (up_rows, up_rows, own, 8)),
         in_specs=[whole()],
         out_specs=tuple(whole() for _ in range(4)),
+        cost_estimate=pl.CostEstimate(flops=2_000_000_000, bytes_accessed=2_000_000, transcendentals=0),
         name="finished",
     )(total)
 
 
+def total_kernel(base_ref, *refs):
+    total = base_ref[...]
+    for ref in refs[:-1]:
+        total = total + ref[...].astype(f32)
+    refs[-1][...] = total
+
+
+def token_total(base, pieces):
+    rows, width = base.shape
+    tile = 256
+    tall = pl.BlockSpec((tile, width), lambda i: (i, 0))
+    return pl.pallas_call(
+        total_kernel,
+        grid=(rows // tile,),
+        out_shape=jax.ShapeDtypeStruct(base.shape, f32),
+        in_specs=[tall] * (1 + len(pieces)),
+        out_specs=tall,
+        compiler_params=pltpu.CompilerParams(vmem_limit_bytes=VMEM_BYTES),
+        cost_estimate=pl.CostEstimate(flops=TOTAL_FLOPS, bytes_accessed=9_000_000, transcendentals=0),
+        name="token_total",
+    )(base, *pieces)
+
+
+TOTAL_FLOPS = 1_000_000_000
 ALL = ("dp", "seq", "ffn")
 
 
@@ -963,11 +986,14 @@
         near[k] = flip_send(features if bit == k else near[k ^ bit], "seq", bit)
 
     vec = jnp.stack([b_output, b_down, gain_attn, shift_attn, gain_ffn, shift_ffn, b_query, b_value], axis=1)
+    up_rows = w_up.shape[0]
+    share_up = lax.dynamic_slice(b_up, (here // ffn_n * up_rows,), (up_rows,)).reshape(ffn_n, own).T
+    more = jnp.pad(share_up, ((0, 0), (HEAD_DIM + 8, PAIR - HEAD_DIM - 8 - ffn_n)))
     vec = jnp.pad(vec, ((0, 0), (HEAD_DIM, PAIR - HEAD_DIM - 8)))
     seg = segment_ids[0].reshape(seq_n, rows)
     rand = random_blocks.reshape(-1)
     pack, rest = packed_weights(
-        w_query, w_key, w_value, w_output, w_up, w_down, b_up[None], vec, dp_n, seq_n, ffn_n
+        w_query, w_key, w_value, w_output, w_up, w_down, vec, more, dp_n, seq_n, ffn_n
     )
     lanes = pack.shape[4]
     pack, seg, rand = lax.optimization_barrier((pack, seg, rand))
@@ -979,6 +1005,8 @@
     share = devices // seq_n
     vecs = w_own[:, lanes - HEAD_DIM : lanes - HEAD_DIM + 8].astype(f32).T
     biases = lax.dynamic_slice(vecs, (6, me * group), (2, group))
+    bias_up = w_own[:, lanes - HEAD_DIM + 8 : lanes - HEAD_DIM + 8 + ffn_n].reshape(outer, ffn_n, own, ffn_n)
+    bias_up = bias_up.transpose(1, 0, 3, 2).reshape(ffn_n, width).astype(f32)
     by_head = biases[1].reshape(heads, 1, HEAD_DIM)
     b_kv = jnp.concatenate([jnp.zeros_like(by_head), by_head], axis=1).reshape(1, heads * PAIR)
 
@@ -994,11 +1022,9 @@
     for k in range(1, far):
         ctx_parts[k] = flip_send(ctx_near[k], "seq", k)
 
-    up_rows = w_up.shape[0]
     at = 2 * up_rows
     rest = rest.reshape(outer, ffn_n, rest.shape[1], width)
     w_o = rest[:, :, at : at + own].reshape(width, width)
-    bias_up = rest[0, :, at + own_pad + 7].astype(f32)
     direct = up_rows % 16 == 0 and own % 8 == 0 and outer % seq_n == 0 and (outer // seq_n) * ffn_n * own == group
     if not direct:
         rest = rest[:, :, :at].reshape(outer, ffn_n, 2, up_rows, width).transpose(1, 2, 0, 3, 4)
@@ -1007,7 +1033,7 @@
 
     got = rows_chain(
         me_ref, ctx_parts, features, cotangent[0], rest, slab_rows, own if direct else 0,
-        vecs if direct else w_o, vecs, vecs if direct else bias_up,
+        vecs if direct else w_o, vecs, bias_up,
     )
     out, grad_resid_one, hidden, grad_pre, normed_t, grad_ffn_t, grad_branch = got[:7]
     grad_ctx, (sums, grad_bias_up) = got[7 : 7 + seq_n], got[7 + seq_n :]
@@ -1052,11 +1078,14 @@
     grad_w, apart = lax.optimization_barrier((grad_w, apart))
     part = [None] + part
     bit = seq_n // 2
-    part[bit], total = lax.optimization_barrier((part[bit], total))
+    staged = total
     total = lax.psum_scatter(total, "ffn", scatter_dimension=0, tiled=True)
+    pieces = []
     while bit:
-        grad_features = grad_features + flip_send(part[bit], "seq", bit).astype(f32)
+        pieces.append(flip_send(part[bit], "seq", bit))
         bit //= 2
+    pieces = lax.optimization_barrier((pieces, staged))[0]
+    grad_features = token_total(grad_features, pieces)
     grad_w = lax.all_to_all(grad_w, ALL, split_axis=0, concat_axis=0, tiled=True)
     if direct:
         out_up, out_down, out_output, notes = finished(total, up_rows, own)

time: 324 us -> 324 us (level)
  other arithmetic: 8.93 us -> 4.56 us
  Pallas kernels: 169 us -> 173 us
  waiting for transfers between devices: 99.4 us -> 95.9 us
  local copies, waits for them, and re-layouts: 12.9 us -> 16.4 us
    ppermute x12, waiting for transfers between devices: 60.8 us -> 55.7 us  [flip_send(): return lax.ppermute(array, axis, [(i, i ^ bits) for i in range(count)])]
    pallas_call x1 -> x2, Pallas kernels: 1.77 us -> 6.67 us  [the longest x1 4.89 us: token_total(): pl.pallas_call(total_kernel, grid=(rows // tile,), out_shape=jax.ShapeDty...]
    broadcast_in_dim x1 -> x0, other arithmetic: 4.43 us -> none  [shards(): grad_features[None]]
  transfers between devices with their start and end apart: 17 -> 17, of which waited for: 8 -> 7; matrix products, arithmetic and copies ran while one was open for 5% -> 5% of each run, Pallas kernels for 39% -> 41%
where the time goes in v12:
time: 324 us; the launch traced here: 323 us
  Pallas kernels  173 us (53%)
  waiting for transfers between devices  95.9 us (30%)
  starting transfers between devices  18.7 us (6%)
  local copies, waits for them, and re-layouts  16.4 us (5%)
  between operations  13.9 us (4%)
  other arithmetic  4.56 us (1%)
    pallas_call x1, Pallas kernels, attention_backward(): pl.pallas_call(functools.partial(backward_kernel, heads, chunks), out_sha...  60.2 us
    ppermute x12, waiting for transfers between devices, flip_send(): return lax.ppermute(array, axis, [(i, i ^ bits) for i in range(count)])  55.7 us
    pallas_call x1, Pallas kernels, rows_chain(): pl.pallas_call(functools.partial(rows_kernel, parts, blocks, up_rows, own...  37.9 us
    all_to_all x1, waiting for transfers between devices, shards(): lax.all_to_all(grad_w, ALL, split_axis=0, concat_axis=0, tiled=True)  28.3 us
    pallas_call x1, Pallas kernels, attention_forward(): pl.pallas_call(functools.partial(forward_kernel, heads, chunks), out_shap...  23.8 us
    pallas_call x1, Pallas kernels, outer_products(): pl.pallas_call(functools.partial(outer_kernel, parts, up_rows, own, apart...  17.6 us
    pallas_call x1, Pallas kernels, attention_near(): pl.pallas_call(functools.partial(near_kernel, heads, chunks), out_shape=(...  11.6 us
    ppermute x12, starting transfers between devices, flip_send(): return lax.ppermute(array, axis, [(i, i ^ bits) for i in range(count)])  10.2 us
  transfers between devices with their start and end apart: 17, of which 7 were waited for; matrix products, arithmetic and copies ran while one was open for 5% of the time, Pallas kernels for 41%

profile of v12, /device:TPU:0, one launch (start us, length us, event | category | flops | bytes accessed | tf_op | source)
XLA Modules:
  0.0 322.8 jit_solution(8000497353712897300)
XLA Ops:
  7.2 1.8 rest_weights.1
  9.0 3.0 collective-permute-start.1
  19.3 1.9 packed_weights.1
  21.2 4.9 %all-to-all-start = ((bf16[32,24,640]{2,1,0:T(8,128)(2,1)}), bf16[32,24,640]{2,1,0:T(8,128)(2,1)S(1)}, u32[]{:S(2)}, u32[]{:S(2)}) async-start(bf16[32,24,640]{2,1,0:T(8,128)(2,1)} %bitcast.46), calls=%async_computation | async-start | bytes 1966080 | tf_op jit(solution)/shard_map/all_to_all | solution.py:1000
  26.5 39.4 %collective-permute-done.1.refs_2_ = bf16[1024,768]{1,0:T(8,128)(2,1)} collective-permute-done((bf16[1024,768]{1,0:T(8,128)(2,1)}, bf16[1024,768]{1,0:T(8,128)(2,1)}, u32[]{:S(2)}, u32[]{:S(2)}) %collective-permute-start.1) | collective-permute-done | bytes 1572896 | tf_op jit(solution)/shard_map/ppermute | solution.py:963
  65.9 4.3 %all-to-all-done = bf16[32,24,640]{2,1,0:T(8,128)(2,1)S(1)} async-done(((bf16[32,24,640]{2,1,0:T(8,128)(2,1)}), bf16[32,24,640]{2,1,0:T(8,128)(2,1)S(1)}, u32[]{:S(2)}, u32[]{:S(2)}) %all-to-all-start) | async-done | bytes 983072 | tf_op jit(solution)/shard_map/all_to_all | solution.py:1000
  72.0 23.8 %attention_forward.1 = (bf16[192,1024]{1,0:T(8,128)(2,1)}, bf16[192,1024]{1,0:T(8,128)(2,1)}, f32[3,16,128]{2,1,0:T(8,128)}, f32[3,128]{1,0:T(4,128)}, f32[3,64,...) custom-call(s32[1]{0:T(128)} %bitcast.me_ref, ...), custom_call_target="tpu_custom_call" | custom-call | flops 10000000000 | bytes 16000000 | tf_op jit(solution)/shard_map/attention_forward/pallas_call | solution.py:258
  96.5 11.6 %attention_near.1 = (bf16[192,1024]{1,0:T(8,128)(2,1)}, bf16[192,1024]{1,0:T(8,128)(2,1)}, f32[3,16,128]{2,1,0:T(8,128)}) custom-call(s32[1]{0:T(128)} %bitcast.me_ref, s32[576]{0:T(1024)} %reshape.65.rand_ref, s32[1,2]{1,0:T(1,128)} %glob_ref.5, bf16[4160,384]{1,0:T(8,128)(2,1)} %get-tuple-element.77.k_ref.refs_4_, ...), custom_call_target="tpu_custom_call" | custom-call | flops 6000000000 | bytes 9000000 | tf_op jit(solution)/shard_map/attention_near/pallas_call | solution.py:309
  112.5 6.8 %collective-permute-done.4.refs_3_ = bf16[192,1024]{1,0:T(8,128)(2,1)S(1)} collective-permute-done((bf16[192,1024]{1,0:T(8,128)(2,1)}, bf16[192,1024]{1,0:T(8,128)(2,1)S(1)}, u32[]{:S(2)}, u32[]{:S(2)}) %collective-permute-start.4) | collective-permute-done | bytes 393248 | tf_op jit(solution)/shard_map/ppermute | solution.py:963
  119.3 3.0 all-gather.3.cloned.1.call-done
  122.3 37.9 %rows_chain.1 = (bf16[1024,768]{1,0:T(8,128)(2,1)}, f32[1024,768]{1,0:T(8,128)}, bf16[4,1024,768]{2,1,0:T(8,128)(2,1)}, bf16[4,1024,768]{2,1,0:T(8,128)(2,1)}, b...) custom-call(s32[1]{0:T(128)} %bitcast.me_ref, ...), custom_call_target="tpu_custom_call" | custom-call | flops 22000001024 | bytes 40000000 | tf_op jit(solution)/shard_map/rows_chain/pallas_call | solution.py:815
  160.6 1.5 collective-permute-start.8
  162.1 17.6 %outer_products.1 = bf16[8,4,224,768]{3,2,1,0:T(8,128)(2,1)} custom-call(s32[1]{0:T(128)} %bitcast.me_ref, bf16[192,1024]{1,0:T(8,128)(2,1)} %get-tuple-element.83.refs_0_, bf16[192,1024]{1,0:T(8,128)(2,1)} %copy-done.6, bf16[192,1024]{1,0:T(8,128)(2,1)} %copy-done.3, bf16[192,1024]{1,0:T(8,128)(2,1)} %copy-done.4, ...), custom_call_target="tpu_custom_call" | custom-call | flops 11000000512 | bytes 28000000 | tf_op jit(solution)/shard_map/outer_products/pallas_call | solution.py:889
  180.8 60.2 %attention_backward.1 = (bf16[4,192,1024]{2,1,0:T(8,128)(2,1)}, bf16[4,1024,384]{2,1,0:T(8,128)(2,1)}, f32[1024,768]{1,0:T(8,128)}, bf16[1024,768]{1,0:T(8,128)(...) custom-call(s32[1]{0:T(128)} %bitcast.me_ref, s32[576]{0:T(1024)} %reshape.65.rand_ref, s32[1,2]{1,0:T(1,128)} %glob_ref.5, ...), custom_call_target="tpu_custom_call" | custom-call | flops 30000001024 | bytes 24000000 | tf_op jit(solution)/shard_map/attention_backward/pallas_call | solution.py:491
  241.9 9.6 %projection_gradients.1 = bf16[32,24,640]{2,1,0:T(8,128)(2,1)} custom-call(bf16[1024,768]{1,0:T(8,128)(2,1)} %bitcast.10.refs_0_.refs_4_, bf16[1024,768]{1,0:T(8,128)(2,1)} %collective-permute-done.refs_1_, bf16[1024,768]{1,0:T(8,128)(2,1)} %collective-permute-done.1.refs_2_, bf16[1024,768]{1,0:T(8,128)(2,1)} %collective-permute-done.2.refs_3_, ...), custom_call_target="tpu_custom_call" | custom-call | flops 4000000000 | bytes 12000000 | tf_op jit(solution)/shard_map/projection_gradients/pallas_call | solution.py:649
  251.5 3.0 add_convert_fusion
  254.5 3.5 %all-to-all-start.1 = ((bf16[32,24,640]{2,1,0:T(8,128)(2,1)}), bf16[32,24,640]{2,1,0:T(8,128)(2,1)}, u32[]{:S(2)}, u32[]{:S(2)}) async-start(bf16[32,24,640]{2,1,0:T(8,128)(2,1)} %projection_gradients.1), calls=%async_computation.2 | async-start | bytes 1966080 | tf_op jit(solution)/shard_map/all_to_all | solution.py:1089
  258.1 1.8 collective-permute-start.10
  259.9 4.6 %reduce-scatter.3.cloned.1.call-done = bf16[896,768]{1,0:T(8,128)(2,1)} async-done(((bf16[7168,768]{1,0:T(8,128)(2,1)}), bf16[896,768]{1,0:T(8,128)(2,1)}) %reduce-scatter.3.cloned.1.call-update) | async-done | bytes 1376272 | tf_op jit(solution)/shard_map/reduce_scatter | solution.py:1057
  264.5 28.3 %all-to-all-done.1 = bf16[32,24,640]{2,1,0:T(8,128)(2,1)} async-done(((bf16[32,24,640]{2,1,0:T(8,128)(2,1)}), bf16[32,24,640]{2,1,0:T(8,128)(2,1)}, u32[]{:S(2)}, u32[]{:S(2)}) %all-to-all-start.1) | async-done | bytes 983072 | tf_op jit(solution)/shard_map/all_to_all | solution.py:1089
  292.8 2.0 unpacked_gradients.1
  296.2 9.4 %collective-permute-done.10.refs_0_ = bf16[1024,768]{1,0:T(8,128)(2,1)S(1)} collective-permute-done((bf16[1024,768]{1,0:T(8,128)(2,1)}, bf16[1024,768]{1,0:T(8,128)(2,1)S(1)}, u32[]{:S(2)}, u32[]{:S(2)}) %collective-permute-start.10) | collective-permute-done | bytes 1572896 | tf_op jit(solution)/shard_map/ppermute | solution.py:963
  306.9 4.9 %token_total.1 = f32[1024,768]{1,0:T(8,128)} custom-call(f32[1024,768]{1,0:T(8,128)} %get-tuple-element.107.base_ref, bf16[1024,768]{1,0:T(8,128)(2,1)} %copy-done.1, bf16[1024,768]{1,0:T(8,128)(2,1)} %collective-permute-done.11.refs_1_), custom_call_target="tpu_custom_call" | custom-call | flops 1000000000 | bytes 9000000 | tf_op jit(solution)/shard_map/token_total/pallas_call | solution.py:945
  311.7 1.8 finished.1
  (71 shorter events, 22.0 us)
Async XLA Ops:
  7.2 115.1 %all-gather.3.cloned.1.call-start = ((), (), s32[]{:S(2)}) async-start(), calls=%async_computation.6 | async-start | bytes 10948608 | tf_op jit(solution)/shard_map/all_gather | solution.py:1003
  9.0 56.9 %collective-permute-start.1 = (bf16[1024,768]{1,0:T(8,128)(2,1)}, bf16[1024,768]{1,0:T(8,128)(2,1)}, u32[]{:S(2)}, u32[]{:S(2)}) collective-permute-start(bf16[1024,768]{1,0:T(8,128)(2,1)} %bitcast.10.refs_0_.refs_4_), channel_id=1, source_target_pairs={{0,8},{4,12},{8,0},{12,4},{1,9},{5,13},{9,1},{13,5},{2,10},{6,14},... | collective-permute-start | bytes 4718600 | tf_op jit(solution)/shard_map/ppermute | solution.py:963
  21.2 49.0 %all-to-all-start = ((bf16[32,24,640]{2,1,0:T(8,128)(2,1)}), bf16[32,24,640]{2,1,0:T(8,128)(2,1)S(1)}, u32[]{:S(2)}, u32[]{:S(2)}) async-start(bf16[32,24,640]{2,1,0:T(8,128)(2,1)} %bitcast.46), calls=%async_computation | async-start | bytes 1966080 | tf_op jit(solution)/shard_map/all_to_all | solution.py:1000
  26.2 238.3 %reduce-scatter.3.cloned.1.call-start = ((), (), s32[]{:S(2)}) async-start(), calls=%async_computation.4 | async-start | bytes 12386304 | tf_op jit(solution)/shard_map/reduce_scatter | solution.py:1057
  26.2 45.7 %collective-permute-start = (bf16[1024,768]{1,0:T(8,128)(2,1)}, bf16[1024,768]{1,0:T(8,128)(2,1)}, u32[]{:S(2)}, u32[]{:S(2)}) collective-permute-start(bf16[1024,768]{1,0:T(8,128)(2,1)} %bitcast.10.refs_0_.refs_4_), channel_id=1, source_target_pairs={{0,4},{4,0},{8,12},{12,8},{1,5},{5,1},{9,13},{13,9},{2,6},{6,2},{1... | collective-permute-start | bytes 4718600 | tf_op jit(solution)/shard_map/ppermute | solution.py:963
  65.9 6.0 %collective-permute-start.2 = (bf16[1024,768]{1,0:T(8,128)(2,1)}, bf16[1024,768]{1,0:T(8,128)(2,1)}, u32[]{:S(2)}, u32[]{:S(2)}) collective-permute-start(bf16[1024,768]{1,0:T(8,128)(2,1)} %collective-permute-done.1.refs_2_), channel_id=1, source_target_pairs={{0,4},{4,0},{8,12},{12,8},{1,5},{5,1},{9,13},{13,9},{2,6},{6,2},{1... | collective-permute-start | bytes 4718600 | tf_op jit(solution)/shard_map/ppermute | solution.py:963
  70.2 1.7 copy-start
  95.7 16.7 %collective-permute-start.3 = (bf16[192,1024]{1,0:T(8,128)(2,1)}, bf16[192,1024]{1,0:T(8,128)(2,1)S(1)}, u32[]{:S(2)}, u32[]{:S(2)}) collective-permute-start(bf16[192,1024]{1,0:T(8,128)(2,1)} %get-tuple-element.75), channel_id=1, source_target_pairs={{0,8},{4,12},{8,0},{12,4},{1,9},{5,13},{9,1},{13,5},{2,10},{6,14},... | collective-permute-start | bytes 1179656 | tf_op jit(solution)/shard_map/ppermute | solution.py:963
  96.4 22.9 %collective-permute-start.4 = (bf16[192,1024]{1,0:T(8,128)(2,1)}, bf16[192,1024]{1,0:T(8,128)(2,1)S(1)}, u32[]{:S(2)}, u32[]{:S(2)}) collective-permute-start(bf16[192,1024]{1,0:T(8,128)(2,1)} %get-tuple-element.76), channel_id=1, source_target_pairs={{0,12},{4,8},{8,4},{12,0},{1,13},{5,9},{9,5},{13,1},{2,14},{6,10},... | collective-permute-start | bytes 1179656 | tf_op jit(solution)/shard_map/ppermute | solution.py:963
  108.1 11.2 %collective-permute-start.5 = (bf16[192,1024]{1,0:T(8,128)(2,1)}, bf16[192,1024]{1,0:T(8,128)(2,1)S(1)}, u32[]{:S(2)}, u32[]{:S(2)}) collective-permute-start(bf16[192,1024]{1,0:T(8,128)(2,1)} %get-tuple-element.84), channel_id=1, source_target_pairs={{0,4},{4,0},{8,12},{12,8},{1,5},{5,1},{9,13},{13,9},{2,6},{6,2},{1... | collective-permute-start | bytes 1179656 | tf_op jit(solution)/shard_map/ppermute | solution.py:963
  112.5 9.8 %copy-start.3 = (bf16[192,1024]{1,0:T(8,128)(2,1)}, bf16[192,1024]{1,0:T(8,128)(2,1)S(1)}, u32[]{:S(2)}) copy-start(bf16[192,1024]{1,0:T(8,128)(2,1)S(1)} %collective-permute-done.3.refs_2_) | copy-start | bytes 1179652
  119.3 3.0 copy-start.4
  119.3 3.0 copy-start.6
  160.2 19.6 %collective-permute-start.6 = (bf16[192,1024]{1,0:T(8,128)(2,1)}, bf16[192,1024]{1,0:T(8,128)(2,1)S(1)}, u32[]{:S(2)}, u32[]{:S(2)}) collective-permute-start(bf16[192,1024]{1,0:T(8,128)(2,1)} %get-tuple-element.96), channel_id=1, source_target_pairs={{0,4},{4,0},{8,12},{12,8},{1,5},{5,1},{9,13},{13,9},{2,6},{6,2},{1... | collective-permute-start | bytes 1179656 | tf_op jit(solution)/shard_map/ppermute | solution.py:963
  160.6 19.2 %collective-permute-start.7 = (bf16[192,1024]{1,0:T(8,128)(2,1)}, bf16[192,1024]{1,0:T(8,128)(2,1)S(1)}, u32[]{:S(2)}, u32[]{:S(2)}) collective-permute-start(bf16[192,1024]{1,0:T(8,128)(2,1)} %get-tuple-element.97), channel_id=1, source_target_pairs={{0,8},{4,12},{8,0},{12,4},{1,9},{5,13},{9,1},{13,5},{2,10},{6,14},... | collective-permute-start | bytes 1179656 | tf_op jit(solution)/shard_map/ppermute | solution.py:963
  160.6 19.2 %collective-permute-start.8 = (bf16[192,1024]{1,0:T(8,128)(2,1)}, bf16[192,1024]{1,0:T(8,128)(2,1)S(1)}, u32[]{:S(2)}, u32[]{:S(2)}) collective-permute-start(bf16[192,1024]{1,0:T(8,128)(2,1)} %get-tuple-element.98), channel_id=1, source_target_pairs={{0,12},{4,8},{8,4},{12,0},{1,13},{5,9},{9,5},{13,1},{2,14},{6,10},... | collective-permute-start | bytes 1179656 | tf_op jit(solution)/shard_map/ppermute | solution.py:963
  179.8 1.0 copy-start.8
  241.0 10.5 %collective-permute-start.9 = (bf16[1024,768]{1,0:T(8,128)(2,1)}, bf16[1024,768]{1,0:T(8,128)(2,1)}, u32[]{:S(2)}, u32[]{:S(2)}) collective-permute-start(bf16[1024,768]{1,0:T(8,128)(2,1)} %get-tuple-element.112), channel_id=1, source_target_pairs={{0,4},{4,0},{8,12},{12,8},{1,5},{5,1},{9,13},{13,9},{2,6},{6,2},{1... | collective-permute-start | bytes 4718600 | tf_op jit(solution)/shard_map/ppermute | solution.py:963
  241.9 9.6 %copy-start.2 = (bf16[1024,768]{1,0:T(8,128)(2,1)S(1)}, bf16[1024,768]{1,0:T(8,128)(2,1)}, u32[]{:S(2)}) copy-start(bf16[1024,768]{1,0:T(8,128)(2,1)} %get-tuple-element.111) | copy-start | bytes 4718596
  254.5 38.3 %all-to-all-start.1 = ((bf16[32,24,640]{2,1,0:T(8,128)(2,1)}), bf16[32,24,640]{2,1,0:T(8,128)(2,1)}, u32[]{:S(2)}, u32[]{:S(2)}) async-start(bf16[32,24,640]{2,1,0:T(8,128)(2,1)} %projection_gradients.1), calls=%async_computation.2 | async-start | bytes 1966080 | tf_op jit(solution)/shard_map/all_to_all | solution.py:1089
  258.0 53.7 %reduce-scatter.5.cloned.1.call-start = ((), (), s32[]{:S(2)}) async-start(), calls=%async_computation.5 | async-start | bytes 1720320 | tf_op jit(solution)/shard_map/reduce_scatter | solution.py:1082
  258.1 47.6 %collective-permute-start.10 = (bf16[1024,768]{1,0:T(8,128)(2,1)}, bf16[1024,768]{1,0:T(8,128)(2,1)S(1)}, u32[]{:S(2)}, u32[]{:S(2)}) collective-permute-start(bf16[1024,768]{1,0:T(8,128)(2,1)} %add_convert_fusion), channel_id=1, source_target_pairs={{0,8},{4,12},{8,0},{12,4},{1,9},{5,13},{9,1},{13,5},{2,10},{6,14},... | collective-permute-start | bytes 4718600 | tf_op jit(solution)/shard_map/ppermute | solution.py:963
  259.9 45.8 %collective-permute-start.11 = (bf16[1024,768]{1,0:T(8,128)(2,1)}, bf16[1024,768]{1,0:T(8,128)(2,1)}, u32[]{:S(2)}, u32[]{:S(2)}) collective-permute-start(bf16[1024,768]{1,0:T(8,128)(2,1)} %get-tuple-element.114), channel_id=1, source_target_pairs={{0,4},{4,0},{8,12},{12,8},{1,5},{5,1},{9,13},{13,9},{2,6},{6,2},{1... | collective-permute-start | bytes 4718600 | tf_op jit(solution)/shard_map/ppermute | solution.py:963
  305.7 1.2 copy-start.1
  (2 other events, 1.6 us)
Sparse Core Ops, SparseCore 0:
  10.8 111.4 all-gather.2
  179.9 84.5 reduce-scatter.2
  266.8 38.0 reduce-scatter.4

commit v13 on v12

--- a/solution.py
+++ b/solution.py
@@ -931,27 +931,33 @@
     )(total)
 
 
-def total_kernel(base_ref, *refs):
+def total_kernel(pieces, base_ref, *refs):
     total = base_ref[...]
-    for ref in refs[:-1]:
+    for ref in refs[:pieces]:
         total = total + ref[...].astype(f32)
     refs[-1][...] = total
 
 
-def token_total(base, pieces):
+def token_total(base, whole_pieces, part, first, done=None):
     rows, width = base.shape
-    tile = 256
-    tall = pl.BlockSpec((tile, width), lambda i: (i, 0))
+    tile = 128
+    skip = first // tile
+    here = pl.BlockSpec((tile, width), lambda i: (i + skip, 0))
+    count = len(whole_pieces) + 1
+    args = [base, *whole_pieces, part] + ([] if done is None else [done])
     return pl.pallas_call(
-        total_kernel,
-        grid=(rows // tile,),
+        functools.partial(total_kernel, count),
+        grid=(part.shape[0] // tile,),
         out_shape=jax.ShapeDtypeStruct(base.shape, f32),
-        in_specs=[tall] * (1 + len(pieces)),
-        out_specs=tall,
+        in_specs=[here] * count
+        + [pl.BlockSpec((tile, width), lambda i: (i, 0))]
+        + ([] if done is None else [pl.BlockSpec(memory_space=pl.ANY)]),
+        out_specs=here,
+        input_output_aliases={} if done is None else {count + 1: 0},
         compiler_params=pltpu.CompilerParams(vmem_limit_bytes=VMEM_BYTES),
-        cost_estimate=pl.CostEstimate(flops=TOTAL_FLOPS, bytes_accessed=9_000_000, transcendentals=0),
+        cost_estimate=pl.CostEstimate(flops=TOTAL_FLOPS, bytes_accessed=5_000_000, transcendentals=0),
         name="token_total",
-    )(base, *pieces)
+    )(*args)
 
 
 TOTAL_FLOPS = 1_000_000_000
@@ -1080,12 +1086,18 @@
     bit = seq_n // 2
     staged = total
     total = lax.psum_scatter(total, "ffn", scatter_dimension=0, tiled=True)
-    pieces = []
+    half = rows // 2
+    first, second = part[bit][:half], part[bit][half:]
+    first, second = flip_send(first, "seq", bit), flip_send(second, "seq", bit)
+    bit //= 2
+    others = []
     while bit:
-        pieces.append(flip_send(part[bit], "seq", bit))
+        others.append(flip_send(part[bit], "seq", bit))
         bit //= 2
-    pieces = lax.optimization_barrier((pieces, staged))[0]
-    grad_features = token_total(grad_features, pieces)
+    first = lax.optimization_barrier((first, staged))[0]
+    base = grad_features
+    grad_features = token_total(base, others, first, 0)
+    grad_features = token_total(base, others, second, half, grad_features)
     grad_w = lax.all_to_all(grad_w, ALL, split_axis=0, concat_axis=0, tiled=True)
     if direct:
         out_up, out_down, out_output, notes = finished(total, up_rows, own)

time: 324 us -> 322 us (level)
  waiting for transfers between devices: 95.9 us -> 90.5 us
    all_to_all x1, waiting for transfers between devices: 28.3 us -> 10.6 us  [shards(): lax.all_to_all(grad_w, ALL, split_axis=0, concat_axis=0, tiled=True)]
    ppermute x12 -> x13, waiting for transfers between devices: 55.7 us -> 62.9 us  [flip_send(): return lax.ppermute(array, axis, [(i, i ^ bits) for i in range(count)])]
    reduce_scatter x1, waiting for transfers between devices: 4.63 us -> 9.67 us  [shards(): lax.psum_scatter(payload.reshape(-1, width), ('dp', 'seq'), scatter_dimen...]
    pallas_call x1 -> x2, Pallas kernels: 4.89 us -> 7.82 us  [token_total(): pl.pallas_call(functools.partial(total_kernel, count), grid=(part.shape[0...]
    ppermute x12 -> x13, starting transfers between devices: 10.2 us -> 10.3 us  [flip_send(): return lax.ppermute(array, axis, [(i, i ^ bits) for i in range(count)])]
  transfers between devices with their start and end apart: 17 -> 18, of which waited for: 7 -> 8; matrix products, arithmetic and copies ran while one was open for 5% -> 5% of each run, Pallas kernels for 41% -> 42%
where the time goes in v13:
time: 322 us; the launch traced here: 321 us
  Pallas kernels  176 us (55%)
  waiting for transfers between devices  90.5 us (28%)
  starting transfers between devices  19 us (6%)
  local copies, waits for them, and re-layouts  17.7 us (5%)
  between operations  13.9 us (4%)
  other arithmetic  3.42 us (1%)
    ppermute x13, waiting for transfers between devices, flip_send(): return lax.ppermute(array, axis, [(i, i ^ bits) for i in range(count)])  62.9 us
    pallas_call x1, Pallas kernels, attention_backward(): pl.pallas_call(functools.partial(backward_kernel, heads, chunks), out_sha...  60.2 us
    pallas_call x1, Pallas kernels, rows_chain(): pl.pallas_call(functools.partial(rows_kernel, parts, blocks, up_rows, own...  37.9 us
    pallas_call x1, Pallas kernels, attention_forward(): pl.pallas_call(functools.partial(forward_kernel, heads, chunks), out_shap...  23.8 us
    pallas_call x1, Pallas kernels, outer_products(): pl.pallas_call(functools.partial(outer_kernel, parts, up_rows, own, apart...  17.6 us
    pallas_call x1, Pallas kernels, attention_near(): pl.pallas_call(functools.partial(near_kernel, heads, chunks), out_shape=(...  11.6 us
    all_to_all x1, waiting for transfers between devices, shards(): lax.all_to_all(grad_w, ALL, split_axis=0, concat_axis=0, tiled=True)  10.6 us
    ppermute x13, starting transfers between devices, flip_send(): return lax.ppermute(array, axis, [(i, i ^ bits) for i in range(count)])  10.3 us
  transfers between devices with their start and end apart: 18, of which 8 were waited for; matrix products, arithmetic and copies ran while one was open for 5% of the time, Pallas kernels for 42%

profile of v13, /device:TPU:0, one launch (start us, length us, event | category | flops | bytes accessed | tf_op | source)
XLA Modules:
  0.0 320.7 jit_solution(9258301174664924361)
XLA Ops:
  7.2 1.8 rest_weights.1
  9.0 3.0 collective-permute-start.1
  19.3 1.9 packed_weights.1
  21.2 4.9 %all-to-all-start = ((bf16[32,24,640]{2,1,0:T(8,128)(2,1)}), bf16[32,24,640]{2,1,0:T(8,128)(2,1)S(1)}, u32[]{:S(2)}, u32[]{:S(2)}) async-start(bf16[32,24,640]{2,1,0:T(8,128)(2,1)} %bitcast.47), calls=%async_computation | async-start | bytes 1966080 | tf_op jit(solution)/shard_map/all_to_all | solution.py:1006
  26.5 39.4 %collective-permute-done.1.refs_2_ = bf16[1024,768]{1,0:T(8,128)(2,1)} collective-permute-done((bf16[1024,768]{1,0:T(8,128)(2,1)}, bf16[1024,768]{1,0:T(8,128)(2,1)}, u32[]{:S(2)}, u32[]{:S(2)}) %collective-permute-start.1) | collective-permute-done | bytes 1572896 | tf_op jit(solution)/shard_map/ppermute | solution.py:969
  65.9 4.3 %all-to-all-done = bf16[32,24,640]{2,1,0:T(8,128)(2,1)S(1)} async-done(((bf16[32,24,640]{2,1,0:T(8,128)(2,1)}), bf16[32,24,640]{2,1,0:T(8,128)(2,1)S(1)}, u32[]{:S(2)}, u32[]{:S(2)}) %all-to-all-start) | async-done | bytes 983072 | tf_op jit(solution)/shard_map/all_to_all | solution.py:1006
  71.9 23.8 %attention_forward.1 = (bf16[192,1024]{1,0:T(8,128)(2,1)}, bf16[192,1024]{1,0:T(8,128)(2,1)}, f32[3,16,128]{2,1,0:T(8,128)}, f32[3,128]{1,0:T(4,128)}, f32[3,64,...) custom-call(s32[1]{0:T(128)} %bitcast.me_ref, ...), custom_call_target="tpu_custom_call" | custom-call | flops 10000000000 | bytes 16000000 | tf_op jit(solution)/shard_map/attention_forward/pallas_call | solution.py:258
  96.5 11.6 %attention_near.1 = (bf16[192,1024]{1,0:T(8,128)(2,1)}, bf16[192,1024]{1,0:T(8,128)(2,1)}, f32[3,16,128]{2,1,0:T(8,128)}) custom-call(s32[1]{0:T(128)} %bitcast.me_ref, s32[576]{0:T(1024)} %reshape.65.rand_ref, s32[1,2]{1,0:T(1,128)} %glob_ref.5, bf16[4160,384]{1,0:T(8,128)(2,1)} %get-tuple-element.76.k_ref.refs_4_, ...), custom_call_target="tpu_custom_call" | custom-call | flops 6000000000 | bytes 9000000 | tf_op jit(solution)/shard_map/attention_near/pallas_call | solution.py:309
  112.5 6.8 %collective-permute-done.4.refs_3_ = bf16[192,1024]{1,0:T(8,128)(2,1)S(1)} collective-permute-done((bf16[192,1024]{1,0:T(8,128)(2,1)}, bf16[192,1024]{1,0:T(8,128)(2,1)S(1)}, u32[]{:S(2)}, u32[]{:S(2)}) %collective-permute-start.4) | collective-permute-done | bytes 393248 | tf_op jit(solution)/shard_map/ppermute | solution.py:969
  119.3 3.0 all-gather.3.cloned.1.call-done
  122.3 37.9 %rows_chain.1 = (bf16[1024,768]{1,0:T(8,128)(2,1)}, f32[1024,768]{1,0:T(8,128)}, bf16[4,1024,768]{2,1,0:T(8,128)(2,1)}, bf16[4,1024,768]{2,1,0:T(8,128)(2,1)}, b...) custom-call(s32[1]{0:T(128)} %bitcast.me_ref, ...), custom_call_target="tpu_custom_call" | custom-call | flops 22000001024 | bytes 40000000 | tf_op jit(solution)/shard_map/rows_chain/pallas_call | solution.py:815
  162.1 17.6 %outer_products.1 = bf16[8,4,224,768]{3,2,1,0:T(8,128)(2,1)} custom-call(s32[1]{0:T(128)} %bitcast.me_ref, bf16[192,1024]{1,0:T(8,128)(2,1)} %get-tuple-element.82.refs_0_, bf16[192,1024]{1,0:T(8,128)(2,1)} %copy-done.6, bf16[192,1024]{1,0:T(8,128)(2,1)} %copy-done.3, bf16[192,1024]{1,0:T(8,128)(2,1)} %copy-done.4, ...), custom_call_target="tpu_custom_call" | custom-call | flops 11000000512 | bytes 28000000 | tf_op jit(solution)/shard_map/outer_products/pallas_call | solution.py:889
  180.8 60.2 %attention_backward.1 = (bf16[4,192,1024]{2,1,0:T(8,128)(2,1)}, bf16[4,1024,384]{2,1,0:T(8,128)(2,1)}, f32[1024,768]{1,0:T(8,128)}, bf16[1024,768]{1,0:T(8,128)(...) custom-call(s32[1]{0:T(128)} %bitcast.me_ref, s32[576]{0:T(1024)} %reshape.65.rand_ref, s32[1,2]{1,0:T(1,128)} %glob_ref.5, ...), custom_call_target="tpu_custom_call" | custom-call | flops 30000001024 | bytes 24000000 | tf_op jit(solution)/shard_map/attention_backward/pallas_call | solution.py:491
  241.8 9.6 %projection_gradients.1 = bf16[32,24,640]{2,1,0:T(8,128)(2,1)} custom-call(bf16[1024,768]{1,0:T(8,128)(2,1)} %bitcast.10.refs_0_.refs_4_, bf16[1024,768]{1,0:T(8,128)(2,1)} %collective-permute-done.refs_1_, bf16[1024,768]{1,0:T(8,128)(2,1)} %collective-permute-done.1.refs_2_, bf16[1024,768]{1,0:T(8,128)(2,1)} %collective-permute-done.2.refs_3_, ...), custom_call_target="tpu_custom_call" | custom-call | flops 4000000000 | bytes 12000000 | tf_op jit(solution)/shard_map/projection_gradients/pallas_call | solution.py:649
  251.4 1.9 add_convert_fusion
  253.2 3.6 %all-to-all-start.1 = ((bf16[32,24,640]{2,1,0:T(8,128)(2,1)}), bf16[32,24,640]{2,1,0:T(8,128)(2,1)}, u32[]{:S(2)}, u32[]{:S(2)}) async-start(bf16[32,24,640]{2,1,0:T(8,128)(2,1)} %projection_gradients.1), calls=%async_computation.2 | async-start | bytes 1966080 | tf_op jit(solution)/shard_map/all_to_all | solution.py:1101
  260.2 9.7 %reduce-scatter.3.cloned.1.call-done = bf16[896,768]{1,0:T(8,128)(2,1)} async-done(((bf16[7168,768]{1,0:T(8,128)(2,1)}), bf16[896,768]{1,0:T(8,128)(2,1)}) %reduce-scatter.3.cloned.1.call-update) | async-done | bytes 1376272 | tf_op jit(solution)/shard_map/reduce_scatter | solution.py:1063
  269.9 10.6 %all-to-all-done.1 = bf16[32,24,640]{2,1,0:T(8,128)(2,1)} async-done(((bf16[32,24,640]{2,1,0:T(8,128)(2,1)}), bf16[32,24,640]{2,1,0:T(8,128)(2,1)}, u32[]{:S(2)}, u32[]{:S(2)}) %all-to-all-start.1) | async-done | bytes 983072 | tf_op jit(solution)/shard_map/all_to_all | solution.py:1101
  280.6 2.0 unpacked_gradients.1
  284.0 5.1 %collective-permute-done.12.refs_1_ = bf16[512,768]{1,0:T(8,128)(2,1)} collective-permute-done((bf16[512,768]{1,0:T(8,128)(2,1)}, bf16[512,768]{1,0:T(8,128)(2,1)}, u32[]{:S(2)}, u32[]{:S(2)}) %collective-permute-start.12) | collective-permute-done | bytes 786464 | tf_op jit(solution)/shard_map/ppermute | solution.py:969
  290.3 3.9 %token_total.2.refs_2_ = f32[1024,768]{1,0:T(8,128)} custom-call(f32[1024,768]{1,0:T(8,128)} %get-tuple-element.106.base_ref, bf16[1024,768]{1,0:T(8,128)(2,1)} %copy-done, bf16[512,768]{1,0:T(8,128)(2,1)} %collective-permute-done.12.refs_1_), custom_call_target="tpu_custom_call" | custom-call | flops 1000000000 | bytes 5000000 | tf_op jit(solution)/shard_map/token_total/pallas_call | solution.py:948
  294.2 11.6 %collective-permute-done.11.refs_1_ = bf16[512,768]{1,0:T(8,128)(2,1)} collective-permute-done((bf16[512,768]{1,0:T(8,128)(2,1)}, bf16[512,768]{1,0:T(8,128)(2,1)}, u32[]{:S(2)}, u32[]{:S(2)}) %collective-permute-start.11) | collective-permute-done | bytes 786464 | tf_op jit(solution)/shard_map/ppermute | solution.py:969
  305.8 3.9 %token_total.3 = f32[1024,768]{1,0:T(8,128)} custom-call(f32[1024,768]{1,0:T(8,128)} %get-tuple-element.106.base_ref, bf16[1024,768]{1,0:T(8,128)(2,1)} %copy-done, bf16[512,768]{1,0:T(8,128)(2,1)} %collective-permute-done.11.refs_1_, f32[1024,768]{1,0:T(8,128)} %token_total.2.refs_2_), custom_call_target="tpu_custom_call", output_to_operand_aliasing={{}: (3, {})} | custom-call | flops 1000000000 | bytes 5000000 | tf_op jit(solution)/shard_map/token_total/pallas_call | solution.py:948
  309.7 1.8 finished.1
  (75 shorter events, 26.8 us)
Async XLA Ops:
  7.2 115.1 %all-gather.3.cloned.1.call-start = ((), (), s32[]{:S(2)}) async-start(), calls=%async_computation.6 | async-start | bytes 10948608 | tf_op jit(solution)/shard_map/all_gather | solution.py:1009
  9.0 56.9 %collective-permute-start.1 = (bf16[1024,768]{1,0:T(8,128)(2,1)}, bf16[1024,768]{1,0:T(8,128)(2,1)}, u32[]{:S(2)}, u32[]{:S(2)}) collective-permute-start(bf16[1024,768]{1,0:T(8,128)(2,1)} %bitcast.10.refs_0_.refs_4_), channel_id=1, source_target_pairs={{0,8},{4,12},{8,0},{12,4},{1,9},{5,13},{9,1},{13,5},{2,10},{6,14},... | collective-permute-start | bytes 4718600 | tf_op jit(solution)/shard_map/ppermute | solution.py:969
  21.2 49.0 %all-to-all-start = ((bf16[32,24,640]{2,1,0:T(8,128)(2,1)}), bf16[32,24,640]{2,1,0:T(8,128)(2,1)S(1)}, u32[]{:S(2)}, u32[]{:S(2)}) async-start(bf16[32,24,640]{2,1,0:T(8,128)(2,1)} %bitcast.47), calls=%async_computation | async-start | bytes 1966080 | tf_op jit(solution)/shard_map/all_to_all | solution.py:1006
  26.1 243.8 %reduce-scatter.3.cloned.1.call-start = ((), (), s32[]{:S(2)}) async-start(), calls=%async_computation.4 | async-start | bytes 12386304 | tf_op jit(solution)/shard_map/reduce_scatter | solution.py:1063
  26.2 45.7 %collective-permute-start = (bf16[1024,768]{1,0:T(8,128)(2,1)}, bf16[1024,768]{1,0:T(8,128)(2,1)}, u32[]{:S(2)}, u32[]{:S(2)}) collective-permute-start(bf16[1024,768]{1,0:T(8,128)(2,1)} %bitcast.10.refs_0_.refs_4_), channel_id=1, source_target_pairs={{0,4},{4,0},{8,12},{12,8},{1,5},{5,1},{9,13},{13,9},{2,6},{6,2},{1... | collective-permute-start | bytes 4718600 | tf_op jit(solution)/shard_map/ppermute | solution.py:969
  65.9 6.0 %collective-permute-start.2 = (bf16[1024,768]{1,0:T(8,128)(2,1)}, bf16[1024,768]{1,0:T(8,128)(2,1)}, u32[]{:S(2)}, u32[]{:S(2)}) collective-permute-start(bf16[1024,768]{1,0:T(8,128)(2,1)} %collective-permute-done.1.refs_2_), channel_id=1, source_target_pairs={{0,4},{4,0},{8,12},{12,8},{1,5},{5,1},{9,13},{13,9},{2,6},{6,2},{1... | collective-permute-start | bytes 4718600 | tf_op jit(solution)/shard_map/ppermute | solution.py:969
  70.2 1.7 copy-start.1
  95.7 16.7 %collective-permute-start.3 = (bf16[192,1024]{1,0:T(8,128)(2,1)}, bf16[192,1024]{1,0:T(8,128)(2,1)S(1)}, u32[]{:S(2)}, u32[]{:S(2)}) collective-permute-start(bf16[192,1024]{1,0:T(8,128)(2,1)} %get-tuple-element.74), channel_id=1, source_target_pairs={{0,8},{4,12},{8,0},{12,4},{1,9},{5,13},{9,1},{13,5},{2,10},{6,14},... | collective-permute-start | bytes 1179656 | tf_op jit(solution)/shard_map/ppermute | solution.py:969
  96.4 22.9 %collective-permute-start.4 = (bf16[192,1024]{1,0:T(8,128)(2,1)}, bf16[192,1024]{1,0:T(8,128)(2,1)S(1)}, u32[]{:S(2)}, u32[]{:S(2)}) collective-permute-start(bf16[192,1024]{1,0:T(8,128)(2,1)} %get-tuple-element.75), channel_id=1, source_target_pairs={{0,12},{4,8},{8,4},{12,0},{1,13},{5,9},{9,5},{13,1},{2,14},{6,10},... | collective-permute-start | bytes 1179656 | tf_op jit(solution)/shard_map/ppermute | solution.py:969
  108.1 11.2 %collective-permute-start.5 = (bf16[192,1024]{1,0:T(8,128)(2,1)}, bf16[192,1024]{1,0:T(8,128)(2,1)S(1)}, u32[]{:S(2)}, u32[]{:S(2)}) collective-permute-start(bf16[192,1024]{1,0:T(8,128)(2,1)} %get-tuple-element.83), channel_id=1, source_target_pairs={{0,4},{4,0},{8,12},{12,8},{1,5},{5,1},{9,13},{13,9},{2,6},{6,2},{1... | collective-permute-start | bytes 1179656 | tf_op jit(solution)/shard_map/ppermute | solution.py:969
  112.5 9.8 %copy-start.3 = (bf16[192,1024]{1,0:T(8,128)(2,1)}, bf16[192,1024]{1,0:T(8,128)(2,1)S(1)}, u32[]{:S(2)}) copy-start(bf16[192,1024]{1,0:T(8,128)(2,1)S(1)} %collective-permute-done.3.refs_2_) | copy-start | bytes 1179652
  119.3 3.0 copy-start.4
  119.3 3.0 copy-start.6
  160.1 19.6 %collective-permute-start.6 = (bf16[192,1024]{1,0:T(8,128)(2,1)}, bf16[192,1024]{1,0:T(8,128)(2,1)S(1)}, u32[]{:S(2)}, u32[]{:S(2)}) collective-permute-start(bf16[192,1024]{1,0:T(8,128)(2,1)} %get-tuple-element.95), channel_id=1, source_target_pairs={{0,4},{4,0},{8,12},{12,8},{1,5},{5,1},{9,13},{13,9},{2,6},{6,2},{1... | collective-permute-start | bytes 1179656 | tf_op jit(solution)/shard_map/ppermute | solution.py:969
  160.5 19.3 %collective-permute-start.7 = (bf16[192,1024]{1,0:T(8,128)(2,1)}, bf16[192,1024]{1,0:T(8,128)(2,1)S(1)}, u32[]{:S(2)}, u32[]{:S(2)}) collective-permute-start(bf16[192,1024]{1,0:T(8,128)(2,1)} %get-tuple-element.96), channel_id=1, source_target_pairs={{0,8},{4,12},{8,0},{12,4},{1,9},{5,13},{9,1},{13,5},{2,10},{6,14},... | collective-permute-start | bytes 1179656 | tf_op jit(solution)/shard_map/ppermute | solution.py:969
  160.5 19.3 %collective-permute-start.8 = (bf16[192,1024]{1,0:T(8,128)(2,1)}, bf16[192,1024]{1,0:T(8,128)(2,1)S(1)}, u32[]{:S(2)}, u32[]{:S(2)}) collective-permute-start(bf16[192,1024]{1,0:T(8,128)(2,1)} %get-tuple-element.97), channel_id=1, source_target_pairs={{0,12},{4,8},{8,4},{12,0},{1,13},{5,9},{9,5},{13,1},{2,14},{6,10},... | collective-permute-start | bytes 1179656 | tf_op jit(solution)/shard_map/ppermute | solution.py:969
  241.0 10.4 %collective-permute-start.9 = (bf16[1024,768]{1,0:T(8,128)(2,1)}, bf16[1024,768]{1,0:T(8,128)(2,1)}, u32[]{:S(2)}, u32[]{:S(2)}) collective-permute-start(bf16[1024,768]{1,0:T(8,128)(2,1)} %get-tuple-element.111), channel_id=1, source_target_pairs={{0,4},{4,0},{8,12},{12,8},{1,5},{5,1},{9,13},{13,9},{2,6},{6,2},{1... | collective-permute-start | bytes 4718600 | tf_op jit(solution)/shard_map/ppermute | solution.py:969
  241.8 9.6 %copy-start.2 = (bf16[1024,768]{1,0:T(8,128)(2,1)S(1)}, bf16[1024,768]{1,0:T(8,128)(2,1)}, u32[]{:S(2)}) copy-start(bf16[1024,768]{1,0:T(8,128)(2,1)} %get-tuple-element.110) | copy-start | bytes 4718596
  253.2 27.3 %all-to-all-start.1 = ((bf16[32,24,640]{2,1,0:T(8,128)(2,1)}), bf16[32,24,640]{2,1,0:T(8,128)(2,1)}, u32[]{:S(2)}, u32[]{:S(2)}) async-start(bf16[32,24,640]{2,1,0:T(8,128)(2,1)} %projection_gradients.1), calls=%async_computation.2 | async-start | bytes 1966080 | tf_op jit(solution)/shard_map/all_to_all | solution.py:1101
  256.9 52.8 %reduce-scatter.5.cloned.1.call-start = ((), (), s32[]{:S(2)}) async-start(), calls=%async_computation.5 | async-start | bytes 1720320 | tf_op jit(solution)/shard_map/reduce_scatter | solution.py:1088
  258.2 30.9 %collective-permute-start.12 = (bf16[512,768]{1,0:T(8,128)(2,1)}, bf16[512,768]{1,0:T(8,128)(2,1)}, u32[]{:S(2)}, u32[]{:S(2)}) collective-permute-start(bf16[512,768]{1,0:T(8,128)(2,1)} %get-tuple-element.127), channel_id=1, source_target_pairs={{0,8},{4,12},{8,0},{12,4},{1,9},{5,13},{9,1},{13,5},{2,10},{6,14},... | collective-permute-start | bytes 2359304 | tf_op jit(solution)/shard_map/ppermute | solution.py:969
  259.9 45.9 %collective-permute-start.11 = (bf16[512,768]{1,0:T(8,128)(2,1)}, bf16[512,768]{1,0:T(8,128)(2,1)}, u32[]{:S(2)}, u32[]{:S(2)}) collective-permute-start(bf16[512,768]{1,0:T(8,128)(2,1)} %get-tuple-element.128), channel_id=1, source_target_pairs={{0,8},{4,12},{8,0},{12,4},{1,9},{5,13},{9,1},{13,5},{2,10},{6,14},... | collective-permute-start | bytes 2359304 | tf_op jit(solution)/shard_map/ppermute | solution.py:969
  260.2 28.9 %collective-permute-start.10 = (bf16[1024,768]{1,0:T(8,128)(2,1)}, bf16[1024,768]{1,0:T(8,128)(2,1)S(1)}, u32[]{:S(2)}, u32[]{:S(2)}) collective-permute-start(bf16[1024,768]{1,0:T(8,128)(2,1)} %get-tuple-element.112), channel_id=1, source_target_pairs={{0,4},{4,0},{8,12},{12,8},{1,5},{5,1},{9,13},{13,9},{2,6},{6,2},{1... | collective-permute-start | bytes 4718600 | tf_op jit(solution)/shard_map/ppermute | solution.py:969
  289.1 1.2 copy-start
  (3 other events, 2.6 us)
Sparse Core Ops, SparseCore 0:
  10.8 111.3 all-gather.2
  179.9 89.9 reduce-scatter.2
  272.2 32.2 reduce-scatter.4

commit v14 on v13

--- a/solution.py
+++ b/solution.py
@@ -1086,7 +1086,7 @@
     bit = seq_n // 2
     staged = total
     total = lax.psum_scatter(total, "ffn", scatter_dimension=0, tiled=True)
-    half = rows // 2
+    half = rows * 3 // 4
     first, second = part[bit][:half], part[bit][half:]
     first, second = flip_send(first, "seq", bit), flip_send(second, "seq", bit)
     bit //= 2

time: 322 us -> 327 us (1.016)
  waiting for transfers between devices: 90.5 us -> 95.1 us
    ppermute x13, waiting for transfers between devices: 62.9 us -> 68 us  [flip_send(): return lax.ppermute(array, axis, [(i, i ^ bits) for i in range(count)])]
  transfers between devices with their start and end apart: 18 -> 18, of which waited for: 8 -> 7; matrix products, arithmetic and copies ran while one was open for 5% -> 5% of each run, Pallas kernels for 42% -> 41%
where the time goes in v14:
time: 327 us; the launch traced here: 326 us
  Pallas kernels  176 us (54%)
  waiting for transfers between devices  95.1 us (29%)
  local copies, waits for them, and re-layouts  19.1 us (6%)
  starting transfers between devices  19 us (6%)
  between operations  14 us (4%)
  other arithmetic  3.42 us (1%)
    ppermute x13, waiting for transfers between devices, flip_send(): return lax.ppermute(array, axis, [(i, i ^ bits) for i in range(count)])  68 us
    pallas_call x1, Pallas kernels, attention_backward(): pl.pallas_call(functools.partial(backward_kernel, heads, chunks), out_sha...  60.2 us
    pallas_call x1, Pallas kernels, rows_chain(): pl.pallas_call(functools.partial(rows_kernel, parts, blocks, up_rows, own...  37.9 us
    pallas_call x1, Pallas kernels, attention_forward(): pl.pallas_call(functools.partial(forward_kernel, heads, chunks), out_shap...  23.8 us
    pallas_call x1, Pallas kernels, outer_products(): pl.pallas_call(functools.partial(outer_kernel, parts, up_rows, own, apart...  17.6 us
    pallas_call x1, Pallas kernels, attention_near(): pl.pallas_call(functools.partial(near_kernel, heads, chunks), out_shape=(...  11.6 us
    all_to_all x1, waiting for transfers between devices, shards(): lax.all_to_all(grad_w, ALL, split_axis=0, concat_axis=0, tiled=True)  10.6 us
    ppermute x13, starting transfers between devices, flip_send(): return lax.ppermute(array, axis, [(i, i ^ bits) for i in range(count)])  10.3 us
  transfers between devices with their start and end apart: 18, of which 7 were waited for; matrix products, arithmetic and copies ran while one was open for 5% of the time, Pallas kernels for 41%

profile of v14, /device:TPU:0, one launch (start us, length us, event | category | flops | bytes accessed | tf_op | source)
XLA Modules:
  0.0 326.4 jit_solution(4444417934965484807)
XLA Ops:
  7.2 1.8 rest_weights.1
  9.0 3.0 collective-permute-start.1
  19.3 1.9 packed_weights.1
  21.2 4.9 %all-to-all-start = ((bf16[32,24,640]{2,1,0:T(8,128)(2,1)}), bf16[32,24,640]{2,1,0:T(8,128)(2,1)S(1)}, u32[]{:S(2)}, u32[]{:S(2)}) async-start(bf16[32,24,640]{2,1,0:T(8,128)(2,1)} %bitcast.47), calls=%async_computation | async-start | bytes 1966080 | tf_op jit(solution)/shard_map/all_to_all | solution.py:1006
  26.5 39.4 %collective-permute-done.1.refs_2_ = bf16[1024,768]{1,0:T(8,128)(2,1)} collective-permute-done((bf16[1024,768]{1,0:T(8,128)(2,1)}, bf16[1024,768]{1,0:T(8,128)(2,1)}, u32[]{:S(2)}, u32[]{:S(2)}) %collective-permute-start.1) | collective-permute-done | bytes 1572896 | tf_op jit(solution)/shard_map/ppermute | solution.py:969
  65.9 4.3 %all-to-all-done = bf16[32,24,640]{2,1,0:T(8,128)(2,1)S(1)} async-done(((bf16[32,24,640]{2,1,0:T(8,128)(2,1)}), bf16[32,24,640]{2,1,0:T(8,128)(2,1)S(1)}, u32[]{:S(2)}, u32[]{:S(2)}) %all-to-all-start) | async-done | bytes 983072 | tf_op jit(solution)/shard_map/all_to_all | solution.py:1006
  71.9 23.8 %attention_forward.1 = (bf16[192,1024]{1,0:T(8,128)(2,1)}, bf16[192,1024]{1,0:T(8,128)(2,1)}, f32[3,16,128]{2,1,0:T(8,128)}, f32[3,128]{1,0:T(4,128)}, f32[3,64,...) custom-call(s32[1]{0:T(128)} %bitcast.me_ref, ...), custom_call_target="tpu_custom_call" | custom-call | flops 10000000000 | bytes 16000000 | tf_op jit(solution)/shard_map/attention_forward/pallas_call | solution.py:258
  96.5 11.6 %attention_near.1 = (bf16[192,1024]{1,0:T(8,128)(2,1)}, bf16[192,1024]{1,0:T(8,128)(2,1)}, f32[3,16,128]{2,1,0:T(8,128)}) custom-call(s32[1]{0:T(128)} %bitcast.me_ref, s32[576]{0:T(1024)} %reshape.65.rand_ref, s32[1,2]{1,0:T(1,128)} %glob_ref.5, bf16[4160,384]{1,0:T(8,128)(2,1)} %get-tuple-element.76.k_ref.refs_4_, ...), custom_call_target="tpu_custom_call" | custom-call | flops 6000000000 | bytes 9000000 | tf_op jit(solution)/shard_map/attention_near/pallas_call | solution.py:309
  112.5 6.8 %collective-permute-done.4.refs_3_ = bf16[192,1024]{1,0:T(8,128)(2,1)S(1)} collective-permute-done((bf16[192,1024]{1,0:T(8,128)(2,1)}, bf16[192,1024]{1,0:T(8,128)(2,1)S(1)}, u32[]{:S(2)}, u32[]{:S(2)}) %collective-permute-start.4) | collective-permute-done | bytes 393248 | tf_op jit(solution)/shard_map/ppermute | solution.py:969
  119.3 3.0 all-gather.3.cloned.1.call-done
  122.3 37.9 %rows_chain.1 = (bf16[1024,768]{1,0:T(8,128)(2,1)}, f32[1024,768]{1,0:T(8,128)}, bf16[4,1024,768]{2,1,0:T(8,128)(2,1)}, bf16[4,1024,768]{2,1,0:T(8,128)(2,1)}, b...) custom-call(s32[1]{0:T(128)} %bitcast.me_ref, ...), custom_call_target="tpu_custom_call" | custom-call | flops 22000001024 | bytes 40000000 | tf_op jit(solution)/shard_map/rows_chain/pallas_call | solution.py:815
  162.1 17.6 %outer_products.1 = bf16[8,4,224,768]{3,2,1,0:T(8,128)(2,1)} custom-call(s32[1]{0:T(128)} %bitcast.me_ref, bf16[192,1024]{1,0:T(8,128)(2,1)} %get-tuple-element.82.refs_0_, bf16[192,1024]{1,0:T(8,128)(2,1)} %copy-done.7, bf16[192,1024]{1,0:T(8,128)(2,1)} %copy-done.4, bf16[192,1024]{1,0:T(8,128)(2,1)} %copy-done.5, ...), custom_call_target="tpu_custom_call" | custom-call | flops 11000000512 | bytes 28000000 | tf_op jit(solution)/shard_map/outer_products/pallas_call | solution.py:889
  180.8 60.2 %attention_backward.1 = (bf16[4,192,1024]{2,1,0:T(8,128)(2,1)}, bf16[4,1024,384]{2,1,0:T(8,128)(2,1)}, f32[1024,768]{1,0:T(8,128)}, bf16[1024,768]{1,0:T(8,128)(...) custom-call(s32[1]{0:T(128)} %bitcast.me_ref, s32[576]{0:T(1024)} %reshape.65.rand_ref, s32[1,2]{1,0:T(1,128)} %glob_ref.5, ...), custom_call_target="tpu_custom_call" | custom-call | flops 30000001024 | bytes 24000000 | tf_op jit(solution)/shard_map/attention_backward/pallas_call | solution.py:491
  241.8 9.6 %projection_gradients.1 = bf16[32,24,640]{2,1,0:T(8,128)(2,1)} custom-call(bf16[1024,768]{1,0:T(8,128)(2,1)} %bitcast.10.refs_0_.refs_4_, bf16[1024,768]{1,0:T(8,128)(2,1)} %collective-permute-done.refs_1_, bf16[1024,768]{1,0:T(8,128)(2,1)} %collective-permute-done.1.refs_2_, bf16[1024,768]{1,0:T(8,128)(2,1)} %collective-permute-done.2.refs_3_, ...), custom_call_target="tpu_custom_call" | custom-call | flops 4000000000 | bytes 12000000 | tf_op jit(solution)/shard_map/projection_gradients/pallas_call | solution.py:649
  251.4 1.9 add_convert_fusion
  253.3 3.6 %all-to-all-start.1 = ((bf16[32,24,640]{2,1,0:T(8,128)(2,1)}), bf16[32,24,640]{2,1,0:T(8,128)(2,1)}, u32[]{:S(2)}, u32[]{:S(2)}) async-start(bf16[32,24,640]{2,1,0:T(8,128)(2,1)} %projection_gradients.1), calls=%async_computation.2 | async-start | bytes 1966080 | tf_op jit(solution)/shard_map/all_to_all | solution.py:1101
  258.8 1.7 collective-permute-start.11
  260.8 9.1 %reduce-scatter.3.cloned.1.call-done = bf16[896,768]{1,0:T(8,128)(2,1)} async-done(((bf16[7168,768]{1,0:T(8,128)(2,1)}), bf16[896,768]{1,0:T(8,128)(2,1)}) %reduce-scatter.3.cloned.1.call-update) | async-done | bytes 1376272 | tf_op jit(solution)/shard_map/reduce_scatter | solution.py:1063
  269.9 10.6 %all-to-all-done.1 = bf16[32,24,640]{2,1,0:T(8,128)(2,1)} async-done(((bf16[32,24,640]{2,1,0:T(8,128)(2,1)}), bf16[32,24,640]{2,1,0:T(8,128)(2,1)}, u32[]{:S(2)}, u32[]{:S(2)}) %all-to-all-start.1) | async-done | bytes 983072 | tf_op jit(solution)/shard_map/all_to_all | solution.py:1101
  280.6 2.0 unpacked_gradients.1
  284.0 21.8 %collective-permute-done.12.refs_1_ = bf16[768,768]{1,0:T(8,128)(2,1)} collective-permute-done((bf16[768,768]{1,0:T(8,128)(2,1)}, bf16[768,768]{1,0:T(8,128)(2,1)}, u32[]{:S(2)}, u32[]{:S(2)}) %collective-permute-start.12) | collective-permute-done | bytes 1179680 | tf_op jit(solution)/shard_map/ppermute | solution.py:969
  307.0 5.4 %token_total.2.refs_2_ = f32[1024,768]{1,0:T(8,128)} custom-call(f32[1024,768]{1,0:T(8,128)} %get-tuple-element.106.base_ref, bf16[1024,768]{1,0:T(8,128)(2,1)} %copy-done, bf16[768,768]{1,0:T(8,128)(2,1)} %collective-permute-done.12.refs_1_), custom_call_target="tpu_custom_call" | custom-call | flops 1000000000 | bytes 5000000 | tf_op jit(solution)/shard_map/token_total/pallas_call | solution.py:948
  313.2 2.2 token_total.3
  315.4 1.8 finished.1
  (78 shorter events, 26.5 us)
Async XLA Ops:
  7.2 115.1 %all-gather.3.cloned.1.call-start = ((), (), s32[]{:S(2)}) async-start(), calls=%async_computation.6 | async-start | bytes 10948608 | tf_op jit(solution)/shard_map/all_gather | solution.py:1009
  9.0 56.9 %collective-permute-start.1 = (bf16[1024,768]{1,0:T(8,128)(2,1)}, bf16[1024,768]{1,0:T(8,128)(2,1)}, u32[]{:S(2)}, u32[]{:S(2)}) collective-permute-start(bf16[1024,768]{1,0:T(8,128)(2,1)} %bitcast.10.refs_0_.refs_4_), channel_id=1, source_target_pairs={{0,8},{4,12},{8,0},{12,4},{1,9},{5,13},{9,1},{13,5},{2,10},{6,14},... | collective-permute-start | bytes 4718600 | tf_op jit(solution)/shard_map/ppermute | solution.py:969
  21.2 49.0 %all-to-all-start = ((bf16[32,24,640]{2,1,0:T(8,128)(2,1)}), bf16[32,24,640]{2,1,0:T(8,128)(2,1)S(1)}, u32[]{:S(2)}, u32[]{:S(2)}) async-start(bf16[32,24,640]{2,1,0:T(8,128)(2,1)} %bitcast.47), calls=%async_computation | async-start | bytes 1966080 | tf_op jit(solution)/shard_map/all_to_all | solution.py:1006
  26.1 243.8 %reduce-scatter.3.cloned.1.call-start = ((), (), s32[]{:S(2)}) async-start(), calls=%async_computation.4 | async-start | bytes 12386304 | tf_op jit(solution)/shard_map/reduce_scatter | solution.py:1063
  26.2 45.7 %collective-permute-start = (bf16[1024,768]{1,0:T(8,128)(2,1)}, bf16[1024,768]{1,0:T(8,128)(2,1)}, u32[]{:S(2)}, u32[]{:S(2)}) collective-permute-start(bf16[1024,768]{1,0:T(8,128)(2,1)} %bitcast.10.refs_0_.refs_4_), channel_id=1, source_target_pairs={{0,4},{4,0},{8,12},{12,8},{1,5},{5,1},{9,13},{13,9},{2,6},{6,2},{1... | collective-permute-start | bytes 4718600 | tf_op jit(solution)/shard_map/ppermute | solution.py:969
  65.9 6.0 %collective-permute-start.2 = (bf16[1024,768]{1,0:T(8,128)(2,1)}, bf16[1024,768]{1,0:T(8,128)(2,1)}, u32[]{:S(2)}, u32[]{:S(2)}) collective-permute-start(bf16[1024,768]{1,0:T(8,128)(2,1)} %collective-permute-done.1.refs_2_), channel_id=1, source_target_pairs={{0,4},{4,0},{8,12},{12,8},{1,5},{5,1},{9,13},{13,9},{2,6},{6,2},{1... | collective-permute-start | bytes 4718600 | tf_op jit(solution)/shard_map/ppermute | solution.py:969
  70.2 1.7 copy-start.1
  95.7 16.7 %collective-permute-start.3 = (bf16[192,1024]{1,0:T(8,128)(2,1)}, bf16[192,1024]{1,0:T(8,128)(2,1)S(1)}, u32[]{:S(2)}, u32[]{:S(2)}) collective-permute-start(bf16[192,1024]{1,0:T(8,128)(2,1)} %get-tuple-element.74), channel_id=1, source_target_pairs={{0,8},{4,12},{8,0},{12,4},{1,9},{5,13},{9,1},{13,5},{2,10},{6,14},... | collective-permute-start | bytes 1179656 | tf_op jit(solution)/shard_map/ppermute | solution.py:969
  96.3 22.9 %collective-permute-start.4 = (bf16[192,1024]{1,0:T(8,128)(2,1)}, bf16[192,1024]{1,0:T(8,128)(2,1)S(1)}, u32[]{:S(2)}, u32[]{:S(2)}) collective-permute-start(bf16[192,1024]{1,0:T(8,128)(2,1)} %get-tuple-element.75), channel_id=1, source_target_pairs={{0,12},{4,8},{8,4},{12,0},{1,13},{5,9},{9,5},{13,1},{2,14},{6,10},... | collective-permute-start | bytes 1179656 | tf_op jit(solution)/shard_map/ppermute | solution.py:969
  108.1 11.2 %collective-permute-start.5 = (bf16[192,1024]{1,0:T(8,128)(2,1)}, bf16[192,1024]{1,0:T(8,128)(2,1)S(1)}, u32[]{:S(2)}, u32[]{:S(2)}) collective-permute-start(bf16[192,1024]{1,0:T(8,128)(2,1)} %get-tuple-element.83), channel_id=1, source_target_pairs={{0,4},{4,0},{8,12},{12,8},{1,5},{5,1},{9,13},{13,9},{2,6},{6,2},{1... | collective-permute-start | bytes 1179656 | tf_op jit(solution)/shard_map/ppermute | solution.py:969
  112.5 9.8 %copy-start.4 = (bf16[192,1024]{1,0:T(8,128)(2,1)}, bf16[192,1024]{1,0:T(8,128)(2,1)S(1)}, u32[]{:S(2)}) copy-start(bf16[192,1024]{1,0:T(8,128)(2,1)S(1)} %collective-permute-done.3.refs_2_) | copy-start | bytes 1179652
  119.3 3.0 copy-start.5
  119.3 3.0 copy-start.7
  160.2 19.6 %collective-permute-start.6 = (bf16[192,1024]{1,0:T(8,128)(2,1)}, bf16[192,1024]{1,0:T(8,128)(2,1)S(1)}, u32[]{:S(2)}, u32[]{:S(2)}) collective-permute-start(bf16[192,1024]{1,0:T(8,128)(2,1)} %get-tuple-element.95), channel_id=1, source_target_pairs={{0,4},{4,0},{8,12},{12,8},{1,5},{5,1},{9,13},{13,9},{2,6},{6,2},{1... | collective-permute-start | bytes 1179656 | tf_op jit(solution)/shard_map/ppermute | solution.py:969
  160.5 19.3 %collective-permute-start.7 = (bf16[192,1024]{1,0:T(8,128)(2,1)}, bf16[192,1024]{1,0:T(8,128)(2,1)S(1)}, u32[]{:S(2)}, u32[]{:S(2)}) collective-permute-start(bf16[192,1024]{1,0:T(8,128)(2,1)} %get-tuple-element.96), channel_id=1, source_target_pairs={{0,8},{4,12},{8,0},{12,4},{1,9},{5,13},{9,1},{13,5},{2,10},{6,14},... | collective-permute-start | bytes 1179656 | tf_op jit(solution)/shard_map/ppermute | solution.py:969
  160.5 19.3 %collective-permute-start.8 = (bf16[192,1024]{1,0:T(8,128)(2,1)}, bf16[192,1024]{1,0:T(8,128)(2,1)S(1)}, u32[]{:S(2)}, u32[]{:S(2)}) collective-permute-start(bf16[192,1024]{1,0:T(8,128)(2,1)} %get-tuple-element.97), channel_id=1, source_target_pairs={{0,12},{4,8},{8,4},{12,0},{1,13},{5,9},{9,5},{13,1},{2,14},{6,10},... | collective-permute-start | bytes 1179656 | tf_op jit(solution)/shard_map/ppermute | solution.py:969
  241.0 10.3 %collective-permute-start.9 = (bf16[1024,768]{1,0:T(8,128)(2,1)}, bf16[1024,768]{1,0:T(8,128)(2,1)}, u32[]{:S(2)}, u32[]{:S(2)}) collective-permute-start(bf16[1024,768]{1,0:T(8,128)(2,1)} %get-tuple-element.111), channel_id=1, source_target_pairs={{0,4},{4,0},{8,12},{12,8},{1,5},{5,1},{9,13},{13,9},{2,6},{6,2},{1... | collective-permute-start | bytes 4718600 | tf_op jit(solution)/shard_map/ppermute | solution.py:969
  241.8 9.6 %copy-start.2 = (bf16[1024,768]{1,0:T(8,128)(2,1)S(1)}, bf16[1024,768]{1,0:T(8,128)(2,1)}, u32[]{:S(2)}) copy-start(bf16[1024,768]{1,0:T(8,128)(2,1)} %get-tuple-element.110) | copy-start | bytes 4718596
  253.3 27.3 %all-to-all-start.1 = ((bf16[32,24,640]{2,1,0:T(8,128)(2,1)}), bf16[32,24,640]{2,1,0:T(8,128)(2,1)}, u32[]{:S(2)}, u32[]{:S(2)}) async-start(bf16[32,24,640]{2,1,0:T(8,128)(2,1)} %projection_gradients.1), calls=%async_computation.2 | async-start | bytes 1966080 | tf_op jit(solution)/shard_map/all_to_all | solution.py:1101
  256.9 58.5 %reduce-scatter.5.cloned.1.call-start = ((), (), s32[]{:S(2)}) async-start(), calls=%async_computation.5 | async-start | bytes 1720320 | tf_op jit(solution)/shard_map/reduce_scatter | solution.py:1088
  258.8 53.6 %collective-permute-start.11 = (bf16[256,768]{1,0:T(8,128)(2,1)}, bf16[256,768]{1,0:T(8,128)(2,1)S(1)}, u32[]{:S(2)}, u32[]{:S(2)}) collective-permute-start(bf16[256,768]{1,0:T(8,128)(2,1)} %slice.52), channel_id=1, source_target_pairs={{0,8},{4,12},{8,0},{12,4},{1,9},{5,13},{9,1},{13,5},{2,10},{6,14},... | collective-permute-start | bytes 1179656 | tf_op jit(solution)/shard_map/ppermute | solution.py:969
  260.5 45.3 %collective-permute-start.12 = (bf16[768,768]{1,0:T(8,128)(2,1)}, bf16[768,768]{1,0:T(8,128)(2,1)}, u32[]{:S(2)}, u32[]{:S(2)}) collective-permute-start(bf16[768,768]{1,0:T(8,128)(2,1)} %slice.53), channel_id=1, source_target_pairs={{0,8},{4,12},{8,0},{12,4},{1,9},{5,13},{9,1},{13,5},{2,10},{6,14},... | collective-permute-start | bytes 3538952 | tf_op jit(solution)/shard_map/ppermute | solution.py:969
  260.8 45.0 %collective-permute-start.10 = (bf16[1024,768]{1,0:T(8,128)(2,1)}, bf16[1024,768]{1,0:T(8,128)(2,1)S(1)}, u32[]{:S(2)}, u32[]{:S(2)}) collective-permute-start(bf16[1024,768]{1,0:T(8,128)(2,1)} %get-tuple-element.112), channel_id=1, source_target_pairs={{0,4},{4,0},{8,12},{12,8},{1,5},{5,1},{9,13},{13,9},{2,6},{6,2},{1... | collective-permute-start | bytes 4718600 | tf_op jit(solution)/shard_map/ppermute | solution.py:969
  305.8 1.2 copy-start
  (4 other events, 3.4 us)
Sparse Core Ops, SparseCore 0:
  10.8 111.4 all-gather.2
  179.9 89.9 reduce-scatter.2
  272.2 32.2 reduce-scatter.4
